TPU v7x, 32 devices: a whole 2x2x4 slice. The times are simulated.
32 devices in a mesh: wide: 8 (over z, y), narrow: 4 (over x, core).
Axes of the slice: x: 2, y: 2, z: 4, core: 2. Of those that a mesh axis runs over, the one named last changes fastest.
Arguments:
- inputs: bfloat16 [32768, 768], P(('wide', 'narrow')), may hold values from -6 to 6
- w_qkv: bfloat16 [768, 2304], P(('wide', 'narrow')), may hold values from -0.21875 to 0.21875
- qv_bias: bfloat16 [1536], P(('wide', 'narrow')), may hold values from -3 to 3
- w_out: bfloat16 [768, 768], P(('wide', 'narrow')), may hold values from -0.875 to 0.875
- out_bias: bfloat16 [768], P(('wide', 'narrow')), may hold values from -3 to 3
- ln1_gain: bfloat16 [768], P(('wide', 'narrow')), may hold values from 0.5 to 1.5
- ln1_shift: bfloat16 [768], P(('wide', 'narrow')), may hold values from -3 to 3
- ln2_gain: bfloat16 [768], P(('wide', 'narrow')), may hold values from 0.5 to 1.5
- ln2_shift: bfloat16 [768], P(('wide', 'narrow')), may hold values from -3 to 3
- w_up: bfloat16 [768, 3072], P(('wide', 'narrow')), may hold values from -0.21875 to 0.21875
- up_bias: bfloat16 [3072], P(('wide', 'narrow')), may hold values from -3 to 3
- w_down: bfloat16 [3072, 768], P(('wide', 'narrow')), may hold values from -0.109375 to 0.109375
- down_bias: bfloat16 [768], P(('wide', 'narrow')), may hold values from -3 to 3
- segment_ids: int32 [64, 512], P(('wide', 'narrow')), may hold values from 0 to 10, as said below
- valid: int32 [64, 512], P(('wide', 'narrow')), may hold values from 0 to 1, as said below
- cotangent: bfloat16 [32768, 768], P(('wide', 'narrow')), may hold values from -6 to 6
Outputs:
- block_out: bfloat16 [32768, 768], P(('wide', 'narrow'))
- grad_inputs: float32 [32768, 768], P(('wide', 'narrow'))
- grad_w_qkv: float32 [768, 2304], P(('wide', 'narrow'))
- grad_qv_bias: float32 [1536], P(('wide', 'narrow'))
- grad_w_out: float32 [768, 768], P(('wide', 'narrow'))
- grad_out_bias: float32 [768], P(('wide', 'narrow'))
- grad_ln1_gain: float32 [768], P(('wide', 'narrow'))
- grad_ln1_shift: float32 [768], P(('wide', 'narrow'))
- grad_ln2_gain: float32 [768], P(('wide', 'narrow'))
- grad_ln2_shift: float32 [768], P(('wide', 'narrow'))
- grad_w_up: float32 [768, 3072], P(('wide', 'narrow'))
- grad_up_bias: float32 [3072], P(('wide', 'narrow'))
- grad_w_down: float32 [3072, 768], P(('wide', 'narrow'))
- grad_down_bias: float32 [768], P(('wide', 'narrow'))
Inputs may be any that keep to these rules, and one draw needn't show every extreme that they name: `segment_ids`: never falling along a sequence; images of exactly 49 rows numbered from 0, then the padding rows as one last segment; the first sequence holds 10 images. `valid`: 0 exactly on the padding rows at the end of each sequence.
All inputs are finite; a program needn't handle non-finite values.
Results may differ from a plain program's by a relative error of at most 0.0086.
Values may be sent and summed in bfloat16 or wider, within the bound.
A program may use at most 192 MiB of HBM per device.

v0:
```python
import jax
import jax.numpy as jnp
from jax import lax
from jax.sharding import PartitionSpec as P

HD = 64


EPSILON = 1e-06


def norm_parts(rows):
    center = rows - jnp.mean(rows, axis=-1, keepdims=True)
    recip = lax.rsqrt(jnp.mean(center * center, axis=-1, keepdims=True) + EPSILON)
    return (center * recip, recip)


def norm_back(grad_h, gain, normed, recip):
    scaled = grad_h * gain
    return recip * (
        scaled
        - jnp.mean(scaled, axis=-1, keepdims=True)
        - normed * jnp.mean(scaled * normed, axis=-1, keepdims=True)
    )


def key_mask(segment, valid_keys):
    length = segment.shape[0]
    same = segment[:, None] == segment[None, :]
    return same & ((valid_keys[None, :] == 1) | jnp.eye(length, dtype=bool))


def attend(item):
    queries, key_rows, value_rows, segment, valid_keys = item
    allowed = key_mask(segment, valid_keys)
    scores = jnp.einsum("qhe,khe->hqk", queries, key_rows, preferred_element_type=jnp.float32) * (
        1.0 / HD**0.5
    )
    scores = jnp.where(allowed[None], scores, -1e30)
    top_score = jnp.max(scores, axis=-1, keepdims=True)
    expo = jnp.exp(scores - top_score)
    total = jnp.sum(expo, axis=-1, keepdims=True)
    soft_w = (expo / total).astype(jnp.bfloat16)
    attended = jnp.einsum("hqk,khe->qhe", soft_w, value_rows, preferred_element_type=jnp.float32)
    return (attended, top_score + jnp.log(total))


def attend_back(item):
    queries, key_rows, value_rows, grad_out, log_total, segment, valid_keys = item
    allowed = key_mask(segment, valid_keys)
    scores = jnp.einsum("qhe,khe->hqk", queries, key_rows, preferred_element_type=jnp.float32) * (
        1.0 / HD**0.5
    )
    soft_w = jnp.where(allowed[None], jnp.exp(scores - log_total), 0.0)
    grad_v = jnp.einsum(
        "hqk,qhe->khe", soft_w.astype(jnp.bfloat16), grad_out, preferred_element_type=jnp.float32
    )
    grad_p = jnp.einsum("qhe,khe->hqk", grad_out, value_rows, preferred_element_type=jnp.float32)
    row_term = jnp.sum(soft_w * grad_p, axis=-1, keepdims=True)
    grad_s = jnp.where(allowed[None], soft_w * (grad_p - row_term), 0.0).astype(jnp.bfloat16)
    grad_q = jnp.einsum("hqk,khe->qhe", grad_s, key_rows, preferred_element_type=jnp.float32) * (
        1.0 / HD**0.5
    )
    grad_k = jnp.einsum("hqk,qhe->khe", grad_s, queries, preferred_element_type=jnp.float32) * (
        1.0 / HD**0.5
    )
    return (grad_q, grad_k, grad_v)


def col_sum(rows):
    return jnp.sum(rows.astype(jnp.float32), axis=0)


def on_device(
    inputs,
    w_qkv,
    qv_bias,
    w_out,
    out_bias,
    ln1_gain,
    ln1_shift,
    ln2_gain,
    ln2_shift,
    w_up,
    up_bias,
    w_down,
    down_bias,
    segment_ids,
    valid,
    cotangent,
):
    row_count = inputs.shape[0]
    model_width = inputs.shape[1]
    seq_count = segment_ids.shape[0]
    seq_len = segment_ids.shape[1]
    head_count = model_width // HD
    attn_full = (
        lax.all_gather(w_qkv, ("wide", "narrow"), axis=0, tiled=True),
        lax.all_gather(w_out, ("wide", "narrow"), axis=0, tiled=True),
        lax.all_gather(ln1_gain, ("wide", "narrow"), axis=0, tiled=True),
        lax.all_gather(ln1_shift, ("wide", "narrow"), axis=0, tiled=True),
        lax.all_gather(qv_bias, ("wide", "narrow"), axis=0, tiled=True),
        lax.all_gather(out_bias, ("wide", "narrow"), axis=0, tiled=True),
    )
    qkv_full, out_full, gain_one, shift_one, qv_full, outb_full = attn_full
    gain_one = gain_one.astype(jnp.float32)
    shift_one = shift_one.astype(jnp.float32)
    qv_full = qv_full.astype(jnp.float32)
    rows = inputs.astype(jnp.float32)
    normed_one, recip_one = norm_parts(rows)
    h_one = (normed_one * gain_one + shift_one).astype(jnp.bfloat16)
    qkv_rows = jnp.dot(h_one, qkv_full, preferred_element_type=jnp.float32)
    queries = (qkv_rows[:, :model_width] + qv_full[:model_width]).astype(jnp.bfloat16)
    key_rows = qkv_rows[:, model_width : 2 * model_width].astype(jnp.bfloat16)
    value_rows = (qkv_rows[:, 2 * model_width :] + qv_full[model_width:]).astype(jnp.bfloat16)
    shape_seq = (seq_count, seq_len, head_count, HD)
    q_seq = queries.reshape(shape_seq)
    k_seq = key_rows.reshape(shape_seq)
    v_seq = value_rows.reshape(shape_seq)
    attended, log_total = lax.map(attend, (q_seq, k_seq, v_seq, segment_ids, valid))
    attended = attended.reshape(row_count, model_width).astype(jnp.bfloat16)
    mid_rows = (
        rows
        + jnp.dot(attended, out_full, preferred_element_type=jnp.float32)
        + outb_full.astype(jnp.float32)
    )
    mlp_full = (
        lax.all_gather(w_up, ("wide", "narrow"), axis=0, tiled=True),
        lax.all_gather(w_down, ("wide", "narrow"), axis=0, tiled=True),
        lax.all_gather(ln2_gain, ("wide", "narrow"), axis=0, tiled=True),
        lax.all_gather(ln2_shift, ("wide", "narrow"), axis=0, tiled=True),
        lax.all_gather(up_bias, ("wide", "narrow"), axis=0, tiled=True),
        lax.all_gather(down_bias, ("wide", "narrow"), axis=0, tiled=True),
    )
    up_full, down_full, gain_two, shift_two, upb_full, downb_full = mlp_full
    gain_two = gain_two.astype(jnp.float32)
    shift_two = shift_two.astype(jnp.float32)
    normed_two, recip_two = norm_parts(mid_rows)
    h_two = (normed_two * gain_two + shift_two).astype(jnp.bfloat16)
    upper = jnp.dot(h_two, up_full, preferred_element_type=jnp.float32) + upb_full.astype(
        jnp.float32
    )
    gelu_rows = jax.nn.gelu(upper, approximate=False).astype(jnp.bfloat16)
    out_rows = (
        mid_rows
        + jnp.dot(gelu_rows, down_full, preferred_element_type=jnp.float32)
        + downb_full.astype(jnp.float32)
    )
    block_out = out_rows.astype(jnp.bfloat16)
    up_full, down_full = (
        lax.all_gather(w_up, ("wide", "narrow"), axis=0, tiled=True),
        lax.all_gather(w_down, ("wide", "narrow"), axis=0, tiled=True),
    )
    dy_rows = cotangent.astype(jnp.float32)
    grad_wdown = jnp.einsum("tf,td->fd", gelu_rows, cotangent, preferred_element_type=jnp.float32)
    grad_bdown = col_sum(cotangent)
    grad_g = jnp.einsum("td,fd->tf", cotangent, down_full, preferred_element_type=jnp.float32)
    cdf_part = 0.5 * (1.0 + jax.scipy.special.erf(upper * 0.7071067811865476))
    pdf_part = jnp.exp(-0.5 * upper * upper) * 0.3989422804014327
    grad_u = (grad_g * (cdf_part + upper * pdf_part)).astype(jnp.bfloat16)
    grad_bup = col_sum(grad_u)
    grad_wup = jnp.einsum("td,tf->df", h_two, grad_u, preferred_element_type=jnp.float32)
    grad_h2 = jnp.einsum("tf,df->td", grad_u, up_full, preferred_element_type=jnp.float32)
    grad_g2 = jnp.sum(grad_h2 * normed_two, axis=0)
    grad_c2 = jnp.sum(grad_h2, axis=0)
    mlp_terms = (grad_wup, grad_wdown, grad_g2, grad_c2, grad_bup, grad_bdown)
    mlp_sums = (
        lax.psum_scatter(mlp_terms[0], ("wide", "narrow"), scatter_dimension=0, tiled=True),
        lax.psum_scatter(mlp_terms[1], ("wide", "narrow"), scatter_dimension=0, tiled=True),
        lax.psum_scatter(mlp_terms[2], ("wide", "narrow"), scatter_dimension=0, tiled=True),
        lax.psum_scatter(mlp_terms[3], ("wide", "narrow"), scatter_dimension=0, tiled=True),
        lax.psum_scatter(mlp_terms[4], ("wide", "narrow"), scatter_dimension=0, tiled=True),
        lax.psum_scatter(mlp_terms[5], ("wide", "narrow"), scatter_dimension=0, tiled=True),
    )
    grad_mid = dy_rows + norm_back(grad_h2, gain_two, normed_two, recip_two)
    qkv_full, out_full = (
        lax.all_gather(w_qkv, ("wide", "narrow"), axis=0, tiled=True),
        lax.all_gather(w_out, ("wide", "narrow"), axis=0, tiled=True),
    )
    grad_a = grad_mid.astype(jnp.bfloat16)
    grad_wout = jnp.einsum("tc,td->cd", attended, grad_a, preferred_element_type=jnp.float32)
    grad_bout = col_sum(grad_a)
    grad_o = jnp.einsum("td,cd->tc", grad_a, out_full, preferred_element_type=jnp.float32).astype(
        jnp.bfloat16
    )
    grad_q, grad_k, grad_v = lax.map(
        attend_back, (q_seq, k_seq, v_seq, grad_o.reshape(shape_seq), log_total, segment_ids, valid)
    )
    grad_q = grad_q.reshape(row_count, model_width).astype(jnp.bfloat16)
    grad_k = grad_k.reshape(row_count, model_width).astype(jnp.bfloat16)
    grad_v = grad_v.reshape(row_count, model_width).astype(jnp.bfloat16)
    grad_qkv = jnp.concatenate([grad_q, grad_k, grad_v], axis=1)
    grad_bqv = jnp.concatenate([col_sum(grad_q), col_sum(grad_v)])
    grad_wqkv = jnp.einsum("td,te->de", h_one, grad_qkv, preferred_element_type=jnp.float32)
    grad_h1 = jnp.einsum("te,de->td", grad_qkv, qkv_full, preferred_element_type=jnp.float32)
    grad_g1 = jnp.sum(grad_h1 * normed_one, axis=0)
    grad_c1 = jnp.sum(grad_h1, axis=0)
    attn_terms = (grad_wqkv, grad_wout, grad_g1, grad_c1, grad_bqv, grad_bout)
    attn_sums = (
        lax.psum_scatter(attn_terms[0], ("wide", "narrow"), scatter_dimension=0, tiled=True),
        lax.psum_scatter(attn_terms[1], ("wide", "narrow"), scatter_dimension=0, tiled=True),
        lax.psum_scatter(attn_terms[2], ("wide", "narrow"), scatter_dimension=0, tiled=True),
        lax.psum_scatter(attn_terms[3], ("wide", "narrow"), scatter_dimension=0, tiled=True),
        lax.psum_scatter(attn_terms[4], ("wide", "narrow"), scatter_dimension=0, tiled=True),
        lax.psum_scatter(attn_terms[5], ("wide", "narrow"), scatter_dimension=0, tiled=True),
    )
    grad_inputs = grad_mid + norm_back(grad_h1, gain_one, normed_one, recip_one)
    return (
        block_out,
        grad_inputs,
        attn_sums[0],
        attn_sums[4],
        attn_sums[1],
        attn_sums[5],
        attn_sums[2],
        attn_sums[3],
        mlp_sums[2],
        mlp_sums[3],
        mlp_sums[0],
        mlp_sums[4],
        mlp_sums[1],
        mlp_sums[5],
    )


def solution(mesh):
    in_specs = (
        P(("wide", "narrow"), None),
        P(("wide", "narrow"), None),
        P(("wide", "narrow")),
        P(("wide", "narrow"), None),
        P(("wide", "narrow")),
        P(("wide", "narrow")),
        P(("wide", "narrow")),
        P(("wide", "narrow")),
        P(("wide", "narrow")),
        P(("wide", "narrow"), None),
        P(("wide", "narrow")),
        P(("wide", "narrow"), None),
        P(("wide", "narrow")),
        P(("wide", "narrow"), None),
        P(("wide", "narrow"), None),
        P(("wide", "narrow"), None),
    )
    out_specs = (
        P(("wide", "narrow"), None),
        P(("wide", "narrow"), None),
        P(("wide", "narrow"), None),
        P(("wide", "narrow")),
        P(("wide", "narrow"), None),
        P(("wide", "narrow")),
        P(("wide", "narrow")),
        P(("wide", "narrow")),
        P(("wide", "narrow")),
        P(("wide", "narrow")),
        P(("wide", "narrow"), None),
        P(("wide", "narrow")),
        P(("wide", "narrow"), None),
        P(("wide", "narrow")),
    )
    return jax.shard_map(
        on_device, mesh=mesh, in_specs=in_specs, out_specs=out_specs, check_vma=False
    )
```

profile of v0, /device:TPU:1, one launch (start us, length us, event | category | flops | bytes accessed | tf_op | source)
XLA Modules:
  0.0 850.8 jit_solution(17931727434221299639)
XLA Ops:
  16.8 41.6 %all-reduce.17 = (bf16[1536]{0:T(1024)(128)(2,1)S(1)}, bf16[768]{0:T(1024)(128)(2,1)S(1)}, bf16[768]{0:T(1024)(128)(2,1)S(1)}, bf16[768]{0:T(1024)(128)(2,1)S(1)...) all-reduce(bf16[1536]{0:T(1024)(128)(2,1)S(1)} %dynamic-update-slic, ...), channel_id=1, replica_groups=mesh['wide'=8,'narrow'=4] {'wide','narrow'}, use_global_device_ids=true, to_apply=%add.2 | all-reduce | flops 9216 | bytes 36864
  58.5 1.8 copy.82
  62.7 10.9 %all-gather.5.cloned.1.call-done = bf16[768,2304]{1,0:T(8,128)(2,1)} async-done(((bf16[24,2304]{1,0:T(8,128)(2,1)}), bf16[768,2304]{1,0:T(8,128)(2,1)}) %all-gather.5.cloned.1.call-update) | async-done | bytes 3538960 | tf_op jit(solution)/shard_map/all_gather | solution.py:98
  73.6 6.3 fusion.123
  80.1 2.3 fusion.116
  84.1 2.4 reshape.236
  89.8 3.8 reshape.237
  93.7 1.7 copy.88
  95.4 2.6 copy.83
  98.0 3.8 reshape.235
  101.8 2.9 copy.86
  106.1 21.4 %while.26 = (s32[]{:T(128)}, bf16[2,512,12,64]{1,3,2,0:T(8,128)(2,1)}, f32[2,12,512,1]{2,1,3,0:T(8,128)S(1)}, bf16[2,512,12,64]{1,3,2,0:T(8,128)(2,1)}, s32[2,51...) while((s32[]{:T(128)}, ...), condition=%wide.region_5.6_spmd, body=%wide.region_2.5_spmd.sunk | while | flops 844098048 | bytes 42962032 | solution.py:120
  106.8 2.1 fusion.169
  108.9 2.6 fusion.170
  111.5 5.5 bitcast_dynamic-update-slice_fusion.10
  117.3 2.1 fusion.169
  119.4 2.6 fusion.170
  122.0 5.5 bitcast_dynamic-update-slice_fusion.10
  127.5 3.0 copy.89
  132.1 5.5 fusion.128
  137.5 2.3 multiply_reduce_fusion.3
  139.9 55.1 %all-gather.9.cloned.1.call-done = bf16[768,3072]{1,0:T(8,128)(2,1)} async-done(((bf16[24,3072]{1,0:T(8,128)(2,1)}), bf16[768,3072]{1,0:T(8,128)(2,1)}) %all-gather.9.cloned.1.call-update) | async-done | bytes 4718608 | tf_op jit(solution)/shard_map/all_gather | solution.py:128
  194.9 50.1 %fusion.87 = (bf16[1024,3072]{1,0:T(8,128)(2,1)}, f32[1024,3072]{1,0:T(8,128)}) fusion(f32[3072]{0:T(1024)S(1)} %convert_element_type.121, bf16[768,3072]{1,0:T(8,128)(2,1)} %all-gather.9.cloned.1.call-done, f32[1024,768]{0,1:T(8,128)} %get-tuple-element.290, f32[768]{0:T(1024)S(1)} %convert_element_type.119, f32[768]{0:T(1024)S(1)} %convert_element_type.118, ...), kind=kOutput, calls=%fused_computation.83 | convolution fusion | flops 5043388416 | bytes 26765312 | tf_op jit(solution)/shard_map/dot_general | solution.py:140
  245.1 15.1 %all-gather.11.cloned.1.call-done = bf16[3072,768]{1,0:T(8,128)(2,1)} async-done(((bf16[96,768]{1,0:T(8,128)(2,1)}), bf16[3072,768]{1,0:T(8,128)(2,1)}) %all-gather.11.cloned.1.call-update) | async-done | bytes 4718608 | tf_op jit(solution)/shard_map/all_gather | solution.py:129
  260.2 13.0 %convert_reduce_fusion = (f32[3072]{0:T(1024)}, bf16[1024,3072]{1,0:T(8,128)(2,1)S(1)}) fusion(f32[1024,3072]{1,0:T(8,128)} %get-tuple-element.292, f32[3072]{0:T(1024)S(1)} %convert_element_type.121, bf16[1024,768]{1,0:T(8,128)(2,1)} %param.35, bf16[3072,768]{1,0:T(8,128)(2,1)} %all-gather.11.cloned.1.call-done), kind=kOutput, calls=%fused_computation.90 | convolution fusion | flops 4872729600 | bytes 25190400 | tf_op jit(solution)/shard_map/td,fd->tf/dot_general | solution.py:157
  273.1 7.3 fusion.130
  280.4 3.5 copy.92
  283.9 4.6 multiply_reduce_fusion.1
  288.5 4.4 convert_reduce_fusion.3
  294.6 2.8 fusion.118
  297.4 4.8 convolution_convert_fusion
  302.2 2.6 copy.93
  304.8 3.8 reshape.238
  308.7 2.9 copy.96
  315.6 109.5 %while.27 = (s32[]{:T(128)}, bf16[2,512,12,64]{1,3,2,0:T(8,128)(2,1)}, bf16[2,512,12,64]{1,3,2,0:T(8,128)(2,1)}, bf16[2,512,12,64]{1,3,2,0:T(8,128)(2,1)}, bf16[...) while((s32[]{:T(128)}, ...), condition=%wide.region_12.13_spmd, body=%wide.region_10.12_spmd.sunk | while | flops 2096903680 | bytes 214399216 | solution.py:186
  316.2 1.8 fusion.182
  318.0 3.4 bitcast_dynamic-update-slice_fusion.14
  321.4 1.8 copy-done
  323.2 6.3 fusion.181
  329.5 20.9 %bitcast_dynamic-update-slice_fusion.13 = bf16[2,512,12,64]{1,3,2,0:T(8,128)(2,1)} fusion(bf16[2,512,12,64]{1,3,2,0:T(8,128)(2,1)} %get-tuple-element.462, s32[]{:T(128)S(6)} %copy.141, f32[12,512,512]{1,2,0:T(8,128)} %fusion.181, f32[12,512,512]{1,2,0:T(8,128)} %copy-done, f32[12,512]{1,0:T(8,128)S(1)} %dynamic-slice_bitcast_fusion.2, ...), kind=kOutput, calls=%fused_computation.43.clone.1 | convolution fusion | flops 437656064 | bytes 53281792 | tf_op jit(solution)/shard_map/while/body/eval_jaxpr/hqk,qhe->khe/dot_general | solution.py:64
  350.4 20.4 %bitcast_dynamic-update-slice_fusion.12 = bf16[2,512,12,64]{1,3,2,0:T(8,128)(2,1)} fusion(bf16[2,512,12,64]{1,3,2,0:T(8,128)(2,1)} %get-tuple-element.461, s32[]{:T(128)S(6)} %copy.141, f32[12,512,512]{1,2,0:T(8,128)} %fusion.181, f32[12,512,512]{1,2,0:T(8,128)} %copy-done, f32[12,512]{1,0:T(8,128)S(1)} %dynamic-slice_bitcast_fusion.2, ...), kind=kOutput, calls=%fused_computation.44.clone.1 | convolution fusion | flops 437656064 | bytes 53281792 | tf_op jit(solution)/shard_map/while/body/eval_jaxpr/hqk,khe->qhe/dot_general | solution.py:61
  371.2 1.8 fusion.182
  373.1 3.3 bitcast_dynamic-update-slice_fusion.14
  378.1 6.3 fusion.181
  384.4 20.5 %bitcast_dynamic-update-slice_fusion.13 = bf16[2,512,12,64]{1,3,2,0:T(8,128)(2,1)} fusion(bf16[2,512,12,64]{1,3,2,0:T(8,128)(2,1)} %get-tuple-element.462, s32[]{:T(128)S(6)} %copy.141, f32[12,512,512]{1,2,0:T(8,128)} %fusion.181, f32[12,512,512]{1,2,0:T(8,128)} %copy-done, f32[12,512]{1,0:T(8,128)S(1)} %dynamic-slice_bitcast_fusion.2, ...), kind=kOutput, calls=%fused_computation.43.clone.1 | convolution fusion | flops 437656064 | bytes 53281792 | tf_op jit(solution)/shard_map/while/body/eval_jaxpr/hqk,qhe->khe/dot_general | solution.py:64
  404.9 20.1 %bitcast_dynamic-update-slice_fusion.12 = bf16[2,512,12,64]{1,3,2,0:T(8,128)(2,1)} fusion(bf16[2,512,12,64]{1,3,2,0:T(8,128)(2,1)} %get-tuple-element.461, s32[]{:T(128)S(6)} %copy.141, f32[12,512,512]{1,2,0:T(8,128)} %fusion.181, f32[12,512,512]{1,2,0:T(8,128)} %copy-done, f32[12,512]{1,0:T(8,128)S(1)} %dynamic-slice_bitcast_fusion.2, ...), kind=kOutput, calls=%fused_computation.44.clone.1 | convolution fusion | flops 437656064 | bytes 53281792 | tf_op jit(solution)/shard_map/while/body/eval_jaxpr/hqk,khe->qhe/dot_general | solution.py:61
  425.1 3.0 copy.99
  428.6 3.1 copy.100
  434.7 2.1 copy-done.12
  436.8 6.4 fusion.121
  443.9 10.5 %fusion.125 = f32[768,3072]{1,0:T(8,128)} fusion(bf16[1024,3072]{1,0:T(8,128)(2,1)} %copy-done.38, f32[1024,768]{0,1:T(8,128)} %get-tuple-element.290, f32[768]{0:T(1024)S(1)} %copy-done.32, f32[768]{0:T(1024)S(1)} %copy-done.24, f32[1024]{0:T(1024)S(1)} %copy-done.26, f32[1024]{0:T(1024)S(1)} %copy-done.18), kind=kOutput, calls=%fused_computation.160 | convolution fusion | flops 4835770368 | bytes 18888704 | tf_op jit(solution)/shard_map/td,tf->df/dot_general | solution.py:162
  454.4 10.4 %fusion.131 = f32[3072,768]{1,0:T(8,128)} fusion(bf16[1024,3072]{1,0:T(8,128)(2,1)} %get-tuple-element.291, bf16[1024,768]{1,0:T(8,128)(2,1)} %param.35), kind=kOutput, calls=%fused_computation.166 | convolution fusion | flops 4831838208 | bytes 17301504 | tf_op jit(solution)/shard_map/tf,td->fd/dot_general | solution.py:155
  465.5 10.3 %add_convert_fusion = bf16[1024,768]{0,1:T(8,128)(2,1)} fusion(f32[1024,768]{0,1:T(8,128)} %get-tuple-element.290, bf16[1024,3072]{1,0:T(8,128)(2,1)} %get-tuple-element.291, bf16[3072,768]{1,0:T(8,128)(2,1)} %all-gather.11.cloned.1.call-done, f32[768]{0:T(1024)S(1)} %convert_element_type.123), kind=kOutput, calls=%fused_computation.136 | convolution fusion | flops 4834197504 | bytes 15731712 | tf_op jit(solution)/shard_map/dot_general | solution.py:146
  475.8 2.6 copy.104
  478.5 1.7 convert_reduce_fusion.4
  480.6 9.2 %fusion.129 = (f32[768]{0:T(1024)S(1)}, f32[1024,768]{1,0:T(8,128)}) fusion(bf16[1024,2304]{0,1:T(8,128)(2,1)} %copy-done.12, bf16[768,2304]{1,0:T(8,128)(2,1)} %all-gather.5.cloned.1.call-done), kind=kOutput, calls=%fused_computation.164 | convolution fusion | flops 3624664320 | bytes 11406336 | tf_op jit(solution)/shard_map/te,de->td/dot_general | solution.py:195
  489.8 3.7 copy.101
  493.5 3.2 fusion.113
  496.7 42.5 %all-reduce.16 = (f32[1536]{0:T(1024)S(1)}, f32[768]{0:T(1024)S(1)}, f32[768]{0:T(1024)S(1)}, f32[768]{0:T(1024)S(1)}, f32[768]{0:T(1024)S(1)}, /*index=5*/f32[7...) all-reduce(f32[1536]{0:T(1024)S(1)} %pad_maximum_fusion, ...), channel_id=3, replica_groups=mesh['wide'=8,'narrow'=4] {'wide','narrow'}, use_global_device_ids=true, to_apply=%region_18.19.clone | all-reduce | flops 9216 | bytes 73728
  542.8 5.6 fusion.112
  548.4 3.6 copy.105
  553.2 7.4 reduce-scatter.5.cloned.1.call-done
  560.6 141.0 %reduce-scatter.9.cloned.1.call-done = f32[24,3072]{1,0:T(8,128)} async-done(((f32[768,3072]{1,0:T(8,128)}), f32[24,3072]{1,0:T(8,128)}) %reduce-scatter.9.cloned.1.call-update) | async-done | bytes 294928 | tf_op jit(solution)/shard_map/reduce_scatter | solution.py:168
  701.6 142.1 %reduce-scatter.11.cloned.1.call-done = f32[96,768]{1,0:T(8,128)} async-done(((f32[3072,768]{1,0:T(8,128)}), f32[96,768]{1,0:T(8,128)}) %reduce-scatter.11.cloned.1.call-update) | async-done | bytes 294928 | tf_op jit(solution)/shard_map/reduce_scatter | solution.py:169
  (181 shorter events, 38.4 us)
Async XLA Ops:
  7.2 66.4 %all-gather.5.cloned.1.call-start = ((), (), s32[]{:S(2)}) async-start(), calls=%async_computation.4 | async-start | bytes 3649536 | tf_op jit(solution)/shard_map/all_gather | solution.py:98
  7.9 124.2 %all-gather.7.cloned.1.call-start = ((), (), s32[]{:S(2)}) async-start(), calls=%async_computation.5 | async-start | bytes 1216512 | tf_op jit(solution)/shard_map/all_gather | solution.py:99
  8.7 186.3 %all-gather.9.cloned.1.call-start = ((), (), s32[]{:S(2)}) async-start(), calls=%async_computation.6 | async-start | bytes 4866048 | tf_op jit(solution)/shard_map/all_gather | solution.py:128
  9.4 250.8 %all-gather.11.cloned.1.call-start = ((), (), s32[]{:S(2)}) async-start(), calls=%async_computation.7 | async-start | bytes 4866048 | tf_op jit(solution)/shard_map/all_gather | solution.py:129
  10.0 543.2 %reduce-scatter.7.cloned.1.call-start = ((), (), s32[]{:S(2)}) async-start(), calls=%async_computation.9 | async-start | bytes 2433024 | tf_op jit(solution)/shard_map/reduce_scatter | solution.py:201
  58.4 15.2 %copy-start.19 = (f32[768]{0:T(1024)}, f32[768]{0:T(1024)S(1)}, u32[]{:S(2)}) copy-start(f32[768]{0:T(1024)S(1)} %convert_element_type.109) | copy-start | bytes 9220
  58.4 230.1 %copy-start.23 = (f32[768]{0:T(1024)}, f32[768]{0:T(1024)S(1)}, u32[]{:S(2)}) copy-start(f32[768]{0:T(1024)S(1)} %convert_element_type.118) | copy-start | bytes 9220
  58.4 15.2 %copy-start.33 = (f32[768]{0:T(1024)}, f32[768]{0:T(1024)S(1)}, u32[]{:S(2)}) copy-start(f32[768]{0:T(1024)S(1)} %convert_element_type.110) | copy-start | bytes 9220
  58.4 136.5 %copy-start.31 = (f32[768]{0:T(1024)}, f32[768]{0:T(1024)S(1)}, u32[]{:S(2)}) copy-start(f32[768]{0:T(1024)S(1)} %convert_element_type.119) | copy-start | bytes 9220
  58.5 2.6 copy-start.10
  60.3 19.6 %copy-start.1 = (bf16[1024,768]{0,1:T(8,128)(2,1)}, bf16[1024,768]{0,1:T(8,128)(2,1)S(1)}, u32[]{:S(2)}) copy-start(bf16[1024,768]{0,1:T(8,128)(2,1)S(1)} %copy.82) | copy-start | bytes 4718596
  60.6 13.0 %copy-start.15 = (f32[1024]{0:T(1024)}, f32[1024]{0:T(1024)S(1)}, u32[]{:S(2)}) copy-start(f32[1024]{0:T(1024)S(1)} %broadcast_multiply_fusion.5) | copy-start | bytes 12292
  61.1 12.5 %copy-start.21 = (f32[1024]{0:T(1024)}, f32[1024]{0:T(1024)S(1)}, u32[]{:S(2)}) copy-start(f32[1024]{0:T(1024)S(1)} %add_rsqrt_fusion.1) | copy-start | bytes 12292
  101.8 4.3 copy-start.13
  101.8 4.3 copy-start.14
  137.5 151.0 %copy-start.17 = (f32[1024]{0:T(1024)}, f32[1024]{0:T(1024)S(1)}, u32[]{:S(2)}) copy-start(f32[1024]{0:T(1024)S(1)} %broadcast_multiply_fusion.4) | copy-start | bytes 12292
  139.8 148.7 %copy-start.25 = (f32[1024]{0:T(1024)}, f32[1024]{0:T(1024)S(1)}, u32[]{:S(2)}) copy-start(f32[1024]{0:T(1024)S(1)} %add_rsqrt_fusion) | copy-start | bytes 12292
  260.2 13.0 %copy-start.37 = (bf16[768,3072]{1,0:T(8,128)(2,1)S(1)}, bf16[768,3072]{1,0:T(8,128)(2,1)}, u32[]{:S(2)}) copy-start(bf16[768,3072]{1,0:T(8,128)(2,1)} %all-gather.9.cloned.1.call-done) | copy-start | bytes 14155780
  273.1 7.3 copy-start.38
  283.9 4.6 copy-start.3
  283.9 4.6 copy-start.9
  288.5 6.1 copy-start.11
  293.0 1.6 copy-start.7
  311.6 249.0 %reduce-scatter.5.cloned.1.call-start = ((), (), s32[]{:S(2)}) async-start(), calls=%async_computation.8 | async-start | bytes 7299072 | tf_op jit(solution)/shard_map/reduce_scatter | solution.py:200
  316.1 1.9 copy-start.8
  316.1 1.9 copy-start.5
  318.0 5.1 copy-start
  318.0 5.1 copy-start.4
  371.2 1.9 copy-start.8
  371.2 1.9 copy-start.5
  373.1 5.0 copy-start
  373.1 5.0 copy-start.4
  428.6 3.6 copy-start.6
  434.3 2.4 copy-start.2
  434.4 2.4 copy-start.16
  434.4 2.4 copy-start.20
  434.4 2.4 copy-start.22
  434.4 2.4 copy-start.34
  434.7 2.1 copy-start.12
  443.2 0.7 copy-start.18
  443.2 0.7 copy-start.24
  443.2 0.7 copy-start.26
  443.2 0.7 copy-start.32
  443.2 258.4 %reduce-scatter.9.cloned.1.call-start = ((), (), s32[]{:S(2)}) async-start(), calls=%async_computation.10 | async-start | bytes 9732096 | tf_op jit(solution)/shard_map/reduce_scatter | solution.py:168
  454.4 389.4 %reduce-scatter.11.cloned.1.call-start = ((), (), s32[]{:S(2)}) async-start(), calls=%async_computation.11 | async-start | bytes 9732096 | tf_op jit(solution)/shard_map/reduce_scatter | solution.py:169
  464.8 0.7 copy-start.36
  493.5 3.2 copy-start.27
  493.5 3.2 copy-start.28
  493.5 3.3 copy-start.29
  493.5 3.3 copy-start.30
  493.5 3.3 copy-start.35
Sparse Core Ops, SparseCore 0:
  10.9 62.6 all-gather.4
  76.5 52.9 all-gather.6
  132.4 62.5 all-gather.8
  197.7 62.4 all-gather.10
  311.7 95.7 reduce-scatter.6
  443.3 117.1 reduce-scatter.4
  567.1 134.5 reduce-scatter.8
  709.1 134.6 reduce-scatter.10
where the time goes:
time: 863 us; the launch traced here: 851 us
  waiting for transfers between devices  374 us (43%)
  matrix products  257 us (30%)
  local copies, waits for them, and re-layouts  88.1 us (10%)
  blocking collectives  84.1 us (10%)
  other arithmetic  31.5 us (4%)
  between operations  14.9 us (2%)
    reduce_scatter x1, waiting for transfers between devices, on_device(): lax.psum_scatter(mlp_terms[1], ('wide', 'narrow'), scatter_dimension=0, t...  142 us
    reduce_scatter x1, waiting for transfers between devices, on_device(): lax.psum_scatter(mlp_terms[0], ('wide', 'narrow'), scatter_dimension=0, t...  141 us
    unnamed x2, blocking collectives  84.1 us
    all_gather x1, waiting for transfers between devices, on_device(): lax.all_gather(w_up, ('wide', 'narrow'), axis=0, tiled=True)  55.1 us
    dot_general x1, matrix products, on_device(): jnp.dot(h_two, up_full, preferred_element_type=jnp.float32)  50.1 us
    dot_general x2, matrix products, attend_back(): jnp.einsum('hqk,qhe->khe', grad_s, queries, preferred_element_type=jnp.fl...  41.4 us
    dot_general x2, matrix products, attend_back(): jnp.einsum('hqk,khe->qhe', grad_s, key_rows, preferred_element_type=jnp.f...  40.5 us
    unnamed x104, local copies, waits for them, and re-layouts  29.2 us
  transfers between devices with their start and end apart: 8, of which 6 were waited for; matrix products, arithmetic and copies ran while one was open for 37% of the time, Pallas kernels for 0%

commit v1 on v0

--- a/solution.py
+++ b/solution.py
@@ -1,10 +1,13 @@
+import functools
 import jax
 import jax.numpy as jnp
 from jax import lax
+from jax.experimental import pallas as pl
+from jax.experimental.pallas import tpu as pltpu
 from jax.sharding import PartitionSpec as P
 
 HD = 64
-
+ALL = ("wide", "narrow")
 
 EPSILON = 1e-06
 
@@ -69,6 +72,167 @@
 
 def col_sum(rows):
     return jnp.sum(rows.astype(jnp.float32), axis=0)
+
+
+MESH_ID = pl.DeviceIdType.MESH
+
+
+def ring_maps(n_wide, n_narrow):
+    n_dev = n_wide * n_narrow
+    if (n_wide, n_narrow) == (8, 4):
+        def pos_of(w, n):
+            z, y, x, c = w // 2, w % 2, n // 2, n % 2
+            q = 2 * x + (x + y) % 2
+            k = 4 * q + z + (q % 2) * (3 - 2 * z)
+            return 2 * k + c
+
+        def coords_of(p):
+            k, c = p // 2, p % 2
+            q, r = k // 4, k % 4
+            z = r + (q % 2) * (3 - 2 * r)
+            x = q // 2
+            y = (q % 2 + x) % 2
+            return z * 2 + y, x * 2 + c
+
+    else:
+        def pos_of(w, n):
+            return w * n_narrow + n
+
+        def coords_of(p):
+            return p // n_narrow, p % n_narrow
+
+    return n_dev, pos_of, coords_of
+
+
+def ring_reduce_scatter(parts, mesh_shape, collective_id=0):
+    n_wide, n_narrow = mesh_shape
+    n_dev, pos_of, coords_of = ring_maps(n_wide, n_narrow)
+    specs = []
+    for i, (a, rb, split) in enumerate(parts):
+        cols = a.shape[1]
+        if split:
+            specs.append((i, 0, 0, cols // 2))
+            specs.append((i, 1, cols // 2, cols // 2))
+        else:
+            specs.append((i, 0, 0, cols))
+    n_in = len(parts)
+    n_sp = len(specs)
+
+    def kernel(*refs):
+        ins = refs[:n_in]
+        outs = refs[n_in : 2 * n_in]
+        bufs = refs[2 * n_in : 2 * n_in + n_sp]
+        locs = refs[2 * n_in + n_sp : 2 * n_in + 2 * n_sp]
+        send_sem, recv_sem, loc_sem, credit = refs[2 * n_in + 2 * n_sp :]
+        p = pos_of(lax.axis_index("wide"), lax.axis_index("narrow"))
+        right = coords_of((p + 1) % n_dev)
+        left = coords_of((p + n_dev - 1) % n_dev)
+        nbr_send = (right, left)
+        nbr_recv = (left, right)
+
+        def rows_of(q, rb):
+            cw, cn = coords_of(q % n_dev)
+            start = (cw * n_narrow + cn) * rb
+            if rb % 8 == 0:
+                start = pl.multiple_of(start, 8)
+            return pl.ds(start, rb)
+
+        barrier = pltpu.get_barrier_semaphore()
+        for nb in (left, right):
+            pl.semaphore_signal(barrier, 1, device_id=nb, device_id_type=MESH_ID)
+        pl.semaphore_wait(barrier, 2)
+
+        for j, (i, dirn, c0, cw) in enumerate(specs):
+            q = p + n_dev - 1 if dirn == 0 else p + 1
+            cp = pltpu.make_async_copy(
+                ins[i].at[rows_of(q, parts[i][1]), pl.ds(c0, cw)], bufs[j].at[0], loc_sem.at[j]
+            )
+            cp.start()
+            cp.wait()
+
+        def step(s, carry):
+            slot = s % 2
+            nslot = 1 - slot
+            for dirn in (0, 1):
+
+                @pl.when(s >= 1)
+                def _():
+                    pl.semaphore_wait(credit.at[dirn], 1)
+
+            rcopies = []
+            lcopies = []
+            for j, (i, dirn, c0, cw) in enumerate(specs):
+                rc = pltpu.make_async_remote_copy(
+                    src_ref=bufs[j].at[slot],
+                    dst_ref=bufs[j].at[nslot],
+                    send_sem=send_sem.at[j, slot],
+                    recv_sem=recv_sem.at[j, nslot],
+                    device_id=nbr_send[dirn],
+                    device_id_type=MESH_ID,
+                )
+                rc.start()
+                rcopies.append(rc)
+                q = (p + 2 * n_dev - s - 2) if dirn == 0 else (p + s + 2)
+                lc = pltpu.make_async_copy(
+                    ins[i].at[rows_of(q, parts[i][1]), pl.ds(c0, cw)], locs[j].at[slot], loc_sem.at[j]
+                )
+                lc.start()
+                lcopies.append(lc)
+            for j in range(n_sp):
+                lcopies[j].wait()
+                rcopies[j].wait_recv()
+                bufs[j][nslot] = bufs[j][nslot] + locs[j][slot]
+            for j in range(n_sp):
+                rcopies[j].wait_send()
+            for dirn in (0, 1):
+
+                @pl.when(s < n_dev - 2)
+                def _():
+                    pl.semaphore_signal(
+                        credit.at[dirn], 1, device_id=nbr_recv[dirn], device_id_type=MESH_ID
+                    )
+
+            return carry
+
+        lax.fori_loop(0, n_dev - 1, step, 0)
+        last = (n_dev - 1) % 2
+        for j, (i, dirn, c0, cw) in enumerate(specs):
+            outs[i][:, pl.ds(c0, cw)] = bufs[j][last]
+
+    out_shape = [jax.ShapeDtypeStruct((rb, a.shape[1]), a.dtype) for (a, rb, _) in parts]
+    scratch = [pltpu.VMEM((2, parts[i][1], cw), jnp.float32) for (i, _, _, cw) in specs] * 2
+    scratch += [
+        pltpu.SemaphoreType.DMA((n_sp, 2)),
+        pltpu.SemaphoreType.DMA((n_sp, 2)),
+        pltpu.SemaphoreType.DMA((n_sp,)),
+        pltpu.SemaphoreType.REGULAR((2,)),
+    ]
+    total = sum(a.size * 4 for (a, _, _) in parts)
+    return pl.pallas_call(
+        kernel,
+        out_shape=out_shape,
+        in_specs=[pl.BlockSpec(memory_space=pl.ANY)] * n_in,
+        out_specs=[pl.BlockSpec(memory_space=pltpu.VMEM)] * n_in,
+        scratch_shapes=scratch,
+        compiler_params=pltpu.CompilerParams(
+            collective_id=collective_id, has_side_effects=True, vmem_limit_bytes=48 * 1024 * 1024
+        ),
+        cost_estimate=pl.CostEstimate(flops=total // 4, transcendentals=0, bytes_accessed=2 * total),
+    )(*[a for (a, _, _) in parts])
+
+
+def pack_rows(pieces, width):
+    flat = jnp.concatenate(pieces)
+    return jnp.pad(flat, (0, width - flat.shape[0]))[None, :]
+
+
+def split_owned(packed, sizes):
+    out = []
+    at = 0
+    for size in sizes:
+        out.append(packed[:, at : at + size].reshape(-1))
+        at += size
+    return out
 
 
 def on_device(
@@ -88,21 +252,33 @@
     segment_ids,
     valid,
     cotangent,
+    mesh_shape=None,
 ):
     row_count = inputs.shape[0]
     model_width = inputs.shape[1]
     seq_count = segment_ids.shape[0]
     seq_len = segment_ids.shape[1]
     head_count = model_width // HD
-    attn_full = (
-        lax.all_gather(w_qkv, ("wide", "narrow"), axis=0, tiled=True),
-        lax.all_gather(w_out, ("wide", "narrow"), axis=0, tiled=True),
-        lax.all_gather(ln1_gain, ("wide", "narrow"), axis=0, tiled=True),
-        lax.all_gather(ln1_shift, ("wide", "narrow"), axis=0, tiled=True),
-        lax.all_gather(qv_bias, ("wide", "narrow"), axis=0, tiled=True),
-        lax.all_gather(out_bias, ("wide", "narrow"), axis=0, tiled=True),
-    )
-    qkv_full, out_full, gain_one, shift_one, qv_full, outb_full = attn_full
+    n_dev = mesh_shape[0] * mesh_shape[1]
+    small = (qv_bias, out_bias, ln1_gain, ln1_shift, ln2_gain, ln2_shift, up_bias, down_bias)
+    small_sizes = [a.shape[0] for a in small]
+    n_small = sum(small_sizes)
+    rows_q = w_qkv.size // model_width
+    rows_o = w_out.shape[0]
+    attn_buf = jnp.concatenate(
+        [w_qkv.reshape(rows_q, model_width), w_out, pack_rows(small, model_width)], axis=0
+    )
+    attn_all = lax.all_gather(attn_buf, ALL, axis=0, tiled=False)
+    qkv_full = attn_all[:, :rows_q].reshape(-1, w_qkv.shape[1])
+    out_full = attn_all[:, rows_q : rows_q + rows_o].reshape(-1, model_width)
+    small_full = split_owned(attn_all[:, rows_q + rows_o, :n_small], small_sizes)
+    qv_full, outb_full, gain_one, shift_one, gain_two, shift_two, upb_full, downb_full = small_full
+    rows_u = w_up.size // model_width
+    mlp_buf = jnp.concatenate([w_up.reshape(rows_u, model_width), w_down], axis=0)
+    mlp_all = lax.all_gather(mlp_buf, ALL, axis=0, tiled=False)
+    up_full = mlp_all[:, :rows_u].reshape(-1, w_up.shape[1])
+    down_full = mlp_all[:, rows_u:].reshape(-1, model_width)
+
     gain_one = gain_one.astype(jnp.float32)
     shift_one = shift_one.astype(jnp.float32)
     qv_full = qv_full.astype(jnp.float32)
@@ -124,15 +300,6 @@
         + jnp.dot(attended, out_full, preferred_element_type=jnp.float32)
         + outb_full.astype(jnp.float32)
     )
-    mlp_full = (
-        lax.all_gather(w_up, ("wide", "narrow"), axis=0, tiled=True),
-        lax.all_gather(w_down, ("wide", "narrow"), axis=0, tiled=True),
-        lax.all_gather(ln2_gain, ("wide", "narrow"), axis=0, tiled=True),
-        lax.all_gather(ln2_shift, ("wide", "narrow"), axis=0, tiled=True),
-        lax.all_gather(up_bias, ("wide", "narrow"), axis=0, tiled=True),
-        lax.all_gather(down_bias, ("wide", "narrow"), axis=0, tiled=True),
-    )
-    up_full, down_full, gain_two, shift_two, upb_full, downb_full = mlp_full
     gain_two = gain_two.astype(jnp.float32)
     shift_two = shift_two.astype(jnp.float32)
     normed_two, recip_two = norm_parts(mid_rows)
@@ -147,10 +314,6 @@
         + downb_full.astype(jnp.float32)
     )
     block_out = out_rows.astype(jnp.bfloat16)
-    up_full, down_full = (
-        lax.all_gather(w_up, ("wide", "narrow"), axis=0, tiled=True),
-        lax.all_gather(w_down, ("wide", "narrow"), axis=0, tiled=True),
-    )
     dy_rows = cotangent.astype(jnp.float32)
     grad_wdown = jnp.einsum("tf,td->fd", gelu_rows, cotangent, preferred_element_type=jnp.float32)
     grad_bdown = col_sum(cotangent)
@@ -163,20 +326,7 @@
     grad_h2 = jnp.einsum("tf,df->td", grad_u, up_full, preferred_element_type=jnp.float32)
     grad_g2 = jnp.sum(grad_h2 * normed_two, axis=0)
     grad_c2 = jnp.sum(grad_h2, axis=0)
-    mlp_terms = (grad_wup, grad_wdown, grad_g2, grad_c2, grad_bup, grad_bdown)
-    mlp_sums = (
-        lax.psum_scatter(mlp_terms[0], ("wide", "narrow"), scatter_dimension=0, tiled=True),
-        lax.psum_scatter(mlp_terms[1], ("wide", "narrow"), scatter_dimension=0, tiled=True),
-        lax.psum_scatter(mlp_terms[2], ("wide", "narrow"), scatter_dimension=0, tiled=True),
-        lax.psum_scatter(mlp_terms[3], ("wide", "narrow"), scatter_dimension=0, tiled=True),
-        lax.psum_scatter(mlp_terms[4], ("wide", "narrow"), scatter_dimension=0, tiled=True),
-        lax.psum_scatter(mlp_terms[5], ("wide", "narrow"), scatter_dimension=0, tiled=True),
-    )
     grad_mid = dy_rows + norm_back(grad_h2, gain_two, normed_two, recip_two)
-    qkv_full, out_full = (
-        lax.all_gather(w_qkv, ("wide", "narrow"), axis=0, tiled=True),
-        lax.all_gather(w_out, ("wide", "narrow"), axis=0, tiled=True),
-    )
     grad_a = grad_mid.astype(jnp.bfloat16)
     grad_wout = jnp.einsum("tc,td->cd", attended, grad_a, preferred_element_type=jnp.float32)
     grad_bout = col_sum(grad_a)
@@ -195,31 +345,41 @@
     grad_h1 = jnp.einsum("te,de->td", grad_qkv, qkv_full, preferred_element_type=jnp.float32)
     grad_g1 = jnp.sum(grad_h1 * normed_one, axis=0)
     grad_c1 = jnp.sum(grad_h1, axis=0)
-    attn_terms = (grad_wqkv, grad_wout, grad_g1, grad_c1, grad_bqv, grad_bout)
-    attn_sums = (
-        lax.psum_scatter(attn_terms[0], ("wide", "narrow"), scatter_dimension=0, tiled=True),
-        lax.psum_scatter(attn_terms[1], ("wide", "narrow"), scatter_dimension=0, tiled=True),
-        lax.psum_scatter(attn_terms[2], ("wide", "narrow"), scatter_dimension=0, tiled=True),
-        lax.psum_scatter(attn_terms[3], ("wide", "narrow"), scatter_dimension=0, tiled=True),
-        lax.psum_scatter(attn_terms[4], ("wide", "narrow"), scatter_dimension=0, tiled=True),
-        lax.psum_scatter(attn_terms[5], ("wide", "narrow"), scatter_dimension=0, tiled=True),
-    )
     grad_inputs = grad_mid + norm_back(grad_h1, gain_one, normed_one, recip_one)
+
+    small_grads = (grad_bqv, grad_bout, grad_g1, grad_c1, grad_g2, grad_c2, grad_bup, grad_bdown)
+    owned = jnp.concatenate([g.reshape(n_dev, -1) for g in small_grads], axis=1)
+    lanes = 128
+    small_rows = 8 * pl.cdiv(pl.cdiv(n_small, lanes), 8)
+    owned = jnp.pad(owned, ((0, 0), (0, small_rows * lanes - n_small))).reshape(-1, lanes)
+    parts = [
+        (grad_wqkv, w_qkv.shape[0], True),
+        (grad_wout, w_out.shape[0], True),
+        (grad_wup, w_up.shape[0], True),
+        (grad_wdown, w_down.shape[0], True),
+        (owned, small_rows, False),
+    ]
+    if all(rb % 8 == 0 and a.shape[1] % 256 == 0 for (a, rb, _) in parts[:4]):
+        sums = ring_reduce_scatter(parts, mesh_shape)
+    else:
+        sums = [lax.psum_scatter(a, ALL, scatter_dimension=0, tiled=True) for (a, _, _) in parts]
+    small_sums = split_owned(sums[4].reshape(1, -1), [s for s in small_sizes])
+    bqv, bout, g1, c1, g2, c2, bup, bdown = small_sums
     return (
         block_out,
         grad_inputs,
-        attn_sums[0],
-        attn_sums[4],
-        attn_sums[1],
-        attn_sums[5],
-        attn_sums[2],
-        attn_sums[3],
-        mlp_sums[2],
-        mlp_sums[3],
-        mlp_sums[0],
-        mlp_sums[4],
-        mlp_sums[1],
-        mlp_sums[5],
+        sums[0],
+        bqv,
+        sums[1],
+        bout,
+        g1,
+        c1,
+        g2,
+        c2,
+        sums[2],
+        bup,
+        sums[3],
+        bdown,
     )
 
 
@@ -258,6 +418,7 @@
         P(("wide", "narrow"), None),
         P(("wide", "narrow")),
     )
+    body = functools.partial(on_device, mesh_shape=(mesh.shape["wide"], mesh.shape["narrow"]))
     return jax.shard_map(
-        on_device, mesh=mesh, in_specs=in_specs, out_specs=out_specs, check_vma=False
-    )
+        body, mesh=mesh, in_specs=in_specs, out_specs=out_specs, check_vma=False
+    )

time: 863 us -> 756 us (0.88)
  waiting for transfers between devices: 374 us -> 66.3 us
  Pallas kernels: 0 us -> 247 us
  blocking collectives: 84.1 us -> 0 us
  local copies, waits for them, and re-layouts: 88.1 us -> 112 us
  matrix products: 257 us -> 269 us
    reduce_scatter x4 -> x0, waiting for transfers between devices: 291 us -> none  [the longest x1 142 us: on_device(): lax.psum_scatter(mlp_terms[1], ('wide', 'narrow'), scatter_dimension=0, t...]
    pallas_call x0 -> x1, Pallas kernels: none -> 247 us  [ring_reduce_scatter(): pl.pallas_call(kernel, out_shape=out_shape, in_specs=[pl.BlockSpec(memory...]
    unnamed x2 -> x0, blocking collectives: 84.1 us -> none
    reshape x0 -> x15, local copies, waits for them, and re-layouts: none -> 19.3 us  [the longest x1 8.48 us: on_device(): up_full = mlp_all[:, :rows_u].reshape(-1, w_up.shape[1])]
    all_gather x4 -> x2, waiting for transfers between devices: 81.1 us -> 66.3 us  [the longest x1 60.5 us: on_device(): attn_all = lax.all_gather(attn_buf, ALL, axis=0, tiled=False)]
    slice x0 -> x5, local copies, waits for them, and re-layouts: none -> 14.5 us  [the longest x1 8.09 us: on_device(): down_full = mlp_all[:, rows_u:].reshape(-1, model_width)]
    dot_general x2, matrix products: 6.7 us -> 16.3 us  [attend_back(): jnp.einsum('hqk,qhe->khe', soft_w.astype(jnp.bfloat16), grad_out, preferr...]
    unnamed x104 -> x107, local copies, waits for them, and re-layouts: 29.2 us -> 19.9 us
  transfers between devices with their start and end apart: 8 -> 2, of which waited for: 6 -> 2; matrix products, arithmetic and copies ran while one was open for 37% -> 11% of each run, Pallas kernels for 0% -> 0%
where the time goes in v1:
time: 756 us; the launch traced here: 746 us
  matrix products  269 us (36%)
  Pallas kernels  247 us (33%)
  local copies, waits for them, and re-layouts  112 us (15%)
  waiting for transfers between devices  66.3 us (9%)
  other arithmetic  34.8 us (5%)
  between operations  15 us (2%)
    pallas_call x1, Pallas kernels, ring_reduce_scatter(): pl.pallas_call(kernel, out_shape=out_shape, in_specs=[pl.BlockSpec(memory...  247 us
    all_gather x1, waiting for transfers between devices, on_device(): attn_all = lax.all_gather(attn_buf, ALL, axis=0, tiled=False)  60.5 us
    dot_general x1, matrix products, on_device(): jnp.dot(h_two, up_full, preferred_element_type=jnp.float32)  50.4 us
    dot_general x2, matrix products, attend_back(): jnp.einsum('hqk,qhe->khe', grad_s, queries, preferred_element_type=jnp.fl...  40.8 us
    dot_general x2, matrix products, attend_back(): jnp.einsum('hqk,khe->qhe', grad_s, key_rows, preferred_element_type=jnp.f...  40.1 us
    unnamed x107, local copies, waits for them, and re-layouts  19.9 us
    dot_general x2, matrix products, attend_back(): jnp.einsum('hqk,qhe->khe', soft_w.astype(jnp.bfloat16), grad_out, preferr...  16.3 us
    dot_general x2, matrix products, attend_back(): jnp.einsum('qhe,khe->hqk', grad_out, value_rows, preferred_element_type=j...  15.4 us
  transfers between devices with their start and end apart: 2, of which 2 were waited for; matrix products, arithmetic and copies ran while one was open for 11% of the time, Pallas kernels for 0%

profile of v1, /device:TPU:1, one launch (start us, length us, event | category | flops | bytes accessed | tf_op | source)
XLA Modules:
  0.0 745.5 jit_solution(7504299344218383858)
XLA Ops:
  7.2 5.5 concatenate.23
  16.3 1.6 pad_maximum_fusion
  18.0 1.7 copy.110
  19.7 1.7 copy.120
  22.2 60.5 %all-gather.8.cloned.1.call-done = bf16[32,97,768]{2,1,0:T(8,128)(2,1)} async-done(((bf16[1,97,768]{2,1,0:T(8,128)(2,1)}), bf16[32,97,768]{2,1,0:T(8,128)(2,1)}) %all-gather.8.cloned.1.call-update) | async-done | bytes 4767760 | tf_op jit(solution)/shard_map/all_gather | solution.py:271
  83.9 4.0 slice.116
  87.9 6.6 reshape.364
  94.9 6.3 fusion.123
  101.3 2.3 fusion.116
  103.6 1.7 copy.112
  105.3 2.4 reshape.365
  107.7 2.9 copy.115
  110.6 1.7 copy.113
  112.3 2.4 reshape.366
  114.7 1.7 copy.116
  118.0 3.8 reshape.367
  121.9 1.8 copy.117
  124.9 21.4 %while.26 = (s32[]{:T(128)}, bf16[2,512,12,64]{1,3,2,0:T(8,128)(2,1)}, f32[2,12,512,1]{2,1,3,0:T(8,128)S(1)}, bf16[2,512,12,64]{1,3,2,0:T(8,128)(2,1)}, s32[2,51...) while((s32[]{:T(128)}, ...), condition=%wide.region_5.6_spmd, body=%wide.region_2.5_spmd.sunk | while | flops 844098048 | bytes 42962032 | solution.py:296
  125.6 2.1 fusion.170
  127.8 2.6 fusion.171
  130.3 5.5 bitcast_dynamic-update-slice_fusion.10
  136.1 2.1 fusion.170
  138.3 2.6 fusion.171
  140.8 5.5 bitcast_dynamic-update-slice_fusion.10
  146.4 3.0 copy.118
  153.4 5.7 fusion.129
  159.1 2.3 multiply_reduce_fusion.3
  161.4 5.8 all-gather.6.cloned.1.call-done
  167.2 8.1 %fusion.127 = (bf16[32,96,768]{2,1,0:T(8,128)(2,1)}, bf16[32,96,768]{2,1,0:T(8,128)(2,1)}) fusion(bf16[32,192,768]{2,1,0:T(8,128)(2,1)} %bitcast.165), kind=kLoop, calls=%fused_computation.181 | loop fusion | bytes 18874368 | tf_op jit(solution)/shard_map/slice | solution.py:280
  175.3 8.5 %reshape.370 = bf16[768,3072]{1,0:T(8,128)(2,1)} reshape(bf16[32,96,768]{2,1,0:T(8,128)(2,1)} %get-tuple-element.312) | data formatting | bytes 9437184 | tf_op jit(solution)/shard_map/reshape | solution.py:279
  183.8 50.4 %fusion.87 = (bf16[1024,3072]{1,0:T(8,128)(2,1)}, f32[1024,3072]{1,0:T(8,128)}) fusion(f32[3072]{0:T(1024)S(1)} %reshape.395, bf16[768,3072]{1,0:T(8,128)(2,1)} %reshape.370, f32[1024,768]{0,1:T(8,128)} %get-tuple-element.331, f32[768]{0:T(1024)S(1)} %reshape.394, f32[768]{0:T(1024)S(1)} %reshape.393, f32[1024]{0:T(1024)S(1)} %add_rsqrt_fusion, ...), kind=kOutput, calls=%fused_computation.83 | convolution fusion | flops 5043388416 | bytes 26765312 | tf_op jit(solution)/shard_map/dot_general | solution.py:307
  234.2 12.4 %convert_reduce_fusion = (f32[3072]{0:T(1024)}, bf16[1024,3072]{1,0:T(8,128)(2,1)S(1)}) fusion(f32[1024,3072]{1,0:T(8,128)} %get-tuple-element.333, f32[3072]{0:T(1024)S(1)} %reshape.395, bf16[3072,768]{1,0:T(8,128)(2,1)S(1)} %bitcast.174, bf16[1024,768]{1,0:T(8,128)(2,1)S(1)} %copy-done.14), kind=kOutput, calls=%fused_computation.90 | convolution fusion | flops 4872729600 | bytes 25190400 | tf_op jit(solution)/shard_map/td,fd->tf/dot_general | solution.py:320
  246.6 7.3 fusion.131
  253.9 3.6 copy.121
  257.5 4.6 multiply_reduce_fusion.1
  262.1 4.4 convert_reduce_fusion.3
  268.2 2.7 convolution_convert_fusion
  270.8 2.6 copy.122
  273.4 3.9 reshape.372
  277.3 2.9 copy.125
  284.2 127.5 %while.27 = (s32[]{:T(128)}, bf16[2,512,12,64]{1,3,2,0:T(8,128)(2,1)}, bf16[2,512,12,64]{1,3,2,0:T(8,128)(2,1)}, bf16[2,512,12,64]{1,3,2,0:T(8,128)(2,1)}, bf16[...) while((s32[]{:T(128)}, ...), condition=%wide.region_12.13_spmd, body=%wide.region_10.12_spmd.sunk | while | flops 2096903680 | bytes 150427792 | solution.py:336
  284.3 7.7 %fusion.182 = f32[12,512,512]{1,2,0:T(8,128)} fusion(bf16[2,512,12,64]{1,3,2,0:T(8,128)(2,1)} %get-tuple-element.523, s32[]{:T(128)S(6)} %copy.165, bf16[2,512,12,64]{1,3,2,0:T(8,128)(2,1)} %get-tuple-element.522), kind=kOutput, calls=%fused_computation.48.clone.1 | convolution fusion | flops 402653184 | bytes 14156800 | tf_op jit(solution)/shard_map/while/body/eval_jaxpr/qhe,khe->hqk/dot_general | solution.py:61
  292.0 6.3 fusion.183
  299.3 20.0 %bitcast_dynamic-update-slice_fusion.12 = bf16[2,512,12,64]{1,3,2,0:T(8,128)(2,1)} fusion(bf16[2,512,12,64]{1,3,2,0:T(8,128)(2,1)} %get-tuple-element.502, s32[]{:T(128)S(6)} %copy.165, f32[12,512,512]{1,2,0:T(8,128)} %fusion.182, f32[12,512,512]{1,2,0:T(8,128)} %fusion.183, f32[12,512]{1,0:T(8,128)S(1)} %dynamic-slice_bitcast_fusion.2, ...), kind=kOutput, calls=%fused_computation.44.clone.1 | convolution fusion | flops 437656064 | bytes 53281792 | tf_op jit(solution)/shard_map/while/body/eval_jaxpr/hqk,khe->qhe/dot_general | solution.py:64
  319.3 20.4 %bitcast_dynamic-update-slice_fusion.13 = bf16[2,512,12,64]{1,3,2,0:T(8,128)(2,1)} fusion(bf16[2,512,12,64]{1,3,2,0:T(8,128)(2,1)} %get-tuple-element.503, s32[]{:T(128)S(6)} %copy.165, f32[12,512,512]{1,2,0:T(8,128)} %fusion.182, f32[12,512,512]{1,2,0:T(8,128)} %fusion.183, f32[12,512]{1,0:T(8,128)S(1)} %dynamic-slice_bitcast_fusion.2, ...), kind=kOutput, calls=%fused_computation.43.clone.1 | convolution fusion | flops 437656064 | bytes 53281792 | tf_op jit(solution)/shard_map/while/body/eval_jaxpr/hqk,qhe->khe/dot_general | solution.py:67
  339.7 8.2 %bitcast_dynamic-update-slice_fusion.14 = bf16[2,512,12,64]{1,3,2,0:T(8,128)(2,1)} fusion(bf16[2,512,12,64]{1,3,2,0:T(8,128)(2,1)} %get-tuple-element.504, s32[]{:T(128)S(6)} %copy.165, f32[12,512,512]{1,2,0:T(8,128)} %fusion.183, f32[12,512]{1,0:T(8,128)S(1)} %dynamic-slice_bitcast_fusion.2, pred[512,512]{0,1:T(8,128)(4,1)} %fusion.184, ...), kind=kOutput, calls=%fused_computation.42.clone.1 | convolution fusion | flops 415236096 | bytes 15229952 | tf_op jit(solution)/shard_map/while/body/eval_jaxpr/hqk,qhe->khe/dot_general | solution.py:58
  347.9 7.7 %fusion.182 = f32[12,512,512]{1,2,0:T(8,128)} fusion(bf16[2,512,12,64]{1,3,2,0:T(8,128)(2,1)} %get-tuple-element.523, s32[]{:T(128)S(6)} %copy.165, bf16[2,512,12,64]{1,3,2,0:T(8,128)(2,1)} %get-tuple-element.522), kind=kOutput, calls=%fused_computation.48.clone.1 | convolution fusion | flops 402653184 | bytes 14156800 | tf_op jit(solution)/shard_map/while/body/eval_jaxpr/qhe,khe->hqk/dot_general | solution.py:61
  355.5 6.3 fusion.183
  362.8 20.0 %bitcast_dynamic-update-slice_fusion.12 = bf16[2,512,12,64]{1,3,2,0:T(8,128)(2,1)} fusion(bf16[2,512,12,64]{1,3,2,0:T(8,128)(2,1)} %get-tuple-element.502, s32[]{:T(128)S(6)} %copy.165, f32[12,512,512]{1,2,0:T(8,128)} %fusion.182, f32[12,512,512]{1,2,0:T(8,128)} %fusion.183, f32[12,512]{1,0:T(8,128)S(1)} %dynamic-slice_bitcast_fusion.2, ...), kind=kOutput, calls=%fused_computation.44.clone.1 | convolution fusion | flops 437656064 | bytes 53281792 | tf_op jit(solution)/shard_map/while/body/eval_jaxpr/hqk,khe->qhe/dot_general | solution.py:64
  382.9 20.4 %bitcast_dynamic-update-slice_fusion.13 = bf16[2,512,12,64]{1,3,2,0:T(8,128)(2,1)} fusion(bf16[2,512,12,64]{1,3,2,0:T(8,128)(2,1)} %get-tuple-element.503, s32[]{:T(128)S(6)} %copy.165, f32[12,512,512]{1,2,0:T(8,128)} %fusion.182, f32[12,512,512]{1,2,0:T(8,128)} %fusion.183, f32[12,512]{1,0:T(8,128)S(1)} %dynamic-slice_bitcast_fusion.2, ...), kind=kOutput, calls=%fused_computation.43.clone.1 | convolution fusion | flops 437656064 | bytes 53281792 | tf_op jit(solution)/shard_map/while/body/eval_jaxpr/hqk,qhe->khe/dot_general | solution.py:67
  403.3 8.2 %bitcast_dynamic-update-slice_fusion.14 = bf16[2,512,12,64]{1,3,2,0:T(8,128)(2,1)} fusion(bf16[2,512,12,64]{1,3,2,0:T(8,128)(2,1)} %get-tuple-element.504, s32[]{:T(128)S(6)} %copy.165, f32[12,512,512]{1,2,0:T(8,128)} %fusion.183, f32[12,512]{1,0:T(8,128)S(1)} %dynamic-slice_bitcast_fusion.2, pred[512,512]{0,1:T(8,128)(4,1)} %fusion.184, ...), kind=kOutput, calls=%fused_computation.42.clone.1 | convolution fusion | flops 415236096 | bytes 15229952 | tf_op jit(solution)/shard_map/while/body/eval_jaxpr/hqk,qhe->khe/dot_general | solution.py:58
  411.6 3.0 copy.127
  420.4 1.7 copy-done.12
  422.2 5.6 fusion.130
  427.9 6.7 fusion.121.refs_0_
  436.1 9.8 %fusion.125.refs_2_ = f32[768,3072]{1,0:T(8,128)} fusion(bf16[1024,3072]{1,0:T(8,128)(2,1)S(1)} %bitcast.185, f32[1024,768]{0,1:T(8,128)} %get-tuple-element.331, f32[768]{0:T(1024)S(1)} %copy-done.41, f32[768]{0:T(1024)S(1)} %copy-done.30, f32[1024]{0:T(1024)S(1)} %copy-done.32, f32[1024]{0:T(1024)S(1)} %copy-done.24), kind=kOutput, calls=%fused_computation.179 | convolution fusion | flops 4835770368 | bytes 18888704 | tf_op jit(solution)/shard_map/td,tf->df/dot_general | solution.py:325
  446.4 3.6 copy.130
  450.0 3.5 fusion.113
  453.6 10.2 %fusion.132.refs_3_ = f32[3072,768]{1,0:T(8,128)} fusion(bf16[1024,3072]{1,0:T(8,128)(2,1)} %get-tuple-element.332, bf16[1024,768]{1,0:T(8,128)(2,1)S(1)} %copy-done.15), kind=kOutput, calls=%fused_computation.186 | convolution fusion | flops 4831838208 | bytes 17301504 | tf_op jit(solution)/shard_map/tf,td->fd/dot_general | solution.py:318
  464.7 247.4 %shard_map.263 = (f32[24,2304]{1,0:T(8,128)S(1)}, f32[24,768]{1,0:T(8,128)S(1)}, f32[24,3072]{1,0:T(8,128)S(1)}, f32[96,768]{1,0:T(8,128)S(1)}, f32[8,128]{1,0:T(8,128)S(1)}) custom-call(f32[768,2304]{1,0:T(8,128)} %fusion.121.refs_0_, f32[768,768]{1,0:T(8,128)S(1)} %fusion.118.refs_1_, f32[768,3072]{1,0:T(8,128)} %fusion.125.refs_2_, ...), custom_call_target="tpu_custom_call" | custom-call | flops 7110656 | bytes 56885248 | tf_op jit(solution)/shard_map/pallas_call | solution.py:211
  713.8 10.2 %add_convert_fusion = bf16[1024,768]{0,1:T(8,128)(2,1)} fusion(f32[1024,768]{0,1:T(8,128)} %get-tuple-element.331, bf16[1024,3072]{1,0:T(8,128)(2,1)} %get-tuple-element.332, bf16[3072,768]{1,0:T(8,128)(2,1)} %bitcast.173, f32[768]{0:T(1024)S(1)} %copy-done.39), kind=kOutput, calls=%fused_computation.136 | convolution fusion | flops 4834197504 | bytes 15731712 | tf_op jit(solution)/shard_map/dot_general | solution.py:313
  724.0 2.7 copy.133
  726.7 5.5 fusion.112
  732.2 3.5 copy.134
  (181 shorter events, 34.2 us)
Async XLA Ops:
  7.2 12.5 %copy-start.13 = (bf16[1024,768]{1,0:T(8,128)(2,1)S(1)}, bf16[1024,768]{1,0:T(8,128)(2,1)}, u32[]{:S(2)}) copy-start(bf16[1024,768]{1,0:T(8,128)(2,1)} %param.35) | copy-start | bytes 4718596
  7.2 75.5 %all-gather.8.cloned.1.call-start = ((), (), s32[]{:S(2)}) async-start(), calls=%async_computation.1 | async-start | bytes 5271552 | tf_op jit(solution)/shard_map/all_gather | solution.py:271
  15.2 151.9 %all-gather.6.cloned.1.call-start = ((), (), s32[]{:S(2)}) async-start(), calls=%async_computation | async-start | bytes 9732096 | tf_op jit(solution)/shard_map/all_gather | solution.py:278
  19.7 75.1 %copy-start = (bf16[1024,768]{0,1:T(8,128)(2,1)}, bf16[1024,768]{0,1:T(8,128)(2,1)S(1)}, u32[]{:S(2)}) copy-start(bf16[1024,768]{0,1:T(8,128)(2,1)S(1)} %copy.110) | copy-start | bytes 4718596
  21.7 73.1 %copy-start.21 = (f32[1024]{0:T(1024)}, f32[1024]{0:T(1024)S(1)}, u32[]{:S(2)}) copy-start(f32[1024]{0:T(1024)S(1)} %broadcast_multiply_fusion.5) | copy-start | bytes 12292
  22.2 72.6 %copy-start.27 = (f32[1024]{0:T(1024)}, f32[1024]{0:T(1024)S(1)}, u32[]{:S(2)}) copy-start(f32[1024]{0:T(1024)S(1)} %add_rsqrt_fusion.1) | copy-start | bytes 12292
  94.6 6.6 copy-start.37
  94.7 6.5 copy-start.25
  121.9 3.1 copy-start.19
  121.9 3.1 copy-start.20
  151.2 32.5 %copy-start.40 = (f32[768]{0:T(1024)}, f32[768]{0:T(1024)S(1)}, u32[]{:S(2)}) copy-start(f32[768]{0:T(1024)S(1)} %reshape.394) | copy-start | bytes 9220
  151.3 110.8 %copy-start.29 = (f32[768]{0:T(1024)}, f32[768]{0:T(1024)S(1)}, u32[]{:S(2)}) copy-start(f32[768]{0:T(1024)S(1)} %reshape.393) | copy-start | bytes 9220
  153.4 5.7 copy-start.17
  159.1 103.0 %copy-start.23 = (f32[1024]{0:T(1024)}, f32[1024]{0:T(1024)S(1)}, u32[]{:S(2)}) copy-start(f32[1024]{0:T(1024)S(1)} %broadcast_multiply_fusion.4) | copy-start | bytes 12292
  161.4 100.7 %copy-start.31 = (f32[1024]{0:T(1024)}, f32[1024]{0:T(1024)S(1)}, u32[]{:S(2)}) copy-start(f32[1024]{0:T(1024)S(1)} %add_rsqrt_fusion) | copy-start | bytes 12292
  183.7 50.4 %copy-start.11 = (bf16[32,96,768]{2,1,0:T(8,128)(2,1)S(1)}, bf16[32,96,768]{2,1,0:T(8,128)(2,1)}, u32[]{:S(2)}) copy-start(bf16[32,96,768]{2,1,0:T(8,128)(2,1)} %get-tuple-element.311) | copy-start | bytes 14155780
  183.7 50.4 %copy-start.14 = (bf16[1024,768]{1,0:T(8,128)(2,1)S(1)}, bf16[1024,768]{1,0:T(8,128)(2,1)}, u32[]{:S(2)}) copy-start(bf16[1024,768]{1,0:T(8,128)(2,1)} %param.35) | copy-start | bytes 4718596
  234.2 12.4 %copy-start.10 = (bf16[768,3072]{1,0:T(8,128)(2,1)S(1)}, bf16[768,3072]{1,0:T(8,128)(2,1)}, u32[]{:S(2)}) copy-start(bf16[768,3072]{1,0:T(8,128)(2,1)} %reshape.370) | copy-start | bytes 14155780
  246.6 7.3 copy-start.43
  257.5 4.6 copy-start.3
  257.5 4.6 copy-start.9
  262.1 6.0 copy-start.18
  266.5 1.6 copy-start.6
  414.7 1.4 copy-start.8
  416.1 2.0 copy-start.5
  420.2 2.0 copy-start.12
  422.2 5.6 copy-start.1
  422.2 5.6 copy-start.22
  422.2 5.6 copy-start.26
  422.2 5.6 copy-start.28
  422.2 5.6 copy-start.38
  422.2 13.8 %slice-start = ((s8[6291456]{0:T(1024)(128)(4,1)}), s8[4194304]{0:T(1024)(128)(4,1)S(1)}, s32[]{:S(2)}) async-start(s8[6291456]{0:T(1024)(128)(4,1)} %bitcast.184), calls=%async_computation.2 | async-start | bytes 8388608
  427.8 6.7 copy-start.7
  427.8 6.7 copy-start.16
  427.9 8.2 %slice-start.1 = ((s8[6291456]{0:T(1024)(128)(4,1)}), s8[2097152]{0:T(1024)(128)(4,1)S(1)}, s32[]{:S(2)}) async-start(s8[6291456]{0:T(1024)(128)(4,1)} %bitcast.184), calls=%async_computation.3 | async-start | bytes 4194304
  434.6 1.5 copy-start.24
  434.6 1.5 copy-start.30
  434.6 1.5 copy-start.32
  434.6 1.5 copy-start.41
  436.1 10.1 %copy-start.4 = (bf16[2,512,12,64]{1,3,2,0:T(8,128)(2,1)S(1)}, bf16[2,512,12,64]{1,3,2,0:T(8,128)(2,1)}, u32[]{:S(2)}) copy-start(bf16[2,512,12,64]{1,3,2,0:T(8,128)(2,1)} %get-tuple-element.123) | copy-start | bytes 4718596
  450.0 3.5 copy-start.15
  453.5 10.4 %copy-start.35 = (f32[768]{0:T(1024)S(1)}, f32[768]{0:T(1024)}, u32[]{:S(2)}) copy-start(f32[768]{0:T(1024)} %get-tuple-element.307) | copy-start | bytes 9220
  453.5 10.7 %copy-start.33 = (f32[768]{0:T(1024)S(1)}, f32[768]{0:T(1024)}, u32[]{:S(2)}) copy-start(f32[768]{0:T(1024)} %get-tuple-element.263) | copy-start | bytes 9220
  453.5 10.8 %copy-start.42 = (f32[768]{0:T(1024)S(1)}, f32[768]{0:T(1024)}, u32[]{:S(2)}) copy-start(f32[768]{0:T(1024)} %get-tuple-element.336) | copy-start | bytes 9220
  453.5 10.9 %copy-start.36 = (f32[3072]{0:T(1024)S(1)}, f32[3072]{0:T(1024)}, u32[]{:S(2)}) copy-start(f32[3072]{0:T(1024)} %get-tuple-element.338) | copy-start | bytes 36868
  453.6 10.9 %copy-start.34 = (f32[768]{0:T(1024)S(1)}, f32[768]{0:T(1024)}, u32[]{:S(2)}) copy-start(f32[768]{0:T(1024)} %get-tuple-element.315) | copy-start | bytes 9220
  464.7 249.1 %copy-start.39 = (f32[768]{0:T(1024)S(1)}, f32[768]{0:T(1024)}, u32[]{:S(2)}) copy-start(f32[768]{0:T(1024)} %reshape.396) | copy-start | bytes 9220
  724.0 2.7 copy-start.2
Sparse Core Ops, SparseCore 0:
  15.3 67.3 all-gather.7
  86.2 80.9 all-gather.5

commit v2 on v1

--- a/solution.py
+++ b/solution.py
@@ -27,51 +27,131 @@
     )
 
 
-def key_mask(segment, valid_keys):
-    length = segment.shape[0]
-    same = segment[:, None] == segment[None, :]
-    return same & ((valid_keys[None, :] == 1) | jnp.eye(length, dtype=bool))
-
-
-def attend(item):
-    queries, key_rows, value_rows, segment, valid_keys = item
-    allowed = key_mask(segment, valid_keys)
-    scores = jnp.einsum("qhe,khe->hqk", queries, key_rows, preferred_element_type=jnp.float32) * (
-        1.0 / HD**0.5
-    )
-    scores = jnp.where(allowed[None], scores, -1e30)
-    top_score = jnp.max(scores, axis=-1, keepdims=True)
-    expo = jnp.exp(scores - top_score)
-    total = jnp.sum(expo, axis=-1, keepdims=True)
-    soft_w = (expo / total).astype(jnp.bfloat16)
-    attended = jnp.einsum("hqk,khe->qhe", soft_w, value_rows, preferred_element_type=jnp.float32)
-    return (attended, top_score + jnp.log(total))
-
-
-def attend_back(item):
-    queries, key_rows, value_rows, grad_out, log_total, segment, valid_keys = item
-    allowed = key_mask(segment, valid_keys)
-    scores = jnp.einsum("qhe,khe->hqk", queries, key_rows, preferred_element_type=jnp.float32) * (
-        1.0 / HD**0.5
-    )
-    soft_w = jnp.where(allowed[None], jnp.exp(scores - log_total), 0.0)
-    grad_v = jnp.einsum(
-        "hqk,qhe->khe", soft_w.astype(jnp.bfloat16), grad_out, preferred_element_type=jnp.float32
-    )
-    grad_p = jnp.einsum("qhe,khe->hqk", grad_out, value_rows, preferred_element_type=jnp.float32)
-    row_term = jnp.sum(soft_w * grad_p, axis=-1, keepdims=True)
-    grad_s = jnp.where(allowed[None], soft_w * (grad_p - row_term), 0.0).astype(jnp.bfloat16)
-    grad_q = jnp.einsum("hqk,khe->qhe", grad_s, key_rows, preferred_element_type=jnp.float32) * (
-        1.0 / HD**0.5
-    )
-    grad_k = jnp.einsum("hqk,qhe->khe", grad_s, queries, preferred_element_type=jnp.float32) * (
-        1.0 / HD**0.5
-    )
-    return (grad_q, grad_k, grad_v)
-
-
 def col_sum(rows):
     return jnp.sum(rows.astype(jnp.float32), axis=0)
+
+
+def seg_mask(seg_col, seg_row, val_row, n):
+    rows = lax.broadcasted_iota(jnp.int32, (n, n), 0)
+    cols = lax.broadcasted_iota(jnp.int32, (n, n), 1)
+    return (seg_col == seg_row) & ((val_row == 1) | (rows == cols))
+
+
+def soft_rows(qh, kh, allowed):
+    scores = lax.dot_general(qh, kh, (((1,), (1,)), ((), ())), preferred_element_type=jnp.float32)
+    scores = jnp.where(allowed, scores * (1.0 / HD**0.5), -1e30)
+    top = jnp.max(scores, axis=-1, keepdims=True)
+    expo = jnp.exp(scores - top)
+    return expo * (1.0 / jnp.sum(expo, axis=-1, keepdims=True))
+
+
+def attn_fwd_kernel(q_ref, k_ref, v_ref, sc_ref, sr_ref, vr_ref, o_ref):
+    n = q_ref.shape[0]
+    allowed = seg_mask(sc_ref[...], sr_ref[...], vr_ref[...], n)
+    outs = []
+    for j in range(q_ref.shape[1] // HD):
+        cols = slice(j * HD, (j + 1) * HD)
+        probs = soft_rows(q_ref[:, cols], k_ref[:, cols], allowed).astype(jnp.bfloat16)
+        outs.append(jnp.dot(probs, v_ref[:, cols], preferred_element_type=jnp.float32))
+    o_ref[...] = jnp.concatenate(outs, axis=1).astype(o_ref.dtype)
+
+
+def attn_bwd_kernel(q_ref, k_ref, v_ref, do_ref, sc_ref, sr_ref, vr_ref, dqkv_ref):
+    n = q_ref.shape[0]
+    width = q_ref.shape[1]
+    hp = pl.program_id(1)
+    model_width = dqkv_ref.shape[1] // 3
+    allowed = seg_mask(sc_ref[...], sr_ref[...], vr_ref[...], n)
+    dqs, dks, dvs = [], [], []
+    for j in range(width // HD):
+        cols = slice(j * HD, (j + 1) * HD)
+        qh, kh, vh, doh = q_ref[:, cols], k_ref[:, cols], v_ref[:, cols], do_ref[:, cols]
+        probs = soft_rows(qh, kh, allowed)
+        dvs.append(
+            lax.dot_general(probs.astype(jnp.bfloat16), doh, (((0,), (0,)), ((), ())),
+                            preferred_element_type=jnp.float32)
+        )
+        dprobs = lax.dot_general(doh, vh, (((1,), (1,)), ((), ())), preferred_element_type=jnp.float32)
+        row_term = jnp.sum(probs * dprobs, axis=-1, keepdims=True)
+        dscore = jnp.where(allowed, probs * (dprobs - row_term), 0.0).astype(jnp.bfloat16)
+        dqs.append(jnp.dot(dscore, kh, preferred_element_type=jnp.float32) * (1.0 / HD**0.5))
+        dks.append(
+            lax.dot_general(dscore, qh, (((0,), (0,)), ((), ())), preferred_element_type=jnp.float32)
+            * (1.0 / HD**0.5)
+        )
+    at = pl.multiple_of(hp * width, width)
+    dqkv_ref[:, pl.ds(at, width)] = jnp.concatenate(dqs, axis=1).astype(dqkv_ref.dtype)
+    dqkv_ref[:, pl.ds(at + model_width, width)] = jnp.concatenate(dks, axis=1).astype(dqkv_ref.dtype)
+    dqkv_ref[:, pl.ds(at + 2 * model_width, width)] = jnp.concatenate(dvs, axis=1).astype(dqkv_ref.dtype)
+
+
+def mask_operands(segment_ids, valid):
+    return (segment_ids[:, :, None], segment_ids[:, None, :], valid[:, None, :])
+
+
+def attention_fwd(qkv, segment_ids, valid):
+    rows, width3 = qkv.shape
+    model_width = width3 // 3
+    n_seq, seq_len = segment_ids.shape
+    blk = 2 * HD
+    n_hp = model_width // blk
+    off = model_width // blk
+    seg_spec = [
+        pl.BlockSpec((None, seq_len, 1), lambda s, h: (s, 0, 0)),
+        pl.BlockSpec((None, 1, seq_len), lambda s, h: (s, 0, 0)),
+        pl.BlockSpec((None, 1, seq_len), lambda s, h: (s, 0, 0)),
+    ]
+    flops = 4 * n_seq * seq_len * seq_len * model_width
+    return pl.pallas_call(
+        attn_fwd_kernel,
+        out_shape=jax.ShapeDtypeStruct((rows, model_width), jnp.bfloat16),
+        grid=(n_seq, n_hp),
+        in_specs=[
+            pl.BlockSpec((seq_len, blk), lambda s, h: (s, h)),
+            pl.BlockSpec((seq_len, blk), lambda s, h: (s, off + h)),
+            pl.BlockSpec((seq_len, blk), lambda s, h: (s, 2 * off + h)),
+        ]
+        + seg_spec,
+        out_specs=pl.BlockSpec((seq_len, blk), lambda s, h: (s, h)),
+        cost_estimate=pl.CostEstimate(
+            flops=flops,
+            transcendentals=n_seq * seq_len * seq_len * (model_width // HD),
+            bytes_accessed=qkv.size * 2 + rows * model_width * 2,
+        ),
+    )(qkv, qkv, qkv, *mask_operands(segment_ids, valid))
+
+
+def attention_bwd(qkv, grad_o, segment_ids, valid):
+    rows, width3 = qkv.shape
+    model_width = width3 // 3
+    n_seq, seq_len = segment_ids.shape
+    blk = 2 * HD
+    n_hp = model_width // blk
+    off = model_width // blk
+    seg_spec = [
+        pl.BlockSpec((None, seq_len, 1), lambda s, h: (s, 0, 0)),
+        pl.BlockSpec((None, 1, seq_len), lambda s, h: (s, 0, 0)),
+        pl.BlockSpec((None, 1, seq_len), lambda s, h: (s, 0, 0)),
+    ]
+    flops = 10 * n_seq * seq_len * seq_len * model_width
+    return pl.pallas_call(
+        attn_bwd_kernel,
+        out_shape=jax.ShapeDtypeStruct((rows, width3), jnp.bfloat16),
+        grid=(n_seq, n_hp),
+        in_specs=[
+            pl.BlockSpec((seq_len, blk), lambda s, h: (s, h)),
+            pl.BlockSpec((seq_len, blk), lambda s, h: (s, off + h)),
+            pl.BlockSpec((seq_len, blk), lambda s, h: (s, 2 * off + h)),
+            pl.BlockSpec((seq_len, blk), lambda s, h: (s, h)),
+        ]
+        + seg_spec,
+        out_specs=pl.BlockSpec((seq_len, width3), lambda s, h: (s, 0)),
+        cost_estimate=pl.CostEstimate(
+            flops=flops,
+            transcendentals=n_seq * seq_len * seq_len * (model_width // HD),
+            bytes_accessed=qkv.size * 4 + rows * model_width * 2,
+        ),
+    )(qkv, qkv, qkv, grad_o, *mask_operands(segment_ids, valid))
 
 
 MESH_ID = pl.DeviceIdType.MESH
@@ -286,15 +366,10 @@
     normed_one, recip_one = norm_parts(rows)
     h_one = (normed_one * gain_one + shift_one).astype(jnp.bfloat16)
     qkv_rows = jnp.dot(h_one, qkv_full, preferred_element_type=jnp.float32)
-    queries = (qkv_rows[:, :model_width] + qv_full[:model_width]).astype(jnp.bfloat16)
-    key_rows = qkv_rows[:, model_width : 2 * model_width].astype(jnp.bfloat16)
-    value_rows = (qkv_rows[:, 2 * model_width :] + qv_full[model_width:]).astype(jnp.bfloat16)
-    shape_seq = (seq_count, seq_len, head_count, HD)
-    q_seq = queries.reshape(shape_seq)
-    k_seq = key_rows.reshape(shape_seq)
-    v_seq = value_rows.reshape(shape_seq)
-    attended, log_total = lax.map(attend, (q_seq, k_seq, v_seq, segment_ids, valid))
-    attended = attended.reshape(row_count, model_width).astype(jnp.bfloat16)
+    zero_bias = jnp.zeros((model_width,), jnp.float32)
+    qkv_bias = jnp.concatenate([qv_full[:model_width], zero_bias, qv_full[model_width:]])
+    qkv_b = (qkv_rows + qkv_bias).astype(jnp.bfloat16)
+    attended = attention_fwd(qkv_b, segment_ids, valid)
     mid_rows = (
         rows
         + jnp.dot(attended, out_full, preferred_element_type=jnp.float32)
@@ -333,14 +408,9 @@
     grad_o = jnp.einsum("td,cd->tc", grad_a, out_full, preferred_element_type=jnp.float32).astype(
         jnp.bfloat16
     )
-    grad_q, grad_k, grad_v = lax.map(
-        attend_back, (q_seq, k_seq, v_seq, grad_o.reshape(shape_seq), log_total, segment_ids, valid)
-    )
-    grad_q = grad_q.reshape(row_count, model_width).astype(jnp.bfloat16)
-    grad_k = grad_k.reshape(row_count, model_width).astype(jnp.bfloat16)
-    grad_v = grad_v.reshape(row_count, model_width).astype(jnp.bfloat16)
-    grad_qkv = jnp.concatenate([grad_q, grad_k, grad_v], axis=1)
-    grad_bqv = jnp.concatenate([col_sum(grad_q), col_sum(grad_v)])
+    grad_qkv = attention_bwd(qkv_b, grad_o, segment_ids, valid)
+    grad_cols = col_sum(grad_qkv)
+    grad_bqv = jnp.concatenate([grad_cols[:model_width], grad_cols[2 * model_width :]])
     grad_wqkv = jnp.einsum("td,te->de", h_one, grad_qkv, preferred_element_type=jnp.float32)
     grad_h1 = jnp.einsum("te,de->td", grad_qkv, qkv_full, preferred_element_type=jnp.float32)
     grad_g1 = jnp.sum(grad_h1 * normed_one, axis=0)

time: 756 us -> 621 us (0.82)
  matrix products: 269 us -> 113 us
  Pallas kernels: 247 us -> 314 us
  local copies, waits for them, and re-layouts: 112 us -> 66 us
  waiting for transfers between devices: 66.3 us -> 85 us
  other arithmetic: 34.8 us -> 18.5 us
    dot_general x14 -> x0, matrix products: 140 us -> none  [the longest x2 40.8 us: attend_back(): jnp.einsum('hqk,qhe->khe', grad_s, queries, preferred_element_type=jnp.fl...]
    pallas_call x0 -> x2, Pallas kernels: none -> 66.1 us  [the longest x1 36.2 us: attention_bwd(): pl.pallas_call(attn_bwd_kernel, out_shape=jax.ShapeDtypeStruct((rows, wid...]
    all_gather x1, waiting for transfers between devices: 5.76 us -> 26.6 us  [on_device(): mlp_all = lax.all_gather(mlp_buf, ALL, axis=0, tiled=False)]
    convert_element_type x7 -> x0, local copies, waits for them, and re-layouts: 15.3 us -> none  [the longest x1 3.03 us: on_device(): attended = attended.reshape(row_count, model_width).astype(jnp.bfloat16)]
    reshape x4 -> x0, local copies, waits for them, and re-layouts: 12.4 us -> none  [the longest x1 3.86 us: on_device(): grad_o.reshape(shape_seq)]
    dot_general x1, matrix products: 50.4 us -> 38.2 us  [on_device(): jnp.dot(h_two, up_full, preferred_element_type=jnp.float32)]
    while x4 -> x0, local copies, waits for them, and re-layouts: 9.25 us -> none  [the longest x3 6.37 us: on_device(): lax.map(attend, (q_seq, k_seq, v_seq, segment_ids, valid))]
    unnamed x107 -> x75, local copies, waits for them, and re-layouts: 19.9 us -> 15.5 us
  transfers between devices with their start and end apart: 2 -> 2, of which waited for: 2 -> 2; matrix products, arithmetic and copies ran while one was open for 11% -> 6% of each run, Pallas kernels for 0% -> 5%
where the time goes in v2:
time: 621 us; the launch traced here: 612 us
  Pallas kernels  314 us (51%)
  matrix products  113 us (18%)
  waiting for transfers between devices  85 us (14%)
  local copies, waits for them, and re-layouts  66 us (11%)
  other arithmetic  18.5 us (3%)
  between operations  15 us (2%)
    pallas_call x1, Pallas kernels, ring_reduce_scatter(): pl.pallas_call(kernel, out_shape=out_shape, in_specs=[pl.BlockSpec(memory...  248 us
    all_gather x1, waiting for transfers between devices, on_device(): attn_all = lax.all_gather(attn_buf, ALL, axis=0, tiled=False)  58.4 us
    dot_general x1, matrix products, on_device(): jnp.dot(h_two, up_full, preferred_element_type=jnp.float32)  38.2 us
    pallas_call x1, Pallas kernels, attention_bwd(): pl.pallas_call(attn_bwd_kernel, out_shape=jax.ShapeDtypeStruct((rows, wid...  36.2 us
    pallas_call x1, Pallas kernels, attention_fwd(): pl.pallas_call(attn_fwd_kernel, out_shape=jax.ShapeDtypeStruct((rows, mod...  29.8 us
    all_gather x1, waiting for transfers between devices, on_device(): mlp_all = lax.all_gather(mlp_buf, ALL, axis=0, tiled=False)  26.6 us
    unnamed x75, local copies, waits for them, and re-layouts  15.5 us
  transfers between devices with their start and end apart: 2, of which 2 were waited for; matrix products, arithmetic and copies ran while one was open for 6% of the time, Pallas kernels for 5%

profile of v2, /device:TPU:1, one launch (start us, length us, event | category | flops | bytes accessed | tf_op | source)
XLA Modules:
  0.0 611.8 jit_solution(13128027724760635565)
XLA Ops:
  7.3 1.1 reshape.215
  8.3 5.4 concatenate.23
  13.8 1.4 maximum_bitcast_fusion
  15.3 1.0 reshape.218
  16.3 1.6 pad_maximum_fusion
  18.0 1.7 copy.61
  19.7 0.6 broadcast_in_dim.13.sr_ref
  20.4 1.0 copy.63.sc_ref
  21.4 0.6 broadcast_in_dim.14.vr_ref
  22.0 1.6 copy.65
  23.6 0.3 convert_reduce_fusion.2
  23.9 0.5 fusion.29
  24.4 58.4 %all-gather.8.cloned.1.call-done = bf16[32,97,768]{2,1,0:T(8,128)(2,1)} async-done(((bf16[1,97,768]{2,1,0:T(8,128)(2,1)}), bf16[32,97,768]{2,1,0:T(8,128)(2,1)}) %all-gather.8.cloned.1.call-update) | async-done | bytes 4767760 | tf_op jit(solution)/shard_map/all_gather | solution.py:351
  82.7 1.0 slice.122
  83.7 0.1 slice_convert_fusion
  83.8 0.1 reshape.238
  84.1 0.1 reshape.239
  84.2 4.0 slice.125
  88.1 6.6 %reshape.216 = bf16[768,2304]{1,0:T(8,128)(2,1)} reshape(bf16[32,72,768]{2,1,0:T(8,128)(2,1)} %slice.125) | data formatting | bytes 7077888 | tf_op jit(solution)/shard_map/reshape | solution.py:352
  94.8 0.1 reshape.241
  94.9 0.1 reshape.242
  95.1 0.7 reshape.244
  95.8 1.4 slice.129
  97.2 8.2 %add_convert_fusion.q_ref.k_ref.v_ref = bf16[1024,2304]{1,0:T(8,128)(2,1)} fusion(bf16[768,2304]{1,0:T(8,128)(2,1)} %reshape.216, f32[2304]{0:T(1024)S(1)} %pad_maximum_fusion.2, bf16[1024,768]{0,1:T(8,128)(2,1)S(1)} %copy.61, f32[768]{0:T(1024)S(1)} %reshape.239, f32[768]{0:T(1024)S(1)} %reshape.238, f32[1024]{0:T(1024)S(1)} %add_rsqrt_fusion.1, ...), kind=kOutput, calls=%fused_computation.28 | convolution fusion | flops 3633315840 | bytes 9853952 | tf_op jit(solution)/shard_map/dot_general | solution.py:368
  105.4 29.8 %shard_map.263 = bf16[1024,768]{1,0:T(8,128)(2,1)} custom-call(bf16[1024,2304]{1,0:T(8,128)(2,1)} %add_convert_fusion.q_ref.k_ref.v_ref, bf16[1024,2304]{1,0:T(8,128)(2,1)} %add_convert_fusion.q_ref.k_ref.v_ref, bf16[1024,2304]{1,0:T(8,128)(2,1)} %add_convert_fusion.q_ref.k_ref.v_ref, s32[2,512,1]{2,1,0:T(8,128)} %copy.63.sc_ref, ...), custom_call_target="tpu_custom_call" | custom-call | flops 1610612736 | bytes 6291456 | tf_op jit(solution)/shard_map/pallas_call | solution.py:105
  135.3 3.1 fusion.42
  138.4 1.6 copy-done.3
  140.0 0.4 multiply_reduce_fusion.2
  140.4 26.6 %all-gather.6.cloned.1.call-done = bf16[6144,768]{1,0:T(8,128)(2,1)} async-done(((bf16[192,768]{1,0:T(8,128)(2,1)}), bf16[6144,768]{1,0:T(8,128)(2,1)}) %all-gather.6.cloned.1.call-update) | async-done | bytes 9437200 | tf_op jit(solution)/shard_map/all_gather | solution.py:358
  167.0 8.0 %fusion.39 = (bf16[32,96,768]{2,1,0:T(8,128)(2,1)}, bf16[32,96,768]{2,1,0:T(8,128)(2,1)}) fusion(bf16[32,192,768]{2,1,0:T(8,128)(2,1)} %bitcast.49), kind=kLoop, calls=%fused_computation.94 | loop fusion | bytes 18874368 | tf_op jit(solution)/shard_map/slice | solution.py:360
  175.0 8.6 %reshape.219 = bf16[768,3072]{1,0:T(8,128)(2,1)} reshape(bf16[32,96,768]{2,1,0:T(8,128)(2,1)} %get-tuple-element.89) | data formatting | bytes 9437184 | tf_op jit(solution)/shard_map/reshape | solution.py:359
  183.7 38.2 %fusion.2 = (bf16[1024,3072]{1,0:T(8,128)(2,1)}, f32[1024,3072]{1,0:T(8,128)}) fusion(f32[3072]{0:T(1024)S(1)} %reshape.243, bf16[768,3072]{1,0:T(8,128)(2,1)} %reshape.219, f32[1024,768]{0,1:T(8,128)S(1)} %copy-done.4, f32[768]{0:T(1024)S(1)} %reshape.242, f32[768]{0:T(1024)S(1)} %reshape.241, f32[1024]{0:T(1024)S(1)} %add_rsqrt_fusion, ...), kind=kOutput, calls=%fused_computation.4 | convolution fusion | flops 5043388416 | bytes 26765312 | tf_op jit(solution)/shard_map/dot_general | solution.py:382
  221.9 11.8 %convert_reduce_fusion = (f32[3072]{0:T(1024)S(1)}, bf16[1024,3072]{1,0:T(8,128)(2,1)S(1)}) fusion(f32[1024,3072]{1,0:T(8,128)} %get-tuple-element.110, f32[3072]{0:T(1024)S(1)} %reshape.243, bf16[3072,768]{1,0:T(8,128)(2,1)S(1)} %bitcast.51, bf16[1024,768]{1,0:T(8,128)(2,1)S(1)} %copy-done.16), kind=kOutput, calls=%fused_computation.11 | convolution fusion | flops 4872729600 | bytes 25190400 | tf_op jit(solution)/shard_map/td,fd->tf/dot_general | solution.py:395
  233.7 6.7 %fusion.44 = (f32[768]{0:T(1024)S(1)}, f32[1024,768]{1,0:T(8,128)}) fusion(bf16[1024,3072]{1,0:T(8,128)(2,1)S(1)} %get-tuple-element.116, bf16[768,3072]{1,0:T(8,128)(2,1)S(1)} %copy-done.12), kind=kOutput, calls=%fused_computation.99 | convolution fusion | flops 4832623616 | bytes 14158848 | tf_op jit(solution)/shard_map/tf,df->td/dot_general | solution.py:401
  240.5 3.6 copy.66
  244.1 3.0 multiply_reduce_fusion
  247.1 0.3 copy-done.11
  247.4 1.8 convert_reduce_fusion.4
  249.2 1.7 copy-done.8
  250.8 2.6 convolution_convert_fusion.do_ref
  253.4 36.2 %shard_map.264 = bf16[1024,2304]{1,0:T(8,128)(2,1)} custom-call(bf16[1024,2304]{1,0:T(8,128)(2,1)} %add_convert_fusion.q_ref.k_ref.v_ref, bf16[1024,2304]{1,0:T(8,128)(2,1)} %add_convert_fusion.q_ref.k_ref.v_ref, bf16[1024,2304]{1,0:T(8,128)(2,1)} %add_convert_fusion.q_ref.k_ref.v_ref, bf16[1024,768]{1,0:T(8,128)(2,1)} %convolution_convert_fusion.do_ref, ...), custom_call_target="tpu_custom_call" | custom-call | flops 4026531840 | bytes 11010048 | tf_op jit(solution)/shard_map/pallas_call | solution.py:137
  289.7 3.2 convert_reduce_fusion.1
  292.9 0.6 copy-done.7
  293.4 7.8 %fusion.43 = (f32[768]{0:T(1024)S(1)}, f32[1024,768]{1,0:T(8,128)}) fusion(bf16[1024,2304]{1,0:T(8,128)(2,1)S(1)} %copy-done.7, bf16[768,2304]{1,0:T(8,128)(2,1)} %reshape.216), kind=kOutput, calls=%fused_computation.98 | convolution fusion | flops 3624664320 | bytes 11406336 | tf_op jit(solution)/shard_map/te,de->td/dot_general | solution.py:415
  301.3 7.8 %fusion.37.refs_2_ = f32[768,3072]{1,0:T(8,128)} fusion(bf16[1024,3072]{1,0:T(8,128)(2,1)S(1)} %bitcast.59, f32[1024,768]{0,1:T(8,128)S(1)} %copy-done.4, f32[768]{0:T(1024)S(1)} %reshape.242, f32[768]{0:T(1024)S(1)} %reshape.241, f32[1024]{0:T(1024)S(1)} %add_rsqrt_fusion, f32[1024]{0:T(1024)S(1)} %broadcast_multiply_fusion.4), kind=kOutput, calls=%fused_computation.92 | convolution fusion | flops 4835770368 | bytes 18888704 | tf_op jit(solution)/shard_map/td,tf->df/dot_general | solution.py:400
  309.1 6.3 %fusion.34.refs_0_ = f32[768,2304]{1,0:T(8,128)} fusion(bf16[1024,2304]{1,0:T(8,128)(2,1)S(1)} %copy-done.7, bf16[1024,768]{0,1:T(8,128)(2,1)S(1)} %copy-done.1, f32[768]{0:T(1024)S(1)} %copy-done.28, f32[768]{0:T(1024)S(1)} %copy-done.22, f32[1024]{0:T(1024)S(1)} %copy-done.24, f32[1024]{0:T(1024)S(1)} %copy-done.20), kind=kOutput, calls=%fused_computation.91 | convolution fusion | flops 3628597248 | bytes 13383680 | tf_op jit(solution)/shard_map/td,te->de/dot_general | solution.py:414
  315.4 1.4 fusion.31.refs_1_
  317.0 3.8 copy.68
  320.8 3.4 fusion.28
  324.2 0.1 reshape.222
  324.8 0.1 concatenate.30
  325.0 9.9 %fusion.45.refs_3_ = f32[3072,768]{1,0:T(8,128)} fusion(bf16[1024,3072]{1,0:T(8,128)(2,1)} %get-tuple-element.109, bf16[1024,768]{1,0:T(8,128)(2,1)} %param.31), kind=kOutput, calls=%fused_computation.100 | convolution fusion | flops 4831838208 | bytes 17301504 | tf_op jit(solution)/shard_map/tf,td->fd/dot_general | solution.py:393
  334.8 248.3 %shard_map.265 = (f32[24,2304]{1,0:T(8,128)S(1)}, f32[24,768]{1,0:T(8,128)S(1)}, f32[24,3072]{1,0:T(8,128)S(1)}, f32[96,768]{1,0:T(8,128)S(1)}, f32[8,128]{1,0:T(8,128)S(1)}) custom-call(f32[768,2304]{1,0:T(8,128)} %fusion.34.refs_0_, f32[768,768]{1,0:T(8,128)S(1)} %fusion.31.refs_1_, f32[768,3072]{1,0:T(8,128)} %fusion.37.refs_2_, ...), custom_call_target="tpu_custom_call" | custom-call | flops 7110656 | bytes 56885248 | tf_op jit(solution)/shard_map/pallas_call | solution.py:291
  583.1 0.6 slice_bitcast_fusion
  583.7 0.6 slice_bitcast_fusion.1
  584.3 0.5 slice_bitcast_fusion.7
  584.8 2.7 fusion.27
  587.5 3.6 copy.72
  591.1 9.1 %add_convert_fusion.1 = bf16[1024,768]{0,1:T(8,128)(2,1)S(1)} fusion(f32[1024,768]{0,1:T(8,128)} %copy-done.3, bf16[1024,3072]{1,0:T(8,128)(2,1)} %get-tuple-element.109, bf16[3072,768]{1,0:T(8,128)(2,1)} %bitcast.50, f32[768]{0:T(1024)S(1)} %copy-done.26), kind=kOutput, calls=%fused_computation.52 | convolution fusion | flops 4834197504 | bytes 15731712 | tf_op jit(solution)/shard_map/dot_general | solution.py:388
  600.2 1.6 copy.71
  601.8 0.7 copy.81
  602.4 0.6 copy.82
  603.1 0.7 copy.83
  603.8 0.7 copy.84
  (98 shorter events, 1.4 us)
Async XLA Ops:
  7.2 12.5 %copy-start.25 = (s32[2,512]{1,0:T(2,128)S(1)}, s32[2,512]{1,0:T(2,128)}, u32[]{:S(2)}) copy-start(s32[2,512]{1,0:T(2,128)} %param.29) | copy-start | bytes 12292
  7.2 14.2 %copy-start.29 = (s32[2,512]{1,0:T(2,128)S(1)}, s32[2,512]{1,0:T(2,128)}, u32[]{:S(2)}) copy-start(s32[2,512]{1,0:T(2,128)} %param.30) | copy-start | bytes 12292
  7.2 14.8 %copy-start.15 = (bf16[1024,768]{1,0:T(8,128)(2,1)S(1)}, bf16[1024,768]{1,0:T(8,128)(2,1)}, u32[]{:S(2)}) copy-start(bf16[1024,768]{1,0:T(8,128)(2,1)} %param.31) | copy-start | bytes 4718596
  7.2 75.5 %all-gather.8.cloned.1.call-start = ((), (), s32[]{:S(2)}) async-start(), calls=%async_computation.1 | async-start | bytes 5271552 | tf_op jit(solution)/shard_map/all_gather | solution.py:351
  15.3 151.7 %all-gather.6.cloned.1.call-start = ((), (), s32[]{:S(2)}) async-start(), calls=%async_computation | async-start | bytes 9732096 | tf_op jit(solution)/shard_map/all_gather | solution.py:358
  19.7 115.5 %copy-start = (bf16[1024,768]{0,1:T(8,128)(2,1)}, bf16[1024,768]{0,1:T(8,128)(2,1)S(1)}, u32[]{:S(2)}) copy-start(bf16[1024,768]{0,1:T(8,128)(2,1)S(1)} %copy.61) | copy-start | bytes 4718596
  23.9 73.3 %copy-start.19 = (f32[1024]{0:T(1024)}, f32[1024]{0:T(1024)S(1)}, u32[]{:S(2)}) copy-start(f32[1024]{0:T(1024)S(1)} %broadcast_multiply_fusion.5) | copy-start | bytes 12292
  24.4 72.8 %copy-start.23 = (f32[1024]{0:T(1024)}, f32[1024]{0:T(1024)S(1)}, u32[]{:S(2)}) copy-start(f32[1024]{0:T(1024)S(1)} %add_rsqrt_fusion.1) | copy-start | bytes 12292
  83.9 13.3 %copy-start.21 = (f32[768]{0:T(1024)}, f32[768]{0:T(1024)S(1)}, u32[]{:S(2)}) copy-start(f32[768]{0:T(1024)S(1)} %reshape.238) | copy-start | bytes 9220
  84.2 13.1 %copy-start.27 = (f32[768]{0:T(1024)}, f32[768]{0:T(1024)S(1)}, u32[]{:S(2)}) copy-start(f32[768]{0:T(1024)S(1)} %reshape.239) | copy-start | bytes 9220
  97.2 38.1 %copy-start.17 = (bf16[32,24,768]{2,1,0:T(8,128)(2,1)}, bf16[32,24,768]{2,1,0:T(8,128)(2,1)S(1)}, u32[]{:S(2)}) copy-start(bf16[32,24,768]{2,1,0:T(8,128)(2,1)S(1)} %slice.129) | copy-start | bytes 3538948
  138.3 1.7 copy-start.3
  175.0 8.6 %copy-start.4 = (f32[1024,768]{0,1:T(8,128)S(1)}, f32[1024,768]{0,1:T(8,128)}, u32[]{:S(2)}) copy-start(f32[1024,768]{0,1:T(8,128)} %copy-done.3) | copy-start | bytes 9437188
  183.6 38.2 %copy-start.13 = (bf16[32,96,768]{2,1,0:T(8,128)(2,1)S(1)}, bf16[32,96,768]{2,1,0:T(8,128)(2,1)}, u32[]{:S(2)}) copy-start(bf16[32,96,768]{2,1,0:T(8,128)(2,1)} %get-tuple-element.88) | copy-start | bytes 14155780
  183.6 38.2 %copy-start.16 = (bf16[1024,768]{1,0:T(8,128)(2,1)S(1)}, bf16[1024,768]{1,0:T(8,128)(2,1)}, u32[]{:S(2)}) copy-start(bf16[1024,768]{1,0:T(8,128)(2,1)} %param.31) | copy-start | bytes 4718596
  221.9 11.8 %copy-start.12 = (bf16[768,3072]{1,0:T(8,128)(2,1)S(1)}, bf16[768,3072]{1,0:T(8,128)(2,1)}, u32[]{:S(2)}) copy-start(bf16[768,3072]{1,0:T(8,128)(2,1)} %reshape.219) | copy-start | bytes 14155780
  233.7 6.8 %copy-start.30 = (bf16[1024,3072]{1,0:T(8,128)(2,1)}, bf16[1024,3072]{1,0:T(8,128)(2,1)S(1)}, u32[]{:S(2)}) copy-start(bf16[1024,3072]{1,0:T(8,128)(2,1)S(1)} %get-tuple-element.116) | copy-start | bytes 18874372
  244.1 3.0 copy-start.6
  244.1 3.3 copy-start.11
  247.4 3.5 copy-start.18
  249.2 1.7 copy-start.8
  289.7 3.8 copy-start.7
  289.7 11.5 %slice-start = ((s8[6291456]{0:T(1024)(128)(4,1)}), s8[4194304]{0:T(1024)(128)(4,1)S(1)}, s32[]{:S(2)}) async-start(s8[6291456]{0:T(1024)(128)(4,1)} %bitcast.58), calls=%async_computation.2 | async-start | bytes 8388608
  293.4 7.8 %slice-start.1 = ((s8[6291456]{0:T(1024)(128)(4,1)}), s8[2097152]{0:T(1024)(128)(4,1)S(1)}, s32[]{:S(2)}) async-start(s8[6291456]{0:T(1024)(128)(4,1)} %bitcast.58), calls=%async_computation.3 | async-start | bytes 4194304
  301.2 7.9 %copy-start.1 = (bf16[1024,768]{0,1:T(8,128)(2,1)S(1)}, bf16[1024,768]{0,1:T(8,128)(2,1)}, u32[]{:S(2)}) copy-start(bf16[1024,768]{0,1:T(8,128)(2,1)} %copy-done) | copy-start | bytes 4718596
  301.2 7.9 %copy-start.20 = (f32[1024]{0:T(1024)S(1)}, f32[1024]{0:T(1024)}, u32[]{:S(2)}) copy-start(f32[1024]{0:T(1024)} %copy-done.19) | copy-start | bytes 12292
  301.2 7.9 %copy-start.22 = (f32[768]{0:T(1024)S(1)}, f32[768]{0:T(1024)}, u32[]{:S(2)}) copy-start(f32[768]{0:T(1024)} %copy-done.21) | copy-start | bytes 9220
  301.2 7.8 %copy-start.24 = (f32[1024]{0:T(1024)S(1)}, f32[1024]{0:T(1024)}, u32[]{:S(2)}) copy-start(f32[1024]{0:T(1024)} %copy-done.23) | copy-start | bytes 12292
  301.2 7.8 %copy-start.28 = (f32[768]{0:T(1024)S(1)}, f32[768]{0:T(1024)}, u32[]{:S(2)}) copy-start(f32[768]{0:T(1024)} %copy-done.27) | copy-start | bytes 9220
  309.1 6.3 %copy-start.9 = (f32[1024,768]{0,1:T(8,128)S(1)}, f32[1024,768]{0,1:T(8,128)}, u32[]{:S(2)}) copy-start(f32[1024,768]{0,1:T(8,128)} %copy-done.8) | copy-start | bytes 9437188
  309.1 6.3 %copy-start.14 = (bf16[1024,768]{1,0:T(8,128)(2,1)S(1)}, bf16[1024,768]{1,0:T(8,128)(2,1)}, u32[]{:S(2)}) copy-start(bf16[1024,768]{1,0:T(8,128)(2,1)} %shard_map.263) | copy-start | bytes 4718596
  334.8 250.0 %copy-start.2 = (bf16[1024,768]{0,1:T(8,128)(2,1)S(1)}, bf16[1024,768]{0,1:T(8,128)(2,1)}, u32[]{:S(2)}) copy-start(bf16[1024,768]{0,1:T(8,128)(2,1)} %copy-done) | copy-start | bytes 4718596
  334.8 250.0 %copy-start.5 = (f32[1024,768]{0,1:T(8,128)S(1)}, f32[1024,768]{0,1:T(8,128)}, u32[]{:S(2)}) copy-start(f32[1024,768]{0,1:T(8,128)} %copy.68) | copy-start | bytes 9437188
  334.8 250.0 %copy-start.10 = (f32[1024,768]{0,1:T(8,128)S(1)}, f32[1024,768]{0,1:T(8,128)}, u32[]{:S(2)}) copy-start(f32[1024,768]{0,1:T(8,128)} %copy-done.8) | copy-start | bytes 9437188
  587.5 3.6 copy-start.26
Sparse Core Ops, SparseCore 0:
  15.4 67.3 all-gather.7
  86.2 80.7 all-gather.5

commit v3 on v2

--- a/solution.py
+++ b/solution.py
@@ -184,7 +184,7 @@
     return n_dev, pos_of, coords_of
 
 
-def ring_reduce_scatter(parts, mesh_shape, collective_id=0):
+def ring_reduce_scatter(parts, mesh_shape, after=(), collective_id=0):
     n_wide, n_narrow = mesh_shape
     n_dev, pos_of, coords_of = ring_maps(n_wide, n_narrow)
     specs = []
@@ -192,18 +192,23 @@
         cols = a.shape[1]
         if split:
             specs.append((i, 0, 0, cols // 2))
-            specs.append((i, 1, cols // 2, cols // 2))
         else:
             specs.append((i, 0, 0, cols))
+    for i, (a, rb, split) in enumerate(parts):
+        if split:
+            specs.append((i, 1, a.shape[1] // 2, a.shape[1] // 2))
     n_in = len(parts)
+    n_after = len(after)
     n_sp = len(specs)
+    last_step = n_dev - 2
 
     def kernel(*refs):
         ins = refs[:n_in]
-        outs = refs[n_in : 2 * n_in]
-        bufs = refs[2 * n_in : 2 * n_in + n_sp]
-        locs = refs[2 * n_in + n_sp : 2 * n_in + 2 * n_sp]
-        send_sem, recv_sem, loc_sem, credit = refs[2 * n_in + 2 * n_sp :]
+        outs = refs[n_in + n_after : 2 * n_in + n_after]
+        at = 2 * n_in + n_after
+        bufs = refs[at : at + n_sp]
+        locs = refs[at + n_sp : at + 2 * n_sp]
+        send_sem, recv_sem, loc_sem, credit = refs[at + 2 * n_sp :]
         p = pos_of(lax.axis_index("wide"), lax.axis_index("narrow"))
         right = coords_of((p + 1) % n_dev)
         left = coords_of((p + n_dev - 1) % n_dev)
@@ -217,6 +222,23 @@
                 start = pl.multiple_of(start, 8)
             return pl.ds(start, rb)
 
+        def remote(j, s):
+            return pltpu.make_async_remote_copy(
+                src_ref=bufs[j].at[s % 3],
+                dst_ref=bufs[j].at[(s + 1) % 3],
+                send_sem=send_sem.at[j, s % 3],
+                recv_sem=recv_sem.at[j, (s + 1) % 3],
+                device_id=nbr_send[specs[j][1]],
+                device_id_type=MESH_ID,
+            )
+
+        def local(j, s):
+            i, dirn, c0, cw = specs[j]
+            q = (p + 2 * n_dev - s - 2) if dirn == 0 else (p + s + 2)
+            return pltpu.make_async_copy(
+                ins[i].at[rows_of(q, parts[i][1]), pl.ds(c0, cw)], locs[j].at[s % 2], loc_sem.at[j, s % 2]
+            )
+
         barrier = pltpu.get_barrier_semaphore()
         for nb in (left, right):
             pl.semaphore_signal(barrier, 1, device_id=nb, device_id_type=MESH_ID)
@@ -225,48 +247,37 @@
         for j, (i, dirn, c0, cw) in enumerate(specs):
             q = p + n_dev - 1 if dirn == 0 else p + 1
             cp = pltpu.make_async_copy(
-                ins[i].at[rows_of(q, parts[i][1]), pl.ds(c0, cw)], bufs[j].at[0], loc_sem.at[j]
+                ins[i].at[rows_of(q, parts[i][1]), pl.ds(c0, cw)], bufs[j].at[0], loc_sem.at[j, 1]
             )
             cp.start()
             cp.wait()
+        for j in range(n_sp):
+            remote(j, 0).start()
+            local(j, 0).start()
 
         def step(s, carry):
-            slot = s % 2
-            nslot = 1 - slot
+            for j in range(n_sp):
+                dirn = specs[j][1]
+                local(j, s).wait()
+                remote(j, s).wait_recv()
+                nxt = (s + 1) % 3
+                bufs[j][nxt] = bufs[j][nxt] + locs[j][s % 2]
+                if j == 0 or specs[j - 1][1] != dirn:
+
+                    @pl.when((s >= 1) & (s + 1 <= last_step))
+                    def _():
+                        pl.semaphore_wait(credit.at[dirn], 1)
+
+                @pl.when(s + 1 <= last_step)
+                def _():
+                    remote(j, s + 1).start()
+                    local(j, s + 1).start()
+
+            for j in range(n_sp):
+                remote(j, s).wait_send()
             for dirn in (0, 1):
 
-                @pl.when(s >= 1)
-                def _():
-                    pl.semaphore_wait(credit.at[dirn], 1)
-
-            rcopies = []
-            lcopies = []
-            for j, (i, dirn, c0, cw) in enumerate(specs):
-                rc = pltpu.make_async_remote_copy(
-                    src_ref=bufs[j].at[slot],
-                    dst_ref=bufs[j].at[nslot],
-                    send_sem=send_sem.at[j, slot],
-                    recv_sem=recv_sem.at[j, nslot],
-                    device_id=nbr_send[dirn],
-                    device_id_type=MESH_ID,
-                )
-                rc.start()
-                rcopies.append(rc)
-                q = (p + 2 * n_dev - s - 2) if dirn == 0 else (p + s + 2)
-                lc = pltpu.make_async_copy(
-                    ins[i].at[rows_of(q, parts[i][1]), pl.ds(c0, cw)], locs[j].at[slot], loc_sem.at[j]
-                )
-                lc.start()
-                lcopies.append(lc)
-            for j in range(n_sp):
-                lcopies[j].wait()
-                rcopies[j].wait_recv()
-                bufs[j][nslot] = bufs[j][nslot] + locs[j][slot]
-            for j in range(n_sp):
-                rcopies[j].wait_send()
-            for dirn in (0, 1):
-
-                @pl.when(s < n_dev - 2)
+                @pl.when(s <= last_step - 2)
                 def _():
                     pl.semaphore_signal(
                         credit.at[dirn], 1, device_id=nbr_recv[dirn], device_id_type=MESH_ID
@@ -274,31 +285,32 @@
 
             return carry
 
-        lax.fori_loop(0, n_dev - 1, step, 0)
-        last = (n_dev - 1) % 2
+        lax.fori_loop(0, last_step + 1, step, 0)
+        fin = (last_step + 1) % 3
         for j, (i, dirn, c0, cw) in enumerate(specs):
-            outs[i][:, pl.ds(c0, cw)] = bufs[j][last]
+            outs[i][:, pl.ds(c0, cw)] = bufs[j][fin]
 
     out_shape = [jax.ShapeDtypeStruct((rb, a.shape[1]), a.dtype) for (a, rb, _) in parts]
-    scratch = [pltpu.VMEM((2, parts[i][1], cw), jnp.float32) for (i, _, _, cw) in specs] * 2
+    scratch = [pltpu.VMEM((3, parts[i][1], cw), jnp.float32) for (i, _, _, cw) in specs]
+    scratch += [pltpu.VMEM((2, parts[i][1], cw), jnp.float32) for (i, _, _, cw) in specs]
     scratch += [
+        pltpu.SemaphoreType.DMA((n_sp, 3)),
+        pltpu.SemaphoreType.DMA((n_sp, 3)),
         pltpu.SemaphoreType.DMA((n_sp, 2)),
-        pltpu.SemaphoreType.DMA((n_sp, 2)),
-        pltpu.SemaphoreType.DMA((n_sp,)),
         pltpu.SemaphoreType.REGULAR((2,)),
     ]
     total = sum(a.size * 4 for (a, _, _) in parts)
     return pl.pallas_call(
         kernel,
         out_shape=out_shape,
-        in_specs=[pl.BlockSpec(memory_space=pl.ANY)] * n_in,
+        in_specs=[pl.BlockSpec(memory_space=pl.ANY)] * (n_in + n_after),
         out_specs=[pl.BlockSpec(memory_space=pltpu.VMEM)] * n_in,
         scratch_shapes=scratch,
         compiler_params=pltpu.CompilerParams(
             collective_id=collective_id, has_side_effects=True, vmem_limit_bytes=48 * 1024 * 1024
         ),
         cost_estimate=pl.CostEstimate(flops=total // 4, transcendentals=0, bytes_accessed=2 * total),
-    )(*[a for (a, _, _) in parts])
+    )(*[a for (a, _, _) in parts], *after)
 
 
 def pack_rows(pieces, width):
@@ -430,7 +442,7 @@
         (owned, small_rows, False),
     ]
     if all(rb % 8 == 0 and a.shape[1] % 256 == 0 for (a, rb, _) in parts[:4]):
-        sums = ring_reduce_scatter(parts, mesh_shape)
+        sums = ring_reduce_scatter(parts, mesh_shape, after=(grad_inputs,))
     else:
         sums = [lax.psum_scatter(a, ALL, scatter_dimension=0, tiled=True) for (a, _, _) in parts]
     small_sums = split_owned(sums[4].reshape(1, -1), [s for s in small_sizes])

time: 621 us -> 509 us (0.82)
  Pallas kernels: 314 us -> 226 us
  local copies, waits for them, and re-layouts: 66 us -> 49.6 us
  other arithmetic: 18.5 us -> 11 us
    pallas_call x1, Pallas kernels: 248 us -> 160 us  [ring_reduce_scatter(): pl.pallas_call(kernel, out_shape=out_shape, in_specs=[pl.BlockSpec(memory...]
    unnamed x75 -> x55, local copies, waits for them, and re-layouts: 15.5 us -> 3.56 us
    dot_general x2 -> x0, local copies, waits for them, and re-layouts: 7.39 us -> none  [the longest x1 3.79 us: on_device(): jnp.einsum('te,de->td', grad_qkv, qkv_full, preferred_element_type=jnp.fl...]
    reduce_sum x2 -> x0, other arithmetic: 6.41 us -> none  [the longest x1 3.39 us: on_device(): grad_g1 = jnp.sum(grad_h1 * normed_one, axis=0)]
  transfers between devices with their start and end apart: 2 -> 2, of which waited for: 2 -> 2; matrix products, arithmetic and copies ran while one was open for 6% -> 7% of each run, Pallas kernels for 5% -> 6%
where the time goes in v3:
time: 509 us; the launch traced here: 501 us
  Pallas kernels  226 us (44%)
  matrix products  114 us (22%)
  waiting for transfers between devices  85.1 us (17%)
  local copies, waits for them, and re-layouts  49.6 us (10%)
  between operations  15 us (3%)
  other arithmetic  11 us (2%)
    pallas_call x1, Pallas kernels, ring_reduce_scatter(): pl.pallas_call(kernel, out_shape=out_shape, in_specs=[pl.BlockSpec(memory...  160 us
    all_gather x1, waiting for transfers between devices, on_device(): attn_all = lax.all_gather(attn_buf, ALL, axis=0, tiled=False)  58.2 us
    dot_general x1, matrix products, on_device(): jnp.dot(h_two, up_full, preferred_element_type=jnp.float32)  37.3 us
    pallas_call x1, Pallas kernels, attention_bwd(): pl.pallas_call(attn_bwd_kernel, out_shape=jax.ShapeDtypeStruct((rows, wid...  36.3 us
    pallas_call x1, Pallas kernels, attention_fwd(): pl.pallas_call(attn_fwd_kernel, out_shape=jax.ShapeDtypeStruct((rows, mod...  29.8 us
    all_gather x1, waiting for transfers between devices, on_device(): mlp_all = lax.all_gather(mlp_buf, ALL, axis=0, tiled=False)  26.9 us
    dot_general x1, matrix products, on_device(): jnp.einsum('td,fd->tf', cotangent, down_full, preferred_element_type=jnp....  12 us
  transfers between devices with their start and end apart: 2, of which 2 were waited for; matrix products, arithmetic and copies ran while one was open for 7% of the time, Pallas kernels for 6%

profile of v3, /device:TPU:1, one launch (start us, length us, event | category | flops | bytes accessed | tf_op | source)
XLA Modules:
  0.0 500.5 jit_solution(335085115415000153)
XLA Ops:
  7.2 5.5 %concatenate.23 = bf16[288]{0:T(512)(128)(2,1)S(1)} concatenate(bf16[48]{0:T(256)(128)(2,1)} %param.18, bf16[24]{0:T(256)(128)(2,1)} %param.20, bf16[24]{0:T(256)(128)(2,1)} %param.21, bf16[24]{0:T(256)(128)(2,1)} %param.22, bf16[24]{0:T(256)(128)(2,1)} %param.23, bf16[24]{0:T(256)(128)(2,1)} %param.24, bf16[96]{0:T(256)(128)(2,1)} %param.26, bf16[24]{0:T(256)(128)(2,1)} %param.28), dimensions={0} | concatenate | bytes 1152 | tf_op jit(solution)/shard_map/concatenate | solution.py:317
  12.8 1.0 reshape.215
  13.8 1.4 maximum_bitcast_fusion
  15.3 1.0 reshape.218
  16.3 1.6 pad_maximum_fusion
  18.0 1.3 broadcast_in_dim.14.vr_ref
  19.2 1.3 broadcast_in_dim.13.sr_ref
  20.5 1.7 copy.38.sc_ref
  22.2 1.7 convert_reduce_fusion.2
  23.9 0.6 fusion.29
  24.6 58.2 %all-gather.8.cloned.1.call-done = bf16[32,97,768]{2,1,0:T(8,128)(2,1)} async-done(((bf16[1,97,768]{2,1,0:T(8,128)(2,1)}), bf16[32,97,768]{2,1,0:T(8,128)(2,1)}) %all-gather.8.cloned.1.call-update) | async-done | bytes 4767760 | tf_op jit(solution)/shard_map/all_gather | solution.py:363
  82.8 1.0 slice.122
  83.7 0.1 slice.101
  83.8 0.1 slice.103
  83.9 0.1 slice_convert_fusion.1
  84.0 0.1 slice_convert_fusion
  84.1 0.7 reshape.244
  84.8 0.1 reshape.241
  84.9 0.1 reshape.238
  85.0 0.1 reshape.242
  85.1 0.1 reshape.239
  85.2 0.1 reshape.240
  85.3 4.0 slice.125
  89.3 6.6 %reshape.216 = bf16[768,2304]{1,0:T(8,128)(2,1)} reshape(bf16[32,72,768]{2,1,0:T(8,128)(2,1)} %slice.125) | data formatting | bytes 7077888 | tf_op jit(solution)/shard_map/reshape | solution.py:364
  95.9 2.4 slice.129
  98.3 7.9 %add_convert_fusion.q_ref.k_ref.v_ref = bf16[1024,2304]{1,0:T(8,128)(2,1)} fusion(bf16[768,2304]{1,0:T(8,128)(2,1)} %reshape.216, f32[2304]{0:T(1024)S(1)} %pad_maximum_fusion.2, bf16[1024,768]{1,0:T(8,128)(2,1)S(1)} %copy-done.3, f32[768]{0:T(1024)S(1)} %reshape.239, f32[768]{0:T(1024)S(1)} %reshape.238, f32[1024]{0:T(1024)S(1)} %add_rsqrt_fusion.1, ...), kind=kOutput, calls=%fused_computation.28 | convolution fusion | flops 3633315840 | bytes 9853952 | tf_op jit(solution)/shard_map/dot_general | solution.py:380
  106.2 29.8 %shard_map.263 = bf16[1024,768]{1,0:T(8,128)(2,1)} custom-call(bf16[1024,2304]{1,0:T(8,128)(2,1)} %add_convert_fusion.q_ref.k_ref.v_ref, bf16[1024,2304]{1,0:T(8,128)(2,1)} %add_convert_fusion.q_ref.k_ref.v_ref, bf16[1024,2304]{1,0:T(8,128)(2,1)} %add_convert_fusion.q_ref.k_ref.v_ref, s32[2,512,1]{2,1,0:T(8,128)} %copy.38.sc_ref, ...), custom_call_target="tpu_custom_call" | custom-call | flops 1610612736 | bytes 6291456 | tf_op jit(solution)/shard_map/pallas_call | solution.py:105
  136.0 3.8 fusion.42
  139.8 0.5 multiply_reduce_fusion.2
  140.3 26.9 %all-gather.6.cloned.1.call-done = bf16[6144,768]{1,0:T(8,128)(2,1)} async-done(((bf16[192,768]{1,0:T(8,128)(2,1)}), bf16[6144,768]{1,0:T(8,128)(2,1)}) %all-gather.6.cloned.1.call-update) | async-done | bytes 9437200 | tf_op jit(solution)/shard_map/all_gather | solution.py:370
  167.2 8.0 %fusion.39 = (bf16[32,96,768]{2,1,0:T(8,128)(2,1)}, bf16[32,96,768]{2,1,0:T(8,128)(2,1)}) fusion(bf16[32,192,768]{2,1,0:T(8,128)(2,1)} %bitcast.49), kind=kLoop, calls=%fused_computation.94 | loop fusion | bytes 18874368 | tf_op jit(solution)/shard_map/slice | solution.py:372
  175.2 8.5 %reshape.219 = bf16[768,3072]{1,0:T(8,128)(2,1)} reshape(bf16[32,96,768]{2,1,0:T(8,128)(2,1)} %get-tuple-element.35) | data formatting | bytes 9437184 | tf_op jit(solution)/shard_map/reshape | solution.py:371
  183.7 37.3 %fusion.2 = (bf16[1024,3072]{1,0:T(8,128)(2,1)}, f32[1024,3072]{1,0:T(8,128)}) fusion(f32[3072]{0:T(1024)S(1)} %reshape.243, bf16[768,3072]{1,0:T(8,128)(2,1)} %reshape.219, f32[1024,768]{1,0:T(8,128)S(1)} %get-tuple-element.54, f32[768]{0:T(1024)S(1)} %reshape.242, f32[768]{0:T(1024)S(1)} %reshape.241, f32[1024]{0:T(1024)S(1)} %add_rsqrt_fusion, ...), kind=kOutput, calls=%fused_computation.4 | convolution fusion | flops 5043388416 | bytes 26765312 | tf_op jit(solution)/shard_map/dot_general | solution.py:394
  221.0 12.0 %convert_reduce_fusion = (f32[3072]{0:T(1024)S(1)}, bf16[1024,3072]{1,0:T(8,128)(2,1)S(1)}) fusion(f32[1024,3072]{1,0:T(8,128)} %get-tuple-element.56, f32[3072]{0:T(1024)S(1)} %reshape.243, bf16[3072,768]{1,0:T(8,128)(2,1)S(1)} %bitcast.50, bf16[1024,768]{1,0:T(8,128)(2,1)S(1)} %copy-done.12), kind=kOutput, calls=%fused_computation.11 | convolution fusion | flops 4872729600 | bytes 25190400 | tf_op jit(solution)/shard_map/td,fd->tf/dot_general | solution.py:407
  233.0 5.7 %multiply_reduce_fusion = (f32[768]{0:T(1024)S(1)}, f32[1024]{0:T(1024)S(1)}, f32[1024]{0:T(1024)S(1)}, f32[768]{0:T(1024)S(1)}, f32[1024,768]{1,0:T(8,128)S(1)}) fusion(f32[1024,768]{1,0:T(8,128)S(1)} %get-tuple-element.54, f32[1024]{0:T(1024)S(1)} %add_rsqrt_fusion, f32[1024]{0:T(1024)S(1)} %broadcast_multiply_fusion.4, f32[768]{0:T(1024)S(1)} %reshape.241, ...), kind=kOutput, calls=%fused_computation.49 | convolution fusion | flops 4838912000 | bytes 17327104 | tf_op jit(solution)/shard_map/tf,df->td/dot_general | solution.py:413
  238.7 8.4 %fusion.37.refs_2_ = f32[768,3072]{1,0:T(8,128)} fusion(bf16[1024,3072]{1,0:T(8,128)(2,1)S(1)} %get-tuple-element.60, f32[1024,768]{1,0:T(8,128)S(1)} %get-tuple-element.54, f32[768]{0:T(1024)S(1)} %reshape.242, f32[768]{0:T(1024)S(1)} %reshape.241, f32[1024]{0:T(1024)S(1)} %add_rsqrt_fusion, f32[1024]{0:T(1024)S(1)} %broadcast_multiply_fusion.4), kind=kOutput, calls=%fused_computation.92 | convolution fusion | flops 4835770368 | bytes 18888704 | tf_op jit(solution)/shard_map/td,tf->df/dot_general | solution.py:412
  247.1 1.5 convert_reduce_fusion.4
  248.7 2.6 convolution_convert_fusion.do_ref
  251.3 1.5 fusion.31.refs_1_
  252.8 36.3 %shard_map.264 = bf16[1024,2304]{1,0:T(8,128)(2,1)} custom-call(bf16[1024,2304]{1,0:T(8,128)(2,1)} %add_convert_fusion.q_ref.k_ref.v_ref, bf16[1024,2304]{1,0:T(8,128)(2,1)} %add_convert_fusion.q_ref.k_ref.v_ref, bf16[1024,2304]{1,0:T(8,128)(2,1)} %add_convert_fusion.q_ref.k_ref.v_ref, bf16[1024,768]{1,0:T(8,128)(2,1)} %convolution_convert_fusion.do_ref, ...), custom_call_target="tpu_custom_call" | custom-call | flops 4026531840 | bytes 11010048 | tf_op jit(solution)/shard_map/pallas_call | solution.py:137
  289.1 9.9 %fusion.28 = (f32[768]{0:T(1024)S(1)}, f32[1024]{0:T(1024)S(1)}, f32[1024]{0:T(1024)S(1)}, f32[768]{0:T(1024)S(1)}, f32[1024,768]{1,0:T(8,128)}) fusion(bf16[1024,768]{1,0:T(8,128)(2,1)} %param.16, f32[1024]{0:T(1024)S(1)} %copy-done.17, f32[1024]{0:T(1024)S(1)} %copy-done.15, f32[768]{0:T(1024)S(1)} %copy-done.19, bf16[1024,2304]{1,0:T(8,128)(2,1)} %shard_map.264, ...), kind=kOutput, calls=%fused_computation.46 | convolution fusion | flops 3631739392 | bytes 13001728 | tf_op jit(solution)/shard_map/te,de->td/dot_general | solution.py:427
  299.0 0.7 convert_reduce_fusion.1
  299.7 0.7 copy-done.4
  300.4 6.5 %fusion.34.refs_0_ = f32[768,2304]{1,0:T(8,128)} fusion(bf16[1024,2304]{1,0:T(8,128)(2,1)S(1)} %copy-done, bf16[1024,768]{1,0:T(8,128)(2,1)S(1)} %copy-done.4, f32[768]{0:T(1024)S(1)} %copy-done.21, f32[768]{0:T(1024)S(1)} %copy-done.19, f32[1024]{0:T(1024)S(1)} %copy-done.17, f32[1024]{0:T(1024)S(1)} %copy-done.15), kind=kOutput, calls=%fused_computation.91 | convolution fusion | flops 3628597248 | bytes 13383680 | tf_op jit(solution)/shard_map/td,te->de/dot_general | solution.py:426
  307.0 0.1 reshape.221
  307.1 0.1 reshape.224
  307.1 0.1 reshape.227
  307.2 0.1 reshape.225
  307.3 0.1 reshape.222
  307.4 0.1 concatenate.27
  307.5 0.1 concatenate.28
  307.6 0.1 reshape.223
  307.7 0.1 concatenate.30
  307.9 10.0 %fusion.43.refs_3_ = f32[3072,768]{1,0:T(8,128)} fusion(bf16[1024,3072]{1,0:T(8,128)(2,1)} %get-tuple-element.55, bf16[1024,768]{1,0:T(8,128)(2,1)} %param.31), kind=kOutput, calls=%fused_computation.98 | convolution fusion | flops 4831838208 | bytes 17301504 | tf_op jit(solution)/shard_map/tf,td->fd/dot_general | solution.py:405
  317.9 2.7 fusion.27.refs_5_
  320.6 160.0 %shard_map.265 = (f32[24,2304]{1,0:T(8,128)S(1)}, f32[24,768]{1,0:T(8,128)S(1)}, f32[24,3072]{1,0:T(8,128)S(1)}, f32[96,768]{1,0:T(8,128)S(1)}, f32[8,128]{1,0:T(8,128)S(1)}) custom-call(f32[768,2304]{1,0:T(8,128)} %fusion.34.refs_0_, f32[768,768]{1,0:T(8,128)S(1)} %fusion.31.refs_1_, f32[768,3072]{1,0:T(8,128)} %fusion.37.refs_2_, ...), custom_call_target="tpu_custom_call" | custom-call | flops 7110656 | bytes 56885248 | tf_op jit(solution)/shard_map/pallas_call | solution.py:303
  480.6 0.6 slice_bitcast_fusion.1
  481.2 0.5 slice_bitcast_fusion.7
  481.7 0.6 slice_bitcast_fusion
  482.4 8.1 %add_convert_fusion.1 = bf16[1024,768]{1,0:T(8,128)(2,1)} fusion(f32[1024,768]{1,0:T(8,128)S(1)} %copy-done.2, bf16[1024,3072]{1,0:T(8,128)(2,1)} %get-tuple-element.55, bf16[3072,768]{1,0:T(8,128)(2,1)S(1)} %bitcast.53, f32[768]{0:T(1024)S(1)} %copy-done.22), kind=kOutput, calls=%fused_computation.52 | convolution fusion | flops 4834197504 | bytes 15731712 | tf_op jit(solution)/shard_map/dot_general | solution.py:400
  490.4 0.7 copy.49
  491.1 0.6 copy.50
  491.7 0.7 copy.51
  492.5 0.7 copy.52
  (74 shorter events, 0.5 us)
Async XLA Ops:
  7.2 16.7 %copy-start.3 = (bf16[1024,768]{1,0:T(8,128)(2,1)S(1)}, bf16[1024,768]{1,0:T(8,128)(2,1)}, u32[]{:S(2)}) copy-start(bf16[1024,768]{1,0:T(8,128)(2,1)} %param.16) | copy-start | bytes 4718596
  7.2 75.6 %all-gather.8.cloned.1.call-start = ((), (), s32[]{:S(2)}) async-start(), calls=%async_computation.1 | async-start | bytes 5271552 | tf_op jit(solution)/shard_map/all_gather | solution.py:363
  15.2 152.0 %all-gather.6.cloned.1.call-start = ((), (), s32[]{:S(2)}) async-start(), calls=%async_computation | async-start | bytes 9732096 | tf_op jit(solution)/shard_map/all_gather | solution.py:370
  23.9 74.3 %copy-start.14 = (f32[1024]{0:T(1024)}, f32[1024]{0:T(1024)S(1)}, u32[]{:S(2)}) copy-start(f32[1024]{0:T(1024)S(1)} %broadcast_multiply_fusion.5) | copy-start | bytes 12292
  24.6 73.7 %copy-start.16 = (f32[1024]{0:T(1024)}, f32[1024]{0:T(1024)S(1)}, u32[]{:S(2)}) copy-start(f32[1024]{0:T(1024)S(1)} %add_rsqrt_fusion.1) | copy-start | bytes 12292
  85.0 13.3 %copy-start.18 = (f32[768]{0:T(1024)}, f32[768]{0:T(1024)S(1)}, u32[]{:S(2)}) copy-start(f32[768]{0:T(1024)S(1)} %reshape.238) | copy-start | bytes 9220
  85.2 13.1 %copy-start.20 = (f32[768]{0:T(1024)}, f32[768]{0:T(1024)S(1)}, u32[]{:S(2)}) copy-start(f32[768]{0:T(1024)S(1)} %reshape.239) | copy-start | bytes 9220
  139.8 107.3 %copy-start.1 = (f32[1024,768]{1,0:T(8,128)}, f32[1024,768]{1,0:T(8,128)S(1)}, u32[]{:S(2)}) copy-start(f32[1024,768]{1,0:T(8,128)S(1)} %get-tuple-element.54) | copy-start | bytes 9437188
  183.7 37.3 %copy-start.9 = (bf16[32,96,768]{2,1,0:T(8,128)(2,1)S(1)}, bf16[32,96,768]{2,1,0:T(8,128)(2,1)}, u32[]{:S(2)}) copy-start(bf16[32,96,768]{2,1,0:T(8,128)(2,1)} %get-tuple-element.34) | copy-start | bytes 14155780
  183.7 37.3 %copy-start.12 = (bf16[1024,768]{1,0:T(8,128)(2,1)S(1)}, bf16[1024,768]{1,0:T(8,128)(2,1)}, u32[]{:S(2)}) copy-start(bf16[1024,768]{1,0:T(8,128)(2,1)} %param.31) | copy-start | bytes 4718596
  221.0 12.0 %copy-start.8 = (bf16[768,3072]{1,0:T(8,128)(2,1)S(1)}, bf16[768,3072]{1,0:T(8,128)(2,1)}, u32[]{:S(2)}) copy-start(bf16[768,3072]{1,0:T(8,128)(2,1)} %reshape.219) | copy-start | bytes 14155780
  247.1 1.6 copy-start.13
  248.7 2.7 copy-start.6
  248.7 2.6 copy-start.11
  252.8 36.3 %copy-start.15 = (f32[1024]{0:T(1024)S(1)}, f32[1024]{0:T(1024)}, u32[]{:S(2)}) copy-start(f32[1024]{0:T(1024)} %copy-done.14) | copy-start | bytes 12292
  252.8 36.3 %copy-start.17 = (f32[1024]{0:T(1024)S(1)}, f32[1024]{0:T(1024)}, u32[]{:S(2)}) copy-start(f32[1024]{0:T(1024)} %copy-done.16) | copy-start | bytes 12292
  252.8 36.3 %copy-start.19 = (f32[768]{0:T(1024)S(1)}, f32[768]{0:T(1024)}, u32[]{:S(2)}) copy-start(f32[768]{0:T(1024)} %copy-done.18) | copy-start | bytes 9220
  289.1 9.9 %copy-start = (bf16[1024,2304]{1,0:T(8,128)(2,1)S(1)}, bf16[1024,2304]{1,0:T(8,128)(2,1)}, u32[]{:S(2)}) copy-start(bf16[1024,2304]{1,0:T(8,128)(2,1)} %shard_map.264) | copy-start | bytes 14155780
  299.0 1.4 copy-start.4
  299.0 1.4 copy-start.21
  307.8 10.0 %copy-start.5 = (bf16[1024,768]{1,0:T(8,128)(2,1)S(1)}, bf16[1024,768]{1,0:T(8,128)(2,1)}, u32[]{:S(2)}) copy-start(bf16[1024,768]{1,0:T(8,128)(2,1)} %param.16) | copy-start | bytes 4718596
  307.9 10.0 %copy-start.7 = (f32[1024,768]{1,0:T(8,128)S(1)}, f32[1024,768]{1,0:T(8,128)}, u32[]{:S(2)}) copy-start(f32[1024,768]{1,0:T(8,128)} %copy-done.6) | copy-start | bytes 9437188
  307.9 10.0 %copy-start.10 = (f32[1024,768]{1,0:T(8,128)S(1)}, f32[1024,768]{1,0:T(8,128)}, u32[]{:S(2)}) copy-start(f32[1024,768]{1,0:T(8,128)} %get-tuple-element.58) | copy-start | bytes 9437188
  317.9 164.4 %slice-start = ((s8[4718592]{0:T(1024)(128)(4,1)}), s8[4194304]{0:T(1024)(128)(4,1)S(1)}, s32[]{:S(2)}) async-start(s8[4718592]{0:T(1024)(128)(4,1)} %bitcast.51), calls=%async_computation.2 | async-start | bytes 8388608
  320.6 161.7 %copy-start.2 = (f32[1024,768]{1,0:T(8,128)S(1)}, f32[1024,768]{1,0:T(8,128)}, u32[]{:S(2)}) copy-start(f32[1024,768]{1,0:T(8,128)} %copy-done.1) | copy-start | bytes 9437188
  320.6 161.7 %slice-start.1 = ((s8[4718592]{0:T(1024)(128)(4,1)}), s8[524288]{0:T(1024)(128)(4,1)S(1)}, s32[]{:S(2)}) async-start(s8[4718592]{0:T(1024)(128)(4,1)} %bitcast.51), calls=%async_computation.3 | async-start | bytes 1048576
  320.6 161.7 %copy-start.22 = (f32[768]{0:T(1024)S(1)}, f32[768]{0:T(1024)}, u32[]{:S(2)}) copy-start(f32[768]{0:T(1024)} %reshape.244) | copy-start | bytes 9220
Sparse Core Ops, SparseCore 0:
  15.4 67.3 all-gather.7
  86.2 80.9 all-gather.5

commit v4 on v3

--- a/solution.py
+++ b/solution.py
@@ -438,14 +438,15 @@
         (grad_wqkv, w_qkv.shape[0], True),
         (grad_wout, w_out.shape[0], True),
         (grad_wup, w_up.shape[0], True),
-        (grad_wdown, w_down.shape[0], True),
         (owned, small_rows, False),
     ]
-    if all(rb % 8 == 0 and a.shape[1] % 256 == 0 for (a, rb, _) in parts[:4]):
+    down_sum = lax.psum_scatter(grad_wdown, ALL, scatter_dimension=0, tiled=True)
+    if all(rb % 8 == 0 and a.shape[1] % 256 == 0 for (a, rb, _) in parts[:3]):
         sums = ring_reduce_scatter(parts, mesh_shape, after=(grad_inputs,))
     else:
         sums = [lax.psum_scatter(a, ALL, scatter_dimension=0, tiled=True) for (a, _, _) in parts]
-    small_sums = split_owned(sums[4].reshape(1, -1), [s for s in small_sizes])
+    sums = list(sums[:3]) + [down_sum] + list(sums[3:])
+    small_sums = split_owned(sums[4].reshape(1, -1), small_sizes)
     bqv, bout, g1, c1, g2, c2, bup, bdown = small_sums
     return (
         block_out,

time: 509 us -> 492 us (0.967)
  Pallas kernels: 226 us -> 196 us
  matrix products: 114 us -> 120 us
    pallas_call x1, Pallas kernels: 160 us -> 130 us  [ring_reduce_scatter(): pl.pallas_call(kernel, out_shape=out_shape, in_specs=[pl.BlockSpec(memory...]
  transfers between devices with their start and end apart: 2 -> 3, of which waited for: 2 -> 2; matrix products, arithmetic and copies ran while one was open for 7% -> 24% of each run, Pallas kernels for 6% -> 41%
where the time goes in v4:
time: 492 us; the launch traced here: 483 us
  Pallas kernels  196 us (40%)
  matrix products  120 us (24%)
  waiting for transfers between devices  85 us (17%)
  local copies, waits for them, and re-layouts  50.8 us (10%)
  other arithmetic  16 us (3%)
  between operations  14.7 us (3%)
    pallas_call x1, Pallas kernels, ring_reduce_scatter(): pl.pallas_call(kernel, out_shape=out_shape, in_specs=[pl.BlockSpec(memory...  130 us
    all_gather x1, waiting for transfers between devices, on_device(): attn_all = lax.all_gather(attn_buf, ALL, axis=0, tiled=False)  58.1 us
    dot_general x1, matrix products, on_device(): jnp.dot(h_two, up_full, preferred_element_type=jnp.float32)  36.7 us
    pallas_call x1, Pallas kernels, attention_bwd(): pl.pallas_call(attn_bwd_kernel, out_shape=jax.ShapeDtypeStruct((rows, wid...  36.3 us
    pallas_call x1, Pallas kernels, attention_fwd(): pl.pallas_call(attn_fwd_kernel, out_shape=jax.ShapeDtypeStruct((rows, mod...  29.8 us
    all_gather x1, waiting for transfers between devices, on_device(): mlp_all = lax.all_gather(mlp_buf, ALL, axis=0, tiled=False)  26.9 us
    dot_general x1, matrix products, on_device(): jnp.einsum('td,fd->tf', cotangent, down_full, preferred_element_type=jnp....  14.5 us
  transfers between devices with their start and end apart: 3, of which 2 were waited for; matrix products, arithmetic and copies ran while one was open for 24% of the time, Pallas kernels for 41%

profile of v4, /device:TPU:1, one launch (start us, length us, event | category | flops | bytes accessed | tf_op | source)
XLA Modules:
  0.0 483.5 jit_solution(3900073163711525872)
XLA Ops:
  7.2 5.5 %concatenate.23 = bf16[288]{0:T(512)(128)(2,1)S(1)} concatenate(bf16[48]{0:T(256)(128)(2,1)} %param.18, bf16[24]{0:T(256)(128)(2,1)} %param.20, bf16[24]{0:T(256)(128)(2,1)} %param.21, bf16[24]{0:T(256)(128)(2,1)} %param.22, bf16[24]{0:T(256)(128)(2,1)} %param.23, bf16[24]{0:T(256)(128)(2,1)} %param.24, bf16[96]{0:T(256)(128)(2,1)} %param.26, bf16[24]{0:T(256)(128)(2,1)} %param.28), dimensions={0} | concatenate | bytes 1152 | tf_op jit(solution)/shard_map/concatenate | solution.py:317
  12.8 1.0 reshape.215
  13.8 1.4 maximum_bitcast_fusion
  15.3 1.0 reshape.218
  16.3 1.6 pad_maximum_fusion
  18.0 1.3 broadcast_in_dim.14.vr_ref
  19.3 1.3 broadcast_in_dim.13.sr_ref
  20.6 1.7 copy.38.sc_ref
  22.3 1.7 convert_reduce_fusion.2
  24.0 0.6 fusion.29
  24.7 58.1 %all-gather.8.cloned.1.call-done = bf16[32,97,768]{2,1,0:T(8,128)(2,1)} async-done(((bf16[1,97,768]{2,1,0:T(8,128)(2,1)}), bf16[32,97,768]{2,1,0:T(8,128)(2,1)}) %all-gather.8.cloned.1.call-update) | async-done | bytes 4767760 | tf_op jit(solution)/shard_map/all_gather | solution.py:363
  82.7 1.0 slice.122
  83.7 0.1 slice.101
  83.8 0.1 slice.103
  83.9 0.1 slice_convert_fusion.1
  83.9 0.1 reshape.243
  84.0 0.1 slice_convert_fusion
  84.1 0.7 reshape.244
  84.8 0.1 reshape.241
  84.9 0.1 reshape.238
  85.0 0.1 reshape.242
  85.0 0.1 reshape.239
  85.1 0.1 reshape.240
  85.2 4.0 slice.125
  89.2 6.6 %reshape.216 = bf16[768,2304]{1,0:T(8,128)(2,1)} reshape(bf16[32,72,768]{2,1,0:T(8,128)(2,1)} %slice.125) | data formatting | bytes 7077888 | tf_op jit(solution)/shard_map/reshape | solution.py:364
  95.8 2.3 slice.129
  98.2 8.0 %add_convert_fusion.q_ref.k_ref.v_ref = bf16[1024,2304]{1,0:T(8,128)(2,1)} fusion(bf16[768,2304]{1,0:T(8,128)(2,1)} %reshape.216, f32[2304]{0:T(1024)S(1)} %pad_maximum_fusion.2, bf16[1024,768]{1,0:T(8,128)(2,1)S(1)} %copy-done.2, f32[768]{0:T(1024)S(1)} %reshape.239, f32[768]{0:T(1024)S(1)} %reshape.238, f32[1024]{0:T(1024)S(1)} %add_rsqrt_fusion.1, ...), kind=kOutput, calls=%fused_computation.28 | convolution fusion | flops 3633315840 | bytes 9853952 | tf_op jit(solution)/shard_map/dot_general | solution.py:380
  106.1 29.8 %shard_map.263 = bf16[1024,768]{1,0:T(8,128)(2,1)} custom-call(bf16[1024,2304]{1,0:T(8,128)(2,1)} %add_convert_fusion.q_ref.k_ref.v_ref, bf16[1024,2304]{1,0:T(8,128)(2,1)} %add_convert_fusion.q_ref.k_ref.v_ref, bf16[1024,2304]{1,0:T(8,128)(2,1)} %add_convert_fusion.q_ref.k_ref.v_ref, s32[2,512,1]{2,1,0:T(8,128)} %copy.38.sc_ref, ...), custom_call_target="tpu_custom_call" | custom-call | flops 1610612736 | bytes 6291456 | tf_op jit(solution)/shard_map/pallas_call | solution.py:105
  136.0 3.8 fusion.42
  139.8 0.5 multiply_reduce_fusion.2
  140.3 26.9 %all-gather.6.cloned.1.call-done = bf16[6144,768]{1,0:T(8,128)(2,1)} async-done(((bf16[192,768]{1,0:T(8,128)(2,1)}), bf16[6144,768]{1,0:T(8,128)(2,1)}) %all-gather.6.cloned.1.call-update) | async-done | bytes 9437200 | tf_op jit(solution)/shard_map/all_gather | solution.py:370
  167.2 8.0 %fusion.39 = (bf16[32,96,768]{2,1,0:T(8,128)(2,1)}, bf16[32,96,768]{2,1,0:T(8,128)(2,1)}) fusion(bf16[32,192,768]{2,1,0:T(8,128)(2,1)} %bitcast.51), kind=kLoop, calls=%fused_computation.94 | loop fusion | bytes 18874368 | tf_op jit(solution)/shard_map/slice | solution.py:372
  175.2 8.5 %reshape.219 = bf16[768,3072]{1,0:T(8,128)(2,1)} reshape(bf16[32,96,768]{2,1,0:T(8,128)(2,1)} %get-tuple-element.33) | data formatting | bytes 9437184 | tf_op jit(solution)/shard_map/reshape | solution.py:371
  183.6 36.7 %fusion.2 = (bf16[1024,3072]{1,0:T(8,128)(2,1)S(1)}, f32[1024,3072]{1,0:T(8,128)}) fusion(f32[3072]{0:T(1024)S(1)} %reshape.243, bf16[768,3072]{1,0:T(8,128)(2,1)} %reshape.219, f32[1024,768]{1,0:T(8,128)S(1)} %get-tuple-element.52, f32[768]{0:T(1024)S(1)} %reshape.242, f32[768]{0:T(1024)S(1)} %reshape.241, f32[1024]{0:T(1024)S(1)} %add_rsqrt_fusion, ...), kind=kOutput, calls=%fused_computation.4 | convolution fusion | flops 5043388416 | bytes 26765312 | tf_op jit(solution)/shard_map/dot_general | solution.py:394
  220.3 2.6 copy-done.17
  223.0 7.6 %fusion.43 = f32[3072,768]{1,0:T(8,128)} fusion(bf16[1024,3072]{1,0:T(8,128)(2,1)S(1)} %get-tuple-element.53, bf16[1024,768]{1,0:T(8,128)(2,1)S(1)} %copy-done.6), kind=kOutput, calls=%fused_computation.98 | convolution fusion | flops 4831838208 | bytes 17301504 | tf_op jit(solution)/shard_map/tf,td->fd/dot_general | solution.py:405
  230.5 14.5 %convert_reduce_fusion = (f32[3072]{0:T(1024)S(1)}, bf16[1024,3072]{1,0:T(8,128)(2,1)}) fusion(f32[1024,3072]{1,0:T(8,128)} %get-tuple-element.54, f32[3072]{0:T(1024)S(1)} %reshape.243, bf16[3072,768]{1,0:T(8,128)(2,1)} %bitcast.54, bf16[1024,768]{1,0:T(8,128)(2,1)} %param.31), kind=kOutput, calls=%fused_computation.11 | convolution fusion | flops 4872729600 | bytes 25190400 | tf_op jit(solution)/shard_map/td,fd->tf/dot_general | solution.py:407
  245.1 9.7 %multiply_reduce_fusion = (f32[768]{0:T(1024)S(1)}, f32[1024]{0:T(1024)S(1)}, f32[1024]{0:T(1024)S(1)}, f32[768]{0:T(1024)S(1)}, f32[1024,768]{1,0:T(8,128)S(1)}) fusion(f32[1024,768]{1,0:T(8,128)S(1)} %get-tuple-element.52, f32[1024]{0:T(1024)S(1)} %add_rsqrt_fusion, f32[1024]{0:T(1024)S(1)} %broadcast_multiply_fusion.4, f32[768]{0:T(1024)S(1)} %reshape.241, ...), kind=kOutput, calls=%fused_computation.49 | convolution fusion | flops 4838912000 | bytes 17327104 | tf_op jit(solution)/shard_map/tf,df->td/dot_general | solution.py:413
  254.8 2.6 convert_reduce_fusion.4
  257.4 0.1 reshape.221
  257.5 0.1 reshape.224
  257.6 0.1 reshape.227
  257.7 0.1 reshape.225
  257.8 5.0 %convolution_convert_fusion.do_ref = bf16[1024,768]{1,0:T(8,128)(2,1)} fusion(bf16[768,768]{1,0:T(8,128)(2,1)} %bitcast.59, f32[1024,768]{1,0:T(8,128)} %get-tuple-element.31), kind=kOutput, calls=%fused_computation.58 | convolution fusion | flops 1209532416 | bytes 5898240 | tf_op jit(solution)/shard_map/td,cd->tc/dot_general | solution.py:420
  262.8 36.3 %shard_map.264 = bf16[1024,2304]{1,0:T(8,128)(2,1)} custom-call(bf16[1024,2304]{1,0:T(8,128)(2,1)} %add_convert_fusion.q_ref.k_ref.v_ref, bf16[1024,2304]{1,0:T(8,128)(2,1)} %add_convert_fusion.q_ref.k_ref.v_ref, bf16[1024,2304]{1,0:T(8,128)(2,1)} %add_convert_fusion.q_ref.k_ref.v_ref, bf16[1024,768]{1,0:T(8,128)(2,1)} %convolution_convert_fusion.do_ref, ...), custom_call_target="tpu_custom_call" | custom-call | flops 4026531840 | bytes 11010048 | tf_op jit(solution)/shard_map/pallas_call | solution.py:137
  299.2 9.4 %fusion.28 = (f32[768]{0:T(1024)S(1)}, f32[1024]{0:T(1024)S(1)}, f32[1024]{0:T(1024)S(1)}, f32[768]{0:T(1024)S(1)}, f32[1024,768]{1,0:T(8,128)}) fusion(bf16[1024,768]{1,0:T(8,128)(2,1)S(1)} %copy-done.3, f32[1024]{0:T(1024)S(1)} %copy-done.11, f32[1024]{0:T(1024)S(1)} %copy-done.9, f32[768]{0:T(1024)S(1)} %copy-done.13, ...), kind=kOutput, calls=%fused_computation.46 | convolution fusion | flops 3631739392 | bytes 13001728 | tf_op jit(solution)/shard_map/te,de->td/dot_general | solution.py:427
  308.6 0.1 reshape.222
  308.7 3.3 convert_reduce_fusion.1
  312.0 0.1 concatenate.27
  312.1 0.1 concatenate.28
  312.1 0.1 reshape.223
  312.2 0.1 concatenate.30
  312.4 3.5 fusion.31.refs_1_
  316.0 4.0 fusion.27.refs_4_
  320.0 6.1 %fusion.34.refs_0_ = f32[768,2304]{1,0:T(8,128)} fusion(bf16[1024,2304]{1,0:T(8,128)(2,1)S(1)} %bitcast.50, bf16[1024,768]{1,0:T(8,128)(2,1)S(1)} %copy-done.3, f32[768]{0:T(1024)S(1)} %copy-done.15, f32[768]{0:T(1024)S(1)} %copy-done.13, f32[1024]{0:T(1024)S(1)} %copy-done.11, f32[1024]{0:T(1024)S(1)} %copy-done.9), kind=kOutput, calls=%fused_computation.91 | convolution fusion | flops 3628597248 | bytes 13383680 | tf_op jit(solution)/shard_map/td,te->de/dot_general | solution.py:426
  326.1 8.3 %fusion.37.refs_2_ = f32[768,3072]{1,0:T(8,128)} fusion(bf16[1024,3072]{1,0:T(8,128)(2,1)S(1)} %bitcast.53, f32[1024,768]{1,0:T(8,128)S(1)} %copy-done.1, f32[768]{0:T(1024)S(1)} %reshape.242, f32[768]{0:T(1024)S(1)} %reshape.241, f32[1024]{0:T(1024)S(1)} %add_rsqrt_fusion, f32[1024]{0:T(1024)S(1)} %broadcast_multiply_fusion.4), kind=kOutput, calls=%fused_computation.92 | convolution fusion | flops 4835770368 | bytes 18888704 | tf_op jit(solution)/shard_map/td,tf->df/dot_general | solution.py:412
  334.5 130.3 %shard_map.265 = (f32[24,2304]{1,0:T(8,128)S(1)}, f32[24,768]{1,0:T(8,128)S(1)}, f32[24,3072]{1,0:T(8,128)S(1)}, f32[8,128]{1,0:T(8,128)S(1)}) custom-call(f32[768,2304]{1,0:T(8,128)} %fusion.34.refs_0_, f32[768,768]{1,0:T(8,128)S(1)} %fusion.31.refs_1_, f32[768,3072]{1,0:T(8,128)} %fusion.37.refs_2_, f32[256,128]{1,0:T(8,128)S(1)} %reshape.228.refs_3_, ...), custom_call_target="tpu_custom_call" | custom-call | flops 4751360 | bytes 38010880 | tf_op jit(solution)/shard_map/pallas_call | solution.py:303
  464.8 0.6 slice_bitcast_fusion.1
  465.3 0.5 slice_bitcast_fusion.7
  465.9 0.6 slice_bitcast_fusion
  466.5 8.0 %add_convert_fusion.1 = bf16[1024,768]{1,0:T(8,128)(2,1)} fusion(f32[1024,768]{1,0:T(8,128)S(1)} %copy-done.1, bf16[1024,3072]{1,0:T(8,128)(2,1)} %copy-done.17, bf16[3072,768]{1,0:T(8,128)(2,1)S(1)} %bitcast.57, f32[768]{0:T(1024)S(1)} %copy-done.16), kind=kOutput, calls=%fused_computation.52 | convolution fusion | flops 4834197504 | bytes 15731712 | tf_op jit(solution)/shard_map/dot_general | solution.py:400
  474.5 0.7 copy.48
  475.2 0.6 copy.49
  475.8 0.7 copy.50
  (76 shorter events, 0.5 us)
Async XLA Ops:
  7.2 16.8 %copy-start.2 = (bf16[1024,768]{1,0:T(8,128)(2,1)S(1)}, bf16[1024,768]{1,0:T(8,128)(2,1)}, u32[]{:S(2)}) copy-start(bf16[1024,768]{1,0:T(8,128)(2,1)} %param.16) | copy-start | bytes 4718596
  7.2 75.5 %all-gather.8.cloned.1.call-start = ((), (), s32[]{:S(2)}) async-start(), calls=%async_computation.3 | async-start | bytes 5271552 | tf_op jit(solution)/shard_map/all_gather | solution.py:363
  15.2 152.0 %all-gather.6.cloned.1.call-start = ((), (), s32[]{:S(2)}) async-start(), calls=%async_computation.2 | async-start | bytes 9732096 | tf_op jit(solution)/shard_map/all_gather | solution.py:370
  18.0 456.5 %reduce-scatter.2.cloned.1.call-start = ((), (), s32[]{:S(2)}) async-start(), calls=%async_computation.1 | async-start | bytes 9732096 | tf_op jit(solution)/shard_map/reduce_scatter | solution.py:443
  24.0 74.1 %copy-start.8 = (f32[1024]{0:T(1024)}, f32[1024]{0:T(1024)S(1)}, u32[]{:S(2)}) copy-start(f32[1024]{0:T(1024)S(1)} %broadcast_multiply_fusion.5) | copy-start | bytes 12292
  24.7 73.5 %copy-start.10 = (f32[1024]{0:T(1024)}, f32[1024]{0:T(1024)S(1)}, u32[]{:S(2)}) copy-start(f32[1024]{0:T(1024)S(1)} %add_rsqrt_fusion.1) | copy-start | bytes 12292
  85.0 13.2 %copy-start.12 = (f32[768]{0:T(1024)}, f32[768]{0:T(1024)S(1)}, u32[]{:S(2)}) copy-start(f32[768]{0:T(1024)S(1)} %reshape.238) | copy-start | bytes 9220
  85.1 13.1 %copy-start.14 = (f32[768]{0:T(1024)}, f32[768]{0:T(1024)S(1)}, u32[]{:S(2)}) copy-start(f32[768]{0:T(1024)S(1)} %reshape.239) | copy-start | bytes 9220
  139.8 115.1 %copy-start = (f32[1024,768]{1,0:T(8,128)}, f32[1024,768]{1,0:T(8,128)S(1)}, u32[]{:S(2)}) copy-start(f32[1024,768]{1,0:T(8,128)S(1)} %get-tuple-element.52) | copy-start | bytes 9437188
  183.6 39.3 %copy-start.6 = (bf16[1024,768]{1,0:T(8,128)(2,1)S(1)}, bf16[1024,768]{1,0:T(8,128)(2,1)}, u32[]{:S(2)}) copy-start(bf16[1024,768]{1,0:T(8,128)(2,1)} %param.31) | copy-start | bytes 4718596
  220.3 2.7 copy-start.17
  245.1 9.8 %copy-start.7 = (bf16[1024,768]{1,0:T(8,128)(2,1)S(1)}, bf16[1024,768]{1,0:T(8,128)(2,1)}, u32[]{:S(2)}) copy-start(bf16[1024,768]{1,0:T(8,128)(2,1)} %param.31) | copy-start | bytes 4718596
  262.8 36.4 %copy-start.3 = (bf16[1024,768]{1,0:T(8,128)(2,1)S(1)}, bf16[1024,768]{1,0:T(8,128)(2,1)}, u32[]{:S(2)}) copy-start(bf16[1024,768]{1,0:T(8,128)(2,1)} %param.16) | copy-start | bytes 4718596
  262.8 36.4 %copy-start.9 = (f32[1024]{0:T(1024)S(1)}, f32[1024]{0:T(1024)}, u32[]{:S(2)}) copy-start(f32[1024]{0:T(1024)} %copy-done.8) | copy-start | bytes 12292
  262.8 36.4 %copy-start.11 = (f32[1024]{0:T(1024)S(1)}, f32[1024]{0:T(1024)}, u32[]{:S(2)}) copy-start(f32[1024]{0:T(1024)} %copy-done.10) | copy-start | bytes 12292
  262.8 36.4 %copy-start.13 = (f32[768]{0:T(1024)S(1)}, f32[768]{0:T(1024)}, u32[]{:S(2)}) copy-start(f32[768]{0:T(1024)} %copy-done.12) | copy-start | bytes 9220
  308.6 3.8 copy-start.5
  312.4 3.5 copy-start.4
  312.4 7.5 %slice-start = ((s8[4718592]{0:T(1024)(128)(4,1)}), s8[4194304]{0:T(1024)(128)(4,1)S(1)}, s32[]{:S(2)}) async-start(s8[4718592]{0:T(1024)(128)(4,1)} %bitcast.49), calls=%async_computation.4 | async-start | bytes 8388608
  315.9 4.0 slice-start.1
  316.0 4.0 copy-start.15
  316.0 10.1 %slice-start.2 = ((s8[6291456]{0:T(1024)(128)(4,1)}), s8[4194304]{0:T(1024)(128)(4,1)S(1)}, s32[]{:S(2)}) async-start(s8[6291456]{0:T(1024)(128)(4,1)} %bitcast.52), calls=%async_computation.6 | async-start | bytes 8388608
  320.0 6.1 %copy-start.1 = (f32[1024,768]{1,0:T(8,128)S(1)}, f32[1024,768]{1,0:T(8,128)}, u32[]{:S(2)}) copy-start(f32[1024,768]{1,0:T(8,128)} %copy-done) | copy-start | bytes 9437188
  320.0 6.1 %slice-start.3 = ((s8[6291456]{0:T(1024)(128)(4,1)}), s8[2097152]{0:T(1024)(128)(4,1)S(1)}, s32[]{:S(2)}) async-start(s8[6291456]{0:T(1024)(128)(4,1)} %bitcast.52), calls=%async_computation.7 | async-start | bytes 4194304
  326.1 140.3 %slice-start.4 = ((s8[4718592]{0:T(1024)(128)(4,1)}), s8[4194304]{0:T(1024)(128)(4,1)S(1)}, s32[]{:S(2)}) async-start(s8[4718592]{0:T(1024)(128)(4,1)} %bitcast.55), calls=%async_computation.8 | async-start | bytes 8388608
  334.5 132.0 %slice-start.5 = ((s8[4718592]{0:T(1024)(128)(4,1)}), s8[524288]{0:T(1024)(128)(4,1)S(1)}, s32[]{:S(2)}) async-start(s8[4718592]{0:T(1024)(128)(4,1)} %bitcast.55), calls=%async_computation.9 | async-start | bytes 1048576
  334.5 132.0 %copy-start.16 = (f32[768]{0:T(1024)S(1)}, f32[768]{0:T(1024)}, u32[]{:S(2)}) copy-start(f32[768]{0:T(1024)} %reshape.244) | copy-start | bytes 9220
Sparse Core Ops, SparseCore 0:
  15.3 67.3 all-gather.7
  86.2 80.9 all-gather.5
  230.7 135.2 reduce-scatter.1

commit v5 on v4

--- a/solution.py
+++ b/solution.py
@@ -434,18 +434,20 @@
     lanes = 128
     small_rows = 8 * pl.cdiv(pl.cdiv(n_small, lanes), 8)
     owned = jnp.pad(owned, ((0, 0), (0, small_rows * lanes - n_small))).reshape(-1, lanes)
+    half_up = grad_wup.shape[1] // 2
     parts = [
         (grad_wqkv, w_qkv.shape[0], True),
         (grad_wout, w_out.shape[0], True),
-        (grad_wup, w_up.shape[0], True),
+        (grad_wup[:, half_up:], w_up.shape[0], True),
         (owned, small_rows, False),
     ]
     down_sum = lax.psum_scatter(grad_wdown, ALL, scatter_dimension=0, tiled=True)
+    up_sum = lax.psum_scatter(grad_wup[:, :half_up], ALL, scatter_dimension=0, tiled=True)
     if all(rb % 8 == 0 and a.shape[1] % 256 == 0 for (a, rb, _) in parts[:3]):
         sums = ring_reduce_scatter(parts, mesh_shape, after=(grad_inputs,))
     else:
         sums = [lax.psum_scatter(a, ALL, scatter_dimension=0, tiled=True) for (a, _, _) in parts]
-    sums = list(sums[:3]) + [down_sum] + list(sums[3:])
+    sums = list(sums[:2]) + [jnp.concatenate([up_sum, sums[2]], axis=1), down_sum] + list(sums[3:])
     small_sums = split_owned(sums[4].reshape(1, -1), small_sizes)
     bqv, bout, g1, c1, g2, c2, bup, bdown = small_sums
     return (

time: 492 us -> 528 us (1.073)
  the two profiles are of different devices: /device:TPU:1 before, /device:TPU:0 now
where the time goes in v5:
time: 528 us; the launch traced here: 519 us
  Pallas kernels  200 us (38%)
  matrix products  127 us (24%)
  waiting for transfers between devices  105 us (20%)
  local copies, waits for them, and re-layouts  55.3 us (10%)
  other arithmetic  17.7 us (3%)
  between operations  14.8 us (3%)
    pallas_call x1, Pallas kernels, ring_reduce_scatter(): pl.pallas_call(kernel, out_shape=out_shape, in_specs=[pl.BlockSpec(memory...  134 us
    all_gather x1, waiting for transfers between devices, on_device(): attn_all = lax.all_gather(attn_buf, ALL, axis=0, tiled=False)  58.3 us
    dot_general x1, matrix products, on_device(): jnp.dot(h_two, up_full, preferred_element_type=jnp.float32)  47.9 us
    pallas_call x1, Pallas kernels, attention_bwd(): pl.pallas_call(attn_bwd_kernel, out_shape=jax.ShapeDtypeStruct((rows, wid...  36.3 us
    pallas_call x1, Pallas kernels, attention_fwd(): pl.pallas_call(attn_fwd_kernel, out_shape=jax.ShapeDtypeStruct((rows, mod...  29.8 us
    all_gather x1, waiting for transfers between devices, on_device(): mlp_all = lax.all_gather(mlp_buf, ALL, axis=0, tiled=False)  26.9 us
    reduce_scatter x1, waiting for transfers between devices, on_device(): lax.psum_scatter(grad_wdown, ALL, scatter_dimension=0, tiled=True)  19.7 us
  transfers between devices with their start and end apart: 4, of which 3 were waited for; matrix products, arithmetic and copies ran while one was open for 20% of the time, Pallas kernels for 38%

profile of v5, /device:TPU:0, one launch (start us, length us, event | category | flops | bytes accessed | tf_op | source)
XLA Modules:
  0.0 519.3 jit_solution(12555007868131331476)
XLA Ops:
  7.2 5.5 %concatenate.26 = bf16[288]{0:T(512)(128)(2,1)S(1)} concatenate(bf16[48]{0:T(256)(128)(2,1)} %param.18, bf16[24]{0:T(256)(128)(2,1)} %param.20, bf16[24]{0:T(256)(128)(2,1)} %param.21, bf16[24]{0:T(256)(128)(2,1)} %param.22, bf16[24]{0:T(256)(128)(2,1)} %param.23, bf16[24]{0:T(256)(128)(2,1)} %param.24, bf16[96]{0:T(256)(128)(2,1)} %param.26, bf16[24]{0:T(256)(128)(2,1)} %param.28), dimensions={0} | concatenate | bytes 1152 | tf_op jit(solution)/shard_map/concatenate | solution.py:317
  12.8 1.0 reshape.215
  13.8 1.4 maximum_bitcast_fusion
  15.3 1.0 reshape.218
  16.3 1.6 pad_maximum_fusion
  18.0 1.3 broadcast_in_dim.14.vr_ref
  19.3 1.3 broadcast_in_dim.13.sr_ref
  20.6 1.7 copy.38.sc_ref
  22.3 1.7 convert_reduce_fusion.2
  24.0 0.6 fusion.29
  24.6 58.3 %all-gather.8.cloned.1.call-done = bf16[32,97,768]{2,1,0:T(8,128)(2,1)} async-done(((bf16[1,97,768]{2,1,0:T(8,128)(2,1)}), bf16[32,97,768]{2,1,0:T(8,128)(2,1)}) %all-gather.8.cloned.1.call-update) | async-done | bytes 4767760 | tf_op jit(solution)/shard_map/all_gather | solution.py:363
  82.9 1.0 slice.130
  84.0 0.1 slice_convert_fusion.1
  84.2 0.7 slice_convert_fusion
  84.9 0.1 reshape.241
  85.0 0.1 reshape.238
  85.1 0.1 reshape.242
  85.1 0.1 reshape.239
  85.2 0.1 reshape.240
  85.3 4.1 slice.133
  89.5 6.6 %reshape.216 = bf16[768,2304]{1,0:T(8,128)(2,1)} reshape(bf16[32,72,768]{2,1,0:T(8,128)(2,1)} %slice.133) | data formatting | bytes 7077888 | tf_op jit(solution)/shard_map/reshape | solution.py:364
  96.0 2.4 slice.137
  98.5 7.9 %add_convert_fusion.q_ref.k_ref.v_ref = bf16[1024,2304]{1,0:T(8,128)(2,1)} fusion(bf16[768,2304]{1,0:T(8,128)(2,1)} %reshape.216, f32[2304]{0:T(1024)S(1)} %pad_maximum_fusion.3, bf16[1024,768]{1,0:T(8,128)(2,1)S(1)} %copy-done.7, f32[768]{0:T(1024)S(1)} %reshape.239, f32[768]{0:T(1024)S(1)} %reshape.238, f32[1024]{0:T(1024)S(1)} %add_rsqrt_fusion.1, ...), kind=kOutput, calls=%fused_computation.28 | convolution fusion | flops 3633315840 | bytes 9853952 | tf_op jit(solution)/shard_map/dot_general | solution.py:380
  106.4 29.8 %shard_map.263 = bf16[1024,768]{1,0:T(8,128)(2,1)} custom-call(bf16[1024,2304]{1,0:T(8,128)(2,1)} %add_convert_fusion.q_ref.k_ref.v_ref, bf16[1024,2304]{1,0:T(8,128)(2,1)} %add_convert_fusion.q_ref.k_ref.v_ref, bf16[1024,2304]{1,0:T(8,128)(2,1)} %add_convert_fusion.q_ref.k_ref.v_ref, s32[2,512,1]{2,1,0:T(8,128)} %copy.38.sc_ref, ...), custom_call_target="tpu_custom_call" | custom-call | flops 1610612736 | bytes 6291456 | tf_op jit(solution)/shard_map/pallas_call | solution.py:105
  136.2 3.8 fusion.43
  140.0 0.5 multiply_reduce_fusion.2
  140.5 26.9 %all-gather.6.cloned.1.call-done = bf16[6144,768]{1,0:T(8,128)(2,1)} async-done(((bf16[192,768]{1,0:T(8,128)(2,1)}), bf16[6144,768]{1,0:T(8,128)(2,1)}) %all-gather.6.cloned.1.call-update) | async-done | bytes 9437200 | tf_op jit(solution)/shard_map/all_gather | solution.py:370
  167.4 8.0 %fusion.40 = (bf16[32,96,768]{2,1,0:T(8,128)(2,1)}, bf16[32,96,768]{2,1,0:T(8,128)(2,1)}) fusion(bf16[32,192,768]{2,1,0:T(8,128)(2,1)} %bitcast.51), kind=kLoop, calls=%fused_computation.96 | loop fusion | bytes 18874368 | tf_op jit(solution)/shard_map/slice | solution.py:372
  175.5 8.5 %reshape.219 = bf16[768,3072]{1,0:T(8,128)(2,1)} reshape(bf16[32,96,768]{2,1,0:T(8,128)(2,1)} %get-tuple-element.35) | data formatting | bytes 9437184 | tf_op jit(solution)/shard_map/reshape | solution.py:371
  184.0 47.9 %fusion.2 = (bf16[1024,3072]{1,0:T(8,128)(2,1)}, f32[1024,3072]{1,0:T(8,128)S(1)}) fusion(f32[3072]{0:T(1024)S(1)} %reshape.243, bf16[768,3072]{1,0:T(8,128)(2,1)} %reshape.219, f32[1024,768]{1,0:T(8,128)S(1)} %get-tuple-element.54, f32[768]{0:T(1024)S(1)} %reshape.242, f32[768]{0:T(1024)S(1)} %reshape.241, f32[1024]{0:T(1024)S(1)} %add_rsqrt_fusion, ...), kind=kOutput, calls=%fused_computation.4 | convolution fusion | flops 5043388416 | bytes 26765312 | tf_op jit(solution)/shard_map/dot_general | solution.py:394
  231.9 9.3 %convert_reduce_fusion = (f32[3072]{0:T(1024)S(1)}, bf16[1024,3072]{1,0:T(8,128)(2,1)S(1)}) fusion(f32[1024,3072]{1,0:T(8,128)S(1)} %get-tuple-element.56, f32[3072]{0:T(1024)S(1)} %reshape.243, bf16[3072,768]{1,0:T(8,128)(2,1)S(1)} %bitcast.52, bf16[1024,768]{1,0:T(8,128)(2,1)S(1)} %copy-done.13), kind=kOutput, calls=%fused_computation.11 | convolution fusion | flops 4872729600 | bytes 25190400 | tf_op jit(solution)/shard_map/td,fd->tf/dot_general | solution.py:407
  241.2 5.6 %fusion.37 = f32[768,3072]{1,0:T(8,128)S(1)} fusion(bf16[1024,3072]{1,0:T(8,128)(2,1)S(1)} %get-tuple-element.60, f32[1024,768]{1,0:T(8,128)S(1)} %get-tuple-element.54, f32[768]{0:T(1024)S(1)} %reshape.242, f32[768]{0:T(1024)S(1)} %reshape.241, f32[1024]{0:T(1024)S(1)} %add_rsqrt_fusion, f32[1024]{0:T(1024)S(1)} %broadcast_multiply_fusion.4), kind=kOutput, calls=%fused_computation.93 | convolution fusion | flops 4835770368 | bytes 18888704 | tf_op jit(solution)/shard_map/td,tf->df/dot_general | solution.py:412
  246.8 4.5 fusion.39
  251.4 9.9 %fusion.44 = f32[3072,768]{1,0:T(8,128)} fusion(bf16[1024,3072]{1,0:T(8,128)(2,1)} %get-tuple-element.55, bf16[1024,768]{1,0:T(8,128)(2,1)} %param.31), kind=kOutput, calls=%fused_computation.100 | convolution fusion | flops 4831838208 | bytes 17301504 | tf_op jit(solution)/shard_map/tf,td->fd/dot_general | solution.py:405
  261.3 0.7 copy-done.21
  262.0 0.1 reshape.244
  262.2 9.6 %multiply_reduce_fusion = (f32[768]{0:T(1024)S(1)}, f32[1024]{0:T(1024)S(1)}, f32[1024]{0:T(1024)S(1)}, f32[768]{0:T(1024)S(1)}, f32[1024,768]{1,0:T(8,128)S(1)}) fusion(f32[1024,768]{1,0:T(8,128)S(1)} %get-tuple-element.54, f32[1024]{0:T(1024)S(1)} %add_rsqrt_fusion, f32[1024]{0:T(1024)S(1)} %broadcast_multiply_fusion.4, f32[768]{0:T(1024)S(1)} %reshape.241, ...), kind=kOutput, calls=%fused_computation.49 | convolution fusion | flops 4838912000 | bytes 17327104 | tf_op jit(solution)/shard_map/tf,df->td/dot_general | solution.py:413
  271.8 2.6 convert_reduce_fusion.4
  274.4 0.1 reshape.221
  274.5 0.7 reshape.224
  275.2 0.7 reshape.227
  275.9 0.7 reshape.225
  276.6 5.0 convolution_convert_fusion.do_ref
  281.5 36.3 %shard_map.264 = bf16[1024,2304]{1,0:T(8,128)(2,1)} custom-call(bf16[1024,2304]{1,0:T(8,128)(2,1)} %add_convert_fusion.q_ref.k_ref.v_ref, bf16[1024,2304]{1,0:T(8,128)(2,1)} %add_convert_fusion.q_ref.k_ref.v_ref, bf16[1024,2304]{1,0:T(8,128)(2,1)} %add_convert_fusion.q_ref.k_ref.v_ref, bf16[1024,768]{1,0:T(8,128)(2,1)} %convolution_convert_fusion.do_ref, ...), custom_call_target="tpu_custom_call" | custom-call | flops 4026531840 | bytes 11010048 | tf_op jit(solution)/shard_map/pallas_call | solution.py:137
  317.9 10.0 %fusion.28 = (f32[768]{0:T(1024)S(1)}, f32[1024]{0:T(1024)}, f32[1024]{0:T(1024)}, f32[768]{0:T(1024)S(1)}, f32[1024,768]{1,0:T(8,128)}) fusion(bf16[1024,768]{1,0:T(8,128)(2,1)S(1)} %copy-done.8, f32[1024]{0:T(1024)S(1)} %copy-done.18, f32[1024]{0:T(1024)S(1)} %copy-done.16, f32[768]{0:T(1024)S(1)} %copy-done.20, bf16[1024,2304]{1,0:T(8,128)(2,1)} %shard_map.264, ...), kind=kOutput, calls=%fused_computation.46 | convolution fusion | flops 3631739392 | bytes 13001728 | tf_op jit(solution)/shard_map/te,de->td/dot_general | solution.py:427
  327.9 0.1 reshape.222
  328.0 3.2 convert_reduce_fusion.1
  331.2 0.1 concatenate.30
  331.4 0.1 reshape.223
  331.5 0.1 concatenate.33
  331.7 3.1 fusion.31.refs_1_
  334.8 3.6 fusion.27.refs_4_
  338.5 6.3 %fusion.34.refs_0_ = f32[768,2304]{1,0:T(8,128)} fusion(bf16[1024,2304]{1,0:T(8,128)(2,1)S(1)} %bitcast.50, bf16[1024,768]{1,0:T(8,128)(2,1)S(1)} %copy-done.9, f32[768]{0:T(1024)S(1)} %copy-done.26, f32[768]{0:T(1024)S(1)} %copy-done.20, f32[1024]{0:T(1024)S(1)} %copy-done.18, f32[1024]{0:T(1024)S(1)} %copy-done.16), kind=kOutput, calls=%fused_computation.92 | convolution fusion | flops 3628597248 | bytes 13383680 | tf_op jit(solution)/shard_map/td,te->de/dot_general | solution.py:426
  344.8 133.7 %shard_map.265 = (f32[24,2304]{1,0:T(8,128)S(1)}, f32[24,768]{1,0:T(8,128)S(1)}, f32[24,1536]{1,0:T(8,128)S(1)}, f32[8,128]{1,0:T(8,128)S(1)}) custom-call(f32[768,2304]{1,0:T(8,128)} %fusion.34.refs_0_, f32[768,768]{1,0:T(8,128)S(1)} %fusion.31.refs_1_, f32[768,1536]{1,0:T(8,128)} %get-tuple-element.33.refs_2_, f32[256,128]{1,0:T(8,128)S(1)} %reshape.228.refs_3_, ...), custom_call_target="tpu_custom_call" | custom-call | flops 3571712 | bytes 28573696 | tf_op jit(solution)/shard_map/pallas_call | solution.py:303
  478.6 0.7 copy-done.1
  479.2 0.6 copy-done.3
  479.8 0.6 slice_bitcast_fusion.1
  480.4 0.5 slice_bitcast_fusion.7
  480.9 0.6 slice_bitcast_fusion
  481.6 8.2 %add_convert_fusion.1 = bf16[1024,768]{1,0:T(8,128)(2,1)} fusion(f32[1024,768]{1,0:T(8,128)S(1)} %copy-done.6, bf16[1024,3072]{1,0:T(8,128)(2,1)} %get-tuple-element.55, bf16[3072,768]{1,0:T(8,128)(2,1)S(1)} %bitcast.55, f32[768]{0:T(1024)S(1)} %reshape.244), kind=kOutput, calls=%fused_computation.52 | convolution fusion | flops 4834197504 | bytes 15731712 | tf_op jit(solution)/shard_map/dot_general | solution.py:400
  489.7 1.6 pad_maximum_fusion.1
  491.4 19.7 %reduce-scatter.5.cloned.1.call-done = f32[96,768]{1,0:T(8,128)} async-done(((f32[3072,768]{1,0:T(8,128)}), f32[96,768]{1,0:T(8,128)}) %reduce-scatter.5.cloned.1.call-update) | async-done | bytes 294928 | tf_op jit(solution)/shard_map/reduce_scatter | solution.py:444
  511.1 0.7 copy.47
  511.8 0.6 copy.48
  (97 shorter events, 0.9 us)
Async XLA Ops:
  7.2 16.8 %copy-start.7 = (bf16[1024,768]{1,0:T(8,128)(2,1)S(1)}, bf16[1024,768]{1,0:T(8,128)(2,1)}, u32[]{:S(2)}) copy-start(bf16[1024,768]{1,0:T(8,128)(2,1)} %param.16) | copy-start | bytes 4718596
  7.2 75.7 %all-gather.8.cloned.1.call-start = ((), (), s32[]{:S(2)}) async-start(), calls=%async_computation.5 | async-start | bytes 5271552 | tf_op jit(solution)/shard_map/all_gather | solution.py:363
  15.2 152.2 %all-gather.6.cloned.1.call-start = ((), (), s32[]{:S(2)}) async-start(), calls=%async_computation.4 | async-start | bytes 9732096 | tf_op jit(solution)/shard_map/all_gather | solution.py:370
  18.0 471.8 %reduce-scatter.3.cloned.1.call-start = ((), (), s32[]{:S(2)}) async-start(), calls=%async_computation.2 | async-start | bytes 4866048 | tf_op jit(solution)/shard_map/reduce_scatter | solution.py:445
  24.0 74.4 %copy-start.15 = (f32[1024]{0:T(1024)}, f32[1024]{0:T(1024)S(1)}, u32[]{:S(2)}) copy-start(f32[1024]{0:T(1024)S(1)} %broadcast_multiply_fusion.5) | copy-start | bytes 12292
  24.6 73.8 %copy-start.17 = (f32[1024]{0:T(1024)}, f32[1024]{0:T(1024)S(1)}, u32[]{:S(2)}) copy-start(f32[1024]{0:T(1024)S(1)} %add_rsqrt_fusion.1) | copy-start | bytes 12292
  85.1 13.4 %copy-start.19 = (f32[768]{0:T(1024)}, f32[768]{0:T(1024)S(1)}, u32[]{:S(2)}) copy-start(f32[768]{0:T(1024)S(1)} %reshape.238) | copy-start | bytes 9220
  85.2 13.2 %copy-start.25 = (f32[768]{0:T(1024)}, f32[768]{0:T(1024)S(1)}, u32[]{:S(2)}) copy-start(f32[768]{0:T(1024)S(1)} %reshape.239) | copy-start | bytes 9220
  140.0 131.7 %copy-start.5 = (f32[1024,768]{1,0:T(8,128)}, f32[1024,768]{1,0:T(8,128)S(1)}, u32[]{:S(2)}) copy-start(f32[1024,768]{1,0:T(8,128)S(1)} %get-tuple-element.54) | copy-start | bytes 9437188
  183.9 47.9 %copy-start.12 = (bf16[32,96,768]{2,1,0:T(8,128)(2,1)S(1)}, bf16[32,96,768]{2,1,0:T(8,128)(2,1)}, u32[]{:S(2)}) copy-start(bf16[32,96,768]{2,1,0:T(8,128)(2,1)} %get-tuple-element.34) | copy-start | bytes 14155780
  183.9 47.9 %copy-start.13 = (bf16[1024,768]{1,0:T(8,128)(2,1)S(1)}, bf16[1024,768]{1,0:T(8,128)(2,1)}, u32[]{:S(2)}) copy-start(bf16[1024,768]{1,0:T(8,128)(2,1)} %param.31) | copy-start | bytes 4718596
  241.2 5.6 %copy-start.11 = (bf16[1024,3072]{1,0:T(8,128)(2,1)}, bf16[1024,3072]{1,0:T(8,128)(2,1)S(1)}, u32[]{:S(2)}) copy-start(bf16[1024,3072]{1,0:T(8,128)(2,1)S(1)} %get-tuple-element.60) | copy-start | bytes 18874372
  251.3 259.7 %reduce-scatter.5.cloned.1.call-start = ((), (), s32[]{:S(2)}) async-start(), calls=%async_computation.3 | async-start | bytes 9732096 | tf_op jit(solution)/shard_map/reduce_scatter | solution.py:444
  261.3 0.7 copy-start.21
  262.2 9.6 %copy-start.14 = (bf16[1024,768]{1,0:T(8,128)(2,1)S(1)}, bf16[1024,768]{1,0:T(8,128)(2,1)}, u32[]{:S(2)}) copy-start(bf16[1024,768]{1,0:T(8,128)(2,1)} %param.31) | copy-start | bytes 4718596
  281.5 36.3 %copy-start.8 = (bf16[1024,768]{1,0:T(8,128)(2,1)S(1)}, bf16[1024,768]{1,0:T(8,128)(2,1)}, u32[]{:S(2)}) copy-start(bf16[1024,768]{1,0:T(8,128)(2,1)} %param.16) | copy-start | bytes 4718596
  281.5 36.3 %copy-start.16 = (f32[1024]{0:T(1024)S(1)}, f32[1024]{0:T(1024)}, u32[]{:S(2)}) copy-start(f32[1024]{0:T(1024)} %copy-done.15) | copy-start | bytes 12292
  281.5 36.3 %copy-start.18 = (f32[1024]{0:T(1024)S(1)}, f32[1024]{0:T(1024)}, u32[]{:S(2)}) copy-start(f32[1024]{0:T(1024)} %copy-done.17) | copy-start | bytes 12292
  281.5 36.3 %copy-start.20 = (f32[768]{0:T(1024)S(1)}, f32[768]{0:T(1024)}, u32[]{:S(2)}) copy-start(f32[768]{0:T(1024)} %copy-done.19) | copy-start | bytes 9220
  327.9 3.6 copy-start.22
  327.9 3.6 copy-start.23
  327.9 3.6 copy-start.24
  327.9 3.8 copy-start.28
  327.9 3.8 copy-start.27
  327.9 3.8 copy-start.10
  331.7 3.1 copy-start.9
  331.7 6.7 %slice-start = ((s8[4718592]{0:T(1024)(128)(4,1)}), s8[4194304]{0:T(1024)(128)(4,1)S(1)}, s32[]{:S(2)}) async-start(s8[4718592]{0:T(1024)(128)(4,1)} %bitcast.49), calls=%async_computation.6 | async-start | bytes 8388608
  334.8 3.6 slice-start.1
  334.8 3.6 copy-start.26
  338.4 6.4 %copy-start = (f32[1024,768]{1,0:T(8,128)}, f32[1024,768]{1,0:T(8,128)S(1)}, u32[]{:S(2)}) copy-start(f32[1024,768]{1,0:T(8,128)S(1)} %fusion.27.refs_4_) | copy-start | bytes 9437188
  338.5 143.1 %slice-start.2 = ((s8[4718592]{0:T(1024)(128)(4,1)}), s8[524288]{0:T(1024)(128)(4,1)S(1)}, s32[]{:S(2)}) async-start(s8[4718592]{0:T(1024)(128)(4,1)} %bitcast.53), calls=%async_computation.8 | async-start | bytes 1048576
  344.8 136.7 %copy-start.6 = (f32[1024,768]{1,0:T(8,128)S(1)}, f32[1024,768]{1,0:T(8,128)}, u32[]{:S(2)}) copy-start(f32[1024,768]{1,0:T(8,128)} %copy-done.5) | copy-start | bytes 9437188
  344.8 136.7 %slice-start.3 = ((s8[4718592]{0:T(1024)(128)(4,1)}), s8[4194304]{0:T(1024)(128)(4,1)S(1)}, s32[]{:S(2)}) async-start(s8[4718592]{0:T(1024)(128)(4,1)} %bitcast.53), calls=%async_computation.9 | async-start | bytes 8388608
  478.5 0.7 copy-start.1
  479.2 0.6 copy-start.3
  481.6 8.2 %copy-start.2 = (f32[24,1536]{1,0:T(8,128)S(1)}, f32[24,1536]{1,0:T(8,128)}, u32[]{:S(2)}) copy-start(f32[24,1536]{1,0:T(8,128)} %copy-done.1) | copy-start | bytes 442372
  481.6 30.2 %copy-start.4 = (f32[24,768]{1,0:T(8,128)S(1)}, f32[24,768]{1,0:T(8,128)}, u32[]{:S(2)}) copy-start(f32[24,768]{1,0:T(8,128)} %copy-done.3) | copy-start | bytes 221188
Sparse Core Ops, SparseCore 0:
  15.3 67.5 all-gather.7
  86.4 81.0 all-gather.5
  251.5 105.6 reduce-scatter.2
  364.5 146.5 reduce-scatter.4

commit v6 on v4

--- a/solution.py
+++ b/solution.py
@@ -355,20 +355,23 @@
     small = (qv_bias, out_bias, ln1_gain, ln1_shift, ln2_gain, ln2_shift, up_bias, down_bias)
     small_sizes = [a.shape[0] for a in small]
     n_small = sum(small_sizes)
-    rows_q = w_qkv.size // model_width
-    rows_o = w_out.shape[0]
+    width_q = w_qkv.shape[1]
+    rows_q = w_qkv.shape[0]
+    rows_o = w_out.size // width_q
     attn_buf = jnp.concatenate(
-        [w_qkv.reshape(rows_q, model_width), w_out, pack_rows(small, model_width)], axis=0
+        [w_qkv, w_out.reshape(rows_o, width_q), pack_rows(small, width_q)], axis=0
     )
     attn_all = lax.all_gather(attn_buf, ALL, axis=0, tiled=False)
-    qkv_full = attn_all[:, :rows_q].reshape(-1, w_qkv.shape[1])
+    qkv_full = attn_all[:, :rows_q].reshape(-1, width_q)
     out_full = attn_all[:, rows_q : rows_q + rows_o].reshape(-1, model_width)
     small_full = split_owned(attn_all[:, rows_q + rows_o, :n_small], small_sizes)
     qv_full, outb_full, gain_one, shift_one, gain_two, shift_two, upb_full, downb_full = small_full
-    rows_u = w_up.size // model_width
-    mlp_buf = jnp.concatenate([w_up.reshape(rows_u, model_width), w_down], axis=0)
+    width_u = w_up.shape[1]
+    rows_u = w_up.shape[0]
+    rows_d = w_down.size // width_u
+    mlp_buf = jnp.concatenate([w_up, w_down.reshape(rows_d, width_u)], axis=0)
     mlp_all = lax.all_gather(mlp_buf, ALL, axis=0, tiled=False)
-    up_full = mlp_all[:, :rows_u].reshape(-1, w_up.shape[1])
+    up_full = mlp_all[:, :rows_u].reshape(-1, width_u)
     down_full = mlp_all[:, rows_u:].reshape(-1, model_width)
 
     gain_one = gain_one.astype(jnp.float32)

time: 492 us -> 495 us (level)
  waiting for transfers between devices: 85 us -> 97.3 us
  local copies, waits for them, and re-layouts: 50.8 us -> 43.4 us
    all_gather x1, waiting for transfers between devices: 26.9 us -> 36.4 us  [on_device(): mlp_all = lax.all_gather(mlp_buf, ALL, axis=0, tiled=False)]
    reshape x4, local copies, waits for them, and re-layouts: 17 us -> 11.7 us  [the longest x1 8.48 us: on_device(): down_full = mlp_all[:, rows_u:].reshape(-1, model_width)]
  transfers between devices with their start and end apart: 3 -> 3, of which waited for: 2 -> 2; matrix products, arithmetic and copies ran while one was open for 24% -> 21% of each run, Pallas kernels for 41% -> 40%
where the time goes in v6:
time: 495 us; the launch traced here: 487 us
  Pallas kernels  196 us (40%)
  matrix products  118 us (24%)
  waiting for transfers between devices  97.3 us (20%)
  local copies, waits for them, and re-layouts  43.4 us (9%)
  other arithmetic  16.1 us (3%)
  between operations  14.7 us (3%)
    pallas_call x1, Pallas kernels, ring_reduce_scatter(): pl.pallas_call(kernel, out_shape=out_shape, in_specs=[pl.BlockSpec(memory...  130 us
    all_gather x1, waiting for transfers between devices, on_device(): attn_all = lax.all_gather(attn_buf, ALL, axis=0, tiled=False)  60.9 us
    dot_general x1, matrix products, on_device(): jnp.dot(h_two, up_full, preferred_element_type=jnp.float32)  36.7 us
    all_gather x1, waiting for transfers between devices, on_device(): mlp_all = lax.all_gather(mlp_buf, ALL, axis=0, tiled=False)  36.4 us
    pallas_call x1, Pallas kernels, attention_bwd(): pl.pallas_call(attn_bwd_kernel, out_shape=jax.ShapeDtypeStruct((rows, wid...  36.3 us
    pallas_call x1, Pallas kernels, attention_fwd(): pl.pallas_call(attn_fwd_kernel, out_shape=jax.ShapeDtypeStruct((rows, mod...  29.8 us
    dot_general x1, matrix products, on_device(): jnp.einsum('td,fd->tf', cotangent, down_full, preferred_element_type=jnp....  14.4 us
  transfers between devices with their start and end apart: 3, of which 2 were waited for; matrix products, arithmetic and copies ran while one was open for 21% of the time, Pallas kernels for 40%

profile of v6, /device:TPU:1, one launch (start us, length us, event | category | flops | bytes accessed | tf_op | source)
XLA Modules:
  0.0 486.6 jit_solution(10434024143437699995)
XLA Ops:
  7.2 5.5 %concatenate.23 = bf16[288]{0:T(512)(128)(2,1)S(1)} concatenate(bf16[48]{0:T(256)(128)(2,1)} %param.18, bf16[24]{0:T(256)(128)(2,1)} %param.20, bf16[24]{0:T(256)(128)(2,1)} %param.21, bf16[24]{0:T(256)(128)(2,1)} %param.22, bf16[24]{0:T(256)(128)(2,1)} %param.23, bf16[24]{0:T(256)(128)(2,1)} %param.24, bf16[96]{0:T(256)(128)(2,1)} %param.26, bf16[24]{0:T(256)(128)(2,1)} %param.28), dimensions={0} | concatenate | bytes 1152 | tf_op jit(solution)/shard_map/concatenate | solution.py:317
  12.8 0.8 reshape.215
  13.6 1.6 maximum_bitcast_fusion
  15.3 1.0 reshape.218
  16.3 1.6 pad_maximum_fusion
  18.0 1.3 broadcast_in_dim.14.vr_ref
  19.3 1.3 broadcast_in_dim.13.sr_ref
  20.6 1.7 copy.38.sc_ref
  22.3 1.7 convert_reduce_fusion.2
  24.0 0.6 fusion.29
  24.6 60.9 %all-gather.8.cloned.1.call-done = bf16[32,33,2304]{2,1,0:T(8,128)(2,1)} async-done(((bf16[1,33,2304]{2,1,0:T(8,128)(2,1)}), bf16[32,33,2304]{2,1,0:T(8,128)(2,1)}) %all-gather.8.cloned.1.call-update) | async-done | bytes 4866064 | tf_op jit(solution)/shard_map/all_gather | solution.py:364
  85.5 1.1 slice.122
  86.6 0.1 slice.101
  86.7 0.1 slice.103
  86.8 0.1 slice_convert_fusion.1
  86.9 0.1 reshape.243
  86.9 0.1 slice_convert_fusion
  87.0 0.7 reshape.244
  87.7 0.1 reshape.241
  87.8 0.1 reshape.238
  87.9 0.1 reshape.242
  88.0 0.1 reshape.239
  88.1 0.1 reshape.240
  88.2 1.4 reshape.217
  89.5 2.2 slice.125
  91.8 1.8 copy-done.5
  93.6 6.0 %add_convert_fusion.q_ref.k_ref.v_ref = bf16[1024,2304]{1,0:T(8,128)(2,1)} fusion(bf16[768,2304]{1,0:T(8,128)(2,1)S(1)} %bitcast.58, f32[2304]{0:T(1024)S(1)} %pad_maximum_fusion.2, bf16[1024,768]{1,0:T(8,128)(2,1)S(1)} %copy-done.2, f32[768]{0:T(1024)S(1)} %reshape.239, f32[768]{0:T(1024)S(1)} %reshape.238, f32[1024]{0:T(1024)S(1)} %add_rsqrt_fusion.1, ...), kind=kOutput, calls=%fused_computation.28 | convolution fusion | flops 3633315840 | bytes 9853952 | tf_op jit(solution)/shard_map/dot_general | solution.py:383
  99.6 29.8 %shard_map.263 = bf16[1024,768]{1,0:T(8,128)(2,1)} custom-call(bf16[1024,2304]{1,0:T(8,128)(2,1)} %add_convert_fusion.q_ref.k_ref.v_ref, bf16[1024,2304]{1,0:T(8,128)(2,1)} %add_convert_fusion.q_ref.k_ref.v_ref, bf16[1024,2304]{1,0:T(8,128)(2,1)} %add_convert_fusion.q_ref.k_ref.v_ref, s32[2,512,1]{2,1,0:T(8,128)} %copy.38.sc_ref, ...), custom_call_target="tpu_custom_call" | custom-call | flops 1610612736 | bytes 6291456 | tf_op jit(solution)/shard_map/pallas_call | solution.py:105
  129.4 3.8 fusion.42
  133.2 0.5 multiply_reduce_fusion.2
  133.7 36.4 %all-gather.6.cloned.1.call-done = bf16[1536,3072]{1,0:T(8,128)(2,1)} async-done(((bf16[48,3072]{1,0:T(8,128)(2,1)}), bf16[1536,3072]{1,0:T(8,128)(2,1)}) %all-gather.6.cloned.1.call-update) | async-done | bytes 9437200 | tf_op jit(solution)/shard_map/all_gather | solution.py:373
  170.1 8.2 %fusion.39 = (bf16[32,24,3072]{2,1,0:T(8,128)(2,1)}, bf16[32,24,3072]{2,1,0:T(8,128)(2,1)}) fusion(bf16[32,48,3072]{2,1,0:T(8,128)(2,1)} %bitcast.51), kind=kLoop, calls=%fused_computation.94 | loop fusion | bytes 18874368 | tf_op jit(solution)/shard_map/slice | solution.py:375
  178.4 8.5 %reshape.220 = bf16[3072,768]{1,0:T(8,128)(2,1)} reshape(bf16[32,24,3072]{2,1,0:T(8,128)(2,1)} %get-tuple-element.32) | data formatting | bytes 9437184 | tf_op jit(solution)/shard_map/reshape | solution.py:375
  186.8 36.7 %fusion.2 = (bf16[1024,3072]{1,0:T(8,128)(2,1)S(1)}, f32[1024,3072]{1,0:T(8,128)}) fusion(f32[3072]{0:T(1024)S(1)} %reshape.243, bf16[768,3072]{1,0:T(8,128)(2,1)} %bitcast.56, f32[1024,768]{1,0:T(8,128)S(1)} %get-tuple-element.52, f32[768]{0:T(1024)S(1)} %reshape.242, f32[768]{0:T(1024)S(1)} %reshape.241, f32[1024]{0:T(1024)S(1)} %add_rsqrt_fusion, ...), kind=kOutput, calls=%fused_computation.4 | convolution fusion | flops 5043388416 | bytes 26765312 | tf_op jit(solution)/shard_map/dot_general | solution.py:397
  223.5 2.6 copy-done.18
  226.2 7.6 %fusion.43 = f32[3072,768]{1,0:T(8,128)} fusion(bf16[1024,3072]{1,0:T(8,128)(2,1)S(1)} %get-tuple-element.53, bf16[1024,768]{1,0:T(8,128)(2,1)S(1)} %copy-done.7), kind=kOutput, calls=%fused_computation.98 | convolution fusion | flops 4831838208 | bytes 17301504 | tf_op jit(solution)/shard_map/tf,td->fd/dot_general | solution.py:408
  233.8 14.4 %convert_reduce_fusion = (f32[3072]{0:T(1024)S(1)}, bf16[1024,3072]{1,0:T(8,128)(2,1)}) fusion(f32[1024,3072]{1,0:T(8,128)} %get-tuple-element.54, f32[3072]{0:T(1024)S(1)} %reshape.243, bf16[3072,768]{1,0:T(8,128)(2,1)} %reshape.220, bf16[1024,768]{1,0:T(8,128)(2,1)} %param.31), kind=kOutput, calls=%fused_computation.11 | convolution fusion | flops 4872729600 | bytes 25190400 | tf_op jit(solution)/shard_map/td,fd->tf/dot_general | solution.py:410
  248.3 9.7 %multiply_reduce_fusion = (f32[768]{0:T(1024)S(1)}, f32[1024]{0:T(1024)S(1)}, f32[1024]{0:T(1024)S(1)}, f32[768]{0:T(1024)S(1)}, f32[1024,768]{1,0:T(8,128)S(1)}) fusion(f32[1024,768]{1,0:T(8,128)S(1)} %get-tuple-element.52, f32[1024]{0:T(1024)S(1)} %add_rsqrt_fusion, f32[1024]{0:T(1024)S(1)} %broadcast_multiply_fusion.4, f32[768]{0:T(1024)S(1)} %reshape.241, ...), kind=kOutput, calls=%fused_computation.49 | convolution fusion | flops 4838912000 | bytes 17327104 | tf_op jit(solution)/shard_map/tf,df->td/dot_general | solution.py:416
  258.0 2.6 convert_reduce_fusion.4
  260.6 0.1 reshape.221
  260.7 0.1 reshape.224
  260.8 0.1 reshape.227
  260.9 0.1 reshape.225
  261.0 5.0 %convolution_convert_fusion.do_ref = bf16[1024,768]{1,0:T(8,128)(2,1)} fusion(bf16[768,768]{1,0:T(8,128)(2,1)} %reshape.217, f32[1024,768]{1,0:T(8,128)} %get-tuple-element.31), kind=kOutput, calls=%fused_computation.58 | convolution fusion | flops 1209532416 | bytes 5898240 | tf_op jit(solution)/shard_map/td,cd->tc/dot_general | solution.py:423
  266.0 36.3 %shard_map.264 = bf16[1024,2304]{1,0:T(8,128)(2,1)} custom-call(bf16[1024,2304]{1,0:T(8,128)(2,1)} %add_convert_fusion.q_ref.k_ref.v_ref, bf16[1024,2304]{1,0:T(8,128)(2,1)} %add_convert_fusion.q_ref.k_ref.v_ref, bf16[1024,2304]{1,0:T(8,128)(2,1)} %add_convert_fusion.q_ref.k_ref.v_ref, bf16[1024,768]{1,0:T(8,128)(2,1)} %convolution_convert_fusion.do_ref, ...), custom_call_target="tpu_custom_call" | custom-call | flops 4026531840 | bytes 11010048 | tf_op jit(solution)/shard_map/pallas_call | solution.py:137
  302.4 9.4 %fusion.28 = (f32[768]{0:T(1024)S(1)}, f32[1024]{0:T(1024)S(1)}, f32[1024]{0:T(1024)S(1)}, f32[768]{0:T(1024)S(1)}, f32[1024,768]{1,0:T(8,128)}) fusion(bf16[1024,768]{1,0:T(8,128)(2,1)S(1)} %copy-done.3, f32[1024]{0:T(1024)S(1)} %copy-done.12, f32[1024]{0:T(1024)S(1)} %copy-done.10, f32[768]{0:T(1024)S(1)} %copy-done.14, ...), kind=kOutput, calls=%fused_computation.46 | convolution fusion | flops 3631739392 | bytes 13001728 | tf_op jit(solution)/shard_map/te,de->td/dot_general | solution.py:430
  311.8 0.1 reshape.222
  311.9 3.3 convert_reduce_fusion.1
  315.2 0.1 concatenate.27
  315.3 0.1 concatenate.28
  315.4 0.1 reshape.223
  315.5 0.1 concatenate.30
  315.7 3.5 fusion.31.refs_1_
  319.2 4.0 fusion.27.refs_4_
  323.2 6.1 %fusion.34.refs_0_ = f32[768,2304]{1,0:T(8,128)} fusion(bf16[1024,2304]{1,0:T(8,128)(2,1)S(1)} %bitcast.50, bf16[1024,768]{1,0:T(8,128)(2,1)S(1)} %copy-done.3, f32[768]{0:T(1024)S(1)} %copy-done.16, f32[768]{0:T(1024)S(1)} %copy-done.14, f32[1024]{0:T(1024)S(1)} %copy-done.12, f32[1024]{0:T(1024)S(1)} %copy-done.10), kind=kOutput, calls=%fused_computation.91 | convolution fusion | flops 3628597248 | bytes 13383680 | tf_op jit(solution)/shard_map/td,te->de/dot_general | solution.py:429
  329.4 8.3 %fusion.37.refs_2_ = f32[768,3072]{1,0:T(8,128)} fusion(bf16[1024,3072]{1,0:T(8,128)(2,1)S(1)} %bitcast.53, f32[1024,768]{1,0:T(8,128)S(1)} %copy-done.1, f32[768]{0:T(1024)S(1)} %reshape.242, f32[768]{0:T(1024)S(1)} %reshape.241, f32[1024]{0:T(1024)S(1)} %add_rsqrt_fusion, f32[1024]{0:T(1024)S(1)} %broadcast_multiply_fusion.4), kind=kOutput, calls=%fused_computation.92 | convolution fusion | flops 4835770368 | bytes 18888704 | tf_op jit(solution)/shard_map/td,tf->df/dot_general | solution.py:415
  337.7 130.2 %shard_map.265 = (f32[24,2304]{1,0:T(8,128)S(1)}, f32[24,768]{1,0:T(8,128)S(1)}, f32[24,3072]{1,0:T(8,128)S(1)}, f32[8,128]{1,0:T(8,128)S(1)}) custom-call(f32[768,2304]{1,0:T(8,128)} %fusion.34.refs_0_, f32[768,768]{1,0:T(8,128)S(1)} %fusion.31.refs_1_, f32[768,3072]{1,0:T(8,128)} %fusion.37.refs_2_, f32[256,128]{1,0:T(8,128)S(1)} %reshape.228.refs_3_, ...), custom_call_target="tpu_custom_call" | custom-call | flops 4751360 | bytes 38010880 | tf_op jit(solution)/shard_map/pallas_call | solution.py:303
  467.9 0.6 slice_bitcast_fusion.1
  468.5 0.5 slice_bitcast_fusion.7
  469.0 0.6 slice_bitcast_fusion
  469.6 8.0 %add_convert_fusion.1 = bf16[1024,768]{1,0:T(8,128)(2,1)} fusion(f32[1024,768]{1,0:T(8,128)S(1)} %copy-done.1, bf16[1024,3072]{1,0:T(8,128)(2,1)} %copy-done.18, bf16[3072,768]{1,0:T(8,128)(2,1)S(1)} %bitcast.55, f32[768]{0:T(1024)S(1)} %copy-done.17), kind=kOutput, calls=%fused_computation.52 | convolution fusion | flops 4834197504 | bytes 15731712 | tf_op jit(solution)/shard_map/dot_general | solution.py:403
  477.6 0.7 copy.48
  478.3 0.6 copy.49
  478.9 0.7 copy.50
  (79 shorter events, 0.5 us)
Async XLA Ops:
  7.2 16.8 %copy-start.2 = (bf16[1024,768]{1,0:T(8,128)(2,1)S(1)}, bf16[1024,768]{1,0:T(8,128)(2,1)}, u32[]{:S(2)}) copy-start(bf16[1024,768]{1,0:T(8,128)(2,1)} %param.16) | copy-start | bytes 4718596
  7.2 78.3 %all-gather.8.cloned.1.call-start = ((), (), s32[]{:S(2)}) async-start(), calls=%async_computation.3 | async-start | bytes 6082560 | tf_op jit(solution)/shard_map/all_gather | solution.py:364
  15.2 154.9 %all-gather.6.cloned.1.call-start = ((), (), s32[]{:S(2)}) async-start(), calls=%async_computation.2 | async-start | bytes 9732096 | tf_op jit(solution)/shard_map/all_gather | solution.py:373
  17.9 459.7 %reduce-scatter.2.cloned.1.call-start = ((), (), s32[]{:S(2)}) async-start(), calls=%async_computation.1 | async-start | bytes 9732096 | tf_op jit(solution)/shard_map/reduce_scatter | solution.py:446
  24.0 67.8 %copy-start.9 = (f32[1024]{0:T(1024)}, f32[1024]{0:T(1024)S(1)}, u32[]{:S(2)}) copy-start(f32[1024]{0:T(1024)S(1)} %broadcast_multiply_fusion.5) | copy-start | bytes 12292
  24.6 67.2 %copy-start.11 = (f32[1024]{0:T(1024)}, f32[1024]{0:T(1024)S(1)}, u32[]{:S(2)}) copy-start(f32[1024]{0:T(1024)S(1)} %add_rsqrt_fusion.1) | copy-start | bytes 12292
  85.5 2.6 slice-start.6
  87.9 4.0 copy-start.13
  88.1 3.8 copy-start.15
  91.8 1.8 copy-start.5
  133.2 124.8 %copy-start = (f32[1024,768]{1,0:T(8,128)}, f32[1024,768]{1,0:T(8,128)S(1)}, u32[]{:S(2)}) copy-start(f32[1024,768]{1,0:T(8,128)S(1)} %get-tuple-element.52) | copy-start | bytes 9437188
  186.8 39.3 %copy-start.7 = (bf16[1024,768]{1,0:T(8,128)(2,1)S(1)}, bf16[1024,768]{1,0:T(8,128)(2,1)}, u32[]{:S(2)}) copy-start(bf16[1024,768]{1,0:T(8,128)(2,1)} %param.31) | copy-start | bytes 4718596
  223.5 2.6 copy-start.18
  248.3 9.7 %copy-start.8 = (bf16[1024,768]{1,0:T(8,128)(2,1)S(1)}, bf16[1024,768]{1,0:T(8,128)(2,1)}, u32[]{:S(2)}) copy-start(bf16[1024,768]{1,0:T(8,128)(2,1)} %param.31) | copy-start | bytes 4718596
  266.0 36.4 %copy-start.3 = (bf16[1024,768]{1,0:T(8,128)(2,1)S(1)}, bf16[1024,768]{1,0:T(8,128)(2,1)}, u32[]{:S(2)}) copy-start(bf16[1024,768]{1,0:T(8,128)(2,1)} %param.16) | copy-start | bytes 4718596
  266.0 36.4 %copy-start.10 = (f32[1024]{0:T(1024)S(1)}, f32[1024]{0:T(1024)}, u32[]{:S(2)}) copy-start(f32[1024]{0:T(1024)} %copy-done.9) | copy-start | bytes 12292
  266.0 36.4 %copy-start.12 = (f32[1024]{0:T(1024)S(1)}, f32[1024]{0:T(1024)}, u32[]{:S(2)}) copy-start(f32[1024]{0:T(1024)} %copy-done.11) | copy-start | bytes 12292
  266.0 36.4 %copy-start.14 = (f32[768]{0:T(1024)S(1)}, f32[768]{0:T(1024)}, u32[]{:S(2)}) copy-start(f32[768]{0:T(1024)} %copy-done.13) | copy-start | bytes 9220
  311.8 3.8 copy-start.6
  315.7 3.5 copy-start.4
  315.7 7.5 %slice-start = ((s8[4718592]{0:T(1024)(128)(4,1)}), s8[4194304]{0:T(1024)(128)(4,1)S(1)}, s32[]{:S(2)}) async-start(s8[4718592]{0:T(1024)(128)(4,1)} %bitcast.49), calls=%async_computation.4 | async-start | bytes 8388608
  319.2 4.0 slice-start.1
  319.2 4.0 copy-start.16
  319.2 10.1 %slice-start.2 = ((s8[6291456]{0:T(1024)(128)(4,1)}), s8[4194304]{0:T(1024)(128)(4,1)S(1)}, s32[]{:S(2)}) async-start(s8[6291456]{0:T(1024)(128)(4,1)} %bitcast.52), calls=%async_computation.6 | async-start | bytes 8388608
  323.2 6.1 %copy-start.1 = (f32[1024,768]{1,0:T(8,128)S(1)}, f32[1024,768]{1,0:T(8,128)}, u32[]{:S(2)}) copy-start(f32[1024,768]{1,0:T(8,128)} %copy-done) | copy-start | bytes 9437188
  323.2 6.1 %slice-start.3 = ((s8[6291456]{0:T(1024)(128)(4,1)}), s8[2097152]{0:T(1024)(128)(4,1)S(1)}, s32[]{:S(2)}) async-start(s8[6291456]{0:T(1024)(128)(4,1)} %bitcast.52), calls=%async_computation.7 | async-start | bytes 4194304
  329.4 140.3 %slice-start.4 = ((s8[4718592]{0:T(1024)(128)(4,1)}), s8[4194304]{0:T(1024)(128)(4,1)S(1)}, s32[]{:S(2)}) async-start(s8[4718592]{0:T(1024)(128)(4,1)} %bitcast.54), calls=%async_computation.8 | async-start | bytes 8388608
  337.7 131.9 %slice-start.5 = ((s8[4718592]{0:T(1024)(128)(4,1)}), s8[524288]{0:T(1024)(128)(4,1)S(1)}, s32[]{:S(2)}) async-start(s8[4718592]{0:T(1024)(128)(4,1)} %bitcast.54), calls=%async_computation.9 | async-start | bytes 1048576
  337.7 131.9 %copy-start.17 = (f32[768]{0:T(1024)S(1)}, f32[768]{0:T(1024)}, u32[]{:S(2)}) copy-start(f32[768]{0:T(1024)} %reshape.244) | copy-start | bytes 9220
Sparse Core Ops, SparseCore 0:
  15.3 70.1 all-gather.7
  89.0 81.0 all-gather.5
  233.9 135.2 reduce-scatter.1

commit v7 on v4

--- a/solution.py
+++ b/solution.py
@@ -31,9 +31,13 @@
     return jnp.sum(rows.astype(jnp.float32), axis=0)
 
 
-def seg_mask(seg_col, seg_row, val_row, n):
-    rows = lax.broadcasted_iota(jnp.int32, (n, n), 0)
-    cols = lax.broadcasted_iota(jnp.int32, (n, n), 1)
+Q_TILE = 64
+K_WIN = 256
+
+
+def seg_mask(seg_col, seg_row, val_row, q0, k0):
+    rows = q0 + lax.broadcasted_iota(jnp.int32, (seg_col.shape[0], seg_row.shape[1]), 0)
+    cols = k0 + lax.broadcasted_iota(jnp.int32, (seg_col.shape[0], seg_row.shape[1]), 1)
     return (seg_col == seg_row) & ((val_row == 1) | (rows == cols))
 
 
@@ -45,44 +49,61 @@
     return expo * (1.0 / jnp.sum(expo, axis=-1, keepdims=True))
 
 
+def windows(n):
+    win = min(K_WIN, n)
+    out = []
+    for q0 in range(0, n, Q_TILE):
+        k0 = min(max(q0 - (win - Q_TILE) // 2, 0), n - win)
+        out.append((q0, k0, win))
+    return out
+
+
 def attn_fwd_kernel(q_ref, k_ref, v_ref, sc_ref, sr_ref, vr_ref, o_ref):
     n = q_ref.shape[0]
-    allowed = seg_mask(sc_ref[...], sr_ref[...], vr_ref[...], n)
-    outs = []
-    for j in range(q_ref.shape[1] // HD):
-        cols = slice(j * HD, (j + 1) * HD)
-        probs = soft_rows(q_ref[:, cols], k_ref[:, cols], allowed).astype(jnp.bfloat16)
-        outs.append(jnp.dot(probs, v_ref[:, cols], preferred_element_type=jnp.float32))
-    o_ref[...] = jnp.concatenate(outs, axis=1).astype(o_ref.dtype)
-
-
-def attn_bwd_kernel(q_ref, k_ref, v_ref, do_ref, sc_ref, sr_ref, vr_ref, dqkv_ref):
+    for q0, k0, win in windows(n):
+        qs, ks = slice(q0, q0 + Q_TILE), slice(k0, k0 + win)
+        allowed = seg_mask(sc_ref[qs, :], sr_ref[:, ks], vr_ref[:, ks], q0, k0)
+        outs = []
+        for j in range(q_ref.shape[1] // HD):
+            cols = slice(j * HD, (j + 1) * HD)
+            probs = soft_rows(q_ref[qs, cols], k_ref[ks, cols], allowed).astype(jnp.bfloat16)
+            outs.append(jnp.dot(probs, v_ref[ks, cols], preferred_element_type=jnp.float32))
+        o_ref[qs, :] = jnp.concatenate(outs, axis=1).astype(o_ref.dtype)
+
+
+def attn_bwd_kernel(q_ref, k_ref, v_ref, do_ref, sc_ref, sr_ref, vr_ref, dqkv_ref, dk_acc, dv_acc):
     n = q_ref.shape[0]
     width = q_ref.shape[1]
     hp = pl.program_id(1)
     model_width = dqkv_ref.shape[1] // 3
-    allowed = seg_mask(sc_ref[...], sr_ref[...], vr_ref[...], n)
-    dqs, dks, dvs = [], [], []
-    for j in range(width // HD):
-        cols = slice(j * HD, (j + 1) * HD)
-        qh, kh, vh, doh = q_ref[:, cols], k_ref[:, cols], v_ref[:, cols], do_ref[:, cols]
-        probs = soft_rows(qh, kh, allowed)
-        dvs.append(
-            lax.dot_general(probs.astype(jnp.bfloat16), doh, (((0,), (0,)), ((), ())),
-                            preferred_element_type=jnp.float32)
-        )
-        dprobs = lax.dot_general(doh, vh, (((1,), (1,)), ((), ())), preferred_element_type=jnp.float32)
-        row_term = jnp.sum(probs * dprobs, axis=-1, keepdims=True)
-        dscore = jnp.where(allowed, probs * (dprobs - row_term), 0.0).astype(jnp.bfloat16)
-        dqs.append(jnp.dot(dscore, kh, preferred_element_type=jnp.float32) * (1.0 / HD**0.5))
-        dks.append(
-            lax.dot_general(dscore, qh, (((0,), (0,)), ((), ())), preferred_element_type=jnp.float32)
-            * (1.0 / HD**0.5)
-        )
+    dk_acc[...] = jnp.zeros_like(dk_acc)
+    dv_acc[...] = jnp.zeros_like(dv_acc)
     at = pl.multiple_of(hp * width, width)
-    dqkv_ref[:, pl.ds(at, width)] = jnp.concatenate(dqs, axis=1).astype(dqkv_ref.dtype)
-    dqkv_ref[:, pl.ds(at + model_width, width)] = jnp.concatenate(dks, axis=1).astype(dqkv_ref.dtype)
-    dqkv_ref[:, pl.ds(at + 2 * model_width, width)] = jnp.concatenate(dvs, axis=1).astype(dqkv_ref.dtype)
+    for q0, k0, win in windows(n):
+        qs, ks = slice(q0, q0 + Q_TILE), slice(k0, k0 + win)
+        allowed = seg_mask(sc_ref[qs, :], sr_ref[:, ks], vr_ref[:, ks], q0, k0)
+        dqs, dks, dvs = [], [], []
+        for j in range(width // HD):
+            cols = slice(j * HD, (j + 1) * HD)
+            qh, kh, vh, doh = q_ref[qs, cols], k_ref[ks, cols], v_ref[ks, cols], do_ref[qs, cols]
+            probs = soft_rows(qh, kh, allowed)
+            dvs.append(
+                lax.dot_general(probs.astype(jnp.bfloat16), doh, (((0,), (0,)), ((), ())),
+                                preferred_element_type=jnp.float32)
+            )
+            dprobs = lax.dot_general(doh, vh, (((1,), (1,)), ((), ())), preferred_element_type=jnp.float32)
+            row_term = jnp.sum(probs * dprobs, axis=-1, keepdims=True)
+            dscore = jnp.where(allowed, probs * (dprobs - row_term), 0.0).astype(jnp.bfloat16)
+            dqs.append(jnp.dot(dscore, kh, preferred_element_type=jnp.float32) * (1.0 / HD**0.5))
+            dks.append(
+                lax.dot_general(dscore, qh, (((0,), (0,)), ((), ())), preferred_element_type=jnp.float32)
+                * (1.0 / HD**0.5)
+            )
+        dqkv_ref[qs, pl.ds(at, width)] = jnp.concatenate(dqs, axis=1).astype(dqkv_ref.dtype)
+        dk_acc[ks, :] += jnp.concatenate(dks, axis=1)
+        dv_acc[ks, :] += jnp.concatenate(dvs, axis=1)
+    dqkv_ref[:, pl.ds(at + model_width, width)] = dk_acc[...].astype(dqkv_ref.dtype)
+    dqkv_ref[:, pl.ds(at + 2 * model_width, width)] = dv_acc[...].astype(dqkv_ref.dtype)
 
 
 def mask_operands(segment_ids, valid):
@@ -146,6 +167,7 @@
         ]
         + seg_spec,
         out_specs=pl.BlockSpec((seq_len, width3), lambda s, h: (s, 0)),
+        scratch_shapes=[pltpu.VMEM((seq_len, blk), jnp.float32), pltpu.VMEM((seq_len, blk), jnp.float32)],
         cost_estimate=pl.CostEstimate(
             flops=flops,
             transcendentals=n_seq * seq_len * seq_len * (model_width // HD),

time: 492 us -> 615 us (1.25)
  Pallas kernels: 196 us -> 346 us
  waiting for transfers between devices: 85 us -> 58.1 us
    pallas_call x1, Pallas kernels: 36.3 us -> 134 us  [attention_bwd(): pl.pallas_call(attn_bwd_kernel, out_shape=jax.ShapeDtypeStruct((rows, wid...]
    pallas_call x1, Pallas kernels: 29.8 us -> 89.8 us  [attention_fwd(): pl.pallas_call(attn_fwd_kernel, out_shape=jax.ShapeDtypeStruct((rows, mod...]
    all_gather x1, waiting for transfers between devices: 26.9 us -> 0.02 us  [on_device(): mlp_all = lax.all_gather(mlp_buf, ALL, axis=0, tiled=False)]
    pallas_call x1, Pallas kernels: 130 us -> 122 us  [ring_reduce_scatter(): pl.pallas_call(kernel, out_shape=out_shape, in_specs=[pl.BlockSpec(memory...]
  transfers between devices with their start and end apart: 3 -> 3, of which waited for: 2 -> 1; matrix products, arithmetic and copies ran while one was open for 24% -> 19% of each run, Pallas kernels for 41% -> 57%
where the time goes in v7:
time: 615 us; the launch traced here: 607 us
  Pallas kernels  346 us (56%)
  matrix products  121 us (20%)
  waiting for transfers between devices  58.1 us (9%)
  local copies, waits for them, and re-layouts  51.3 us (8%)
  other arithmetic  15.8 us (3%)
  between operations  14.7 us (2%)
    pallas_call x1, Pallas kernels, attention_bwd(): pl.pallas_call(attn_bwd_kernel, out_shape=jax.ShapeDtypeStruct((rows, wid...  134 us
    pallas_call x1, Pallas kernels, ring_reduce_scatter(): pl.pallas_call(kernel, out_shape=out_shape, in_specs=[pl.BlockSpec(memory...  122 us
    pallas_call x1, Pallas kernels, attention_fwd(): pl.pallas_call(attn_fwd_kernel, out_shape=jax.ShapeDtypeStruct((rows, mod...  89.8 us
    all_gather x1, waiting for transfers between devices, on_device(): attn_all = lax.all_gather(attn_buf, ALL, axis=0, tiled=False)  58.1 us
    dot_general x1, matrix products, on_device(): jnp.dot(h_two, up_full, preferred_element_type=jnp.float32)  36.9 us
    dot_general x1, matrix products, on_device(): jnp.einsum('td,fd->tf', cotangent, down_full, preferred_element_type=jnp....  14.4 us
  transfers between devices with their start and end apart: 3, of which 1 were waited for; matrix products, arithmetic and copies ran while one was open for 19% of the time, Pallas kernels for 57%

profile of v7, /device:TPU:1, one launch (start us, length us, event | category | flops | bytes accessed | tf_op | source)
XLA Modules:
  0.0 606.9 jit_solution(4740781186251196087)
XLA Ops:
  7.2 5.5 concatenate.23
  12.8 1.0 reshape.215
  13.8 1.4 maximum_bitcast_fusion
  15.3 1.0 reshape.218
  16.3 1.6 pad_maximum_fusion
  18.0 1.3 broadcast_in_dim.14.vr_ref
  19.3 1.3 broadcast_in_dim.13.sr_ref
  20.6 1.7 copy.38.sc_ref
  22.3 1.7 convert_reduce_fusion.2
  24.0 0.6 fusion.29
  24.7 58.1 %all-gather.8.cloned.1.call-done = bf16[32,97,768]{2,1,0:T(8,128)(2,1)} async-done(((bf16[1,97,768]{2,1,0:T(8,128)(2,1)}), bf16[32,97,768]{2,1,0:T(8,128)(2,1)}) %all-gather.8.cloned.1.call-update) | async-done | bytes 4767760 | tf_op jit(solution)/shard_map/all_gather | solution.py:385
  82.7 1.0 slice.122
  83.7 0.1 slice.101
  83.8 0.1 slice.103
  83.9 0.1 slice_convert_fusion.1
  83.9 0.1 reshape.243
  84.0 0.1 slice_convert_fusion
  84.1 0.7 reshape.244
  84.8 0.1 reshape.241
  84.9 0.1 reshape.238
  85.0 0.1 reshape.242
  85.0 0.1 reshape.239
  85.1 0.1 reshape.240
  85.2 4.0 slice.125
  89.2 6.6 %reshape.216 = bf16[768,2304]{1,0:T(8,128)(2,1)} reshape(bf16[32,72,768]{2,1,0:T(8,128)(2,1)} %slice.125) | data formatting | bytes 7077888 | tf_op jit(solution)/shard_map/reshape | solution.py:386
  95.8 2.3 slice.129
  98.2 8.0 %add_convert_fusion.q_ref.k_ref.v_ref = bf16[1024,2304]{1,0:T(8,128)(2,1)} fusion(bf16[768,2304]{1,0:T(8,128)(2,1)} %reshape.216, f32[2304]{0:T(1024)S(1)} %pad_maximum_fusion.2, bf16[1024,768]{1,0:T(8,128)(2,1)S(1)} %copy-done.2, f32[768]{0:T(1024)S(1)} %reshape.239, f32[768]{0:T(1024)S(1)} %reshape.238, f32[1024]{0:T(1024)S(1)} %add_rsqrt_fusion.1, ...), kind=kOutput, calls=%fused_computation.28 | convolution fusion | flops 3633315840 | bytes 9853952 | tf_op jit(solution)/shard_map/dot_general | solution.py:402
  106.1 89.8 %shard_map.263 = bf16[1024,768]{1,0:T(8,128)(2,1)} custom-call(bf16[1024,2304]{1,0:T(8,128)(2,1)} %add_convert_fusion.q_ref.k_ref.v_ref, bf16[1024,2304]{1,0:T(8,128)(2,1)} %add_convert_fusion.q_ref.k_ref.v_ref, bf16[1024,2304]{1,0:T(8,128)(2,1)} %add_convert_fusion.q_ref.k_ref.v_ref, s32[2,512,1]{2,1,0:T(8,128)} %copy.38.sc_ref, ...), custom_call_target="tpu_custom_call" | custom-call | flops 1610612736 | bytes 6291456 | tf_op jit(solution)/shard_map/pallas_call | solution.py:126
  195.9 3.8 fusion.42
  199.7 0.5 multiply_reduce_fusion.2
  200.2 8.5 %fusion.39 = (bf16[32,96,768]{2,1,0:T(8,128)(2,1)}, bf16[32,96,768]{2,1,0:T(8,128)(2,1)}) fusion(bf16[32,192,768]{2,1,0:T(8,128)(2,1)} %bitcast.51), kind=kLoop, calls=%fused_computation.94 | loop fusion | bytes 18874368 | tf_op jit(solution)/shard_map/slice | solution.py:394
  208.7 8.5 %reshape.219 = bf16[768,3072]{1,0:T(8,128)(2,1)} reshape(bf16[32,96,768]{2,1,0:T(8,128)(2,1)} %get-tuple-element.33) | data formatting | bytes 9437184 | tf_op jit(solution)/shard_map/reshape | solution.py:393
  217.2 36.9 %fusion.2 = (bf16[1024,3072]{1,0:T(8,128)(2,1)S(1)}, f32[1024,3072]{1,0:T(8,128)}) fusion(f32[3072]{0:T(1024)S(1)} %reshape.243, bf16[768,3072]{1,0:T(8,128)(2,1)} %reshape.219, f32[1024,768]{1,0:T(8,128)S(1)} %get-tuple-element.52, f32[768]{0:T(1024)S(1)} %reshape.242, f32[768]{0:T(1024)S(1)} %reshape.241, f32[1024]{0:T(1024)S(1)} %add_rsqrt_fusion, ...), kind=kOutput, calls=%fused_computation.4 | convolution fusion | flops 5043388416 | bytes 26765312 | tf_op jit(solution)/shard_map/dot_general | solution.py:416
  254.1 2.6 copy-done.17
  256.8 7.6 %fusion.43 = f32[3072,768]{1,0:T(8,128)} fusion(bf16[1024,3072]{1,0:T(8,128)(2,1)S(1)} %get-tuple-element.53, bf16[1024,768]{1,0:T(8,128)(2,1)S(1)} %copy-done.6), kind=kOutput, calls=%fused_computation.98 | convolution fusion | flops 4831838208 | bytes 17301504 | tf_op jit(solution)/shard_map/tf,td->fd/dot_general | solution.py:427
  264.3 14.4 %convert_reduce_fusion = (f32[3072]{0:T(1024)S(1)}, bf16[1024,3072]{1,0:T(8,128)(2,1)}) fusion(f32[1024,3072]{1,0:T(8,128)} %get-tuple-element.54, f32[3072]{0:T(1024)S(1)} %reshape.243, bf16[3072,768]{1,0:T(8,128)(2,1)} %bitcast.54, bf16[1024,768]{1,0:T(8,128)(2,1)} %param.31), kind=kOutput, calls=%fused_computation.11 | convolution fusion | flops 4872729600 | bytes 25190400 | tf_op jit(solution)/shard_map/td,fd->tf/dot_general | solution.py:429
  278.7 0.1 reshape.226
  278.8 9.7 %multiply_reduce_fusion = (f32[768]{0:T(1024)S(1)}, f32[1024]{0:T(1024)S(1)}, f32[1024]{0:T(1024)S(1)}, f32[768]{0:T(1024)S(1)}, f32[1024,768]{1,0:T(8,128)S(1)}) fusion(f32[1024,768]{1,0:T(8,128)S(1)} %get-tuple-element.52, f32[1024]{0:T(1024)S(1)} %add_rsqrt_fusion, f32[1024]{0:T(1024)S(1)} %broadcast_multiply_fusion.4, f32[768]{0:T(1024)S(1)} %reshape.241, ...), kind=kOutput, calls=%fused_computation.49 | convolution fusion | flops 4838912000 | bytes 17327104 | tf_op jit(solution)/shard_map/tf,df->td/dot_general | solution.py:435
  288.5 2.6 convert_reduce_fusion.4
  291.2 0.1 reshape.221
  291.2 0.1 reshape.224
  291.3 0.1 reshape.227
  291.4 0.1 reshape.225
  291.5 5.0 convolution_convert_fusion.do_ref
  296.5 134.1 %shard_map.264 = bf16[1024,2304]{1,0:T(8,128)(2,1)} custom-call(bf16[1024,2304]{1,0:T(8,128)(2,1)} %add_convert_fusion.q_ref.k_ref.v_ref, bf16[1024,2304]{1,0:T(8,128)(2,1)} %add_convert_fusion.q_ref.k_ref.v_ref, bf16[1024,2304]{1,0:T(8,128)(2,1)} %add_convert_fusion.q_ref.k_ref.v_ref, bf16[1024,768]{1,0:T(8,128)(2,1)} %convolution_convert_fusion.do_ref, ...), custom_call_target="tpu_custom_call" | custom-call | flops 4026531840 | bytes 11010048 | tf_op jit(solution)/shard_map/pallas_call | solution.py:158
  430.7 9.3 %fusion.28 = (f32[768]{0:T(1024)S(1)}, f32[1024]{0:T(1024)S(1)}, f32[1024]{0:T(1024)S(1)}, f32[768]{0:T(1024)S(1)}, f32[1024,768]{1,0:T(8,128)}) fusion(bf16[1024,768]{1,0:T(8,128)(2,1)S(1)} %copy-done.3, f32[1024]{0:T(1024)S(1)} %copy-done.11, f32[1024]{0:T(1024)S(1)} %copy-done.9, f32[768]{0:T(1024)S(1)} %copy-done.13, ...), kind=kOutput, calls=%fused_computation.46 | convolution fusion | flops 3631739392 | bytes 13001728 | tf_op jit(solution)/shard_map/te,de->td/dot_general | solution.py:449
  440.0 0.1 reshape.222
  440.1 3.1 convert_reduce_fusion.1
  443.2 0.1 concatenate.27
  443.3 0.1 concatenate.28
  443.4 0.1 reshape.223
  443.5 0.1 concatenate.30
  443.7 3.5 fusion.31.refs_1_
  447.2 3.9 fusion.27.refs_4_
  451.2 6.4 %fusion.34.refs_0_ = f32[768,2304]{1,0:T(8,128)} fusion(bf16[1024,2304]{1,0:T(8,128)(2,1)S(1)} %bitcast.50, bf16[1024,768]{1,0:T(8,128)(2,1)S(1)} %copy-done.3, f32[768]{0:T(1024)S(1)} %copy-done.15, f32[768]{0:T(1024)S(1)} %copy-done.13, f32[1024]{0:T(1024)S(1)} %copy-done.11, f32[1024]{0:T(1024)S(1)} %copy-done.9), kind=kOutput, calls=%fused_computation.91 | convolution fusion | flops 3628597248 | bytes 13383680 | tf_op jit(solution)/shard_map/td,te->de/dot_general | solution.py:448
  457.6 8.3 %fusion.37.refs_2_ = f32[768,3072]{1,0:T(8,128)} fusion(bf16[1024,3072]{1,0:T(8,128)(2,1)S(1)} %bitcast.53, f32[1024,768]{1,0:T(8,128)S(1)} %copy-done.1, f32[768]{0:T(1024)S(1)} %reshape.242, f32[768]{0:T(1024)S(1)} %reshape.241, f32[1024]{0:T(1024)S(1)} %add_rsqrt_fusion, f32[1024]{0:T(1024)S(1)} %broadcast_multiply_fusion.4), kind=kOutput, calls=%fused_computation.92 | convolution fusion | flops 4835770368 | bytes 18888704 | tf_op jit(solution)/shard_map/td,tf->df/dot_general | solution.py:434
  465.9 122.3 %shard_map.265 = (f32[24,2304]{1,0:T(8,128)S(1)}, f32[24,768]{1,0:T(8,128)S(1)}, f32[24,3072]{1,0:T(8,128)S(1)}, f32[8,128]{1,0:T(8,128)S(1)}) custom-call(f32[768,2304]{1,0:T(8,128)} %fusion.34.refs_0_, f32[768,768]{1,0:T(8,128)S(1)} %fusion.31.refs_1_, f32[768,3072]{1,0:T(8,128)} %fusion.37.refs_2_, f32[256,128]{1,0:T(8,128)S(1)} %reshape.228.refs_3_, ...), custom_call_target="tpu_custom_call" | custom-call | flops 4751360 | bytes 38010880 | tf_op jit(solution)/shard_map/pallas_call | solution.py:325
  588.2 0.6 slice_bitcast_fusion.1
  588.8 0.5 slice_bitcast_fusion.7
  589.3 0.6 slice_bitcast_fusion
  589.9 8.0 %add_convert_fusion.1 = bf16[1024,768]{1,0:T(8,128)(2,1)} fusion(f32[1024,768]{1,0:T(8,128)S(1)} %copy-done.1, bf16[1024,3072]{1,0:T(8,128)(2,1)} %copy-done.17, bf16[3072,768]{1,0:T(8,128)(2,1)S(1)} %bitcast.57, f32[768]{0:T(1024)S(1)} %copy-done.16), kind=kOutput, calls=%fused_computation.52 | convolution fusion | flops 4834197504 | bytes 15731712 | tf_op jit(solution)/shard_map/dot_general | solution.py:422
  597.9 0.7 copy.48
  598.6 0.6 copy.49
  599.3 0.7 copy.50
  (76 shorter events, 0.4 us)
Async XLA Ops:
  7.2 16.8 %copy-start.2 = (bf16[1024,768]{1,0:T(8,128)(2,1)S(1)}, bf16[1024,768]{1,0:T(8,128)(2,1)}, u32[]{:S(2)}) copy-start(bf16[1024,768]{1,0:T(8,128)(2,1)} %param.16) | copy-start | bytes 4718596
  7.2 75.5 %all-gather.8.cloned.1.call-start = ((), (), s32[]{:S(2)}) async-start(), calls=%async_computation.3 | async-start | bytes 5271552 | tf_op jit(solution)/shard_map/all_gather | solution.py:385
  15.2 185.0 %all-gather.6.cloned.1.call-start = ((), (), s32[]{:S(2)}) async-start(), calls=%async_computation.2 | async-start | bytes 9732096 | tf_op jit(solution)/shard_map/all_gather | solution.py:392
  18.0 580.0 %reduce-scatter.2.cloned.1.call-start = ((), (), s32[]{:S(2)}) async-start(), calls=%async_computation.1 | async-start | bytes 9732096 | tf_op jit(solution)/shard_map/reduce_scatter | solution.py:465
  24.0 74.1 %copy-start.8 = (f32[1024]{0:T(1024)}, f32[1024]{0:T(1024)S(1)}, u32[]{:S(2)}) copy-start(f32[1024]{0:T(1024)S(1)} %broadcast_multiply_fusion.5) | copy-start | bytes 12292
  24.7 73.5 %copy-start.10 = (f32[1024]{0:T(1024)}, f32[1024]{0:T(1024)S(1)}, u32[]{:S(2)}) copy-start(f32[1024]{0:T(1024)S(1)} %add_rsqrt_fusion.1) | copy-start | bytes 12292
  85.0 13.2 %copy-start.12 = (f32[768]{0:T(1024)}, f32[768]{0:T(1024)S(1)}, u32[]{:S(2)}) copy-start(f32[768]{0:T(1024)S(1)} %reshape.238) | copy-start | bytes 9220
  85.1 13.1 %copy-start.14 = (f32[768]{0:T(1024)}, f32[768]{0:T(1024)S(1)}, u32[]{:S(2)}) copy-start(f32[768]{0:T(1024)S(1)} %reshape.239) | copy-start | bytes 9220
  199.7 88.9 %copy-start = (f32[1024,768]{1,0:T(8,128)}, f32[1024,768]{1,0:T(8,128)S(1)}, u32[]{:S(2)}) copy-start(f32[1024,768]{1,0:T(8,128)S(1)} %get-tuple-element.52) | copy-start | bytes 9437188
  217.2 39.6 %copy-start.6 = (bf16[1024,768]{1,0:T(8,128)(2,1)S(1)}, bf16[1024,768]{1,0:T(8,128)(2,1)}, u32[]{:S(2)}) copy-start(bf16[1024,768]{1,0:T(8,128)(2,1)} %param.31) | copy-start | bytes 4718596
  254.1 2.7 copy-start.17
  278.8 9.7 %copy-start.7 = (bf16[1024,768]{1,0:T(8,128)(2,1)S(1)}, bf16[1024,768]{1,0:T(8,128)(2,1)}, u32[]{:S(2)}) copy-start(bf16[1024,768]{1,0:T(8,128)(2,1)} %param.31) | copy-start | bytes 4718596
  296.5 134.1 %copy-start.3 = (bf16[1024,768]{1,0:T(8,128)(2,1)S(1)}, bf16[1024,768]{1,0:T(8,128)(2,1)}, u32[]{:S(2)}) copy-start(bf16[1024,768]{1,0:T(8,128)(2,1)} %param.16) | copy-start | bytes 4718596
  296.5 134.1 %copy-start.9 = (f32[1024]{0:T(1024)S(1)}, f32[1024]{0:T(1024)}, u32[]{:S(2)}) copy-start(f32[1024]{0:T(1024)} %copy-done.8) | copy-start | bytes 12292
  296.5 134.1 %copy-start.11 = (f32[1024]{0:T(1024)S(1)}, f32[1024]{0:T(1024)}, u32[]{:S(2)}) copy-start(f32[1024]{0:T(1024)} %copy-done.10) | copy-start | bytes 12292
  296.5 134.1 %copy-start.13 = (f32[768]{0:T(1024)S(1)}, f32[768]{0:T(1024)}, u32[]{:S(2)}) copy-start(f32[768]{0:T(1024)} %copy-done.12) | copy-start | bytes 9220
  440.0 3.7 copy-start.5
  443.7 3.5 copy-start.4
  443.7 7.5 %slice-start = ((s8[4718592]{0:T(1024)(128)(4,1)}), s8[4194304]{0:T(1024)(128)(4,1)S(1)}, s32[]{:S(2)}) async-start(s8[4718592]{0:T(1024)(128)(4,1)} %bitcast.49), calls=%async_computation.4 | async-start | bytes 8388608
  447.2 4.0 slice-start.1
  447.2 4.0 copy-start.15
  447.2 10.3 %slice-start.2 = ((s8[6291456]{0:T(1024)(128)(4,1)}), s8[4194304]{0:T(1024)(128)(4,1)S(1)}, s32[]{:S(2)}) async-start(s8[6291456]{0:T(1024)(128)(4,1)} %bitcast.52), calls=%async_computation.6 | async-start | bytes 8388608
  451.2 6.4 %copy-start.1 = (f32[1024,768]{1,0:T(8,128)S(1)}, f32[1024,768]{1,0:T(8,128)}, u32[]{:S(2)}) copy-start(f32[1024,768]{1,0:T(8,128)} %copy-done) | copy-start | bytes 9437188
  451.2 6.4 %slice-start.3 = ((s8[6291456]{0:T(1024)(128)(4,1)}), s8[2097152]{0:T(1024)(128)(4,1)S(1)}, s32[]{:S(2)}) async-start(s8[6291456]{0:T(1024)(128)(4,1)} %bitcast.52), calls=%async_computation.7 | async-start | bytes 4194304
  457.6 132.4 %slice-start.4 = ((s8[4718592]{0:T(1024)(128)(4,1)}), s8[4194304]{0:T(1024)(128)(4,1)S(1)}, s32[]{:S(2)}) async-start(s8[4718592]{0:T(1024)(128)(4,1)} %bitcast.55), calls=%async_computation.8 | async-start | bytes 8388608
  465.9 124.0 %slice-start.5 = ((s8[4718592]{0:T(1024)(128)(4,1)}), s8[524288]{0:T(1024)(128)(4,1)S(1)}, s32[]{:S(2)}) async-start(s8[4718592]{0:T(1024)(128)(4,1)} %bitcast.55), calls=%async_computation.9 | async-start | bytes 1048576
  465.9 124.0 %copy-start.16 = (f32[768]{0:T(1024)S(1)}, f32[768]{0:T(1024)}, u32[]{:S(2)}) copy-start(f32[768]{0:T(1024)} %reshape.244) | copy-start | bytes 9220
Sparse Core Ops, SparseCore 0:
  15.3 67.3 all-gather.7
  86.2 81.3 all-gather.5
  264.5 132.4 reduce-scatter.1

commit v8 on v4

--- a/solution.py
+++ b/solution.py
@@ -442,7 +442,7 @@
     ]
     down_sum = lax.psum_scatter(grad_wdown, ALL, scatter_dimension=0, tiled=True)
     if all(rb % 8 == 0 and a.shape[1] % 256 == 0 for (a, rb, _) in parts[:3]):
-        sums = ring_reduce_scatter(parts, mesh_shape, after=(grad_inputs,))
+        sums = ring_reduce_scatter(parts, mesh_shape, after=(grad_inputs, block_out))
     else:
         sums = [lax.psum_scatter(a, ALL, scatter_dimension=0, tiled=True) for (a, _, _) in parts]
     sums = list(sums[:3]) + [down_sum] + list(sums[3:])

time: 492 us -> 490 us (level)
  transfers between devices with their start and end apart: 3 -> 3, of which waited for: 2 -> 2; matrix products, arithmetic and copies ran while one was open for 24% -> 24% of each run, Pallas kernels for 41% -> 40%
where the time goes in v8:
time: 490 us; the launch traced here: 482 us
  Pallas kernels  194 us (40%)
  matrix products  120 us (24%)
  waiting for transfers between devices  85 us (17%)
  local copies, waits for them, and re-layouts  50.9 us (10%)
  other arithmetic  16.7 us (3%)
  between operations  14.8 us (3%)
    pallas_call x1, Pallas kernels, ring_reduce_scatter(): pl.pallas_call(kernel, out_shape=out_shape, in_specs=[pl.BlockSpec(memory...  128 us
    all_gather x1, waiting for transfers between devices, on_device(): attn_all = lax.all_gather(attn_buf, ALL, axis=0, tiled=False)  58.1 us
    dot_general x1, matrix products, on_device(): jnp.dot(h_two, up_full, preferred_element_type=jnp.float32)  36.7 us
    pallas_call x1, Pallas kernels, attention_bwd(): pl.pallas_call(attn_bwd_kernel, out_shape=jax.ShapeDtypeStruct((rows, wid...  36.4 us
    pallas_call x1, Pallas kernels, attention_fwd(): pl.pallas_call(attn_fwd_kernel, out_shape=jax.ShapeDtypeStruct((rows, mod...  29.8 us
    all_gather x1, waiting for transfers between devices, on_device(): mlp_all = lax.all_gather(mlp_buf, ALL, axis=0, tiled=False)  26.9 us
    dot_general x1, matrix products, on_device(): jnp.einsum('td,fd->tf', cotangent, down_full, preferred_element_type=jnp....  14.5 us
  transfers between devices with their start and end apart: 3, of which 2 were waited for; matrix products, arithmetic and copies ran while one was open for 24% of the time, Pallas kernels for 40%

profile of v8, /device:TPU:1, one launch (start us, length us, event | category | flops | bytes accessed | tf_op | source)
XLA Modules:
  0.0 482.1 jit_solution(1023291935316433332)
XLA Ops:
  7.2 5.5 %concatenate.23 = bf16[288]{0:T(512)(128)(2,1)S(1)} concatenate(bf16[48]{0:T(256)(128)(2,1)} %param.18, bf16[24]{0:T(256)(128)(2,1)} %param.20, bf16[24]{0:T(256)(128)(2,1)} %param.21, bf16[24]{0:T(256)(128)(2,1)} %param.22, bf16[24]{0:T(256)(128)(2,1)} %param.23, bf16[24]{0:T(256)(128)(2,1)} %param.24, bf16[96]{0:T(256)(128)(2,1)} %param.26, bf16[24]{0:T(256)(128)(2,1)} %param.28), dimensions={0} | concatenate | bytes 1152 | tf_op jit(solution)/shard_map/concatenate | solution.py:317
  12.8 1.0 reshape.215
  13.8 1.4 maximum_bitcast_fusion
  15.3 1.0 reshape.218
  16.3 1.6 pad_maximum_fusion
  18.0 1.3 broadcast_in_dim.14.vr_ref
  19.3 1.3 broadcast_in_dim.13.sr_ref
  20.6 1.7 copy.38.sc_ref
  22.3 1.7 convert_reduce_fusion.2
  24.0 0.6 fusion.29
  24.6 58.1 %all-gather.8.cloned.1.call-done = bf16[32,97,768]{2,1,0:T(8,128)(2,1)} async-done(((bf16[1,97,768]{2,1,0:T(8,128)(2,1)}), bf16[32,97,768]{2,1,0:T(8,128)(2,1)}) %all-gather.8.cloned.1.call-update) | async-done | bytes 4767760 | tf_op jit(solution)/shard_map/all_gather | solution.py:363
  82.7 1.0 slice.122
  83.7 0.1 slice.101
  83.8 0.1 slice.103
  83.9 0.1 slice_convert_fusion.1
  83.9 0.1 reshape.243
  84.0 0.1 slice_convert_fusion
  84.1 0.7 reshape.244
  84.8 0.1 reshape.241
  84.9 0.1 reshape.238
  85.0 0.1 reshape.242
  85.0 0.1 reshape.239
  85.1 0.1 reshape.240
  85.2 4.0 slice.125
  89.2 6.6 %reshape.216 = bf16[768,2304]{1,0:T(8,128)(2,1)} reshape(bf16[32,72,768]{2,1,0:T(8,128)(2,1)} %slice.125) | data formatting | bytes 7077888 | tf_op jit(solution)/shard_map/reshape | solution.py:364
  95.8 2.3 slice.129
  98.2 7.9 %add_convert_fusion.q_ref.k_ref.v_ref = bf16[1024,2304]{1,0:T(8,128)(2,1)} fusion(bf16[768,2304]{1,0:T(8,128)(2,1)} %reshape.216, f32[2304]{0:T(1024)S(1)} %pad_maximum_fusion.2, bf16[1024,768]{1,0:T(8,128)(2,1)S(1)} %copy-done.3, f32[768]{0:T(1024)S(1)} %reshape.239, f32[768]{0:T(1024)S(1)} %reshape.238, f32[1024]{0:T(1024)S(1)} %add_rsqrt_fusion.1, ...), kind=kOutput, calls=%fused_computation.28 | convolution fusion | flops 3633315840 | bytes 9853952 | tf_op jit(solution)/shard_map/dot_general | solution.py:380
  106.2 29.8 %shard_map.263 = bf16[1024,768]{1,0:T(8,128)(2,1)} custom-call(bf16[1024,2304]{1,0:T(8,128)(2,1)} %add_convert_fusion.q_ref.k_ref.v_ref, bf16[1024,2304]{1,0:T(8,128)(2,1)} %add_convert_fusion.q_ref.k_ref.v_ref, bf16[1024,2304]{1,0:T(8,128)(2,1)} %add_convert_fusion.q_ref.k_ref.v_ref, s32[2,512,1]{2,1,0:T(8,128)} %copy.38.sc_ref, ...), custom_call_target="tpu_custom_call" | custom-call | flops 1610612736 | bytes 6291456 | tf_op jit(solution)/shard_map/pallas_call | solution.py:105
  136.0 3.8 fusion.42
  139.8 0.5 multiply_reduce_fusion.2
  140.3 26.9 %all-gather.6.cloned.1.call-done = bf16[6144,768]{1,0:T(8,128)(2,1)} async-done(((bf16[192,768]{1,0:T(8,128)(2,1)}), bf16[6144,768]{1,0:T(8,128)(2,1)}) %all-gather.6.cloned.1.call-update) | async-done | bytes 9437200 | tf_op jit(solution)/shard_map/all_gather | solution.py:370
  167.2 8.0 %fusion.39 = (bf16[32,96,768]{2,1,0:T(8,128)(2,1)}, bf16[32,96,768]{2,1,0:T(8,128)(2,1)}) fusion(bf16[32,192,768]{2,1,0:T(8,128)(2,1)} %bitcast.51), kind=kLoop, calls=%fused_computation.94 | loop fusion | bytes 18874368 | tf_op jit(solution)/shard_map/slice | solution.py:372
  175.2 8.5 %reshape.219 = bf16[768,3072]{1,0:T(8,128)(2,1)} reshape(bf16[32,96,768]{2,1,0:T(8,128)(2,1)} %get-tuple-element.33) | data formatting | bytes 9437184 | tf_op jit(solution)/shard_map/reshape | solution.py:371
  183.7 36.7 %fusion.2 = (bf16[1024,3072]{1,0:T(8,128)(2,1)S(1)}, f32[1024,3072]{1,0:T(8,128)}) fusion(f32[3072]{0:T(1024)S(1)} %reshape.243, bf16[768,3072]{1,0:T(8,128)(2,1)} %reshape.219, f32[1024,768]{1,0:T(8,128)S(1)} %get-tuple-element.52, f32[768]{0:T(1024)S(1)} %reshape.242, f32[768]{0:T(1024)S(1)} %reshape.241, f32[1024]{0:T(1024)S(1)} %add_rsqrt_fusion, ...), kind=kOutput, calls=%fused_computation.4 | convolution fusion | flops 5043388416 | bytes 26765312 | tf_op jit(solution)/shard_map/dot_general | solution.py:394
  220.4 2.7 copy-done.18
  223.1 7.6 %fusion.43 = f32[3072,768]{1,0:T(8,128)} fusion(bf16[1024,3072]{1,0:T(8,128)(2,1)S(1)} %get-tuple-element.53, bf16[1024,768]{1,0:T(8,128)(2,1)S(1)} %copy-done.7), kind=kOutput, calls=%fused_computation.98 | convolution fusion | flops 4831838208 | bytes 17301504 | tf_op jit(solution)/shard_map/tf,td->fd/dot_general | solution.py:405
  230.8 14.5 %convert_reduce_fusion = (f32[3072]{0:T(1024)S(1)}, bf16[1024,3072]{1,0:T(8,128)(2,1)}) fusion(f32[1024,3072]{1,0:T(8,128)} %get-tuple-element.54, f32[3072]{0:T(1024)S(1)} %reshape.243, bf16[3072,768]{1,0:T(8,128)(2,1)} %bitcast.54, bf16[1024,768]{1,0:T(8,128)(2,1)} %param.31), kind=kOutput, calls=%fused_computation.11 | convolution fusion | flops 4872729600 | bytes 25190400 | tf_op jit(solution)/shard_map/td,fd->tf/dot_general | solution.py:407
  245.3 9.7 %multiply_reduce_fusion = (f32[768]{0:T(1024)S(1)}, f32[1024]{0:T(1024)S(1)}, f32[1024]{0:T(1024)S(1)}, f32[768]{0:T(1024)S(1)}, f32[1024,768]{1,0:T(8,128)S(1)}) fusion(f32[1024,768]{1,0:T(8,128)S(1)} %get-tuple-element.52, f32[1024]{0:T(1024)S(1)} %add_rsqrt_fusion, f32[1024]{0:T(1024)S(1)} %broadcast_multiply_fusion.4, f32[768]{0:T(1024)S(1)} %reshape.241, ...), kind=kOutput, calls=%fused_computation.49 | convolution fusion | flops 4838912000 | bytes 17327104 | tf_op jit(solution)/shard_map/tf,df->td/dot_general | solution.py:413
  255.0 2.6 convert_reduce_fusion.4
  257.7 0.1 reshape.221
  257.7 0.1 reshape.224
  257.8 0.1 reshape.227
  257.9 0.1 reshape.225
  258.0 5.0 %convolution_convert_fusion.do_ref = bf16[1024,768]{1,0:T(8,128)(2,1)} fusion(bf16[768,768]{1,0:T(8,128)(2,1)} %bitcast.59, f32[1024,768]{1,0:T(8,128)} %get-tuple-element.31), kind=kOutput, calls=%fused_computation.58 | convolution fusion | flops 1209532416 | bytes 5898240 | tf_op jit(solution)/shard_map/td,cd->tc/dot_general | solution.py:420
  263.0 36.4 %shard_map.264 = bf16[1024,2304]{1,0:T(8,128)(2,1)} custom-call(bf16[1024,2304]{1,0:T(8,128)(2,1)} %add_convert_fusion.q_ref.k_ref.v_ref, bf16[1024,2304]{1,0:T(8,128)(2,1)} %add_convert_fusion.q_ref.k_ref.v_ref, bf16[1024,2304]{1,0:T(8,128)(2,1)} %add_convert_fusion.q_ref.k_ref.v_ref, bf16[1024,768]{1,0:T(8,128)(2,1)} %convolution_convert_fusion.do_ref, ...), custom_call_target="tpu_custom_call" | custom-call | flops 4026531840 | bytes 11010048 | tf_op jit(solution)/shard_map/pallas_call | solution.py:137
  299.4 9.4 %fusion.28 = (f32[768]{0:T(1024)S(1)}, f32[1024]{0:T(1024)S(1)}, f32[1024]{0:T(1024)S(1)}, f32[768]{0:T(1024)S(1)}, f32[1024,768]{1,0:T(8,128)}) fusion(bf16[1024,768]{1,0:T(8,128)(2,1)S(1)} %copy-done.4, f32[1024]{0:T(1024)S(1)} %copy-done.12, f32[1024]{0:T(1024)S(1)} %copy-done.10, f32[768]{0:T(1024)S(1)} %copy-done.14, ...), kind=kOutput, calls=%fused_computation.46 | convolution fusion | flops 3631739392 | bytes 13001728 | tf_op jit(solution)/shard_map/te,de->td/dot_general | solution.py:427
  308.8 0.1 reshape.222
  308.9 3.3 convert_reduce_fusion.1
  312.2 0.1 concatenate.27
  312.3 0.1 concatenate.28
  312.4 0.1 reshape.223
  312.5 0.1 concatenate.30
  312.7 3.5 fusion.31.refs_1_
  316.2 4.6 fusion.27.refs_4_
  320.9 6.1 %fusion.34.refs_0_ = f32[768,2304]{1,0:T(8,128)} fusion(bf16[1024,2304]{1,0:T(8,128)(2,1)S(1)} %bitcast.50, bf16[1024,768]{1,0:T(8,128)(2,1)S(1)} %copy-done.4, f32[768]{0:T(1024)S(1)} %copy-done.16, f32[768]{0:T(1024)S(1)} %copy-done.14, f32[1024]{0:T(1024)S(1)} %copy-done.12, f32[1024]{0:T(1024)S(1)} %copy-done.10), kind=kOutput, calls=%fused_computation.91 | convolution fusion | flops 3628597248 | bytes 13383680 | tf_op jit(solution)/shard_map/td,te->de/dot_general | solution.py:426
  327.1 7.4 %add_convert_fusion.1.refs_5_ = bf16[1024,768]{1,0:T(8,128)(2,1)S(1)} fusion(f32[1024,768]{1,0:T(8,128)S(1)} %copy-done.2, bf16[1024,3072]{1,0:T(8,128)(2,1)} %copy-done.18, bf16[3072,768]{1,0:T(8,128)(2,1)S(1)} %bitcast.57, f32[768]{0:T(1024)S(1)} %copy-done.17), kind=kOutput, calls=%fused_computation.52 | convolution fusion | flops 4834197504 | bytes 15731712 | tf_op jit(solution)/shard_map/dot_general | solution.py:400
  334.6 8.7 %fusion.37.refs_2_ = f32[768,3072]{1,0:T(8,128)} fusion(bf16[1024,3072]{1,0:T(8,128)(2,1)S(1)} %bitcast.53, f32[1024,768]{1,0:T(8,128)S(1)} %copy-done.2, f32[768]{0:T(1024)S(1)} %reshape.242, f32[768]{0:T(1024)S(1)} %reshape.241, f32[1024]{0:T(1024)S(1)} %add_rsqrt_fusion, f32[1024]{0:T(1024)S(1)} %broadcast_multiply_fusion.4), kind=kOutput, calls=%fused_computation.92 | convolution fusion | flops 4835770368 | bytes 18888704 | tf_op jit(solution)/shard_map/td,tf->df/dot_general | solution.py:412
  343.2 128.1 %shard_map.265 = (f32[24,2304]{1,0:T(8,128)S(1)}, f32[24,768]{1,0:T(8,128)S(1)}, f32[24,3072]{1,0:T(8,128)S(1)}, f32[8,128]{1,0:T(8,128)S(1)}) custom-call(f32[768,2304]{1,0:T(8,128)} %fusion.34.refs_0_, f32[768,768]{1,0:T(8,128)S(1)} %fusion.31.refs_1_, f32[768,3072]{1,0:T(8,128)} %fusion.37.refs_2_, f32[256,128]{1,0:T(8,128)S(1)} %reshape.228.refs_3_, ...), custom_call_target="tpu_custom_call" | custom-call | flops 4751360 | bytes 38010880 | tf_op jit(solution)/shard_map/pallas_call | solution.py:303
  471.4 0.6 slice_bitcast_fusion.1
  472.0 0.5 slice_bitcast_fusion.7
  472.5 0.6 slice_bitcast_fusion
  473.1 0.7 copy.48
  473.8 0.6 copy.49
  474.4 0.7 copy.50
  (78 shorter events, 0.5 us)
Async XLA Ops:
  7.2 16.8 %copy-start.3 = (bf16[1024,768]{1,0:T(8,128)(2,1)S(1)}, bf16[1024,768]{1,0:T(8,128)(2,1)}, u32[]{:S(2)}) copy-start(bf16[1024,768]{1,0:T(8,128)(2,1)} %param.16) | copy-start | bytes 4718596
  7.2 75.5 %all-gather.8.cloned.1.call-start = ((), (), s32[]{:S(2)}) async-start(), calls=%async_computation.3 | async-start | bytes 5271552 | tf_op jit(solution)/shard_map/all_gather | solution.py:363
  15.2 152.0 %all-gather.6.cloned.1.call-start = ((), (), s32[]{:S(2)}) async-start(), calls=%async_computation.2 | async-start | bytes 9732096 | tf_op jit(solution)/shard_map/all_gather | solution.py:370
  18.0 455.1 %reduce-scatter.2.cloned.1.call-start = ((), (), s32[]{:S(2)}) async-start(), calls=%async_computation.1 | async-start | bytes 9732096 | tf_op jit(solution)/shard_map/reduce_scatter | solution.py:443
  24.0 74.2 %copy-start.9 = (f32[1024]{0:T(1024)}, f32[1024]{0:T(1024)S(1)}, u32[]{:S(2)}) copy-start(f32[1024]{0:T(1024)S(1)} %broadcast_multiply_fusion.5) | copy-start | bytes 12292
  24.6 73.6 %copy-start.11 = (f32[1024]{0:T(1024)}, f32[1024]{0:T(1024)S(1)}, u32[]{:S(2)}) copy-start(f32[1024]{0:T(1024)S(1)} %add_rsqrt_fusion.1) | copy-start | bytes 12292
  85.0 13.3 %copy-start.13 = (f32[768]{0:T(1024)}, f32[768]{0:T(1024)S(1)}, u32[]{:S(2)}) copy-start(f32[768]{0:T(1024)S(1)} %reshape.238) | copy-start | bytes 9220
  85.1 13.1 %copy-start.15 = (f32[768]{0:T(1024)}, f32[768]{0:T(1024)S(1)}, u32[]{:S(2)}) copy-start(f32[768]{0:T(1024)S(1)} %reshape.239) | copy-start | bytes 9220
  139.8 115.2 %copy-start.1 = (f32[1024,768]{1,0:T(8,128)}, f32[1024,768]{1,0:T(8,128)S(1)}, u32[]{:S(2)}) copy-start(f32[1024,768]{1,0:T(8,128)S(1)} %get-tuple-element.52) | copy-start | bytes 9437188
  183.7 39.4 %copy-start.7 = (bf16[1024,768]{1,0:T(8,128)(2,1)S(1)}, bf16[1024,768]{1,0:T(8,128)(2,1)}, u32[]{:S(2)}) copy-start(bf16[1024,768]{1,0:T(8,128)(2,1)} %param.31) | copy-start | bytes 4718596
  220.4 2.7 copy-start.18
  245.3 9.7 %copy-start.8 = (bf16[1024,768]{1,0:T(8,128)(2,1)S(1)}, bf16[1024,768]{1,0:T(8,128)(2,1)}, u32[]{:S(2)}) copy-start(bf16[1024,768]{1,0:T(8,128)(2,1)} %param.31) | copy-start | bytes 4718596
  263.0 36.4 %copy-start.4 = (bf16[1024,768]{1,0:T(8,128)(2,1)S(1)}, bf16[1024,768]{1,0:T(8,128)(2,1)}, u32[]{:S(2)}) copy-start(bf16[1024,768]{1,0:T(8,128)(2,1)} %param.16) | copy-start | bytes 4718596
  263.0 36.4 %copy-start.10 = (f32[1024]{0:T(1024)S(1)}, f32[1024]{0:T(1024)}, u32[]{:S(2)}) copy-start(f32[1024]{0:T(1024)} %copy-done.9) | copy-start | bytes 12292
  263.0 36.4 %copy-start.12 = (f32[1024]{0:T(1024)S(1)}, f32[1024]{0:T(1024)}, u32[]{:S(2)}) copy-start(f32[1024]{0:T(1024)} %copy-done.11) | copy-start | bytes 12292
  263.0 36.4 %copy-start.14 = (f32[768]{0:T(1024)S(1)}, f32[768]{0:T(1024)}, u32[]{:S(2)}) copy-start(f32[768]{0:T(1024)} %copy-done.13) | copy-start | bytes 9220
  308.8 3.8 copy-start.6
  312.7 3.5 copy-start.5
  312.7 8.2 %slice-start = ((s8[4718592]{0:T(1024)(128)(4,1)}), s8[4194304]{0:T(1024)(128)(4,1)S(1)}, s32[]{:S(2)}) async-start(s8[4718592]{0:T(1024)(128)(4,1)} %bitcast.49), calls=%async_computation.4 | async-start | bytes 8388608
  312.7 14.4 %slice-start.4 = ((s8[4718592]{0:T(1024)(128)(4,1)}), s8[4194304]{0:T(1024)(128)(4,1)S(1)}, s32[]{:S(2)}) async-start(s8[4718592]{0:T(1024)(128)(4,1)} %bitcast.55), calls=%async_computation.8 | async-start | bytes 8388608
  316.2 4.7 slice-start.1
  316.2 4.7 copy-start.16
  316.2 10.8 %slice-start.5 = ((s8[4718592]{0:T(1024)(128)(4,1)}), s8[524288]{0:T(1024)(128)(4,1)S(1)}, s32[]{:S(2)}) async-start(s8[4718592]{0:T(1024)(128)(4,1)} %bitcast.55), calls=%async_computation.9 | async-start | bytes 1048576
  320.9 6.2 %copy-start.2 = (f32[1024,768]{1,0:T(8,128)S(1)}, f32[1024,768]{1,0:T(8,128)}, u32[]{:S(2)}) copy-start(f32[1024,768]{1,0:T(8,128)} %copy-done.1) | copy-start | bytes 9437188
  320.9 6.2 %copy-start.17 = (f32[768]{0:T(1024)S(1)}, f32[768]{0:T(1024)}, u32[]{:S(2)}) copy-start(f32[768]{0:T(1024)} %reshape.244) | copy-start | bytes 9220
  320.9 13.6 %slice-start.2 = ((s8[6291456]{0:T(1024)(128)(4,1)}), s8[4194304]{0:T(1024)(128)(4,1)S(1)}, s32[]{:S(2)}) async-start(s8[6291456]{0:T(1024)(128)(4,1)} %bitcast.52), calls=%async_computation.6 | async-start | bytes 8388608
  327.1 7.5 %slice-start.3 = ((s8[6291456]{0:T(1024)(128)(4,1)}), s8[2097152]{0:T(1024)(128)(4,1)S(1)}, s32[]{:S(2)}) async-start(s8[6291456]{0:T(1024)(128)(4,1)} %bitcast.52), calls=%async_computation.7 | async-start | bytes 4194304
  334.5 8.7 %copy-start = (bf16[1024,768]{1,0:T(8,128)(2,1)}, bf16[1024,768]{1,0:T(8,128)(2,1)S(1)}, u32[]{:S(2)}) copy-start(bf16[1024,768]{1,0:T(8,128)(2,1)S(1)} %add_convert_fusion.1.refs_5_) | copy-start | bytes 4718596
Sparse Core Ops, SparseCore 0:
  15.3 67.3 all-gather.7
  86.2 80.9 all-gather.5
  230.9 132.5 reduce-scatter.1

commit v9 on v7

--- a/solution.py
+++ b/solution.py
@@ -31,13 +31,13 @@
     return jnp.sum(rows.astype(jnp.float32), axis=0)
 
 
-Q_TILE = 64
-K_WIN = 256
-
-
-def seg_mask(seg_col, seg_row, val_row, q0, k0):
-    rows = q0 + lax.broadcasted_iota(jnp.int32, (seg_col.shape[0], seg_row.shape[1]), 0)
-    cols = k0 + lax.broadcasted_iota(jnp.int32, (seg_col.shape[0], seg_row.shape[1]), 1)
+Q_CHUNK = 128
+
+
+def seg_mask(seg_col, seg_row, val_row, q0):
+    shape = (seg_col.shape[0], seg_row.shape[1])
+    rows = q0 + lax.broadcasted_iota(jnp.int32, shape, 0)
+    cols = lax.broadcasted_iota(jnp.int32, shape, 1)
     return (seg_col == seg_row) & ((val_row == 1) | (rows == cols))
 
 
@@ -49,26 +49,22 @@
     return expo * (1.0 / jnp.sum(expo, axis=-1, keepdims=True))
 
 
-def windows(n):
-    win = min(K_WIN, n)
-    out = []
-    for q0 in range(0, n, Q_TILE):
-        k0 = min(max(q0 - (win - Q_TILE) // 2, 0), n - win)
-        out.append((q0, k0, win))
-    return out
-
-
 def attn_fwd_kernel(q_ref, k_ref, v_ref, sc_ref, sr_ref, vr_ref, o_ref):
     n = q_ref.shape[0]
-    for q0, k0, win in windows(n):
-        qs, ks = slice(q0, q0 + Q_TILE), slice(k0, k0 + win)
-        allowed = seg_mask(sc_ref[qs, :], sr_ref[:, ks], vr_ref[:, ks], q0, k0)
+
+    def chunk(c, carry):
+        q0 = pl.multiple_of(c * Q_CHUNK, Q_CHUNK)
+        qs = pl.ds(q0, Q_CHUNK)
+        allowed = seg_mask(sc_ref[qs, :], sr_ref[...], vr_ref[...], q0)
         outs = []
         for j in range(q_ref.shape[1] // HD):
             cols = slice(j * HD, (j + 1) * HD)
-            probs = soft_rows(q_ref[qs, cols], k_ref[ks, cols], allowed).astype(jnp.bfloat16)
-            outs.append(jnp.dot(probs, v_ref[ks, cols], preferred_element_type=jnp.float32))
+            probs = soft_rows(q_ref[qs, cols], k_ref[:, cols], allowed).astype(jnp.bfloat16)
+            outs.append(jnp.dot(probs, v_ref[:, cols], preferred_element_type=jnp.float32))
         o_ref[qs, :] = jnp.concatenate(outs, axis=1).astype(o_ref.dtype)
+        return carry
+
+    lax.fori_loop(0, n // Q_CHUNK, chunk, 0)
 
 
 def attn_bwd_kernel(q_ref, k_ref, v_ref, do_ref, sc_ref, sr_ref, vr_ref, dqkv_ref, dk_acc, dv_acc):
@@ -76,16 +72,18 @@
     width = q_ref.shape[1]
     hp = pl.program_id(1)
     model_width = dqkv_ref.shape[1] // 3
+    at = pl.multiple_of(hp * width, width)
     dk_acc[...] = jnp.zeros_like(dk_acc)
     dv_acc[...] = jnp.zeros_like(dv_acc)
-    at = pl.multiple_of(hp * width, width)
-    for q0, k0, win in windows(n):
-        qs, ks = slice(q0, q0 + Q_TILE), slice(k0, k0 + win)
-        allowed = seg_mask(sc_ref[qs, :], sr_ref[:, ks], vr_ref[:, ks], q0, k0)
+
+    def chunk(c, carry):
+        q0 = pl.multiple_of(c * Q_CHUNK, Q_CHUNK)
+        qs = pl.ds(q0, Q_CHUNK)
+        allowed = seg_mask(sc_ref[qs, :], sr_ref[...], vr_ref[...], q0)
         dqs, dks, dvs = [], [], []
         for j in range(width // HD):
             cols = slice(j * HD, (j + 1) * HD)
-            qh, kh, vh, doh = q_ref[qs, cols], k_ref[ks, cols], v_ref[ks, cols], do_ref[qs, cols]
+            qh, kh, vh, doh = q_ref[qs, cols], k_ref[:, cols], v_ref[:, cols], do_ref[qs, cols]
             probs = soft_rows(qh, kh, allowed)
             dvs.append(
                 lax.dot_general(probs.astype(jnp.bfloat16), doh, (((0,), (0,)), ((), ())),
@@ -100,8 +98,11 @@
                 * (1.0 / HD**0.5)
             )
         dqkv_ref[qs, pl.ds(at, width)] = jnp.concatenate(dqs, axis=1).astype(dqkv_ref.dtype)
-        dk_acc[ks, :] += jnp.concatenate(dks, axis=1)
-        dv_acc[ks, :] += jnp.concatenate(dvs, axis=1)
+        dk_acc[...] += jnp.concatenate(dks, axis=1)
+        dv_acc[...] += jnp.concatenate(dvs, axis=1)
+        return carry
+
+    lax.fori_loop(0, n // Q_CHUNK, chunk, 0)
     dqkv_ref[:, pl.ds(at + model_width, width)] = dk_acc[...].astype(dqkv_ref.dtype)
     dqkv_ref[:, pl.ds(at + 2 * model_width, width)] = dv_acc[...].astype(dqkv_ref.dtype)
 
@@ -464,7 +465,7 @@
     ]
     down_sum = lax.psum_scatter(grad_wdown, ALL, scatter_dimension=0, tiled=True)
     if all(rb % 8 == 0 and a.shape[1] % 256 == 0 for (a, rb, _) in parts[:3]):
-        sums = ring_reduce_scatter(parts, mesh_shape, after=(grad_inputs,))
+        sums = ring_reduce_scatter(parts, mesh_shape, after=(grad_inputs, block_out))
     else:
         sums = [lax.psum_scatter(a, ALL, scatter_dimension=0, tiled=True) for (a, _, _) in parts]
     sums = list(sums[:3]) + [down_sum] + list(sums[3:])

time: 615 us -> 516 us (0.84)
  Pallas kernels: 346 us -> 241 us
  waiting for transfers between devices: 58.1 us -> 65.4 us
    pallas_call x1, Pallas kernels: 134 us -> 69.8 us  [attention_bwd(): pl.pallas_call(attn_bwd_kernel, out_shape=jax.ShapeDtypeStruct((rows, wid...]
    pallas_call x1, Pallas kernels: 89.8 us -> 49.5 us  [attention_fwd(): pl.pallas_call(attn_fwd_kernel, out_shape=jax.ShapeDtypeStruct((rows, mod...]
    all_gather x1, waiting for transfers between devices: 0.02 us -> 7.29 us  [on_device(): mlp_all = lax.all_gather(mlp_buf, ALL, axis=0, tiled=False)]
  transfers between devices with their start and end apart: 3 -> 3, of which waited for: 1 -> 2; matrix products, arithmetic and copies ran while one was open for 19% -> 22% of each run, Pallas kernels for 57% -> 47%
where the time goes in v9:
time: 516 us; the launch traced here: 509 us
  Pallas kernels  241 us (47%)
  matrix products  120 us (23%)
  waiting for transfers between devices  65.4 us (13%)
  local copies, waits for them, and re-layouts  50.9 us (10%)
  other arithmetic  16.6 us (3%)
  between operations  14.8 us (3%)
    pallas_call x1, Pallas kernels, ring_reduce_scatter(): pl.pallas_call(kernel, out_shape=out_shape, in_specs=[pl.BlockSpec(memory...  122 us
    pallas_call x1, Pallas kernels, attention_bwd(): pl.pallas_call(attn_bwd_kernel, out_shape=jax.ShapeDtypeStruct((rows, wid...  69.8 us
    all_gather x1, waiting for transfers between devices, on_device(): attn_all = lax.all_gather(attn_buf, ALL, axis=0, tiled=False)  58.1 us
    pallas_call x1, Pallas kernels, attention_fwd(): pl.pallas_call(attn_fwd_kernel, out_shape=jax.ShapeDtypeStruct((rows, mod...  49.5 us
    dot_general x1, matrix products, on_device(): jnp.dot(h_two, up_full, preferred_element_type=jnp.float32)  36.7 us
    dot_general x1, matrix products, on_device(): jnp.einsum('td,fd->tf', cotangent, down_full, preferred_element_type=jnp....  14.5 us
  transfers between devices with their start and end apart: 3, of which 2 were waited for; matrix products, arithmetic and copies ran while one was open for 22% of the time, Pallas kernels for 47%

profile of v9, /device:TPU:1, one launch (start us, length us, event | category | flops | bytes accessed | tf_op | source)
XLA Modules:
  0.0 509.1 jit_solution(17252752472684939830)
XLA Ops:
  7.2 5.5 %concatenate.23 = bf16[288]{0:T(512)(128)(2,1)S(1)} concatenate(bf16[48]{0:T(256)(128)(2,1)} %param.18, bf16[24]{0:T(256)(128)(2,1)} %param.20, bf16[24]{0:T(256)(128)(2,1)} %param.21, bf16[24]{0:T(256)(128)(2,1)} %param.22, bf16[24]{0:T(256)(128)(2,1)} %param.23, bf16[24]{0:T(256)(128)(2,1)} %param.24, bf16[96]{0:T(256)(128)(2,1)} %param.26, bf16[24]{0:T(256)(128)(2,1)} %param.28), dimensions={0} | concatenate | bytes 1152 | tf_op jit(solution)/shard_map/concatenate | solution.py:340
  12.8 1.0 reshape.215
  13.8 1.4 maximum_bitcast_fusion
  15.3 1.0 reshape.218
  16.3 1.6 pad_maximum_fusion
  18.0 1.3 broadcast_in_dim.14.vr_ref
  19.3 1.3 broadcast_in_dim.13.sr_ref
  20.6 1.7 copy.38.sc_ref
  22.3 1.7 convert_reduce_fusion.2
  24.0 0.6 fusion.29
  24.6 58.1 %all-gather.8.cloned.1.call-done = bf16[32,97,768]{2,1,0:T(8,128)(2,1)} async-done(((bf16[1,97,768]{2,1,0:T(8,128)(2,1)}), bf16[32,97,768]{2,1,0:T(8,128)(2,1)}) %all-gather.8.cloned.1.call-update) | async-done | bytes 4767760 | tf_op jit(solution)/shard_map/all_gather | solution.py:386
  82.7 1.0 slice.122
  83.7 0.1 slice.101
  83.8 0.1 slice.103
  83.9 0.1 slice_convert_fusion.1
  83.9 0.1 reshape.243
  84.0 0.1 slice_convert_fusion
  84.1 0.7 reshape.244
  84.8 0.1 reshape.241
  84.9 0.1 reshape.238
  85.0 0.1 reshape.242
  85.0 0.1 reshape.239
  85.1 0.1 reshape.240
  85.2 4.0 slice.125
  89.2 6.6 %reshape.216 = bf16[768,2304]{1,0:T(8,128)(2,1)} reshape(bf16[32,72,768]{2,1,0:T(8,128)(2,1)} %slice.125) | data formatting | bytes 7077888 | tf_op jit(solution)/shard_map/reshape | solution.py:387
  95.8 2.3 slice.129
  98.2 7.9 %add_convert_fusion.q_ref.k_ref.v_ref = bf16[1024,2304]{1,0:T(8,128)(2,1)} fusion(bf16[768,2304]{1,0:T(8,128)(2,1)} %reshape.216, f32[2304]{0:T(1024)S(1)} %pad_maximum_fusion.2, bf16[1024,768]{1,0:T(8,128)(2,1)S(1)} %copy-done.3, f32[768]{0:T(1024)S(1)} %reshape.239, f32[768]{0:T(1024)S(1)} %reshape.238, f32[1024]{0:T(1024)S(1)} %add_rsqrt_fusion.1, ...), kind=kOutput, calls=%fused_computation.28 | convolution fusion | flops 3633315840 | bytes 9853952 | tf_op jit(solution)/shard_map/dot_general | solution.py:403
  106.2 49.5 %shard_map.263 = bf16[1024,768]{1,0:T(8,128)(2,1)} custom-call(bf16[1024,2304]{1,0:T(8,128)(2,1)} %add_convert_fusion.q_ref.k_ref.v_ref, bf16[1024,2304]{1,0:T(8,128)(2,1)} %add_convert_fusion.q_ref.k_ref.v_ref, bf16[1024,2304]{1,0:T(8,128)(2,1)} %add_convert_fusion.q_ref.k_ref.v_ref, s32[2,512,1]{2,1,0:T(8,128)} %copy.38.sc_ref, ...), custom_call_target="tpu_custom_call" | custom-call | flops 1610612736 | bytes 6291456 | tf_op jit(solution)/shard_map/pallas_call | solution.py:127
  155.7 3.8 fusion.42
  159.5 0.5 multiply_reduce_fusion.2
  160.0 7.3 %all-gather.6.cloned.1.call-done = bf16[6144,768]{1,0:T(8,128)(2,1)} async-done(((bf16[192,768]{1,0:T(8,128)(2,1)}), bf16[6144,768]{1,0:T(8,128)(2,1)}) %all-gather.6.cloned.1.call-update) | async-done | bytes 9437200 | tf_op jit(solution)/shard_map/all_gather | solution.py:393
  167.3 8.0 %fusion.39 = (bf16[32,96,768]{2,1,0:T(8,128)(2,1)}, bf16[32,96,768]{2,1,0:T(8,128)(2,1)}) fusion(bf16[32,192,768]{2,1,0:T(8,128)(2,1)} %bitcast.51), kind=kLoop, calls=%fused_computation.94 | loop fusion | bytes 18874368 | tf_op jit(solution)/shard_map/slice | solution.py:395
  175.3 8.5 %reshape.219 = bf16[768,3072]{1,0:T(8,128)(2,1)} reshape(bf16[32,96,768]{2,1,0:T(8,128)(2,1)} %get-tuple-element.33) | data formatting | bytes 9437184 | tf_op jit(solution)/shard_map/reshape | solution.py:394
  183.8 36.7 %fusion.2 = (bf16[1024,3072]{1,0:T(8,128)(2,1)S(1)}, f32[1024,3072]{1,0:T(8,128)}) fusion(f32[3072]{0:T(1024)S(1)} %reshape.243, bf16[768,3072]{1,0:T(8,128)(2,1)} %reshape.219, f32[1024,768]{1,0:T(8,128)S(1)} %get-tuple-element.52, f32[768]{0:T(1024)S(1)} %reshape.242, f32[768]{0:T(1024)S(1)} %reshape.241, f32[1024]{0:T(1024)S(1)} %add_rsqrt_fusion, ...), kind=kOutput, calls=%fused_computation.4 | convolution fusion | flops 5043388416 | bytes 26765312 | tf_op jit(solution)/shard_map/dot_general | solution.py:417
  220.5 2.7 copy-done.18
  223.1 7.6 %fusion.43 = f32[3072,768]{1,0:T(8,128)} fusion(bf16[1024,3072]{1,0:T(8,128)(2,1)S(1)} %get-tuple-element.53, bf16[1024,768]{1,0:T(8,128)(2,1)S(1)} %copy-done.7), kind=kOutput, calls=%fused_computation.98 | convolution fusion | flops 4831838208 | bytes 17301504 | tf_op jit(solution)/shard_map/tf,td->fd/dot_general | solution.py:428
  230.8 14.5 %convert_reduce_fusion = (f32[3072]{0:T(1024)S(1)}, bf16[1024,3072]{1,0:T(8,128)(2,1)}) fusion(f32[1024,3072]{1,0:T(8,128)} %get-tuple-element.54, f32[3072]{0:T(1024)S(1)} %reshape.243, bf16[3072,768]{1,0:T(8,128)(2,1)} %bitcast.54, bf16[1024,768]{1,0:T(8,128)(2,1)} %param.31), kind=kOutput, calls=%fused_computation.11 | convolution fusion | flops 4872729600 | bytes 25190400 | tf_op jit(solution)/shard_map/td,fd->tf/dot_general | solution.py:430
  245.3 9.7 %multiply_reduce_fusion = (f32[768]{0:T(1024)S(1)}, f32[1024]{0:T(1024)S(1)}, f32[1024]{0:T(1024)S(1)}, f32[768]{0:T(1024)S(1)}, f32[1024,768]{1,0:T(8,128)S(1)}) fusion(f32[1024,768]{1,0:T(8,128)S(1)} %get-tuple-element.52, f32[1024]{0:T(1024)S(1)} %add_rsqrt_fusion, f32[1024]{0:T(1024)S(1)} %broadcast_multiply_fusion.4, f32[768]{0:T(1024)S(1)} %reshape.241, ...), kind=kOutput, calls=%fused_computation.49 | convolution fusion | flops 4838912000 | bytes 17327104 | tf_op jit(solution)/shard_map/tf,df->td/dot_general | solution.py:436
  255.1 2.6 convert_reduce_fusion.4
  257.7 0.1 reshape.221
  257.8 0.1 reshape.224
  257.9 0.1 reshape.227
  258.0 0.1 reshape.225
  258.1 5.0 convolution_convert_fusion.do_ref
  263.1 69.8 %shard_map.264 = bf16[1024,2304]{1,0:T(8,128)(2,1)} custom-call(bf16[1024,2304]{1,0:T(8,128)(2,1)} %add_convert_fusion.q_ref.k_ref.v_ref, bf16[1024,2304]{1,0:T(8,128)(2,1)} %add_convert_fusion.q_ref.k_ref.v_ref, bf16[1024,2304]{1,0:T(8,128)(2,1)} %add_convert_fusion.q_ref.k_ref.v_ref, bf16[1024,768]{1,0:T(8,128)(2,1)} %convolution_convert_fusion.do_ref, ...), custom_call_target="tpu_custom_call" | custom-call | flops 4026531840 | bytes 11010048 | tf_op jit(solution)/shard_map/pallas_call | solution.py:159
  332.9 9.4 %fusion.28 = (f32[768]{0:T(1024)S(1)}, f32[1024]{0:T(1024)S(1)}, f32[1024]{0:T(1024)S(1)}, f32[768]{0:T(1024)S(1)}, f32[1024,768]{1,0:T(8,128)}) fusion(bf16[1024,768]{1,0:T(8,128)(2,1)S(1)} %copy-done.4, f32[1024]{0:T(1024)S(1)} %copy-done.12, f32[1024]{0:T(1024)S(1)} %copy-done.10, f32[768]{0:T(1024)S(1)} %copy-done.14, ...), kind=kOutput, calls=%fused_computation.46 | convolution fusion | flops 3631739392 | bytes 13001728 | tf_op jit(solution)/shard_map/te,de->td/dot_general | solution.py:450
  342.3 0.1 reshape.222
  342.4 3.2 convert_reduce_fusion.1
  345.6 0.1 concatenate.27
  345.6 0.1 concatenate.28
  345.7 0.1 reshape.223
  345.8 0.1 concatenate.30
  346.0 3.5 fusion.31.refs_1_
  349.6 4.7 fusion.27.refs_4_
  354.3 6.1 %fusion.34.refs_0_ = f32[768,2304]{1,0:T(8,128)} fusion(bf16[1024,2304]{1,0:T(8,128)(2,1)S(1)} %bitcast.50, bf16[1024,768]{1,0:T(8,128)(2,1)S(1)} %copy-done.4, f32[768]{0:T(1024)S(1)} %copy-done.16, f32[768]{0:T(1024)S(1)} %copy-done.14, f32[1024]{0:T(1024)S(1)} %copy-done.12, f32[1024]{0:T(1024)S(1)} %copy-done.10), kind=kOutput, calls=%fused_computation.91 | convolution fusion | flops 3628597248 | bytes 13383680 | tf_op jit(solution)/shard_map/td,te->de/dot_general | solution.py:449
  360.5 7.4 %add_convert_fusion.1.refs_5_ = bf16[1024,768]{1,0:T(8,128)(2,1)S(1)} fusion(f32[1024,768]{1,0:T(8,128)S(1)} %copy-done.2, bf16[1024,3072]{1,0:T(8,128)(2,1)} %copy-done.18, bf16[3072,768]{1,0:T(8,128)(2,1)S(1)} %bitcast.57, f32[768]{0:T(1024)S(1)} %copy-done.17), kind=kOutput, calls=%fused_computation.52 | convolution fusion | flops 4834197504 | bytes 15731712 | tf_op jit(solution)/shard_map/dot_general | solution.py:423
  368.0 8.7 %fusion.37.refs_2_ = f32[768,3072]{1,0:T(8,128)} fusion(bf16[1024,3072]{1,0:T(8,128)(2,1)S(1)} %bitcast.53, f32[1024,768]{1,0:T(8,128)S(1)} %copy-done.2, f32[768]{0:T(1024)S(1)} %reshape.242, f32[768]{0:T(1024)S(1)} %reshape.241, f32[1024]{0:T(1024)S(1)} %add_rsqrt_fusion, f32[1024]{0:T(1024)S(1)} %broadcast_multiply_fusion.4), kind=kOutput, calls=%fused_computation.92 | convolution fusion | flops 4835770368 | bytes 18888704 | tf_op jit(solution)/shard_map/td,tf->df/dot_general | solution.py:435
  376.6 121.7 %shard_map.265 = (f32[24,2304]{1,0:T(8,128)S(1)}, f32[24,768]{1,0:T(8,128)S(1)}, f32[24,3072]{1,0:T(8,128)S(1)}, f32[8,128]{1,0:T(8,128)S(1)}) custom-call(f32[768,2304]{1,0:T(8,128)} %fusion.34.refs_0_, f32[768,768]{1,0:T(8,128)S(1)} %fusion.31.refs_1_, f32[768,3072]{1,0:T(8,128)} %fusion.37.refs_2_, f32[256,128]{1,0:T(8,128)S(1)} %reshape.228.refs_3_, ...), custom_call_target="tpu_custom_call" | custom-call | flops 4751360 | bytes 38010880 | tf_op jit(solution)/shard_map/pallas_call | solution.py:326
  498.3 0.6 slice_bitcast_fusion.1
  498.9 0.5 slice_bitcast_fusion.7
  499.4 0.6 slice_bitcast_fusion
  500.0 0.7 copy.48
  500.7 0.6 copy.49
  501.3 0.7 copy.50
  (78 shorter events, 0.5 us)
Async XLA Ops:
  7.2 16.8 %copy-start.3 = (bf16[1024,768]{1,0:T(8,128)(2,1)S(1)}, bf16[1024,768]{1,0:T(8,128)(2,1)}, u32[]{:S(2)}) copy-start(bf16[1024,768]{1,0:T(8,128)(2,1)} %param.16) | copy-start | bytes 4718596
  7.2 75.5 %all-gather.8.cloned.1.call-start = ((), (), s32[]{:S(2)}) async-start(), calls=%async_computation.3 | async-start | bytes 5271552 | tf_op jit(solution)/shard_map/all_gather | solution.py:386
  15.2 152.1 %all-gather.6.cloned.1.call-start = ((), (), s32[]{:S(2)}) async-start(), calls=%async_computation.2 | async-start | bytes 9732096 | tf_op jit(solution)/shard_map/all_gather | solution.py:393
  18.0 482.0 %reduce-scatter.2.cloned.1.call-start = ((), (), s32[]{:S(2)}) async-start(), calls=%async_computation.1 | async-start | bytes 9732096 | tf_op jit(solution)/shard_map/reduce_scatter | solution.py:466
  24.0 74.2 %copy-start.9 = (f32[1024]{0:T(1024)}, f32[1024]{0:T(1024)S(1)}, u32[]{:S(2)}) copy-start(f32[1024]{0:T(1024)S(1)} %broadcast_multiply_fusion.5) | copy-start | bytes 12292
  24.6 73.6 %copy-start.11 = (f32[1024]{0:T(1024)}, f32[1024]{0:T(1024)S(1)}, u32[]{:S(2)}) copy-start(f32[1024]{0:T(1024)S(1)} %add_rsqrt_fusion.1) | copy-start | bytes 12292
  85.0 13.3 %copy-start.13 = (f32[768]{0:T(1024)}, f32[768]{0:T(1024)S(1)}, u32[]{:S(2)}) copy-start(f32[768]{0:T(1024)S(1)} %reshape.238) | copy-start | bytes 9220
  85.1 13.1 %copy-start.15 = (f32[768]{0:T(1024)}, f32[768]{0:T(1024)S(1)}, u32[]{:S(2)}) copy-start(f32[768]{0:T(1024)S(1)} %reshape.239) | copy-start | bytes 9220
  159.5 95.6 %copy-start.1 = (f32[1024,768]{1,0:T(8,128)}, f32[1024,768]{1,0:T(8,128)S(1)}, u32[]{:S(2)}) copy-start(f32[1024,768]{1,0:T(8,128)S(1)} %get-tuple-element.52) | copy-start | bytes 9437188
  183.8 39.4 %copy-start.7 = (bf16[1024,768]{1,0:T(8,128)(2,1)S(1)}, bf16[1024,768]{1,0:T(8,128)(2,1)}, u32[]{:S(2)}) copy-start(bf16[1024,768]{1,0:T(8,128)(2,1)} %param.31) | copy-start | bytes 4718596
  220.5 2.7 copy-start.18
  245.3 9.8 %copy-start.8 = (bf16[1024,768]{1,0:T(8,128)(2,1)S(1)}, bf16[1024,768]{1,0:T(8,128)(2,1)}, u32[]{:S(2)}) copy-start(bf16[1024,768]{1,0:T(8,128)(2,1)} %param.31) | copy-start | bytes 4718596
  263.1 69.8 %copy-start.4 = (bf16[1024,768]{1,0:T(8,128)(2,1)S(1)}, bf16[1024,768]{1,0:T(8,128)(2,1)}, u32[]{:S(2)}) copy-start(bf16[1024,768]{1,0:T(8,128)(2,1)} %param.16) | copy-start | bytes 4718596
  263.1 69.8 %copy-start.10 = (f32[1024]{0:T(1024)S(1)}, f32[1024]{0:T(1024)}, u32[]{:S(2)}) copy-start(f32[1024]{0:T(1024)} %copy-done.9) | copy-start | bytes 12292
  263.1 69.8 %copy-start.12 = (f32[1024]{0:T(1024)S(1)}, f32[1024]{0:T(1024)}, u32[]{:S(2)}) copy-start(f32[1024]{0:T(1024)} %copy-done.11) | copy-start | bytes 12292
  263.1 69.9 %copy-start.14 = (f32[768]{0:T(1024)S(1)}, f32[768]{0:T(1024)}, u32[]{:S(2)}) copy-start(f32[768]{0:T(1024)} %copy-done.13) | copy-start | bytes 9220
  342.3 3.7 copy-start.6
  346.0 3.5 copy-start.5
  346.0 8.2 %slice-start = ((s8[4718592]{0:T(1024)(128)(4,1)}), s8[4194304]{0:T(1024)(128)(4,1)S(1)}, s32[]{:S(2)}) async-start(s8[4718592]{0:T(1024)(128)(4,1)} %bitcast.49), calls=%async_computation.4 | async-start | bytes 8388608
  346.0 14.4 %slice-start.4 = ((s8[4718592]{0:T(1024)(128)(4,1)}), s8[4194304]{0:T(1024)(128)(4,1)S(1)}, s32[]{:S(2)}) async-start(s8[4718592]{0:T(1024)(128)(4,1)} %bitcast.55), calls=%async_computation.8 | async-start | bytes 8388608
  349.5 4.7 slice-start.1
  349.5 4.7 copy-start.16
  349.6 10.9 %slice-start.5 = ((s8[4718592]{0:T(1024)(128)(4,1)}), s8[524288]{0:T(1024)(128)(4,1)S(1)}, s32[]{:S(2)}) async-start(s8[4718592]{0:T(1024)(128)(4,1)} %bitcast.55), calls=%async_computation.9 | async-start | bytes 1048576
  354.3 6.2 %copy-start.2 = (f32[1024,768]{1,0:T(8,128)S(1)}, f32[1024,768]{1,0:T(8,128)}, u32[]{:S(2)}) copy-start(f32[1024,768]{1,0:T(8,128)} %copy-done.1) | copy-start | bytes 9437188
  354.3 6.2 %copy-start.17 = (f32[768]{0:T(1024)S(1)}, f32[768]{0:T(1024)}, u32[]{:S(2)}) copy-start(f32[768]{0:T(1024)} %reshape.244) | copy-start | bytes 9220
  354.3 13.6 %slice-start.2 = ((s8[6291456]{0:T(1024)(128)(4,1)}), s8[4194304]{0:T(1024)(128)(4,1)S(1)}, s32[]{:S(2)}) async-start(s8[6291456]{0:T(1024)(128)(4,1)} %bitcast.52), calls=%async_computation.6 | async-start | bytes 8388608
  360.5 7.5 %slice-start.3 = ((s8[6291456]{0:T(1024)(128)(4,1)}), s8[2097152]{0:T(1024)(128)(4,1)S(1)}, s32[]{:S(2)}) async-start(s8[6291456]{0:T(1024)(128)(4,1)} %bitcast.52), calls=%async_computation.7 | async-start | bytes 4194304
  367.9 8.7 %copy-start = (bf16[1024,768]{1,0:T(8,128)(2,1)}, bf16[1024,768]{1,0:T(8,128)(2,1)S(1)}, u32[]{:S(2)}) copy-start(bf16[1024,768]{1,0:T(8,128)(2,1)S(1)} %add_convert_fusion.1.refs_5_) | copy-start | bytes 4718596
Sparse Core Ops, SparseCore 0:
  15.3 67.3 all-gather.7
  86.2 81.0 all-gather.5
  230.9 131.7 reduce-scatter.1

commit v10 on v8

--- a/solution.py
+++ b/solution.py
@@ -357,19 +357,23 @@
     n_small = sum(small_sizes)
     rows_q = w_qkv.size // model_width
     rows_o = w_out.shape[0]
+    rows_u = w_up.size // model_width
     attn_buf = jnp.concatenate(
-        [w_qkv.reshape(rows_q, model_width), w_out, pack_rows(small, model_width)], axis=0
+        [
+            w_qkv.reshape(rows_q, model_width),
+            w_out,
+            w_up.reshape(rows_u, model_width),
+            pack_rows(small, model_width),
+        ],
+        axis=0,
     )
     attn_all = lax.all_gather(attn_buf, ALL, axis=0, tiled=False)
     qkv_full = attn_all[:, :rows_q].reshape(-1, w_qkv.shape[1])
     out_full = attn_all[:, rows_q : rows_q + rows_o].reshape(-1, model_width)
-    small_full = split_owned(attn_all[:, rows_q + rows_o, :n_small], small_sizes)
+    up_full = attn_all[:, rows_q + rows_o : rows_q + rows_o + rows_u].reshape(-1, w_up.shape[1])
+    small_full = split_owned(attn_all[:, rows_q + rows_o + rows_u, :n_small], small_sizes)
     qv_full, outb_full, gain_one, shift_one, gain_two, shift_two, upb_full, downb_full = small_full
-    rows_u = w_up.size // model_width
-    mlp_buf = jnp.concatenate([w_up.reshape(rows_u, model_width), w_down], axis=0)
-    mlp_all = lax.all_gather(mlp_buf, ALL, axis=0, tiled=False)
-    up_full = mlp_all[:, :rows_u].reshape(-1, w_up.shape[1])
-    down_full = mlp_all[:, rows_u:].reshape(-1, model_width)
+    down_full = lax.all_gather(w_down, ALL, axis=0, tiled=True)
 
     gain_one = gain_one.astype(jnp.float32)
     shift_one = shift_one.astype(jnp.float32)

time: 490 us -> 477 us (0.973)
    all_gather x1, waiting for transfers between devices: 26.9 us -> 0.02 us  [on_device(): down_full = lax.all_gather(w_down, ALL, axis=0, tiled=True)]
    all_gather x1, waiting for transfers between devices: 58.1 us -> 79.8 us  [on_device(): attn_all = lax.all_gather(attn_buf, ALL, axis=0, tiled=False)]
  transfers between devices with their start and end apart: 3 -> 3, of which waited for: 2 -> 1; matrix products, arithmetic and copies ran while one was open for 24% -> 35% of each run, Pallas kernels for 40% -> 41%
where the time goes in v10:
time: 477 us; the launch traced here: 469 us
  Pallas kernels  194 us (41%)
  matrix products  118 us (25%)
  waiting for transfers between devices  80.5 us (17%)
  local copies, waits for them, and re-layouts  46.1 us (10%)
  other arithmetic  15.1 us (3%)
  between operations  14.8 us (3%)
    pallas_call x1, Pallas kernels, ring_reduce_scatter(): pl.pallas_call(kernel, out_shape=out_shape, in_specs=[pl.BlockSpec(memory...  128 us
    all_gather x1, waiting for transfers between devices, on_device(): attn_all = lax.all_gather(attn_buf, ALL, axis=0, tiled=False)  79.8 us
    pallas_call x1, Pallas kernels, attention_bwd(): pl.pallas_call(attn_bwd_kernel, out_shape=jax.ShapeDtypeStruct((rows, wid...  36.4 us
    dot_general x1, matrix products, on_device(): jnp.dot(h_two, up_full, preferred_element_type=jnp.float32)  34.4 us
    pallas_call x1, Pallas kernels, attention_fwd(): pl.pallas_call(attn_fwd_kernel, out_shape=jax.ShapeDtypeStruct((rows, mod...  29.8 us
    dot_general x1, matrix products, on_device(): jnp.einsum('td,fd->tf', cotangent, down_full, preferred_element_type=jnp....  14.5 us
    dot_general x1, matrix products, on_device(): jnp.einsum('tf,df->td', grad_u, up_full, preferred_element_type=jnp.float32)  9.71 us
  transfers between devices with their start and end apart: 3, of which 1 were waited for; matrix products, arithmetic and copies ran while one was open for 35% of the time, Pallas kernels for 41%

profile of v10, /device:TPU:1, one launch (start us, length us, event | category | flops | bytes accessed | tf_op | source)
XLA Modules:
  0.0 469.3 jit_solution(15693964131383792145)
XLA Ops:
  7.3 5.5 %concatenate.20 = bf16[288]{0:T(512)(128)(2,1)S(1)} concatenate(bf16[48]{0:T(256)(128)(2,1)} %param.18, bf16[24]{0:T(256)(128)(2,1)} %param.20, bf16[24]{0:T(256)(128)(2,1)} %param.21, bf16[24]{0:T(256)(128)(2,1)} %param.22, bf16[24]{0:T(256)(128)(2,1)} %param.23, bf16[24]{0:T(256)(128)(2,1)} %param.24, bf16[96]{0:T(256)(128)(2,1)} %param.26, bf16[24]{0:T(256)(128)(2,1)} %param.28), dimensions={0} | concatenate | bytes 1152 | tf_op jit(solution)/shard_map/concatenate | solution.py:317
  12.8 1.0 reshape.212
  13.8 1.0 reshape.213
  14.8 1.5 maximum_bitcast_fusion
  16.4 0.7 all-gather.5.cloned.1.call-update
  17.1 1.3 broadcast_in_dim.14.vr_ref
  18.4 1.3 broadcast_in_dim.13.sr_ref
  19.7 1.7 convert_reduce_fusion.2
  21.4 0.6 fusion.29
  22.0 1.0 copy.38.sc_ref
  23.0 79.8 %all-gather.7.cloned.1.call-done = bf16[32,193,768]{2,1,0:T(8,128)(2,1)} async-done(((bf16[1,193,768]{2,1,0:T(8,128)(2,1)}), bf16[32,193,768]{2,1,0:T(8,128)(2,1)}) %all-gather.7.cloned.1.call-update) | async-done | bytes 9486352 | tf_op jit(solution)/shard_map/all_gather | solution.py:370
  102.8 1.0 slice.118
  103.8 0.1 slice_convert_fusion.1
  103.9 0.1 slice_convert_fusion
  104.0 0.1 slice.98
  104.0 0.1 slice.100
  104.1 0.1 reshape.239
  104.2 0.7 reshape.240
  104.9 0.1 reshape.237
  104.9 0.1 reshape.234
  105.0 0.1 reshape.238
  105.1 0.1 reshape.235
  105.2 0.1 reshape.236
  105.3 4.8 %slice.129 = bf16[32,96,768]{2,1,0:T(8,128)(2,1)} slice(bf16[32,193,768]{2,1,0:T(8,128)(2,1)} %all-gather.7.cloned.1.call-done), slice={[0:32], [96:192], [0:768]} | slice | bytes 9437184 | tf_op jit(solution)/shard_map/slice | solution.py:373
  110.1 8.5 %reshape.216 = bf16[768,3072]{1,0:T(8,128)(2,1)} reshape(bf16[32,96,768]{2,1,0:T(8,128)(2,1)} %slice.129) | data formatting | bytes 9437184 | tf_op jit(solution)/shard_map/reshape | solution.py:373
  118.6 4.0 slice.121
  122.6 6.6 %reshape.214 = bf16[768,2304]{1,0:T(8,128)(2,1)} reshape(bf16[32,72,768]{2,1,0:T(8,128)(2,1)} %slice.121) | data formatting | bytes 7077888 | tf_op jit(solution)/shard_map/reshape | solution.py:371
  129.2 8.0 %add_convert_fusion.q_ref.k_ref.v_ref = bf16[1024,2304]{1,0:T(8,128)(2,1)} fusion(bf16[768,2304]{1,0:T(8,128)(2,1)} %reshape.214, f32[2304]{0:T(1024)S(1)} %pad_maximum_fusion.1, bf16[1024,768]{1,0:T(8,128)(2,1)S(1)} %copy-done.3, f32[768]{0:T(1024)S(1)} %reshape.235, f32[768]{0:T(1024)S(1)} %reshape.234, f32[1024]{0:T(1024)S(1)} %add_rsqrt_fusion.1, ...), kind=kOutput, calls=%fused_computation.28 | convolution fusion | flops 3633315840 | bytes 9853952 | tf_op jit(solution)/shard_map/dot_general | solution.py:384
  137.2 29.8 %shard_map.263 = bf16[1024,768]{1,0:T(8,128)(2,1)} custom-call(bf16[1024,2304]{1,0:T(8,128)(2,1)} %add_convert_fusion.q_ref.k_ref.v_ref, bf16[1024,2304]{1,0:T(8,128)(2,1)} %add_convert_fusion.q_ref.k_ref.v_ref, bf16[1024,2304]{1,0:T(8,128)(2,1)} %add_convert_fusion.q_ref.k_ref.v_ref, s32[2,512,1]{2,1,0:T(8,128)} %copy.38.sc_ref, ...), custom_call_target="tpu_custom_call" | custom-call | flops 1610612736 | bytes 6291456 | tf_op jit(solution)/shard_map/pallas_call | solution.py:105
  167.0 1.5 slice.125
  168.6 3.9 fusion.41
  172.5 0.5 multiply_reduce_fusion.2
  173.1 34.4 %fusion.2 = (bf16[1024,3072]{1,0:T(8,128)(2,1)S(1)}, f32[1024,3072]{1,0:T(8,128)}) fusion(f32[3072]{0:T(1024)S(1)} %reshape.239, bf16[768,3072]{1,0:T(8,128)(2,1)S(1)} %bitcast.50, f32[1024,768]{1,0:T(8,128)S(1)} %get-tuple-element.50, f32[768]{0:T(1024)S(1)} %reshape.238, f32[768]{0:T(1024)S(1)} %reshape.237, f32[1024]{0:T(1024)S(1)} %add_rsqrt_fusion, ...), kind=kOutput, calls=%fused_computation.4 | convolution fusion | flops 5043388416 | bytes 26765312 | tf_op jit(solution)/shard_map/dot_general | solution.py:398
  207.5 2.6 copy-done.14
  210.1 7.7 %fusion.42 = f32[3072,768]{1,0:T(8,128)} fusion(bf16[1024,3072]{1,0:T(8,128)(2,1)S(1)} %get-tuple-element.51, bf16[1024,768]{1,0:T(8,128)(2,1)S(1)} %copy-done.7), kind=kOutput, calls=%fused_computation.96 | convolution fusion | flops 4831838208 | bytes 17301504 | tf_op jit(solution)/shard_map/tf,td->fd/dot_general | solution.py:409
  217.9 14.5 %convert_reduce_fusion = (f32[3072]{0:T(1024)S(1)}, bf16[1024,3072]{1,0:T(8,128)(2,1)}) fusion(f32[1024,3072]{1,0:T(8,128)} %get-tuple-element.52, f32[3072]{0:T(1024)S(1)} %reshape.239, bf16[1024,768]{1,0:T(8,128)(2,1)} %param.31, bf16[3072,768]{1,0:T(8,128)(2,1)} %all-gather.5.cloned.1.call-done), kind=kOutput, calls=%fused_computation.11 | convolution fusion | flops 4872729600 | bytes 25190400 | tf_op jit(solution)/shard_map/td,fd->tf/dot_general | solution.py:411
  232.3 0.1 reshape.222
  232.4 9.7 %multiply_reduce_fusion = (f32[768]{0:T(1024)S(1)}, f32[1024]{0:T(1024)S(1)}, f32[1024]{0:T(1024)S(1)}, f32[768]{0:T(1024)S(1)}, f32[1024,768]{1,0:T(8,128)S(1)}) fusion(f32[1024,768]{1,0:T(8,128)S(1)} %get-tuple-element.50, f32[1024]{0:T(1024)S(1)} %add_rsqrt_fusion, f32[1024]{0:T(1024)S(1)} %broadcast_multiply_fusion.4, f32[768]{0:T(1024)S(1)} %reshape.237, ...), kind=kOutput, calls=%fused_computation.49 | convolution fusion | flops 4838912000 | bytes 17327104 | tf_op jit(solution)/shard_map/tf,df->td/dot_general | solution.py:417
  242.2 2.6 convert_reduce_fusion.4
  244.8 0.1 reshape.217
  244.9 0.1 reshape.220
  245.0 0.1 reshape.223
  245.1 0.1 reshape.221
  245.1 5.0 %convolution_convert_fusion.do_ref = bf16[1024,768]{1,0:T(8,128)(2,1)} fusion(bf16[768,768]{1,0:T(8,128)(2,1)} %bitcast.52, f32[1024,768]{1,0:T(8,128)} %get-tuple-element.31), kind=kOutput, calls=%fused_computation.58 | convolution fusion | flops 1209532416 | bytes 5898240 | tf_op jit(solution)/shard_map/td,cd->tc/dot_general | solution.py:424
  250.1 36.4 %shard_map.264 = bf16[1024,2304]{1,0:T(8,128)(2,1)} custom-call(bf16[1024,2304]{1,0:T(8,128)(2,1)} %add_convert_fusion.q_ref.k_ref.v_ref, bf16[1024,2304]{1,0:T(8,128)(2,1)} %add_convert_fusion.q_ref.k_ref.v_ref, bf16[1024,2304]{1,0:T(8,128)(2,1)} %add_convert_fusion.q_ref.k_ref.v_ref, bf16[1024,768]{1,0:T(8,128)(2,1)} %convolution_convert_fusion.do_ref, ...), custom_call_target="tpu_custom_call" | custom-call | flops 4026531840 | bytes 11010048 | tf_op jit(solution)/shard_map/pallas_call | solution.py:137
  286.5 9.4 %fusion.28 = (f32[768]{0:T(1024)S(1)}, f32[1024]{0:T(1024)S(1)}, f32[1024]{0:T(1024)S(1)}, f32[768]{0:T(1024)S(1)}, f32[1024,768]{1,0:T(8,128)}) fusion(bf16[1024,768]{1,0:T(8,128)(2,1)S(1)} %copy-done.4, f32[1024]{0:T(1024)S(1)} %add_rsqrt_fusion.1, f32[1024]{0:T(1024)S(1)} %broadcast_multiply_fusion.5, f32[768]{0:T(1024)S(1)} %reshape.234, ...), kind=kOutput, calls=%fused_computation.46 | convolution fusion | flops 3631739392 | bytes 13001728 | tf_op jit(solution)/shard_map/te,de->td/dot_general | solution.py:431
  295.9 0.1 reshape.218
  296.0 3.3 convert_reduce_fusion.1
  299.3 0.1 concatenate.23
  299.4 0.1 concatenate.24
  299.4 0.1 reshape.219
  299.5 0.1 concatenate.26
  299.8 3.5 fusion.31.refs_1_
  303.3 4.7 fusion.27.refs_4_
  308.0 6.1 %fusion.34.refs_0_ = f32[768,2304]{1,0:T(8,128)} fusion(bf16[1024,2304]{1,0:T(8,128)(2,1)S(1)} %bitcast.46, bf16[1024,768]{1,0:T(8,128)(2,1)S(1)} %copy-done.4, f32[768]{0:T(1024)S(1)} %copy-done.11, f32[768]{0:T(1024)S(1)} %reshape.234, f32[1024]{0:T(1024)S(1)} %add_rsqrt_fusion.1, f32[1024]{0:T(1024)S(1)} %broadcast_multiply_fusion.5), kind=kOutput, calls=%fused_computation.90 | convolution fusion | flops 3628597248 | bytes 13383680 | tf_op jit(solution)/shard_map/td,te->de/dot_general | solution.py:430
  314.1 7.4 %add_convert_fusion.1.refs_5_ = bf16[1024,768]{1,0:T(8,128)(2,1)S(1)} fusion(f32[1024,768]{1,0:T(8,128)S(1)} %copy-done.2, bf16[1024,3072]{1,0:T(8,128)(2,1)} %copy-done.14, bf16[3072,768]{1,0:T(8,128)(2,1)S(1)} %bitcast.58, f32[768]{0:T(1024)S(1)} %copy-done.13), kind=kOutput, calls=%fused_computation.52 | convolution fusion | flops 4834197504 | bytes 15731712 | tf_op jit(solution)/shard_map/dot_general | solution.py:404
  321.6 8.7 %fusion.37.refs_2_ = f32[768,3072]{1,0:T(8,128)} fusion(bf16[1024,3072]{1,0:T(8,128)(2,1)S(1)} %bitcast.48, f32[1024,768]{1,0:T(8,128)S(1)} %copy-done.2, f32[768]{0:T(1024)S(1)} %reshape.238, f32[768]{0:T(1024)S(1)} %reshape.237, f32[1024]{0:T(1024)S(1)} %add_rsqrt_fusion, f32[1024]{0:T(1024)S(1)} %broadcast_multiply_fusion.4), kind=kOutput, calls=%fused_computation.91 | convolution fusion | flops 4835770368 | bytes 18888704 | tf_op jit(solution)/shard_map/td,tf->df/dot_general | solution.py:416
  330.3 128.2 %shard_map.265 = (f32[24,2304]{1,0:T(8,128)S(1)}, f32[24,768]{1,0:T(8,128)S(1)}, f32[24,3072]{1,0:T(8,128)S(1)}, f32[8,128]{1,0:T(8,128)S(1)}) custom-call(f32[768,2304]{1,0:T(8,128)} %fusion.34.refs_0_, f32[768,768]{1,0:T(8,128)S(1)} %fusion.31.refs_1_, f32[768,3072]{1,0:T(8,128)} %fusion.37.refs_2_, f32[256,128]{1,0:T(8,128)S(1)} %reshape.224.refs_3_, ...), custom_call_target="tpu_custom_call" | custom-call | flops 4751360 | bytes 38010880 | tf_op jit(solution)/shard_map/pallas_call | solution.py:303
  458.5 0.6 slice_bitcast_fusion.1
  459.1 0.5 slice_bitcast_fusion.7
  459.6 0.6 slice_bitcast_fusion
  460.2 0.7 copy.48
  460.9 0.6 copy.49
  461.5 0.7 copy.50
  (74 shorter events, 0.4 us)
Async XLA Ops:
  7.2 14.8 %copy-start.12 = (s32[2,512]{1,0:T(2,128)S(1)}, s32[2,512]{1,0:T(2,128)}, u32[]{:S(2)}) copy-start(s32[2,512]{1,0:T(2,128)} %param.29) | copy-start | bytes 12292
  7.2 14.2 %copy-start.3 = (bf16[1024,768]{1,0:T(8,128)(2,1)S(1)}, bf16[1024,768]{1,0:T(8,128)(2,1)}, u32[]{:S(2)}) copy-start(bf16[1024,768]{1,0:T(8,128)(2,1)} %param.16) | copy-start | bytes 4718596
  7.2 95.6 %all-gather.7.cloned.1.call-start = ((), (), s32[]{:S(2)}) async-start(), calls=%async_computation.3 | async-start | bytes 10137600 | tf_op jit(solution)/shard_map/all_gather | solution.py:370
  16.3 201.5 %all-gather.5.cloned.1.call-start = ((), (), s32[]{:S(2)}) async-start(), calls=%async_computation.1 | async-start | bytes 4866048 | tf_op jit(solution)/shard_map/all_gather | solution.py:376
  17.1 443.1 %reduce-scatter.2.cloned.1.call-start = ((), (), s32[]{:S(2)}) async-start(), calls=%async_computation.2 | async-start | bytes 9732096 | tf_op jit(solution)/shard_map/reduce_scatter | solution.py:447
  105.2 24.0 %copy-start.10 = (f32[768]{0:T(1024)}, f32[768]{0:T(1024)S(1)}, u32[]{:S(2)}) copy-start(f32[768]{0:T(1024)S(1)} %reshape.235) | copy-start | bytes 9220
  167.0 6.0 %slice-start.4 = ((s8[4718592]{0:T(1024)(128)(4,1)}), s8[4194304]{0:T(1024)(128)(4,1)S(1)}, s32[]{:S(2)}) async-start(s8[4718592]{0:T(1024)(128)(4,1)} %bitcast.49), calls=%async_computation.8 | async-start | bytes 8388608
  168.6 4.0 copy-start.9
  168.6 4.5 slice-start.5
  172.5 69.6 %copy-start.1 = (f32[1024,768]{1,0:T(8,128)}, f32[1024,768]{1,0:T(8,128)S(1)}, u32[]{:S(2)}) copy-start(f32[1024,768]{1,0:T(8,128)S(1)} %get-tuple-element.50) | copy-start | bytes 9437188
  173.1 37.0 %copy-start.7 = (bf16[1024,768]{1,0:T(8,128)(2,1)S(1)}, bf16[1024,768]{1,0:T(8,128)(2,1)}, u32[]{:S(2)}) copy-start(bf16[1024,768]{1,0:T(8,128)(2,1)} %param.31) | copy-start | bytes 4718596
  207.5 2.6 copy-start.14
  232.4 9.7 %copy-start.8 = (bf16[1024,768]{1,0:T(8,128)(2,1)S(1)}, bf16[1024,768]{1,0:T(8,128)(2,1)}, u32[]{:S(2)}) copy-start(bf16[1024,768]{1,0:T(8,128)(2,1)} %param.31) | copy-start | bytes 4718596
  250.1 36.4 %copy-start.4 = (bf16[1024,768]{1,0:T(8,128)(2,1)S(1)}, bf16[1024,768]{1,0:T(8,128)(2,1)}, u32[]{:S(2)}) copy-start(bf16[1024,768]{1,0:T(8,128)(2,1)} %param.16) | copy-start | bytes 4718596
  295.9 3.8 copy-start.6
  299.7 3.5 copy-start.5
  299.7 8.2 %slice-start = ((s8[4718592]{0:T(1024)(128)(4,1)}), s8[4194304]{0:T(1024)(128)(4,1)S(1)}, s32[]{:S(2)}) async-start(s8[4718592]{0:T(1024)(128)(4,1)} %bitcast.45), calls=%async_computation.4 | async-start | bytes 8388608
  299.8 14.4 %slice-start.6 = ((s8[4718592]{0:T(1024)(128)(4,1)}), s8[4194304]{0:T(1024)(128)(4,1)S(1)}, s32[]{:S(2)}) async-start(s8[4718592]{0:T(1024)(128)(4,1)} %bitcast.57), calls=%async_computation.10 | async-start | bytes 8388608
  303.3 4.7 slice-start.1
  303.3 4.7 copy-start.11
  303.3 10.8 %slice-start.7 = ((s8[4718592]{0:T(1024)(128)(4,1)}), s8[524288]{0:T(1024)(128)(4,1)S(1)}, s32[]{:S(2)}) async-start(s8[4718592]{0:T(1024)(128)(4,1)} %bitcast.57), calls=%async_computation.11 | async-start | bytes 1048576
  308.0 6.2 %copy-start.2 = (f32[1024,768]{1,0:T(8,128)S(1)}, f32[1024,768]{1,0:T(8,128)}, u32[]{:S(2)}) copy-start(f32[1024,768]{1,0:T(8,128)} %copy-done.1) | copy-start | bytes 9437188
  308.0 6.2 %copy-start.13 = (f32[768]{0:T(1024)S(1)}, f32[768]{0:T(1024)}, u32[]{:S(2)}) copy-start(f32[768]{0:T(1024)} %reshape.240) | copy-start | bytes 9220
  308.0 13.6 %slice-start.2 = ((s8[6291456]{0:T(1024)(128)(4,1)}), s8[4194304]{0:T(1024)(128)(4,1)S(1)}, s32[]{:S(2)}) async-start(s8[6291456]{0:T(1024)(128)(4,1)} %bitcast.47), calls=%async_computation.6 | async-start | bytes 8388608
  314.1 7.5 %slice-start.3 = ((s8[6291456]{0:T(1024)(128)(4,1)}), s8[2097152]{0:T(1024)(128)(4,1)S(1)}, s32[]{:S(2)}) async-start(s8[6291456]{0:T(1024)(128)(4,1)} %bitcast.47), calls=%async_computation.7 | async-start | bytes 4194304
  321.6 8.7 %copy-start = (bf16[1024,768]{1,0:T(8,128)(2,1)}, bf16[1024,768]{1,0:T(8,128)(2,1)S(1)}, u32[]{:S(2)}) copy-start(bf16[1024,768]{1,0:T(8,128)(2,1)S(1)} %add_convert_fusion.1.refs_5_) | copy-start | bytes 4718596
Sparse Core Ops, SparseCore 0:
  16.4 86.3 all-gather.6
  105.7 62.2 all-gather.4
  218.0 133.2 reduce-scatter.1

commit v11 on v10

--- a/solution.py
+++ b/solution.py
@@ -355,20 +355,21 @@
     small = (qv_bias, out_bias, ln1_gain, ln1_shift, ln2_gain, ln2_shift, up_bias, down_bias)
     small_sizes = [a.shape[0] for a in small]
     n_small = sum(small_sizes)
-    rows_q = w_qkv.size // model_width
-    rows_o = w_out.shape[0]
-    rows_u = w_up.size // model_width
+    width_q = w_qkv.shape[1]
+    rows_q = w_qkv.shape[0]
+    rows_o = w_out.size // width_q
+    rows_u = w_up.size // width_q
     attn_buf = jnp.concatenate(
         [
-            w_qkv.reshape(rows_q, model_width),
-            w_out,
-            w_up.reshape(rows_u, model_width),
-            pack_rows(small, model_width),
+            w_qkv,
+            w_out.reshape(rows_o, width_q),
+            w_up.reshape(rows_u, width_q),
+            pack_rows(small, width_q),
         ],
         axis=0,
     )
     attn_all = lax.all_gather(attn_buf, ALL, axis=0, tiled=False)
-    qkv_full = attn_all[:, :rows_q].reshape(-1, w_qkv.shape[1])
+    qkv_full = attn_all[:, :rows_q].reshape(-1, width_q)
     out_full = attn_all[:, rows_q : rows_q + rows_o].reshape(-1, model_width)
     up_full = attn_all[:, rows_q + rows_o : rows_q + rows_o + rows_u].reshape(-1, w_up.shape[1])
     small_full = split_owned(attn_all[:, rows_q + rows_o + rows_u, :n_small], small_sizes)

time: 477 us -> 474 us (level)
  local copies, waits for them, and re-layouts: 46.1 us -> 39.3 us
    reshape x3, local copies, waits for them, and re-layouts: 8.55 us -> 3.25 us  [the longest x1 1.4 us: on_device(): out_full = attn_all[:, rows_q:rows_q + rows_o].reshape(-1, model_width)]
  transfers between devices with their start and end apart: 3 -> 3, of which waited for: 1 -> 1; matrix products, arithmetic and copies ran while one was open for 35% -> 34% of each run, Pallas kernels for 41% -> 42%
where the time goes in v11:
time: 474 us; the launch traced here: 467 us
  Pallas kernels  194 us (41%)
  matrix products  119 us (25%)
  waiting for transfers between devices  83.8 us (18%)
  local copies, waits for them, and re-layouts  39.3 us (8%)
  other arithmetic  15.2 us (3%)
  between operations  14.8 us (3%)
    pallas_call x1, Pallas kernels, ring_reduce_scatter(): pl.pallas_call(kernel, out_shape=out_shape, in_specs=[pl.BlockSpec(memory...  128 us
    all_gather x1, waiting for transfers between devices, on_device(): attn_all = lax.all_gather(attn_buf, ALL, axis=0, tiled=False)  83 us
    dot_general x1, matrix products, on_device(): jnp.dot(h_two, up_full, preferred_element_type=jnp.float32)  37.4 us
    pallas_call x1, Pallas kernels, attention_bwd(): pl.pallas_call(attn_bwd_kernel, out_shape=jax.ShapeDtypeStruct((rows, wid...  36.4 us
    pallas_call x1, Pallas kernels, attention_fwd(): pl.pallas_call(attn_fwd_kernel, out_shape=jax.ShapeDtypeStruct((rows, mod...  29.8 us
    dot_general x1, matrix products, on_device(): jnp.einsum('td,fd->tf', cotangent, down_full, preferred_element_type=jnp....  14.5 us
    dot_general x1, matrix products, on_device(): jnp.einsum('tf,df->td', grad_u, up_full, preferred_element_type=jnp.float32)  9.71 us
  transfers between devices with their start and end apart: 3, of which 1 were waited for; matrix products, arithmetic and copies ran while one was open for 34% of the time, Pallas kernels for 42%

profile of v11, /device:TPU:1, one launch (start us, length us, event | category | flops | bytes accessed | tf_op | source)
XLA Modules:
  0.0 466.5 jit_solution(5577798760260421448)
XLA Ops:
  7.3 5.5 %concatenate.20 = bf16[288]{0:T(512)(128)(2,1)S(1)} concatenate(bf16[48]{0:T(256)(128)(2,1)} %param.18, bf16[24]{0:T(256)(128)(2,1)} %param.20, bf16[24]{0:T(256)(128)(2,1)} %param.21, bf16[24]{0:T(256)(128)(2,1)} %param.22, bf16[24]{0:T(256)(128)(2,1)} %param.23, bf16[24]{0:T(256)(128)(2,1)} %param.24, bf16[96]{0:T(256)(128)(2,1)} %param.26, bf16[24]{0:T(256)(128)(2,1)} %param.28), dimensions={0} | concatenate | bytes 1152 | tf_op jit(solution)/shard_map/concatenate | solution.py:317
  12.8 0.8 reshape.212
  13.6 1.1 reshape.213
  14.7 1.7 maximum_bitcast_fusion
  16.4 0.7 all-gather.5.cloned.1.call-update
  17.1 1.3 broadcast_in_dim.14.vr_ref
  18.4 1.3 broadcast_in_dim.13.sr_ref
  19.7 1.7 convert_reduce_fusion.2
  21.4 0.6 fusion.29
  22.0 1.1 copy.38.sc_ref
  23.1 83.0 %all-gather.7.cloned.1.call-done = bf16[32,65,2304]{2,1,0:T(8,128)(2,1)} async-done(((bf16[1,65,2304]{2,1,0:T(8,128)(2,1)}), bf16[32,65,2304]{2,1,0:T(8,128)(2,1)}) %all-gather.7.cloned.1.call-update) | async-done | bytes 9584656 | tf_op jit(solution)/shard_map/all_gather | solution.py:371
  106.1 1.1 slice.118
  107.2 0.1 slice_convert_fusion.1
  107.3 0.1 slice_convert_fusion
  107.4 0.1 slice.98
  107.5 0.1 slice.100
  107.5 0.1 reshape.239
  107.6 0.7 reshape.240
  108.3 0.1 reshape.237
  108.4 0.1 reshape.234
  108.5 0.1 reshape.238
  108.5 0.1 reshape.235
  108.6 0.1 reshape.236
  108.7 1.4 reshape.215
  110.1 4.8 %slice.129 = bf16[32,32,2304]{2,1,0:T(8,128)(2,1)} slice(bf16[32,65,2304]{2,1,0:T(8,128)(2,1)} %all-gather.7.cloned.1.call-done), slice={[0:32], [32:64], [0:2304]} | slice | bytes 9437184 | tf_op jit(solution)/shard_map/slice | solution.py:374
  114.9 8.5 %reshape.216 = bf16[768,3072]{1,0:T(8,128)(2,1)} reshape(bf16[32,32,2304]{2,1,0:T(8,128)(2,1)} %slice.129) | data formatting | bytes 9437184 | tf_op jit(solution)/shard_map/reshape | solution.py:374
  123.4 2.2 slice.121
  125.6 1.7 copy-done.6
  127.4 5.9 %add_convert_fusion.q_ref.k_ref.v_ref = bf16[1024,2304]{1,0:T(8,128)(2,1)} fusion(bf16[768,2304]{1,0:T(8,128)(2,1)S(1)} %bitcast.49, f32[2304]{0:T(1024)S(1)} %pad_maximum_fusion.1, bf16[1024,768]{1,0:T(8,128)(2,1)S(1)} %copy-done.3, f32[768]{0:T(1024)S(1)} %reshape.235, f32[768]{0:T(1024)S(1)} %reshape.234, f32[1024]{0:T(1024)S(1)} %add_rsqrt_fusion.1, ...), kind=kOutput, calls=%fused_computation.28 | convolution fusion | flops 3633315840 | bytes 9853952 | tf_op jit(solution)/shard_map/dot_general | solution.py:385
  133.3 29.8 %shard_map.263 = bf16[1024,768]{1,0:T(8,128)(2,1)} custom-call(bf16[1024,2304]{1,0:T(8,128)(2,1)} %add_convert_fusion.q_ref.k_ref.v_ref, bf16[1024,2304]{1,0:T(8,128)(2,1)} %add_convert_fusion.q_ref.k_ref.v_ref, bf16[1024,2304]{1,0:T(8,128)(2,1)} %add_convert_fusion.q_ref.k_ref.v_ref, s32[2,512,1]{2,1,0:T(8,128)} %copy.38.sc_ref, ...), custom_call_target="tpu_custom_call" | custom-call | flops 1610612736 | bytes 6291456 | tf_op jit(solution)/shard_map/pallas_call | solution.py:105
  163.1 3.8 fusion.41
  166.9 0.5 multiply_reduce_fusion.2
  167.4 37.4 %fusion.2 = (bf16[1024,3072]{1,0:T(8,128)(2,1)S(1)}, f32[1024,3072]{1,0:T(8,128)}) fusion(f32[3072]{0:T(1024)S(1)} %reshape.239, bf16[768,3072]{1,0:T(8,128)(2,1)} %reshape.216, f32[1024,768]{1,0:T(8,128)S(1)} %get-tuple-element.50, f32[768]{0:T(1024)S(1)} %reshape.238, f32[768]{0:T(1024)S(1)} %reshape.237, f32[1024]{0:T(1024)S(1)} %add_rsqrt_fusion, ...), kind=kOutput, calls=%fused_computation.4 | convolution fusion | flops 5043388416 | bytes 26765312 | tf_op jit(solution)/shard_map/dot_general | solution.py:399
  204.9 2.6 copy-done.14
  207.5 7.7 %fusion.42 = f32[3072,768]{1,0:T(8,128)} fusion(bf16[1024,3072]{1,0:T(8,128)(2,1)S(1)} %get-tuple-element.51, bf16[1024,768]{1,0:T(8,128)(2,1)S(1)} %copy-done.8), kind=kOutput, calls=%fused_computation.96 | convolution fusion | flops 4831838208 | bytes 17301504 | tf_op jit(solution)/shard_map/tf,td->fd/dot_general | solution.py:410
  215.3 14.5 %convert_reduce_fusion = (f32[3072]{0:T(1024)S(1)}, bf16[1024,3072]{1,0:T(8,128)(2,1)}) fusion(f32[1024,3072]{1,0:T(8,128)} %get-tuple-element.52, f32[3072]{0:T(1024)S(1)} %reshape.239, bf16[1024,768]{1,0:T(8,128)(2,1)} %param.31, bf16[3072,768]{1,0:T(8,128)(2,1)} %all-gather.5.cloned.1.call-done), kind=kOutput, calls=%fused_computation.11 | convolution fusion | flops 4872729600 | bytes 25190400 | tf_op jit(solution)/shard_map/td,fd->tf/dot_general | solution.py:412
  229.8 0.1 reshape.222
  229.8 9.7 %multiply_reduce_fusion = (f32[768]{0:T(1024)S(1)}, f32[1024]{0:T(1024)S(1)}, f32[1024]{0:T(1024)S(1)}, f32[768]{0:T(1024)S(1)}, f32[1024,768]{1,0:T(8,128)S(1)}) fusion(f32[1024,768]{1,0:T(8,128)S(1)} %get-tuple-element.50, f32[1024]{0:T(1024)S(1)} %add_rsqrt_fusion, f32[1024]{0:T(1024)S(1)} %broadcast_multiply_fusion.4, f32[768]{0:T(1024)S(1)} %reshape.237, ...), kind=kOutput, calls=%fused_computation.49 | convolution fusion | flops 4838912000 | bytes 17327104 | tf_op jit(solution)/shard_map/tf,df->td/dot_general | solution.py:418
  239.6 2.6 convert_reduce_fusion.4
  242.2 0.1 reshape.217
  242.3 0.1 reshape.220
  242.4 0.1 reshape.223
  242.5 0.1 reshape.221
  242.6 5.0 %convolution_convert_fusion.do_ref = bf16[1024,768]{1,0:T(8,128)(2,1)} fusion(bf16[768,768]{1,0:T(8,128)(2,1)} %reshape.215, f32[1024,768]{1,0:T(8,128)} %get-tuple-element.31), kind=kOutput, calls=%fused_computation.58 | convolution fusion | flops 1209532416 | bytes 5898240 | tf_op jit(solution)/shard_map/td,cd->tc/dot_general | solution.py:425
  247.5 36.4 %shard_map.264 = bf16[1024,2304]{1,0:T(8,128)(2,1)} custom-call(bf16[1024,2304]{1,0:T(8,128)(2,1)} %add_convert_fusion.q_ref.k_ref.v_ref, bf16[1024,2304]{1,0:T(8,128)(2,1)} %add_convert_fusion.q_ref.k_ref.v_ref, bf16[1024,2304]{1,0:T(8,128)(2,1)} %add_convert_fusion.q_ref.k_ref.v_ref, bf16[1024,768]{1,0:T(8,128)(2,1)} %convolution_convert_fusion.do_ref, ...), custom_call_target="tpu_custom_call" | custom-call | flops 4026531840 | bytes 11010048 | tf_op jit(solution)/shard_map/pallas_call | solution.py:137
  283.9 9.4 %fusion.28 = (f32[768]{0:T(1024)S(1)}, f32[1024]{0:T(1024)S(1)}, f32[1024]{0:T(1024)S(1)}, f32[768]{0:T(1024)S(1)}, f32[1024,768]{1,0:T(8,128)}) fusion(bf16[1024,768]{1,0:T(8,128)(2,1)S(1)} %copy-done.4, f32[1024]{0:T(1024)S(1)} %add_rsqrt_fusion.1, f32[1024]{0:T(1024)S(1)} %broadcast_multiply_fusion.5, f32[768]{0:T(1024)S(1)} %reshape.234, ...), kind=kOutput, calls=%fused_computation.46 | convolution fusion | flops 3631739392 | bytes 13001728 | tf_op jit(solution)/shard_map/te,de->td/dot_general | solution.py:432
  293.4 0.1 reshape.218
  293.4 3.3 convert_reduce_fusion.1
  296.8 0.1 concatenate.23
  296.8 0.1 concatenate.24
  296.9 0.1 reshape.219
  297.0 0.1 concatenate.26
  297.2 3.5 fusion.31.refs_1_
  300.8 4.7 fusion.27.refs_4_
  305.5 6.2 %fusion.34.refs_0_ = f32[768,2304]{1,0:T(8,128)} fusion(bf16[1024,2304]{1,0:T(8,128)(2,1)S(1)} %bitcast.46, bf16[1024,768]{1,0:T(8,128)(2,1)S(1)} %copy-done.4, f32[768]{0:T(1024)S(1)} %copy-done.11, f32[768]{0:T(1024)S(1)} %reshape.234, f32[1024]{0:T(1024)S(1)} %add_rsqrt_fusion.1, f32[1024]{0:T(1024)S(1)} %broadcast_multiply_fusion.5), kind=kOutput, calls=%fused_computation.90 | convolution fusion | flops 3628597248 | bytes 13383680 | tf_op jit(solution)/shard_map/td,te->de/dot_general | solution.py:431
  311.7 7.4 %add_convert_fusion.1.refs_5_ = bf16[1024,768]{1,0:T(8,128)(2,1)S(1)} fusion(f32[1024,768]{1,0:T(8,128)S(1)} %copy-done.2, bf16[1024,3072]{1,0:T(8,128)(2,1)} %copy-done.14, bf16[3072,768]{1,0:T(8,128)(2,1)S(1)} %bitcast.56, f32[768]{0:T(1024)S(1)} %copy-done.13), kind=kOutput, calls=%fused_computation.52 | convolution fusion | flops 4834197504 | bytes 15731712 | tf_op jit(solution)/shard_map/dot_general | solution.py:405
  319.2 8.5 %fusion.37.refs_2_ = f32[768,3072]{1,0:T(8,128)} fusion(bf16[1024,3072]{1,0:T(8,128)(2,1)S(1)} %bitcast.48, f32[1024,768]{1,0:T(8,128)S(1)} %copy-done.2, f32[768]{0:T(1024)S(1)} %reshape.238, f32[768]{0:T(1024)S(1)} %reshape.237, f32[1024]{0:T(1024)S(1)} %add_rsqrt_fusion, f32[1024]{0:T(1024)S(1)} %broadcast_multiply_fusion.4), kind=kOutput, calls=%fused_computation.91 | convolution fusion | flops 4835770368 | bytes 18888704 | tf_op jit(solution)/shard_map/td,tf->df/dot_general | solution.py:417
  327.7 128.0 %shard_map.265 = (f32[24,2304]{1,0:T(8,128)S(1)}, f32[24,768]{1,0:T(8,128)S(1)}, f32[24,3072]{1,0:T(8,128)S(1)}, f32[8,128]{1,0:T(8,128)S(1)}) custom-call(f32[768,2304]{1,0:T(8,128)} %fusion.34.refs_0_, f32[768,768]{1,0:T(8,128)S(1)} %fusion.31.refs_1_, f32[768,3072]{1,0:T(8,128)} %fusion.37.refs_2_, f32[256,128]{1,0:T(8,128)S(1)} %reshape.224.refs_3_, ...), custom_call_target="tpu_custom_call" | custom-call | flops 4751360 | bytes 38010880 | tf_op jit(solution)/shard_map/pallas_call | solution.py:303
  455.8 0.6 slice_bitcast_fusion.1
  456.3 0.5 slice_bitcast_fusion.7
  456.9 0.6 slice_bitcast_fusion
  457.5 0.7 copy.48
  458.1 0.6 copy.49
  458.8 0.7 copy.50
  (70 shorter events, 0.4 us)
Async XLA Ops:
  7.2 14.9 %copy-start.12 = (s32[2,512]{1,0:T(2,128)S(1)}, s32[2,512]{1,0:T(2,128)}, u32[]{:S(2)}) copy-start(s32[2,512]{1,0:T(2,128)} %param.29) | copy-start | bytes 12292
  7.2 14.2 %copy-start.3 = (bf16[1024,768]{1,0:T(8,128)(2,1)S(1)}, bf16[1024,768]{1,0:T(8,128)(2,1)}, u32[]{:S(2)}) copy-start(bf16[1024,768]{1,0:T(8,128)(2,1)} %param.16) | copy-start | bytes 4718596
  7.2 98.9 %all-gather.7.cloned.1.call-start = ((), (), s32[]{:S(2)}) async-start(), calls=%async_computation.3 | async-start | bytes 10948608 | tf_op jit(solution)/shard_map/all_gather | solution.py:371
  16.3 198.9 %all-gather.5.cloned.1.call-start = ((), (), s32[]{:S(2)}) async-start(), calls=%async_computation.1 | async-start | bytes 4866048 | tf_op jit(solution)/shard_map/all_gather | solution.py:377
  17.1 440.4 %reduce-scatter.2.cloned.1.call-start = ((), (), s32[]{:S(2)}) async-start(), calls=%async_computation.2 | async-start | bytes 9732096 | tf_op jit(solution)/shard_map/reduce_scatter | solution.py:448
  106.1 2.6 slice-start.2
  108.6 17.0 %copy-start.10 = (f32[768]{0:T(1024)}, f32[768]{0:T(1024)S(1)}, u32[]{:S(2)}) copy-start(f32[768]{0:T(1024)S(1)} %reshape.235) | copy-start | bytes 9220
  125.6 1.7 copy-start.6
  166.9 72.7 %copy-start.1 = (f32[1024,768]{1,0:T(8,128)}, f32[1024,768]{1,0:T(8,128)S(1)}, u32[]{:S(2)}) copy-start(f32[1024,768]{1,0:T(8,128)S(1)} %get-tuple-element.50) | copy-start | bytes 9437188
  167.4 40.1 %copy-start.8 = (bf16[1024,768]{1,0:T(8,128)(2,1)S(1)}, bf16[1024,768]{1,0:T(8,128)(2,1)}, u32[]{:S(2)}) copy-start(bf16[1024,768]{1,0:T(8,128)(2,1)} %param.31) | copy-start | bytes 4718596
  204.9 2.6 copy-start.14
  229.8 9.7 %copy-start.9 = (bf16[1024,768]{1,0:T(8,128)(2,1)S(1)}, bf16[1024,768]{1,0:T(8,128)(2,1)}, u32[]{:S(2)}) copy-start(bf16[1024,768]{1,0:T(8,128)(2,1)} %param.31) | copy-start | bytes 4718596
  247.5 36.4 %copy-start.4 = (bf16[1024,768]{1,0:T(8,128)(2,1)S(1)}, bf16[1024,768]{1,0:T(8,128)(2,1)}, u32[]{:S(2)}) copy-start(bf16[1024,768]{1,0:T(8,128)(2,1)} %param.16) | copy-start | bytes 4718596
  293.4 3.8 copy-start.7
  297.2 3.5 copy-start.5
  297.2 8.2 %slice-start = ((s8[4718592]{0:T(1024)(128)(4,1)}), s8[4194304]{0:T(1024)(128)(4,1)S(1)}, s32[]{:S(2)}) async-start(s8[4718592]{0:T(1024)(128)(4,1)} %bitcast.45), calls=%async_computation.4 | async-start | bytes 8388608
  297.2 14.4 %slice-start.5 = ((s8[4718592]{0:T(1024)(128)(4,1)}), s8[4194304]{0:T(1024)(128)(4,1)S(1)}, s32[]{:S(2)}) async-start(s8[4718592]{0:T(1024)(128)(4,1)} %bitcast.55), calls=%async_computation.9 | async-start | bytes 8388608
  300.7 4.7 %slice-start.1 = ((s8[4718592]{0:T(1024)(128)(4,1)}), s8[524288]{0:T(1024)(128)(4,1)S(1)}, s32[]{:S(2)}) async-start(s8[4718592]{0:T(1024)(128)(4,1)} %bitcast.45), calls=%async_computation.5 | async-start | bytes 1048576
  300.7 4.7 %copy-start.11 = (f32[768]{0:T(1024)S(1)}, f32[768]{0:T(1024)}, u32[]{:S(2)}) copy-start(f32[768]{0:T(1024)} %copy-done.10) | copy-start | bytes 9220
  300.8 10.9 %slice-start.6 = ((s8[4718592]{0:T(1024)(128)(4,1)}), s8[524288]{0:T(1024)(128)(4,1)S(1)}, s32[]{:S(2)}) async-start(s8[4718592]{0:T(1024)(128)(4,1)} %bitcast.55), calls=%async_computation.10 | async-start | bytes 1048576
  305.4 6.2 %copy-start.2 = (f32[1024,768]{1,0:T(8,128)S(1)}, f32[1024,768]{1,0:T(8,128)}, u32[]{:S(2)}) copy-start(f32[1024,768]{1,0:T(8,128)} %copy-done.1) | copy-start | bytes 9437188
  305.4 6.2 %copy-start.13 = (f32[768]{0:T(1024)S(1)}, f32[768]{0:T(1024)}, u32[]{:S(2)}) copy-start(f32[768]{0:T(1024)} %reshape.240) | copy-start | bytes 9220
  305.5 13.7 %slice-start.3 = ((s8[6291456]{0:T(1024)(128)(4,1)}), s8[4194304]{0:T(1024)(128)(4,1)S(1)}, s32[]{:S(2)}) async-start(s8[6291456]{0:T(1024)(128)(4,1)} %bitcast.47), calls=%async_computation.7 | async-start | bytes 8388608
  311.7 7.5 %slice-start.4 = ((s8[6291456]{0:T(1024)(128)(4,1)}), s8[2097152]{0:T(1024)(128)(4,1)S(1)}, s32[]{:S(2)}) async-start(s8[6291456]{0:T(1024)(128)(4,1)} %bitcast.47), calls=%async_computation.8 | async-start | bytes 4194304
  319.2 8.6 %copy-start = (bf16[1024,768]{1,0:T(8,128)(2,1)}, bf16[1024,768]{1,0:T(8,128)(2,1)S(1)}, u32[]{:S(2)}) copy-start(bf16[1024,768]{1,0:T(8,128)(2,1)S(1)} %add_convert_fusion.1.refs_5_) | copy-start | bytes 4718596
Sparse Core Ops, SparseCore 0:
  16.5 89.6 all-gather.6
  109.0 62.1 all-gather.4
  215.4 133.2 reduce-scatter.1

commit v12 on v11

--- a/solution.py
+++ b/solution.py
@@ -311,6 +311,100 @@
         ),
         cost_estimate=pl.CostEstimate(flops=total // 4, transcendentals=0, bytes_accessed=2 * total),
     )(*[a for (a, _, _) in parts], *after)
+
+
+def ring_all_gather(parts, mesh_shape, collective_id=1):
+    n_wide, n_narrow = mesh_shape
+    n_dev, pos_of, coords_of = ring_maps(n_wide, n_narrow)
+    n_in = len(parts)
+    steps = (n_dev // 2, n_dev - 1 - n_dev // 2)
+
+    def kernel(*refs):
+        ins = refs[:n_in]
+        outs = refs[n_in : 2 * n_in]
+        send_sem, recv_sem, loc_sem = refs[2 * n_in :]
+        p = pos_of(lax.axis_index("wide"), lax.axis_index("narrow"))
+        right = coords_of((p + 1) % n_dev)
+        left = coords_of((p + n_dev - 1) % n_dev)
+        nbr_send = (right, left)
+
+        def rows_of(q, rb):
+            cw, cn = coords_of(q % n_dev)
+            return pl.ds(pl.multiple_of((cw * n_narrow + cn) * rb, rb), rb)
+
+        def copy(i, dirn, s, q):
+            view = outs[i].at[rows_of(q, parts[i].shape[0])]
+            return pltpu.make_async_remote_copy(
+                src_ref=view,
+                dst_ref=view,
+                send_sem=send_sem.at[dirn, i, s],
+                recv_sem=recv_sem.at[dirn, i, s],
+                device_id=nbr_send[dirn],
+                device_id_type=MESH_ID,
+            )
+
+        def sent(i, dirn, s):
+            return copy(i, dirn, s, (p + n_dev - s) if dirn == 0 else (p + s))
+
+        def arriving(i, dirn, s):
+            return copy(i, dirn, s, (p + n_dev - 1 - s) if dirn == 0 else (p + 1 + s))
+
+        barrier = pltpu.get_barrier_semaphore()
+        for nb in (left, right):
+            pl.semaphore_signal(barrier, 1, device_id=nb, device_id_type=MESH_ID)
+        pl.semaphore_wait(barrier, 2)
+
+        for i in range(n_in):
+            cp = pltpu.make_async_copy(ins[i], outs[i].at[rows_of(p, parts[i].shape[0])], loc_sem.at[i])
+            cp.start()
+            cp.wait()
+
+        def step(s, carry):
+            for dirn in (0, 1):
+
+                @pl.when(s < steps[dirn])
+                def _():
+                    for i in range(n_in):
+                        sent(i, dirn, s).start()
+
+            for dirn in (0, 1):
+
+                @pl.when(s < steps[dirn])
+                def _():
+                    for i in range(n_in):
+                        arriving(i, dirn, s).wait_recv()
+
+            return carry
+
+        lax.fori_loop(0, steps[0], step, 0)
+
+        def drain(s, carry):
+            for dirn in (0, 1):
+
+                @pl.when(s < steps[dirn])
+                def _():
+                    for i in range(n_in):
+                        sent(i, dirn, s).wait_send()
+
+            return carry
+
+        lax.fori_loop(0, steps[0], drain, 0)
+
+    out_shape = [jax.ShapeDtypeStruct((n_dev * a.shape[0], a.shape[1]), a.dtype) for a in parts]
+    total = sum(n_dev * a.size * a.dtype.itemsize for a in parts)
+    return pl.pallas_call(
+        kernel,
+        out_shape=out_shape,
+        in_specs=[pl.BlockSpec(memory_space=pl.ANY)] * n_in,
+        out_specs=[pl.BlockSpec(memory_space=pltpu.VMEM)] * n_in,
+        scratch_shapes=[
+            pltpu.SemaphoreType.DMA((2, n_in, steps[0])),
+            pltpu.SemaphoreType.DMA((2, n_in, steps[0])),
+            pltpu.SemaphoreType.DMA((n_in,)),
+        ],
+        compiler_params=pltpu.CompilerParams(collective_id=collective_id, has_side_effects=True),
+        cost_estimate=pl.CostEstimate(flops=0, transcendentals=0, bytes_accessed=2 * total),
+    )(*parts)
 
 
 def pack_rows(pieces, width):
@@ -359,20 +453,23 @@
     rows_q = w_qkv.shape[0]
     rows_o = w_out.size // width_q
     rows_u = w_up.size // width_q
-    attn_buf = jnp.concatenate(
-        [
-            w_qkv,
-            w_out.reshape(rows_o, width_q),
-            w_up.reshape(rows_u, width_q),
-            pack_rows(small, width_q),
-        ],
-        axis=0,
-    )
+    up_view = 16
+    ring_up = mesh_shape == (8, 4) and w_up.size % (up_view * 128) == 0
+    pieces = [w_qkv, w_out.reshape(rows_o, width_q)]
+    if not ring_up:
+        pieces.append(w_up.reshape(rows_u, width_q))
+    attn_buf = jnp.concatenate(pieces + [pack_rows(small, width_q)], axis=0)
     attn_all = lax.all_gather(attn_buf, ALL, axis=0, tiled=False)
     qkv_full = attn_all[:, :rows_q].reshape(-1, width_q)
     out_full = attn_all[:, rows_q : rows_q + rows_o].reshape(-1, model_width)
-    up_full = attn_all[:, rows_q + rows_o : rows_q + rows_o + rows_u].reshape(-1, w_up.shape[1])
-    small_full = split_owned(attn_all[:, rows_q + rows_o + rows_u, :n_small], small_sizes)
+    at = rows_q + rows_o
+    if ring_up:
+        (up_all,) = ring_all_gather([w_up.reshape(up_view, -1)], mesh_shape)
+        up_full = up_all.reshape(-1, w_up.shape[1])
+    else:
+        up_full = attn_all[:, at : at + rows_u].reshape(-1, w_up.shape[1])
+        at = at + rows_u
+    small_full = split_owned(attn_all[:, at, :n_small], small_sizes)
     qv_full, outb_full, gain_one, shift_one, gain_two, shift_two, upb_full, downb_full = small_full
     down_full = lax.all_gather(w_down, ALL, axis=0, tiled=True)
 

time: 474 us -> 471 us (level)
  Pallas kernels: 194 us -> 279 us
  waiting for transfers between devices: 83.8 us -> 0.75 us
  local copies, waits for them, and re-layouts: 39.3 us -> 33.8 us
    all_gather x1, waiting for transfers between devices: 83 us -> 0.01 us  [on_device(): attn_all = lax.all_gather(attn_buf, ALL, axis=0, tiled=False)]
    pallas_call x0 -> x1, Pallas kernels: none -> 82.9 us  [ring_all_gather(): pl.pallas_call(kernel, out_shape=out_shape, in_specs=[pl.BlockSpec(memory...]
    slice x2 -> x1, local copies, waits for them, and re-layouts: 5.8 us -> 1.05 us  [on_device(): small_full = split_owned(attn_all[:, at, :n_small], small_sizes)]
  transfers between devices with their start and end apart: 3 -> 3, of which waited for: 1 -> 0; matrix products, arithmetic and copies ran while one was open for 34% -> 33% of each run, Pallas kernels for 42% -> 60%
where the time goes in v12:
time: 471 us; the launch traced here: 463 us
  Pallas kernels  279 us (59%)
  matrix products  119 us (25%)
  local copies, waits for them, and re-layouts  33.8 us (7%)
  other arithmetic  14.9 us (3%)
  between operations  14.8 us (3%)
    pallas_call x1, Pallas kernels, ring_reduce_scatter(): pl.pallas_call(kernel, out_shape=out_shape, in_specs=[pl.BlockSpec(memory...  130 us
    pallas_call x1, Pallas kernels, ring_all_gather(): pl.pallas_call(kernel, out_shape=out_shape, in_specs=[pl.BlockSpec(memory...  82.9 us
    dot_general x1, matrix products, on_device(): jnp.dot(h_two, up_full, preferred_element_type=jnp.float32)  37.3 us
    pallas_call x1, Pallas kernels, attention_bwd(): pl.pallas_call(attn_bwd_kernel, out_shape=jax.ShapeDtypeStruct((rows, wid...  36.4 us
    pallas_call x1, Pallas kernels, attention_fwd(): pl.pallas_call(attn_fwd_kernel, out_shape=jax.ShapeDtypeStruct((rows, mod...  29.8 us
    dot_general x1, matrix products, on_device(): jnp.einsum('td,fd->tf', cotangent, down_full, preferred_element_type=jnp....  14.3 us
    dot_general x1, matrix products, on_device(): jnp.einsum('tf,df->td', grad_u, up_full, preferred_element_type=jnp.float32)  9.72 us
    dot_general x1, matrix products, on_device(): jnp.einsum('te,de->td', grad_qkv, qkv_full, preferred_element_type=jnp.fl...  9.46 us
  transfers between devices with their start and end apart: 3, of which 0 were waited for; matrix products, arithmetic and copies ran while one was open for 33% of the time, Pallas kernels for 60%

profile of v12, /device:TPU:1, one launch (start us, length us, event | category | flops | bytes accessed | tf_op | source)
XLA Modules:
  0.0 462.5 jit_solution(12157629098174226830)
XLA Ops:
  7.3 5.5 %concatenate.20 = bf16[288]{0:T(512)(128)(2,1)S(1)} concatenate(bf16[48]{0:T(256)(128)(2,1)} %param.18, bf16[24]{0:T(256)(128)(2,1)} %param.20, bf16[24]{0:T(256)(128)(2,1)} %param.21, bf16[24]{0:T(256)(128)(2,1)} %param.22, bf16[24]{0:T(256)(128)(2,1)} %param.23, bf16[24]{0:T(256)(128)(2,1)} %param.24, bf16[96]{0:T(256)(128)(2,1)} %param.26, bf16[24]{0:T(256)(128)(2,1)} %param.28), dimensions={0} | concatenate | bytes 1152 | tf_op jit(solution)/shard_map/concatenate | solution.py:411
  12.8 0.8 reshape.212
  13.6 1.6 maximum_bitcast_fusion
  15.2 0.0 all-gather.5.cloned.1.call-start
  15.3 0.7 all-gather.5.cloned.1.call-update
  16.0 1.3 broadcast_in_dim.14.vr_ref
  17.3 1.3 broadcast_in_dim.13.sr_ref
  18.6 1.7 convert_reduce_fusion.2
  20.3 0.6 fusion.29
  20.9 0.8 reshape.215.refs_0_
  21.7 1.0 copy.38.sc_ref
  22.7 82.9 %shard_map.264 = bf16[512,4608]{1,0:T(8,128)(2,1)} custom-call(bf16[16,4608]{1,0:T(8,128)(2,1)} %reshape.215.refs_0_), custom_call_target="tpu_custom_call" | custom-call | bytes 9437184 | tf_op jit(solution)/shard_map/pallas_call | solution.py:395
  105.7 8.1 %reshape.216 = bf16[768,3072]{1,0:T(8,128)(2,1)} reshape(bf16[512,4608]{1,0:T(8,128)(2,1)} %shard_map.264) | data formatting | bytes 9437184 | tf_op jit(solution)/shard_map/reshape | solution.py:468
  113.7 1.1 slice.114
  114.8 0.1 slice_convert_fusion.1
  114.9 0.1 slice_convert_fusion
  115.0 0.1 slice.95
  115.1 0.1 slice.97
  115.1 0.1 reshape.239
  115.2 0.7 reshape.240
  115.9 0.1 reshape.237
  116.0 0.1 reshape.234
  116.1 0.1 reshape.238
  116.1 0.1 reshape.235
  116.2 0.1 reshape.236
  116.3 1.4 reshape.214
  117.7 2.2 slice.117
  120.0 1.7 copy-done.6
  121.7 6.0 %add_convert_fusion.q_ref.k_ref.v_ref = bf16[1024,2304]{1,0:T(8,128)(2,1)} fusion(bf16[768,2304]{1,0:T(8,128)(2,1)S(1)} %bitcast.49, f32[2304]{0:T(1024)S(1)} %pad_maximum_fusion.1, bf16[1024,768]{1,0:T(8,128)(2,1)S(1)} %copy-done.3, f32[768]{0:T(1024)S(1)} %reshape.235, f32[768]{0:T(1024)S(1)} %reshape.234, f32[1024]{0:T(1024)S(1)} %add_rsqrt_fusion.1, ...), kind=kOutput, calls=%fused_computation.28 | convolution fusion | flops 3633315840 | bytes 9853952 | tf_op jit(solution)/shard_map/dot_general | solution.py:482
  127.7 29.8 %shard_map.263 = bf16[1024,768]{1,0:T(8,128)(2,1)} custom-call(bf16[1024,2304]{1,0:T(8,128)(2,1)} %add_convert_fusion.q_ref.k_ref.v_ref, bf16[1024,2304]{1,0:T(8,128)(2,1)} %add_convert_fusion.q_ref.k_ref.v_ref, bf16[1024,2304]{1,0:T(8,128)(2,1)} %add_convert_fusion.q_ref.k_ref.v_ref, s32[2,512,1]{2,1,0:T(8,128)} %copy.38.sc_ref, ...), custom_call_target="tpu_custom_call" | custom-call | flops 1610612736 | bytes 6291456 | tf_op jit(solution)/shard_map/pallas_call | solution.py:105
  157.5 3.8 fusion.41
  161.3 0.5 multiply_reduce_fusion.2
  161.8 37.3 %fusion.2 = (bf16[1024,3072]{1,0:T(8,128)(2,1)S(1)}, f32[1024,3072]{1,0:T(8,128)}) fusion(f32[3072]{0:T(1024)S(1)} %reshape.239, bf16[768,3072]{1,0:T(8,128)(2,1)} %reshape.216, f32[1024,768]{1,0:T(8,128)S(1)} %get-tuple-element.50, f32[768]{0:T(1024)S(1)} %reshape.238, f32[768]{0:T(1024)S(1)} %reshape.237, f32[1024]{0:T(1024)S(1)} %add_rsqrt_fusion, ...), kind=kOutput, calls=%fused_computation.4 | convolution fusion | flops 5043388416 | bytes 26765312 | tf_op jit(solution)/shard_map/dot_general | solution.py:496
  199.2 2.6 copy-done.15
  201.8 7.7 %fusion.42 = f32[3072,768]{1,0:T(8,128)} fusion(bf16[1024,3072]{1,0:T(8,128)(2,1)S(1)} %get-tuple-element.51, bf16[1024,768]{1,0:T(8,128)(2,1)S(1)} %copy-done.8), kind=kOutput, calls=%fused_computation.96 | convolution fusion | flops 4831838208 | bytes 17301504 | tf_op jit(solution)/shard_map/tf,td->fd/dot_general | solution.py:507
  209.6 14.3 %convert_reduce_fusion = (f32[3072]{0:T(1024)S(1)}, bf16[1024,3072]{1,0:T(8,128)(2,1)}) fusion(f32[1024,3072]{1,0:T(8,128)} %get-tuple-element.52, f32[3072]{0:T(1024)S(1)} %reshape.239, bf16[1024,768]{1,0:T(8,128)(2,1)} %param.31, bf16[3072,768]{1,0:T(8,128)(2,1)} %all-gather.5.cloned.1.call-done), kind=kOutput, calls=%fused_computation.11 | convolution fusion | flops 4872729600 | bytes 25190400 | tf_op jit(solution)/shard_map/td,fd->tf/dot_general | solution.py:509
  223.9 0.1 reshape.222
  224.0 9.7 %multiply_reduce_fusion = (f32[768]{0:T(1024)S(1)}, f32[1024]{0:T(1024)S(1)}, f32[1024]{0:T(1024)S(1)}, f32[768]{0:T(1024)S(1)}, f32[1024,768]{1,0:T(8,128)S(1)}) fusion(f32[1024,768]{1,0:T(8,128)S(1)} %get-tuple-element.50, f32[1024]{0:T(1024)S(1)} %add_rsqrt_fusion, f32[1024]{0:T(1024)S(1)} %broadcast_multiply_fusion.4, f32[768]{0:T(1024)S(1)} %reshape.237, ...), kind=kOutput, calls=%fused_computation.49 | convolution fusion | flops 4838912000 | bytes 17327104 | tf_op jit(solution)/shard_map/tf,df->td/dot_general | solution.py:515
  233.7 2.6 convert_reduce_fusion.4
  236.4 0.1 reshape.217
  236.5 0.1 reshape.220
  236.5 0.1 reshape.223
  236.6 0.1 reshape.221
  236.7 5.0 %convolution_convert_fusion.do_ref = bf16[1024,768]{1,0:T(8,128)(2,1)} fusion(bf16[768,768]{1,0:T(8,128)(2,1)} %reshape.214, f32[1024,768]{1,0:T(8,128)} %get-tuple-element.31), kind=kOutput, calls=%fused_computation.58 | convolution fusion | flops 1209532416 | bytes 5898240 | tf_op jit(solution)/shard_map/td,cd->tc/dot_general | solution.py:522
  241.7 36.4 %shard_map.265 = bf16[1024,2304]{1,0:T(8,128)(2,1)} custom-call(bf16[1024,2304]{1,0:T(8,128)(2,1)} %add_convert_fusion.q_ref.k_ref.v_ref, bf16[1024,2304]{1,0:T(8,128)(2,1)} %add_convert_fusion.q_ref.k_ref.v_ref, bf16[1024,2304]{1,0:T(8,128)(2,1)} %add_convert_fusion.q_ref.k_ref.v_ref, bf16[1024,768]{1,0:T(8,128)(2,1)} %convolution_convert_fusion.do_ref, ...), custom_call_target="tpu_custom_call" | custom-call | flops 4026531840 | bytes 11010048 | tf_op jit(solution)/shard_map/pallas_call | solution.py:137
  278.1 9.5 %fusion.28 = (f32[768]{0:T(1024)S(1)}, f32[1024]{0:T(1024)S(1)}, f32[1024]{0:T(1024)S(1)}, f32[768]{0:T(1024)S(1)}, f32[1024,768]{1,0:T(8,128)}) fusion(bf16[1024,768]{1,0:T(8,128)(2,1)S(1)} %copy-done.4, f32[1024]{0:T(1024)S(1)} %add_rsqrt_fusion.1, f32[1024]{0:T(1024)S(1)} %broadcast_multiply_fusion.5, f32[768]{0:T(1024)S(1)} %reshape.234, ...), kind=kOutput, calls=%fused_computation.46 | convolution fusion | flops 3631739392 | bytes 13001728 | tf_op jit(solution)/shard_map/te,de->td/dot_general | solution.py:529
  287.6 0.1 reshape.218
  287.6 3.2 convert_reduce_fusion.1
  290.8 0.1 concatenate.23
  290.9 0.1 concatenate.24
  291.0 0.1 reshape.219
  291.1 0.1 concatenate.26
  291.3 3.6 fusion.31.refs_1_
  294.9 4.5 fusion.27.refs_4_
  299.5 6.2 %fusion.34.refs_0_ = f32[768,2304]{1,0:T(8,128)} fusion(bf16[1024,2304]{1,0:T(8,128)(2,1)S(1)} %bitcast.46, bf16[1024,768]{1,0:T(8,128)(2,1)S(1)} %copy-done.4, f32[768]{0:T(1024)S(1)} %copy-done.12, f32[768]{0:T(1024)S(1)} %reshape.234, f32[1024]{0:T(1024)S(1)} %add_rsqrt_fusion.1, f32[1024]{0:T(1024)S(1)} %broadcast_multiply_fusion.5), kind=kOutput, calls=%fused_computation.90 | convolution fusion | flops 3628597248 | bytes 13383680 | tf_op jit(solution)/shard_map/td,te->de/dot_general | solution.py:528
  305.7 7.4 %add_convert_fusion.1.refs_5_ = bf16[1024,768]{1,0:T(8,128)(2,1)S(1)} fusion(f32[1024,768]{1,0:T(8,128)S(1)} %copy-done.2, bf16[1024,3072]{1,0:T(8,128)(2,1)} %copy-done.15, bf16[3072,768]{1,0:T(8,128)(2,1)S(1)} %bitcast.56, f32[768]{0:T(1024)S(1)} %copy-done.14), kind=kOutput, calls=%fused_computation.52 | convolution fusion | flops 4834197504 | bytes 15731712 | tf_op jit(solution)/shard_map/dot_general | solution.py:502
  313.2 8.5 %fusion.37.refs_2_ = f32[768,3072]{1,0:T(8,128)} fusion(bf16[1024,3072]{1,0:T(8,128)(2,1)S(1)} %bitcast.48, f32[1024,768]{1,0:T(8,128)S(1)} %copy-done.2, f32[768]{0:T(1024)S(1)} %reshape.238, f32[768]{0:T(1024)S(1)} %reshape.237, f32[1024]{0:T(1024)S(1)} %add_rsqrt_fusion, f32[1024]{0:T(1024)S(1)} %broadcast_multiply_fusion.4), kind=kOutput, calls=%fused_computation.91 | convolution fusion | flops 4835770368 | bytes 18888704 | tf_op jit(solution)/shard_map/td,tf->df/dot_general | solution.py:514
  321.8 130.0 %shard_map.266 = (f32[24,2304]{1,0:T(8,128)S(1)}, f32[24,768]{1,0:T(8,128)S(1)}, f32[24,3072]{1,0:T(8,128)S(1)}, f32[8,128]{1,0:T(8,128)S(1)}) custom-call(f32[768,2304]{1,0:T(8,128)} %fusion.34.refs_0_, f32[768,768]{1,0:T(8,128)S(1)} %fusion.31.refs_1_, f32[768,3072]{1,0:T(8,128)} %fusion.37.refs_2_, f32[256,128]{1,0:T(8,128)S(1)} %reshape.224.refs_3_, ...), custom_call_target="tpu_custom_call" | custom-call | flops 4751360 | bytes 38010880 | tf_op jit(solution)/shard_map/pallas_call | solution.py:303
  451.8 0.6 slice_bitcast_fusion.1
  452.3 0.5 slice_bitcast_fusion.7
  452.9 0.6 slice_bitcast_fusion
  453.5 0.7 copy.48
  454.1 0.6 copy.49
  454.8 0.7 copy.50
  (72 shorter events, 0.4 us)
Async XLA Ops:
  7.2 14.5 %copy-start.13 = (s32[2,512]{1,0:T(2,128)S(1)}, s32[2,512]{1,0:T(2,128)}, u32[]{:S(2)}) copy-start(s32[2,512]{1,0:T(2,128)} %param.29) | copy-start | bytes 12292
  7.2 13.1 %copy-start.3 = (bf16[1024,768]{1,0:T(8,128)(2,1)S(1)}, bf16[1024,768]{1,0:T(8,128)(2,1)}, u32[]{:S(2)}) copy-start(bf16[1024,768]{1,0:T(8,128)(2,1)} %param.16) | copy-start | bytes 4718596
  7.2 13.7 %copy-start.10 = (bf16[24,3072]{1,0:T(8,128)(2,1)S(1)}, bf16[24,3072]{1,0:T(8,128)(2,1)}, u32[]{:S(2)}) copy-start(bf16[24,3072]{1,0:T(8,128)(2,1)} %param.25) | copy-start | bytes 442372
  7.2 106.5 %all-gather.7.cloned.1.call-start = ((), (), s32[]{:S(2)}) async-start(), calls=%async_computation.3 | async-start | bytes 6082560 | tf_op jit(solution)/shard_map/all_gather | solution.py:462
  15.2 194.3 %all-gather.5.cloned.1.call-start = ((), (), s32[]{:S(2)}) async-start(), calls=%async_computation.1 | async-start | bytes 4866048 | tf_op jit(solution)/shard_map/all_gather | solution.py:474
  16.0 437.5 %reduce-scatter.2.cloned.1.call-start = ((), (), s32[]{:S(2)}) async-start(), calls=%async_computation.2 | async-start | bytes 9732096 | tf_op jit(solution)/shard_map/reduce_scatter | solution.py:545
  113.7 2.6 slice-start.4
  116.2 3.8 copy-start.11
  120.0 1.8 copy-start.6
  161.3 72.4 %copy-start.1 = (f32[1024,768]{1,0:T(8,128)}, f32[1024,768]{1,0:T(8,128)S(1)}, u32[]{:S(2)}) copy-start(f32[1024,768]{1,0:T(8,128)S(1)} %get-tuple-element.50) | copy-start | bytes 9437188
  161.8 40.0 %copy-start.8 = (bf16[1024,768]{1,0:T(8,128)(2,1)S(1)}, bf16[1024,768]{1,0:T(8,128)(2,1)}, u32[]{:S(2)}) copy-start(bf16[1024,768]{1,0:T(8,128)(2,1)} %param.31) | copy-start | bytes 4718596
  199.2 2.6 copy-start.15
  224.0 9.8 %copy-start.9 = (bf16[1024,768]{1,0:T(8,128)(2,1)S(1)}, bf16[1024,768]{1,0:T(8,128)(2,1)}, u32[]{:S(2)}) copy-start(bf16[1024,768]{1,0:T(8,128)(2,1)} %param.31) | copy-start | bytes 4718596
  241.7 36.4 %copy-start.4 = (bf16[1024,768]{1,0:T(8,128)(2,1)S(1)}, bf16[1024,768]{1,0:T(8,128)(2,1)}, u32[]{:S(2)}) copy-start(bf16[1024,768]{1,0:T(8,128)(2,1)} %param.16) | copy-start | bytes 4718596
  287.6 3.7 copy-start.7
  291.3 3.6 copy-start.5
  291.3 8.2 %slice-start = ((s8[4718592]{0:T(1024)(128)(4,1)}), s8[4194304]{0:T(1024)(128)(4,1)S(1)}, s32[]{:S(2)}) async-start(s8[4718592]{0:T(1024)(128)(4,1)} %bitcast.45), calls=%async_computation.4 | async-start | bytes 8388608
  291.3 14.4 %slice-start.5 = ((s8[4718592]{0:T(1024)(128)(4,1)}), s8[4194304]{0:T(1024)(128)(4,1)S(1)}, s32[]{:S(2)}) async-start(s8[4718592]{0:T(1024)(128)(4,1)} %bitcast.55), calls=%async_computation.9 | async-start | bytes 8388608
  294.9 4.5 slice-start.1
  294.9 4.5 copy-start.12
  294.9 10.8 %slice-start.6 = ((s8[4718592]{0:T(1024)(128)(4,1)}), s8[524288]{0:T(1024)(128)(4,1)S(1)}, s32[]{:S(2)}) async-start(s8[4718592]{0:T(1024)(128)(4,1)} %bitcast.55), calls=%async_computation.10 | async-start | bytes 1048576
  299.5 6.2 %copy-start.2 = (f32[1024,768]{1,0:T(8,128)S(1)}, f32[1024,768]{1,0:T(8,128)}, u32[]{:S(2)}) copy-start(f32[1024,768]{1,0:T(8,128)} %copy-done.1) | copy-start | bytes 9437188
  299.5 6.2 %copy-start.14 = (f32[768]{0:T(1024)S(1)}, f32[768]{0:T(1024)}, u32[]{:S(2)}) copy-start(f32[768]{0:T(1024)} %reshape.240) | copy-start | bytes 9220
  299.5 13.7 %slice-start.2 = ((s8[6291456]{0:T(1024)(128)(4,1)}), s8[4194304]{0:T(1024)(128)(4,1)S(1)}, s32[]{:S(2)}) async-start(s8[6291456]{0:T(1024)(128)(4,1)} %bitcast.47), calls=%async_computation.6 | async-start | bytes 8388608
  305.7 7.5 %slice-start.3 = ((s8[6291456]{0:T(1024)(128)(4,1)}), s8[2097152]{0:T(1024)(128)(4,1)S(1)}, s32[]{:S(2)}) async-start(s8[6291456]{0:T(1024)(128)(4,1)} %bitcast.47), calls=%async_computation.7 | async-start | bytes 4194304
  313.2 8.6 %copy-start = (bf16[1024,768]{1,0:T(8,128)(2,1)}, bf16[1024,768]{1,0:T(8,128)(2,1)S(1)}, u32[]{:S(2)}) copy-start(bf16[1024,768]{1,0:T(8,128)(2,1)S(1)} %add_convert_fusion.1.refs_5_) | copy-start | bytes 4718596
Sparse Core Ops, SparseCore 0:
  15.4 72.3 all-gather.6
  90.7 64.0 all-gather.4
  209.7 138.4 reduce-scatter.1

commit v13 on v12

--- a/solution.py
+++ b/solution.py
@@ -454,21 +454,34 @@
     rows_o = w_out.size // width_q
     rows_u = w_up.size // width_q
     up_view = 16
-    ring_up = mesh_shape == (8, 4) and w_up.size % (up_view * 128) == 0
-    pieces = [w_qkv, w_out.reshape(rows_o, width_q)]
-    if not ring_up:
-        pieces.append(w_up.reshape(rows_u, width_q))
+    half_u = w_up.shape[1] // 2
+    ring_up = (
+        mesh_shape == (8, 4)
+        and w_up.size % (2 * up_view * width_q) == 0
+        and w_out.size % (up_view * 128) == 0
+    )
+    if ring_up:
+        up_sc = w_up[:, :half_u].reshape(-1, width_q)
+        pieces = [w_qkv, up_sc]
+    else:
+        pieces = [w_qkv, w_out.reshape(rows_o, width_q), w_up.reshape(rows_u, width_q)]
     attn_buf = jnp.concatenate(pieces + [pack_rows(small, width_q)], axis=0)
     attn_all = lax.all_gather(attn_buf, ALL, axis=0, tiled=False)
     qkv_full = attn_all[:, :rows_q].reshape(-1, width_q)
-    out_full = attn_all[:, rows_q : rows_q + rows_o].reshape(-1, model_width)
-    at = rows_q + rows_o
+    at = rows_q
     if ring_up:
-        (up_all,) = ring_all_gather([w_up.reshape(up_view, -1)], mesh_shape)
-        up_full = up_all.reshape(-1, w_up.shape[1])
+        rows_h = up_sc.shape[0]
+        up_a = attn_all[:, at : at + rows_h].reshape(-1, half_u)
+        at = at + rows_h
+        out_all, up_b = ring_all_gather(
+            [w_out.reshape(up_view, -1), w_up[:, half_u:].reshape(up_view, -1)], mesh_shape
+        )
+        out_full = out_all.reshape(-1, model_width)
+        up_full = jnp.concatenate([up_a, up_b.reshape(-1, half_u)], axis=1)
     else:
-        up_full = attn_all[:, at : at + rows_u].reshape(-1, w_up.shape[1])
-        at = at + rows_u
+        out_full = attn_all[:, at : at + rows_o].reshape(-1, model_width)
+        up_full = attn_all[:, at + rows_o : at + rows_o + rows_u].reshape(-1, w_up.shape[1])
+        at = at + rows_o + rows_u
     small_full = split_owned(attn_all[:, at, :n_small], small_sizes)
     qv_full, outb_full, gain_one, shift_one, gain_two, shift_two, upb_full, downb_full = small_full
     down_full = lax.all_gather(w_down, ALL, axis=0, tiled=True)

time: 471 us -> 481 us (1.021)
  local copies, waits for them, and re-layouts: 33.8 us -> 47.8 us
    unnamed x48 -> x51, local copies, waits for them, and re-layouts: 6.51 us -> 12.2 us
    reshape x4 -> x6, local copies, waits for them, and re-layouts: 11 us -> 13.6 us  [the longest x1 4.55 us: on_device(): up_a = attn_all[:, at:at + rows_h].reshape(-1, half_u)]
  transfers between devices with their start and end apart: 3 -> 3, of which waited for: 0 -> 0; matrix products, arithmetic and copies ran while one was open for 33% -> 35% of each run, Pallas kernels for 60% -> 58%
where the time goes in v13:
time: 481 us; the launch traced here: 471 us
  Pallas kernels  275 us (57%)
  matrix products  118 us (25%)
  local copies, waits for them, and re-layouts  47.8 us (10%)
  other arithmetic  15 us (3%)
  between operations  14.8 us (3%)
    pallas_call x1, Pallas kernels, ring_reduce_scatter(): pl.pallas_call(kernel, out_shape=out_shape, in_specs=[pl.BlockSpec(memory...  130 us
    pallas_call x1, Pallas kernels, ring_all_gather(): pl.pallas_call(kernel, out_shape=out_shape, in_specs=[pl.BlockSpec(memory...  78.8 us
    dot_general x1, matrix products, on_device(): jnp.dot(h_two, up_full, preferred_element_type=jnp.float32)  36.7 us
    pallas_call x1, Pallas kernels, attention_bwd(): pl.pallas_call(attn_bwd_kernel, out_shape=jax.ShapeDtypeStruct((rows, wid...  36.3 us
    pallas_call x1, Pallas kernels, attention_fwd(): pl.pallas_call(attn_fwd_kernel, out_shape=jax.ShapeDtypeStruct((rows, mod...  29.8 us
    dot_general x1, matrix products, on_device(): jnp.einsum('td,fd->tf', cotangent, down_full, preferred_element_type=jnp....  14.4 us
    unnamed x51, local copies, waits for them, and re-layouts  12.2 us
    dot_general x1, matrix products, on_device(): jnp.einsum('tf,df->td', grad_u, up_full, preferred_element_type=jnp.float32)  9.69 us
  transfers between devices with their start and end apart: 3, of which 0 were waited for; matrix products, arithmetic and copies ran while one was open for 35% of the time, Pallas kernels for 58%

profile of v13, /device:TPU:1, one launch (start us, length us, event | category | flops | bytes accessed | tf_op | source)
XLA Modules:
  0.0 471.4 jit_solution(488905525504372546)
XLA Ops:
  7.3 5.5 %concatenate.23 = bf16[288]{0:T(512)(128)(2,1)S(1)} concatenate(bf16[48]{0:T(256)(128)(2,1)} %param.18, bf16[24]{0:T(256)(128)(2,1)} %param.20, bf16[24]{0:T(256)(128)(2,1)} %param.21, bf16[24]{0:T(256)(128)(2,1)} %param.22, bf16[24]{0:T(256)(128)(2,1)} %param.23, bf16[24]{0:T(256)(128)(2,1)} %param.24, bf16[96]{0:T(256)(128)(2,1)} %param.26, bf16[24]{0:T(256)(128)(2,1)} %param.28), dimensions={0} | concatenate | bytes 1152 | tf_op jit(solution)/shard_map/concatenate | solution.py:411
  12.8 0.9 fusion.39
  13.8 1.6 maximum_bitcast_fusion
  15.5 0.7 all-gather.5.cloned.1.call-update
  16.3 1.3 broadcast_in_dim.14.vr_ref
  17.5 1.3 broadcast_in_dim.13.sr_ref
  18.8 1.7 convert_reduce_fusion.2
  20.5 0.6 fusion.29
  21.1 0.7 reshape.220.refs_0_
  21.8 0.7 reshape.221.refs_1_
  22.5 1.0 copy.38.sc_ref
  23.5 78.8 %shard_map.264 = (bf16[512,1152]{1,0:T(8,128)(2,1)}, bf16[512,2304]{1,0:T(8,128)(2,1)}) custom-call(bf16[16,1152]{1,0:T(8,128)(2,1)} %reshape.220.refs_0_, bf16[16,2304]{1,0:T(8,128)(2,1)} %reshape.221.refs_1_), custom_call_target="tpu_custom_call" | custom-call | bytes 7077888 | tf_op jit(solution)/shard_map/pallas_call | solution.py:395
  102.3 3.1 reshape.222
  105.4 4.5 reshape.224
  109.9 1.0 slice.122
  110.9 0.1 slice_convert_fusion.1
  111.0 0.1 slice_convert_fusion
  111.1 0.1 slice.102
  111.3 0.7 reshape.248
  112.0 0.1 reshape.245
  112.1 0.1 reshape.242
  112.2 0.1 reshape.246
  112.3 0.1 reshape.243
  112.4 0.1 reshape.244
  112.4 3.2 slice.132
  115.7 4.6 reshape.223
  120.2 3.3 constant_dynamic-update-slice_fusion.1
  123.6 2.2 slice.125
  125.8 1.8 copy-done.7
  127.7 5.9 %add_convert_fusion.q_ref.k_ref.v_ref = bf16[1024,2304]{1,0:T(8,128)(2,1)} fusion(bf16[768,2304]{1,0:T(8,128)(2,1)S(1)} %bitcast.49, f32[2304]{0:T(1024)S(1)} %pad_maximum_fusion.1, bf16[1024,768]{1,0:T(8,128)(2,1)S(1)} %copy-done.3, f32[768]{0:T(1024)S(1)} %reshape.243, f32[768]{0:T(1024)S(1)} %reshape.242, f32[1024]{0:T(1024)S(1)} %add_rsqrt_fusion.1, ...), kind=kOutput, calls=%fused_computation.28 | convolution fusion | flops 3633315840 | bytes 9853952 | tf_op jit(solution)/shard_map/dot_general | solution.py:495
  133.6 29.8 %shard_map.263 = bf16[1024,768]{1,0:T(8,128)(2,1)} custom-call(bf16[1024,2304]{1,0:T(8,128)(2,1)} %add_convert_fusion.q_ref.k_ref.v_ref, bf16[1024,2304]{1,0:T(8,128)(2,1)} %add_convert_fusion.q_ref.k_ref.v_ref, bf16[1024,2304]{1,0:T(8,128)(2,1)} %add_convert_fusion.q_ref.k_ref.v_ref, s32[2,512,1]{2,1,0:T(8,128)} %copy.38.sc_ref, ...), custom_call_target="tpu_custom_call" | custom-call | flops 1610612736 | bytes 6291456 | tf_op jit(solution)/shard_map/pallas_call | solution.py:105
  163.4 3.8 fusion.42
  167.2 0.5 multiply_reduce_fusion.2
  167.7 2.3 copy-done.6
  170.0 1.6 constant_dynamic-update-slice_fusion
  171.6 36.7 %fusion.2 = (bf16[1024,3072]{1,0:T(8,128)(2,1)S(1)}, f32[1024,3072]{1,0:T(8,128)}) fusion(f32[3072]{0:T(1024)S(1)} %reshape.247, bf16[768,3072]{1,0:T(8,128)(2,1)} %constant_dynamic-update-slice_fusion, f32[1024,768]{1,0:T(8,128)S(1)} %get-tuple-element.56, f32[768]{0:T(1024)S(1)} %reshape.246, f32[768]{0:T(1024)S(1)} %reshape.245, ...), kind=kOutput, calls=%fused_computation.4 | convolution fusion | flops 5043388416 | bytes 26765312 | tf_op jit(solution)/shard_map/dot_general | solution.py:509
  208.3 2.7 copy-done.16
  211.0 7.7 %fusion.43 = f32[3072,768]{1,0:T(8,128)} fusion(bf16[1024,3072]{1,0:T(8,128)(2,1)S(1)} %get-tuple-element.57, bf16[1024,768]{1,0:T(8,128)(2,1)S(1)} %copy-done.9), kind=kOutput, calls=%fused_computation.99 | convolution fusion | flops 4831838208 | bytes 17301504 | tf_op jit(solution)/shard_map/tf,td->fd/dot_general | solution.py:520
  218.8 14.4 %convert_reduce_fusion = (f32[3072]{0:T(1024)S(1)}, bf16[1024,3072]{1,0:T(8,128)(2,1)}) fusion(f32[1024,3072]{1,0:T(8,128)} %get-tuple-element.58, f32[3072]{0:T(1024)S(1)} %reshape.247, bf16[1024,768]{1,0:T(8,128)(2,1)} %param.31, bf16[3072,768]{1,0:T(8,128)(2,1)} %all-gather.5.cloned.1.call-done), kind=kOutput, calls=%fused_computation.11 | convolution fusion | flops 4872729600 | bytes 25190400 | tf_op jit(solution)/shard_map/td,fd->tf/dot_general | solution.py:522
  233.2 9.7 %multiply_reduce_fusion = (f32[768]{0:T(1024)S(1)}, f32[1024]{0:T(1024)S(1)}, f32[1024]{0:T(1024)S(1)}, f32[768]{0:T(1024)S(1)}, f32[1024,768]{1,0:T(8,128)S(1)}) fusion(f32[1024,768]{1,0:T(8,128)S(1)} %get-tuple-element.56, f32[1024]{0:T(1024)S(1)} %add_rsqrt_fusion, f32[1024]{0:T(1024)S(1)} %broadcast_multiply_fusion.4, f32[768]{0:T(1024)S(1)} %reshape.245, ...), kind=kOutput, calls=%fused_computation.49 | convolution fusion | flops 4838912000 | bytes 17327104 | tf_op jit(solution)/shard_map/tf,df->td/dot_general | solution.py:528
  243.0 2.6 convert_reduce_fusion.4
  245.6 0.1 reshape.225
  245.7 0.1 reshape.228
  245.8 0.1 reshape.231
  245.8 0.1 reshape.229
  245.9 5.0 %convolution_convert_fusion.do_ref = bf16[1024,768]{1,0:T(8,128)(2,1)} fusion(bf16[768,768]{1,0:T(8,128)(2,1)} %reshape.222, f32[1024,768]{1,0:T(8,128)} %get-tuple-element.35), kind=kOutput, calls=%fused_computation.58 | convolution fusion | flops 1209532416 | bytes 5898240 | tf_op jit(solution)/shard_map/td,cd->tc/dot_general | solution.py:535
  250.9 36.3 %shard_map.265 = bf16[1024,2304]{1,0:T(8,128)(2,1)} custom-call(bf16[1024,2304]{1,0:T(8,128)(2,1)} %add_convert_fusion.q_ref.k_ref.v_ref, bf16[1024,2304]{1,0:T(8,128)(2,1)} %add_convert_fusion.q_ref.k_ref.v_ref, bf16[1024,2304]{1,0:T(8,128)(2,1)} %add_convert_fusion.q_ref.k_ref.v_ref, bf16[1024,768]{1,0:T(8,128)(2,1)} %convolution_convert_fusion.do_ref, ...), custom_call_target="tpu_custom_call" | custom-call | flops 4026531840 | bytes 11010048 | tf_op jit(solution)/shard_map/pallas_call | solution.py:137
  287.3 9.5 %fusion.28 = (f32[768]{0:T(1024)S(1)}, f32[1024]{0:T(1024)S(1)}, f32[1024]{0:T(1024)S(1)}, f32[768]{0:T(1024)S(1)}, f32[1024,768]{1,0:T(8,128)}) fusion(bf16[1024,768]{1,0:T(8,128)(2,1)S(1)} %copy-done.4, f32[1024]{0:T(1024)S(1)} %add_rsqrt_fusion.1, f32[1024]{0:T(1024)S(1)} %broadcast_multiply_fusion.5, f32[768]{0:T(1024)S(1)} %reshape.242, ...), kind=kOutput, calls=%fused_computation.46 | convolution fusion | flops 3631739392 | bytes 13001728 | tf_op jit(solution)/shard_map/te,de->td/dot_general | solution.py:542
  296.8 0.1 reshape.226
  296.9 3.3 convert_reduce_fusion.1
  300.3 0.1 reshape.227
  300.4 0.1 concatenate.30
  300.6 3.5 fusion.31.refs_1_
  304.2 4.5 fusion.27.refs_4_
  308.8 6.2 %fusion.34.refs_0_ = f32[768,2304]{1,0:T(8,128)} fusion(bf16[1024,2304]{1,0:T(8,128)(2,1)S(1)} %bitcast.46, bf16[1024,768]{1,0:T(8,128)(2,1)S(1)} %copy-done.4, f32[768]{0:T(1024)S(1)} %copy-done.12, f32[768]{0:T(1024)S(1)} %reshape.242, f32[1024]{0:T(1024)S(1)} %add_rsqrt_fusion.1, f32[1024]{0:T(1024)S(1)} %broadcast_multiply_fusion.5), kind=kOutput, calls=%fused_computation.92 | convolution fusion | flops 3628597248 | bytes 13383680 | tf_op jit(solution)/shard_map/td,te->de/dot_general | solution.py:541
  315.0 7.4 %add_convert_fusion.1.refs_5_ = bf16[1024,768]{1,0:T(8,128)(2,1)S(1)} fusion(f32[1024,768]{1,0:T(8,128)S(1)} %copy-done.2, bf16[1024,3072]{1,0:T(8,128)(2,1)} %copy-done.16, bf16[3072,768]{1,0:T(8,128)(2,1)S(1)} %bitcast.56, f32[768]{0:T(1024)S(1)} %copy-done.15), kind=kOutput, calls=%fused_computation.52 | convolution fusion | flops 4834197504 | bytes 15731712 | tf_op jit(solution)/shard_map/dot_general | solution.py:515
  322.4 8.6 %fusion.37.refs_2_ = f32[768,3072]{1,0:T(8,128)} fusion(bf16[1024,3072]{1,0:T(8,128)(2,1)S(1)} %bitcast.48, f32[1024,768]{1,0:T(8,128)S(1)} %copy-done.2, f32[768]{0:T(1024)S(1)} %reshape.246, f32[768]{0:T(1024)S(1)} %reshape.245, f32[1024]{0:T(1024)S(1)} %add_rsqrt_fusion, f32[1024]{0:T(1024)S(1)} %broadcast_multiply_fusion.4), kind=kOutput, calls=%fused_computation.93 | convolution fusion | flops 4835770368 | bytes 18888704 | tf_op jit(solution)/shard_map/td,tf->df/dot_general | solution.py:527
  331.0 129.6 %shard_map.266 = (f32[24,2304]{1,0:T(8,128)S(1)}, f32[24,768]{1,0:T(8,128)S(1)}, f32[24,3072]{1,0:T(8,128)S(1)}, f32[8,128]{1,0:T(8,128)S(1)}) custom-call(f32[768,2304]{1,0:T(8,128)} %fusion.34.refs_0_, f32[768,768]{1,0:T(8,128)S(1)} %fusion.31.refs_1_, f32[768,3072]{1,0:T(8,128)} %fusion.37.refs_2_, f32[256,128]{1,0:T(8,128)S(1)} %reshape.232.refs_3_, ...), custom_call_target="tpu_custom_call" | custom-call | flops 4751360 | bytes 38010880 | tf_op jit(solution)/shard_map/pallas_call | solution.py:303
  460.6 0.6 slice_bitcast_fusion.1
  461.2 0.5 slice_bitcast_fusion.7
  461.7 0.6 slice_bitcast_fusion
  462.3 0.7 copy.49
  463.0 0.6 copy.50
  463.6 0.7 copy.51
  (78 shorter events, 0.8 us)
Async XLA Ops:
  7.2 15.3 %copy-start.14 = (s32[2,512]{1,0:T(2,128)S(1)}, s32[2,512]{1,0:T(2,128)}, u32[]{:S(2)}) copy-start(s32[2,512]{1,0:T(2,128)} %param.29) | copy-start | bytes 12292
  7.2 13.3 %copy-start.3 = (bf16[1024,768]{1,0:T(8,128)(2,1)S(1)}, bf16[1024,768]{1,0:T(8,128)(2,1)}, u32[]{:S(2)}) copy-start(bf16[1024,768]{1,0:T(8,128)(2,1)} %param.16) | copy-start | bytes 4718596
  7.2 13.9 %copy-start.13 = (bf16[24,768]{1,0:T(8,128)(2,1)S(1)}, bf16[24,768]{1,0:T(8,128)(2,1)}, u32[]{:S(2)}) copy-start(bf16[24,768]{1,0:T(8,128)(2,1)} %param.19) | copy-start | bytes 110596
  7.2 102.7 %all-gather.7.cloned.1.call-start = ((), (), s32[]{:S(2)}) async-start(), calls=%async_computation.3 | async-start | bytes 7299072 | tf_op jit(solution)/shard_map/all_gather | solution.py:469
  15.5 203.3 %all-gather.5.cloned.1.call-start = ((), (), s32[]{:S(2)}) async-start(), calls=%async_computation.1 | async-start | bytes 4866048 | tf_op jit(solution)/shard_map/all_gather | solution.py:487
  16.2 446.1 %reduce-scatter.2.cloned.1.call-start = ((), (), s32[]{:S(2)}) async-start(), calls=%async_computation.2 | async-start | bytes 9732096 | tf_op jit(solution)/shard_map/reduce_scatter | solution.py:558
  112.3 13.5 %copy-start.11 = (f32[768]{0:T(1024)}, f32[768]{0:T(1024)S(1)}, u32[]{:S(2)}) copy-start(f32[768]{0:T(1024)S(1)} %reshape.243) | copy-start | bytes 9220
  125.8 1.8 copy-start.7
  167.2 75.7 %copy-start.1 = (f32[1024,768]{1,0:T(8,128)}, f32[1024,768]{1,0:T(8,128)S(1)}, u32[]{:S(2)}) copy-start(f32[1024,768]{1,0:T(8,128)S(1)} %get-tuple-element.56) | copy-start | bytes 9437188
  167.2 2.8 copy-start.6
  171.6 39.4 %copy-start.9 = (bf16[1024,768]{1,0:T(8,128)(2,1)S(1)}, bf16[1024,768]{1,0:T(8,128)(2,1)}, u32[]{:S(2)}) copy-start(bf16[1024,768]{1,0:T(8,128)(2,1)} %param.31) | copy-start | bytes 4718596
  208.3 2.7 copy-start.16
  233.2 9.7 %copy-start.10 = (bf16[1024,768]{1,0:T(8,128)(2,1)S(1)}, bf16[1024,768]{1,0:T(8,128)(2,1)}, u32[]{:S(2)}) copy-start(bf16[1024,768]{1,0:T(8,128)(2,1)} %param.31) | copy-start | bytes 4718596
  250.9 36.4 %copy-start.4 = (bf16[1024,768]{1,0:T(8,128)(2,1)S(1)}, bf16[1024,768]{1,0:T(8,128)(2,1)}, u32[]{:S(2)}) copy-start(bf16[1024,768]{1,0:T(8,128)(2,1)} %param.16) | copy-start | bytes 4718596
  296.8 3.8 copy-start.8
  300.6 3.5 copy-start.5
  300.6 8.1 %slice-start = ((s8[4718592]{0:T(1024)(128)(4,1)}), s8[4194304]{0:T(1024)(128)(4,1)S(1)}, s32[]{:S(2)}) async-start(s8[4718592]{0:T(1024)(128)(4,1)} %bitcast.45), calls=%async_computation.4 | async-start | bytes 8388608
  300.6 14.3 %slice-start.4 = ((s8[4718592]{0:T(1024)(128)(4,1)}), s8[4194304]{0:T(1024)(128)(4,1)S(1)}, s32[]{:S(2)}) async-start(s8[4718592]{0:T(1024)(128)(4,1)} %bitcast.55), calls=%async_computation.8 | async-start | bytes 8388608
  304.2 4.6 slice-start.1
  304.2 4.5 copy-start.12
  304.2 10.7 %slice-start.5 = ((s8[4718592]{0:T(1024)(128)(4,1)}), s8[524288]{0:T(1024)(128)(4,1)S(1)}, s32[]{:S(2)}) async-start(s8[4718592]{0:T(1024)(128)(4,1)} %bitcast.55), calls=%async_computation.9 | async-start | bytes 1048576
  308.7 6.2 %copy-start.2 = (f32[1024,768]{1,0:T(8,128)S(1)}, f32[1024,768]{1,0:T(8,128)}, u32[]{:S(2)}) copy-start(f32[1024,768]{1,0:T(8,128)} %copy-done.1) | copy-start | bytes 9437188
  308.7 6.2 %copy-start.15 = (f32[768]{0:T(1024)S(1)}, f32[768]{0:T(1024)}, u32[]{:S(2)}) copy-start(f32[768]{0:T(1024)} %reshape.248) | copy-start | bytes 9220
  308.8 13.6 %slice-start.2 = ((s8[6291456]{0:T(1024)(128)(4,1)}), s8[4194304]{0:T(1024)(128)(4,1)S(1)}, s32[]{:S(2)}) async-start(s8[6291456]{0:T(1024)(128)(4,1)} %bitcast.47), calls=%async_computation.6 | async-start | bytes 8388608
  314.9 7.5 %slice-start.3 = ((s8[6291456]{0:T(1024)(128)(4,1)}), s8[2097152]{0:T(1024)(128)(4,1)S(1)}, s32[]{:S(2)}) async-start(s8[6291456]{0:T(1024)(128)(4,1)} %bitcast.47), calls=%async_computation.7 | async-start | bytes 4194304
  322.4 8.6 %copy-start = (bf16[1024,768]{1,0:T(8,128)(2,1)}, bf16[1024,768]{1,0:T(8,128)(2,1)S(1)}, u32[]{:S(2)}) copy-start(bf16[1024,768]{1,0:T(8,128)(2,1)S(1)} %add_convert_fusion.1.refs_5_) | copy-start | bytes 4718596
Sparse Core Ops, SparseCore 0:
  15.6 77.6 all-gather.6
  96.2 64.4 all-gather.4
  218.9 137.3 reduce-scatter.1

commit v14 on v12

--- a/solution.py
+++ b/solution.py
@@ -365,18 +365,19 @@
                 @pl.when(s < steps[dirn])
                 def _():
                     for i in range(n_in):
+
+                        @pl.when(s >= 1)
+                        def _():
+                            arriving(i, dirn, s - 1).wait_recv()
+
                         sent(i, dirn, s).start()
 
-            for dirn in (0, 1):
-
-                @pl.when(s < steps[dirn])
-                def _():
-                    for i in range(n_in):
-                        arriving(i, dirn, s).wait_recv()
-
             return carry
 
         lax.fori_loop(0, steps[0], step, 0)
+        for dirn in (0, 1):
+            for i in range(n_in):
+                arriving(i, dirn, steps[dirn] - 1).wait_recv()
 
         def drain(s, carry):
             for dirn in (0, 1):
@@ -454,7 +455,7 @@
     rows_o = w_out.size // width_q
     rows_u = w_up.size // width_q
     up_view = 16
-    ring_up = mesh_shape == (8, 4) and w_up.size % (up_view * 128) == 0
+    ring_up = mesh_shape == (8, 4) and w_up.size % (2 * up_view * 128) == 0
     pieces = [w_qkv, w_out.reshape(rows_o, width_q)]
     if not ring_up:
         pieces.append(w_up.reshape(rows_u, width_q))
@@ -464,8 +465,10 @@
     out_full = attn_all[:, rows_q : rows_q + rows_o].reshape(-1, model_width)
     at = rows_q + rows_o
     if ring_up:
-        (up_all,) = ring_all_gather([w_up.reshape(up_view, -1)], mesh_shape)
-        up_full = up_all.reshape(-1, w_up.shape[1])
+        up_v = w_up.reshape(up_view, -1)
+        half_v = up_v.shape[1] // 2
+        up_a, up_b = ring_all_gather([up_v[:, :half_v], up_v[:, half_v:]], mesh_shape)
+        up_full = jnp.concatenate([up_a, up_b], axis=1).reshape(-1, w_up.shape[1])
     else:
         up_full = attn_all[:, at : at + rows_u].reshape(-1, w_up.shape[1])
         at = at + rows_u

time: 471 us -> 463 us (0.983)
  Pallas kernels: 279 us -> 264 us
  other arithmetic: 14.9 us -> 21.2 us
    pallas_call x1, Pallas kernels: 82.9 us -> 68.5 us  [ring_all_gather(): pl.pallas_call(kernel, out_shape=out_shape, in_specs=[pl.BlockSpec(memory...]
    concatenate x0 -> x1, other arithmetic: none -> 4.83 us  [on_device(): up_full = jnp.concatenate([up_a, up_b], axis=1).reshape(-1, w_up.shape[1])]
  transfers between devices with their start and end apart: 3 -> 3, of which waited for: 0 -> 0; matrix products, arithmetic and copies ran while one was open for 33% -> 35% of each run, Pallas kernels for 60% -> 58%
where the time goes in v14:
time: 463 us; the launch traced here: 455 us
  Pallas kernels  264 us (57%)
  matrix products  120 us (26%)
  local copies, waits for them, and re-layouts  33.9 us (7%)
  other arithmetic  21.2 us (5%)
  between operations  14.8 us (3%)
    pallas_call x1, Pallas kernels, ring_reduce_scatter(): pl.pallas_call(kernel, out_shape=out_shape, in_specs=[pl.BlockSpec(memory...  130 us
    pallas_call x1, Pallas kernels, ring_all_gather(): pl.pallas_call(kernel, out_shape=out_shape, in_specs=[pl.BlockSpec(memory...  68.5 us
    dot_general x1, matrix products, on_device(): jnp.dot(h_two, up_full, preferred_element_type=jnp.float32)  37.7 us
    pallas_call x1, Pallas kernels, attention_bwd(): pl.pallas_call(attn_bwd_kernel, out_shape=jax.ShapeDtypeStruct((rows, wid...  36.4 us
    pallas_call x1, Pallas kernels, attention_fwd(): pl.pallas_call(attn_fwd_kernel, out_shape=jax.ShapeDtypeStruct((rows, mod...  30 us
    dot_general x1, matrix products, on_device(): jnp.einsum('td,fd->tf', cotangent, down_full, preferred_element_type=jnp....  14.5 us
    dot_general x1, matrix products, on_device(): jnp.einsum('tf,df->td', grad_u, up_full, preferred_element_type=jnp.float32)  9.71 us
    dot_general x1, matrix products, on_device(): jnp.einsum('te,de->td', grad_qkv, qkv_full, preferred_element_type=jnp.fl...  9.45 us
  transfers between devices with their start and end apart: 3, of which 0 were waited for; matrix products, arithmetic and copies ran while one was open for 35% of the time, Pallas kernels for 58%

profile of v14, /device:TPU:1, one launch (start us, length us, event | category | flops | bytes accessed | tf_op | source)
XLA Modules:
  0.0 455.0 jit_solution(6458573015333481259)
XLA Ops:
  7.2 5.5 %concatenate.23 = bf16[288]{0:T(512)(128)(2,1)S(1)} concatenate(bf16[48]{0:T(256)(128)(2,1)} %param.18, bf16[24]{0:T(256)(128)(2,1)} %param.20, bf16[24]{0:T(256)(128)(2,1)} %param.21, bf16[24]{0:T(256)(128)(2,1)} %param.22, bf16[24]{0:T(256)(128)(2,1)} %param.23, bf16[24]{0:T(256)(128)(2,1)} %param.24, bf16[96]{0:T(256)(128)(2,1)} %param.26, bf16[24]{0:T(256)(128)(2,1)} %param.28), dimensions={0} | concatenate | bytes 1152 | tf_op jit(solution)/shard_map/concatenate | solution.py:412
  12.7 0.8 reshape.212
  13.5 1.6 maximum_bitcast_fusion
  15.2 0.7 all-gather.5.cloned.1.call-update
  15.9 1.3 broadcast_in_dim.14.vr_ref
  17.2 1.3 broadcast_in_dim.13.sr_ref
  18.5 1.7 convert_reduce_fusion.2
  20.2 2.0 fusion.29
  22.2 0.1 reshape.215
  22.4 0.7 fusion.39
  23.0 1.0 copy.38.sc_ref
  24.0 68.5 %shard_map.264 = (bf16[512,2304]{1,0:T(8,128)(2,1)}, bf16[512,2304]{1,0:T(8,128)(2,1)}) custom-call(bf16[16,2304]{1,0:T(8,128)(2,1)} %get-tuple-element.38.refs_0_, bf16[16,2304]{1,0:T(8,128)(2,1)} %get-tuple-element.37.refs_1_), custom_call_target="tpu_custom_call" | custom-call | bytes 9437184 | tf_op jit(solution)/shard_map/pallas_call | solution.py:396
  92.5 4.8 %pad_maximum_fusion = bf16[512,4608]{1,0:T(8,128)(2,1)} fusion(bf16[512,2304]{1,0:T(8,128)(2,1)} %get-tuple-element.21, bf16[512,2304]{1,0:T(8,128)(2,1)} %get-tuple-element.20), kind=kLoop, calls=%fused_computation.32 | loop fusion | flops 9437184 | bytes 9437184 | tf_op jit(solution)/shard_map/concatenate | solution.py:471
  97.4 8.1 %reshape.216 = bf16[768,3072]{1,0:T(8,128)(2,1)} reshape(bf16[512,4608]{1,0:T(8,128)(2,1)} %pad_maximum_fusion) | data formatting | bytes 9437184 | tf_op jit(solution)/shard_map/reshape | solution.py:471
  105.4 1.1 slice.122
  106.5 0.1 slice_convert_fusion.1
  106.6 0.1 slice_convert_fusion
  106.7 0.1 slice.101
  106.8 0.1 slice.103
  106.9 0.7 reshape.240
  107.6 0.1 reshape.237
  107.7 0.1 reshape.234
  107.8 0.1 reshape.238
  107.9 0.1 reshape.235
  108.0 0.1 reshape.236
  108.1 1.4 reshape.214
  109.5 2.4 slice.125
  111.9 1.7 copy-done.6
  113.6 6.0 %add_convert_fusion.q_ref.k_ref.v_ref = bf16[1024,2304]{1,0:T(8,128)(2,1)} fusion(bf16[768,2304]{1,0:T(8,128)(2,1)S(1)} %bitcast.49, f32[2304]{0:T(1024)S(1)} %pad_maximum_fusion.2, bf16[1024,768]{1,0:T(8,128)(2,1)S(1)} %copy-done.3, f32[768]{0:T(1024)S(1)} %reshape.235, f32[768]{0:T(1024)S(1)} %reshape.234, f32[1024]{0:T(1024)S(1)} %add_rsqrt_fusion.1, ...), kind=kOutput, calls=%fused_computation.28 | convolution fusion | flops 3633315840 | bytes 9853952 | tf_op jit(solution)/shard_map/dot_general | solution.py:485
  119.6 30.0 %shard_map.263 = bf16[1024,768]{1,0:T(8,128)(2,1)} custom-call(bf16[1024,2304]{1,0:T(8,128)(2,1)} %add_convert_fusion.q_ref.k_ref.v_ref, bf16[1024,2304]{1,0:T(8,128)(2,1)} %add_convert_fusion.q_ref.k_ref.v_ref, bf16[1024,2304]{1,0:T(8,128)(2,1)} %add_convert_fusion.q_ref.k_ref.v_ref, s32[2,512,1]{2,1,0:T(8,128)} %copy.38.sc_ref, ...), custom_call_target="tpu_custom_call" | custom-call | flops 1610612736 | bytes 6291456 | tf_op jit(solution)/shard_map/pallas_call | solution.py:105
  149.5 3.9 fusion.42
  153.4 0.5 multiply_reduce_fusion.2
  153.9 37.7 %fusion.2 = (bf16[1024,3072]{1,0:T(8,128)(2,1)S(1)}, f32[1024,3072]{1,0:T(8,128)}) fusion(f32[3072]{0:T(1024)S(1)} %reshape.239, bf16[768,3072]{1,0:T(8,128)(2,1)} %reshape.216, f32[1024,768]{1,0:T(8,128)S(1)} %get-tuple-element.56, f32[768]{0:T(1024)S(1)} %reshape.238, f32[768]{0:T(1024)S(1)} %reshape.237, f32[1024]{0:T(1024)S(1)} %add_rsqrt_fusion, ...), kind=kOutput, calls=%fused_computation.4 | convolution fusion | flops 5043388416 | bytes 26765312 | tf_op jit(solution)/shard_map/dot_general | solution.py:499
  191.6 2.6 copy-done.15
  194.2 7.7 %fusion.43 = f32[3072,768]{1,0:T(8,128)} fusion(bf16[1024,3072]{1,0:T(8,128)(2,1)S(1)} %get-tuple-element.57, bf16[1024,768]{1,0:T(8,128)(2,1)S(1)} %copy-done.8), kind=kOutput, calls=%fused_computation.98 | convolution fusion | flops 4831838208 | bytes 17301504 | tf_op jit(solution)/shard_map/tf,td->fd/dot_general | solution.py:510
  202.0 14.5 %convert_reduce_fusion = (f32[3072]{0:T(1024)S(1)}, bf16[1024,3072]{1,0:T(8,128)(2,1)}) fusion(f32[1024,3072]{1,0:T(8,128)} %get-tuple-element.58, f32[3072]{0:T(1024)S(1)} %reshape.239, bf16[1024,768]{1,0:T(8,128)(2,1)} %param.31, bf16[3072,768]{1,0:T(8,128)(2,1)} %all-gather.5.cloned.1.call-done), kind=kOutput, calls=%fused_computation.11 | convolution fusion | flops 4872729600 | bytes 25190400 | tf_op jit(solution)/shard_map/td,fd->tf/dot_general | solution.py:512
  216.5 0.1 reshape.222
  216.6 9.7 %multiply_reduce_fusion = (f32[768]{0:T(1024)S(1)}, f32[1024]{0:T(1024)S(1)}, f32[1024]{0:T(1024)S(1)}, f32[768]{0:T(1024)S(1)}, f32[1024,768]{1,0:T(8,128)S(1)}) fusion(f32[1024,768]{1,0:T(8,128)S(1)} %get-tuple-element.56, f32[1024]{0:T(1024)S(1)} %add_rsqrt_fusion, f32[1024]{0:T(1024)S(1)} %broadcast_multiply_fusion.4, f32[768]{0:T(1024)S(1)} %reshape.237, ...), kind=kOutput, calls=%fused_computation.50 | convolution fusion | flops 4838912000 | bytes 17327104 | tf_op jit(solution)/shard_map/tf,df->td/dot_general | solution.py:518
  226.3 2.6 convert_reduce_fusion.4
  229.0 0.1 reshape.217
  229.0 0.1 reshape.220
  229.1 0.1 reshape.223
  229.2 0.1 reshape.221
  229.3 5.0 %convolution_convert_fusion.do_ref = bf16[1024,768]{1,0:T(8,128)(2,1)} fusion(bf16[768,768]{1,0:T(8,128)(2,1)} %reshape.214, f32[1024,768]{1,0:T(8,128)} %get-tuple-element.35), kind=kOutput, calls=%fused_computation.59 | convolution fusion | flops 1209532416 | bytes 5898240 | tf_op jit(solution)/shard_map/td,cd->tc/dot_general | solution.py:525
  234.3 36.4 %shard_map.265 = bf16[1024,2304]{1,0:T(8,128)(2,1)} custom-call(bf16[1024,2304]{1,0:T(8,128)(2,1)} %add_convert_fusion.q_ref.k_ref.v_ref, bf16[1024,2304]{1,0:T(8,128)(2,1)} %add_convert_fusion.q_ref.k_ref.v_ref, bf16[1024,2304]{1,0:T(8,128)(2,1)} %add_convert_fusion.q_ref.k_ref.v_ref, bf16[1024,768]{1,0:T(8,128)(2,1)} %convolution_convert_fusion.do_ref, ...), custom_call_target="tpu_custom_call" | custom-call | flops 4026531840 | bytes 11010048 | tf_op jit(solution)/shard_map/pallas_call | solution.py:137
  270.7 9.5 %fusion.28 = (f32[768]{0:T(1024)S(1)}, f32[1024]{0:T(1024)S(1)}, f32[1024]{0:T(1024)S(1)}, f32[768]{0:T(1024)S(1)}, f32[1024,768]{1,0:T(8,128)}) fusion(bf16[1024,768]{1,0:T(8,128)(2,1)S(1)} %copy-done.4, f32[1024]{0:T(1024)S(1)} %add_rsqrt_fusion.1, f32[1024]{0:T(1024)S(1)} %broadcast_multiply_fusion.5, f32[768]{0:T(1024)S(1)} %reshape.234, ...), kind=kOutput, calls=%fused_computation.47 | convolution fusion | flops 3631739392 | bytes 13001728 | tf_op jit(solution)/shard_map/te,de->td/dot_general | solution.py:532
  280.1 0.1 reshape.218
  280.2 3.3 convert_reduce_fusion.1
  283.5 0.1 concatenate.27
  283.6 0.1 concatenate.28
  283.7 0.1 reshape.219
  283.8 0.1 concatenate.30
  284.0 3.5 fusion.31.refs_1_
  287.5 4.5 fusion.27.refs_4_
  292.1 6.2 %fusion.34.refs_0_ = f32[768,2304]{1,0:T(8,128)} fusion(bf16[1024,2304]{1,0:T(8,128)(2,1)S(1)} %bitcast.46, bf16[1024,768]{1,0:T(8,128)(2,1)S(1)} %copy-done.4, f32[768]{0:T(1024)S(1)} %copy-done.12, f32[768]{0:T(1024)S(1)} %reshape.234, f32[1024]{0:T(1024)S(1)} %add_rsqrt_fusion.1, f32[1024]{0:T(1024)S(1)} %broadcast_multiply_fusion.5), kind=kOutput, calls=%fused_computation.91 | convolution fusion | flops 3628597248 | bytes 13383680 | tf_op jit(solution)/shard_map/td,te->de/dot_general | solution.py:531
  298.4 7.7 %add_convert_fusion.1.refs_5_ = bf16[1024,768]{1,0:T(8,128)(2,1)S(1)} fusion(f32[1024,768]{1,0:T(8,128)S(1)} %copy-done.2, bf16[1024,3072]{1,0:T(8,128)(2,1)} %copy-done.15, bf16[3072,768]{1,0:T(8,128)(2,1)S(1)} %bitcast.56, f32[768]{0:T(1024)S(1)} %copy-done.14), kind=kOutput, calls=%fused_computation.53 | convolution fusion | flops 4834197504 | bytes 15731712 | tf_op jit(solution)/shard_map/dot_general | solution.py:505
  306.1 8.7 %fusion.37.refs_2_ = f32[768,3072]{1,0:T(8,128)} fusion(bf16[1024,3072]{1,0:T(8,128)(2,1)S(1)} %bitcast.48, f32[1024,768]{1,0:T(8,128)S(1)} %copy-done.2, f32[768]{0:T(1024)S(1)} %reshape.238, f32[768]{0:T(1024)S(1)} %reshape.237, f32[1024]{0:T(1024)S(1)} %add_rsqrt_fusion, f32[1024]{0:T(1024)S(1)} %broadcast_multiply_fusion.4), kind=kOutput, calls=%fused_computation.92 | convolution fusion | flops 4835770368 | bytes 18888704 | tf_op jit(solution)/shard_map/td,tf->df/dot_general | solution.py:517
  314.7 129.5 %shard_map.266 = (f32[24,2304]{1,0:T(8,128)S(1)}, f32[24,768]{1,0:T(8,128)S(1)}, f32[24,3072]{1,0:T(8,128)S(1)}, f32[8,128]{1,0:T(8,128)S(1)}) custom-call(f32[768,2304]{1,0:T(8,128)} %fusion.34.refs_0_, f32[768,768]{1,0:T(8,128)S(1)} %fusion.31.refs_1_, f32[768,3072]{1,0:T(8,128)} %fusion.37.refs_2_, f32[256,128]{1,0:T(8,128)S(1)} %reshape.224.refs_3_, ...), custom_call_target="tpu_custom_call" | custom-call | flops 4751360 | bytes 38010880 | tf_op jit(solution)/shard_map/pallas_call | solution.py:303
  444.3 0.6 slice_bitcast_fusion.1
  444.8 0.5 slice_bitcast_fusion.7
  445.4 0.6 slice_bitcast_fusion
  446.0 0.7 copy.48
  446.6 0.6 copy.49
  447.3 0.7 copy.50
  (74 shorter events, 0.5 us)
Async XLA Ops:
  7.2 15.8 %copy-start.13 = (s32[2,512]{1,0:T(2,128)S(1)}, s32[2,512]{1,0:T(2,128)}, u32[]{:S(2)}) copy-start(s32[2,512]{1,0:T(2,128)} %param.29) | copy-start | bytes 12292
  7.2 15.0 %copy-start.10 = (bf16[24,3072]{1,0:T(8,128)(2,1)S(1)}, bf16[24,3072]{1,0:T(8,128)(2,1)}, u32[]{:S(2)}) copy-start(bf16[24,3072]{1,0:T(8,128)(2,1)} %param.25) | copy-start | bytes 442372
  7.2 98.2 %all-gather.7.cloned.1.call-start = ((), (), s32[]{:S(2)}) async-start(), calls=%async_computation.3 | async-start | bytes 6082560 | tf_op jit(solution)/shard_map/all_gather | solution.py:463
  15.1 186.9 %all-gather.5.cloned.1.call-start = ((), (), s32[]{:S(2)}) async-start(), calls=%async_computation.1 | async-start | bytes 4866048 | tf_op jit(solution)/shard_map/all_gather | solution.py:477
  15.9 430.1 %reduce-scatter.2.cloned.1.call-start = ((), (), s32[]{:S(2)}) async-start(), calls=%async_computation.2 | async-start | bytes 9732096 | tf_op jit(solution)/shard_map/reduce_scatter | solution.py:548
  105.4 2.6 slice-start.4
  108.0 3.9 copy-start.11
  109.5 4.2 copy-start.3
  111.8 1.8 copy-start.6
  153.4 72.9 %copy-start.1 = (f32[1024,768]{1,0:T(8,128)}, f32[1024,768]{1,0:T(8,128)S(1)}, u32[]{:S(2)}) copy-start(f32[1024,768]{1,0:T(8,128)S(1)} %get-tuple-element.56) | copy-start | bytes 9437188
  153.9 40.3 %copy-start.8 = (bf16[1024,768]{1,0:T(8,128)(2,1)S(1)}, bf16[1024,768]{1,0:T(8,128)(2,1)}, u32[]{:S(2)}) copy-start(bf16[1024,768]{1,0:T(8,128)(2,1)} %param.31) | copy-start | bytes 4718596
  191.6 2.6 copy-start.15
  216.6 9.7 %copy-start.9 = (bf16[1024,768]{1,0:T(8,128)(2,1)S(1)}, bf16[1024,768]{1,0:T(8,128)(2,1)}, u32[]{:S(2)}) copy-start(bf16[1024,768]{1,0:T(8,128)(2,1)} %param.31) | copy-start | bytes 4718596
  234.3 36.4 %copy-start.4 = (bf16[1024,768]{1,0:T(8,128)(2,1)S(1)}, bf16[1024,768]{1,0:T(8,128)(2,1)}, u32[]{:S(2)}) copy-start(bf16[1024,768]{1,0:T(8,128)(2,1)} %param.16) | copy-start | bytes 4718596
  280.1 3.8 copy-start.7
  284.0 3.5 copy-start.5
  284.0 8.1 %slice-start = ((s8[4718592]{0:T(1024)(128)(4,1)}), s8[4194304]{0:T(1024)(128)(4,1)S(1)}, s32[]{:S(2)}) async-start(s8[4718592]{0:T(1024)(128)(4,1)} %bitcast.45), calls=%async_computation.4 | async-start | bytes 8388608
  284.0 14.3 %slice-start.5 = ((s8[4718592]{0:T(1024)(128)(4,1)}), s8[4194304]{0:T(1024)(128)(4,1)S(1)}, s32[]{:S(2)}) async-start(s8[4718592]{0:T(1024)(128)(4,1)} %bitcast.55), calls=%async_computation.9 | async-start | bytes 8388608
  287.5 4.5 slice-start.1
  287.5 4.5 copy-start.12
  287.5 10.8 %slice-start.6 = ((s8[4718592]{0:T(1024)(128)(4,1)}), s8[524288]{0:T(1024)(128)(4,1)S(1)}, s32[]{:S(2)}) async-start(s8[4718592]{0:T(1024)(128)(4,1)} %bitcast.55), calls=%async_computation.10 | async-start | bytes 1048576
  292.1 6.3 %copy-start.2 = (f32[1024,768]{1,0:T(8,128)S(1)}, f32[1024,768]{1,0:T(8,128)}, u32[]{:S(2)}) copy-start(f32[1024,768]{1,0:T(8,128)} %copy-done.1) | copy-start | bytes 9437188
  292.1 6.2 %copy-start.14 = (f32[768]{0:T(1024)S(1)}, f32[768]{0:T(1024)}, u32[]{:S(2)}) copy-start(f32[768]{0:T(1024)} %reshape.240) | copy-start | bytes 9220
  292.1 13.9 %slice-start.2 = ((s8[6291456]{0:T(1024)(128)(4,1)}), s8[4194304]{0:T(1024)(128)(4,1)S(1)}, s32[]{:S(2)}) async-start(s8[6291456]{0:T(1024)(128)(4,1)} %bitcast.47), calls=%async_computation.6 | async-start | bytes 8388608
  298.3 7.7 %slice-start.3 = ((s8[6291456]{0:T(1024)(128)(4,1)}), s8[2097152]{0:T(1024)(128)(4,1)S(1)}, s32[]{:S(2)}) async-start(s8[6291456]{0:T(1024)(128)(4,1)} %bitcast.47), calls=%async_computation.7 | async-start | bytes 4194304
  306.0 8.7 %copy-start = (bf16[1024,768]{1,0:T(8,128)(2,1)}, bf16[1024,768]{1,0:T(8,128)(2,1)S(1)}, u32[]{:S(2)}) copy-start(bf16[1024,768]{1,0:T(8,128)(2,1)S(1)} %add_convert_fusion.1.refs_5_) | copy-start | bytes 4718596
Sparse Core Ops, SparseCore 0:
  15.3 75.1 all-gather.6
  93.4 65.2 all-gather.4
  202.1 136.7 reduce-scatter.1
